TPU v7x, 32 devices: a whole 2x2x4 slice. The times are simulated.
32 devices in a mesh: dp: 8 (over y, x, core), fsdp: 4 (over z).
Axes of the slice: x: 2, y: 2, z: 4, core: 2. Of those that a mesh axis runs over, the one named last changes fastest.
Arguments:
- images: bfloat16 [64, 256, 1152], P(('dp', 'fsdp')), may hold values from -6 to 6
- time_vector: bfloat16 [64, 1152], P(('dp', 'fsdp')), may hold values from -6 to 6
- timesteps: int32 [64], P(('dp', 'fsdp')), may hold values from 0 to 999
- offset_index: int32 [256, 256], replicated, may hold values from 0 to 960
- query_weight: bfloat16 [1152, 1152], P('dp', 'fsdp'), may hold values from -0.1875 to 0.1875
- key_weight: bfloat16 [1152, 1152], P('dp', 'fsdp'), may hold values from -0.1875 to 0.1875
- value_weight: bfloat16 [1152, 1152], P('dp', 'fsdp'), may hold values from -0.1875 to 0.1875
- tquery_weight: bfloat16 [1152, 1152], P('dp', 'fsdp'), may hold values from -0.1875 to 0.1875
- tvalue_weight: bfloat16 [1152, 1152], P('dp', 'fsdp'), may hold values from -0.1875 to 0.1875
- proj_weight: bfloat16 [1152, 1152], P('dp', 'fsdp'), may hold values from -0.5 to 0.5
- proj_bias: bfloat16 [1152], P('fsdp'), may hold values from -4 to 4
- first_gain: bfloat16 [1152], P('fsdp'), may hold values from 0.5 to 1.5
- first_shift: bfloat16 [1152], P('fsdp'), may hold values from -4 to 4
- second_gain: bfloat16 [1152], P('fsdp'), may hold values from 0.5 to 1.5
- second_shift: bfloat16 [1152], P('fsdp'), may hold values from -4 to 4
- up_weight: bfloat16 [1152, 4608], P('dp', 'fsdp'), may hold values from -0.1875 to 0.1875
- down_weight: bfloat16 [4608, 1152], P('dp', 'fsdp'), may hold values from -0.125 to 0.125
- up_bias: bfloat16 [4608], P('fsdp'), may hold values from -6 to 6
- down_bias: bfloat16 [1152], P('fsdp'), may hold values from -4 to 4
- bias_table: bfloat16 [16, 961], P('fsdp'), may hold values from -6 to 6
- cotangent: bfloat16 [64, 256, 1152], P(('dp', 'fsdp')), may hold values from -6 to 6
Outputs:
- layer_out: bfloat16 [64, 256, 1152], P(('dp', 'fsdp'))
- images_grad: bfloat16 [64, 256, 1152], P(('dp', 'fsdp'))
- time_grad: float32 [64, 1152], P(('dp', 'fsdp'))
- query_grad: float32 [1152, 1152], P('dp', 'fsdp')
- key_grad: float32 [1152, 1152], P('dp', 'fsdp')
- value_grad: float32 [1152, 1152], P('dp', 'fsdp')
- tquery_grad: float32 [1152, 1152], P('dp', 'fsdp')
- tvalue_grad: float32 [1152, 1152], P('dp', 'fsdp')
- proj_grad: float32 [1152, 1152], P('dp', 'fsdp')
- proj_bias_grad: float32 [1152], P('fsdp')
- first_gain_grad: float32 [1152], P('fsdp')
- first_shift_grad: float32 [1152], P('fsdp')
- second_gain_grad: float32 [1152], P('fsdp')
- second_shift_grad: float32 [1152], P('fsdp')
- up_grad: float32 [1152, 4608], P('dp', 'fsdp')
- down_grad: float32 [4608, 1152], P('dp', 'fsdp')
- up_bias_grad: float32 [4608], P('fsdp')
- down_bias_grad: float32 [1152], P('fsdp')
- table_grad: float32 [16, 961], P('fsdp')
All inputs are finite; a program needn't handle non-finite values.
Results may differ from a plain program's by a relative error of at most 0.017.
Values may be sent and summed in bfloat16 or wider, within the bound.
No kernel may reach another device: no remote copies, remote signals or barrier semaphores. Data moves between devices by JAX's collectives and lax.ppermute only.
A program may use at most 384 MiB of HBM per device.

v0:
```python
import math

import jax
import jax.numpy as jnp
from jax import lax
from jax.sharding import PartitionSpec as P

MB = 2


def sinusoid(steps, model_width):
    half_width = model_width // 2
    frequency = jnp.exp(
        -math.log(10000.0) * jnp.arange(half_width).astype(jnp.float32) / half_width
    )
    angles = steps.astype(jnp.float32)[:, None] * frequency[None, :]
    return jnp.concatenate([jnp.sin(angles), jnp.cos(angles)], axis=1)


def matmul(left, right):
    return jnp.dot(left, right, preferred_element_type=jnp.float32)


def contract_rows(left, right):
    return lax.dot_general(
        left, right, (((0,), (0,)), ((), ())), preferred_element_type=jnp.float32
    )


def times_transposed(left, right):
    return lax.dot_general(
        left, right, (((1,), (1,)), ((), ())), preferred_element_type=jnp.float32
    )


def normalize(values, gain, shift):
    row_mean = jnp.mean(values, axis=-1, keepdims=True)
    centered = values - row_mean
    inv_std = lax.rsqrt(jnp.mean(centered * centered, axis=-1, keepdims=True) + 1e-06)
    unit_rows = centered * inv_std
    return (unit_rows * gain + shift, unit_rows, inv_std)


def norm_back(grad_rows, unit_rows, inv_std, gain):
    scaled = grad_rows * gain
    return inv_std * (
        scaled
        - jnp.mean(scaled, axis=-1, keepdims=True)
        - unit_rows * jnp.mean(scaled * unit_rows, axis=-1, keepdims=True)
    )


def gelu_slope(pre_act):
    return 0.5 * (1.0 + lax.erf(pre_act * (1.0 / math.sqrt(2.0)))) + pre_act * jnp.exp(
        -0.5 * pre_act * pre_act
    ) * (1.0 / math.sqrt(2.0 * math.pi))


def gather_attention(shards):
    (
        query_weight,
        key_weight,
        value_weight,
        tquery_weight,
        tvalue_weight,
        proj_weight,
        first_gain,
        first_shift,
        proj_bias,
        bias_table,
    ) = (
        lax.all_gather(shards[0], "fsdp", axis=1, tiled=True),
        lax.all_gather(shards[1], "fsdp", axis=1, tiled=True),
        lax.all_gather(shards[2], "fsdp", axis=1, tiled=True),
        lax.all_gather(shards[3], "fsdp", axis=1, tiled=True),
        lax.all_gather(shards[4], "fsdp", axis=1, tiled=True),
        lax.all_gather(shards[5], "fsdp", axis=1, tiled=True),
        lax.all_gather(shards[6], "fsdp", axis=0, tiled=True),
        lax.all_gather(shards[7], "fsdp", axis=0, tiled=True),
        lax.all_gather(shards[8], "fsdp", axis=0, tiled=True),
        lax.all_gather(shards[9], "fsdp", axis=0, tiled=True),
    )
    query_weight, key_weight, value_weight, tquery_weight, tvalue_weight, proj_weight = (
        lax.all_gather(query_weight, "dp", axis=0, tiled=True),
        lax.all_gather(key_weight, "dp", axis=0, tiled=True),
        lax.all_gather(value_weight, "dp", axis=0, tiled=True),
        lax.all_gather(tquery_weight, "dp", axis=0, tiled=True),
        lax.all_gather(tvalue_weight, "dp", axis=0, tiled=True),
        lax.all_gather(proj_weight, "dp", axis=0, tiled=True),
    )
    return (
        query_weight,
        key_weight,
        value_weight,
        tquery_weight,
        tvalue_weight,
        proj_weight,
        first_gain,
        first_shift,
        proj_bias,
        bias_table,
    )


def gather_mlp(shards):
    up_weight, down_weight, second_gain, second_shift, up_bias, down_bias = (
        lax.all_gather(shards[0], "fsdp", axis=1, tiled=True),
        lax.all_gather(shards[1], "fsdp", axis=1, tiled=True),
        lax.all_gather(shards[2], "fsdp", axis=0, tiled=True),
        lax.all_gather(shards[3], "fsdp", axis=0, tiled=True),
        lax.all_gather(shards[4], "fsdp", axis=0, tiled=True),
        lax.all_gather(shards[5], "fsdp", axis=0, tiled=True),
    )
    up_weight, down_weight = (
        lax.all_gather(up_weight, "dp", axis=0, tiled=True),
        lax.all_gather(down_weight, "dp", axis=0, tiled=True),
    )
    return (up_weight, down_weight, second_gain, second_shift, up_bias, down_bias)


def body(
    images,
    time_vector,
    timesteps,
    offset_index,
    query_weight,
    key_weight,
    value_weight,
    tquery_weight,
    tvalue_weight,
    proj_weight,
    proj_bias,
    first_gain,
    first_shift,
    second_gain,
    second_shift,
    up_weight,
    down_weight,
    up_bias,
    down_bias,
    bias_table,
    cotangent,
):
    img_dev, tokens, model_width = images.shape
    img_mb = img_dev // MB
    row_count = img_mb * tokens
    narrow_size = lax.axis_size("fsdp")
    head_count = bias_table.shape[0] * narrow_size
    head_dim = model_width // head_count
    table_rows = bias_table.shape[1]
    hidden_width = up_weight.shape[1] * narrow_size
    score_scale = 1.0 / math.sqrt(head_dim)
    split_shape = (img_mb, tokens, head_count, head_dim)
    flat_index = offset_index.reshape(-1)
    attn_kept = gather_attention(
        (
            query_weight,
            key_weight,
            value_weight,
            tquery_weight,
            tvalue_weight,
            proj_weight,
            first_gain,
            first_shift,
            proj_bias,
            bias_table,
        )
    )
    mlp_kept = gather_mlp((up_weight, down_weight, second_gain, second_shift, up_bias, down_bias))
    vector = jnp.zeros((model_width,), jnp.float32)
    totals = {
        "proj_bias": vector,
        "first_gain": vector,
        "first_shift": vector,
        "second_gain": vector,
        "second_shift": vector,
        "up_b": jnp.zeros((hidden_width,), jnp.float32),
        "down_b": vector,
        "pairs": jnp.zeros((head_count, tokens * tokens), jnp.float32),
    }
    saved = {
        "normed": [],
        "mixed": [],
        "second": [],
        "activ": [],
        "time": [],
        "query": [],
        "keys": [],
        "values": [],
        "hidden": [],
        "grad": [],
        "pre": [],
        "tquery": [],
        "tvalue": [],
    }
    out_parts = []
    input_parts = []
    time_parts = []
    (
        query_full,
        key_full,
        value_full,
        tquery_full,
        tvalue_full,
        proj_full,
        gain_one,
        shift_one,
        proj_bias_full,
        table_full,
    ) = attn_kept
    up_full, down_full, gain_two, shift_two, up_bias_full, down_bias_full = mlp_kept
    bias_rows = table_full.astype(jnp.float32)[:, offset_index]
    gain_first = gain_one.astype(jnp.float32)
    shift_first = shift_one.astype(jnp.float32)
    gain_second = gain_two.astype(jnp.float32)
    shift_second = shift_two.astype(jnp.float32)
    for micro in range(MB):
        first_img = micro * img_mb
        batch_rows = images[first_img : first_img + img_mb]
        x_rows = batch_rows.reshape(row_count, model_width).astype(jnp.float32)
        time_rows = time_vector[first_img : first_img + img_mb].astype(jnp.float32) + sinusoid(
            timesteps[first_img : first_img + img_mb], model_width
        )
        time_low = time_rows.astype(jnp.bfloat16)
        normed, unit_one, inv_one = normalize(x_rows, gain_first, shift_first)
        normed_low = normed.astype(jnp.bfloat16)
        time_query = matmul(time_low, tquery_full)
        time_value = matmul(time_low, tvalue_full)
        query = (
            (
                matmul(normed_low, query_full).reshape(img_mb, tokens, model_width)
                + time_query[:, None, :]
            )
            .astype(jnp.bfloat16)
            .reshape(split_shape)
        )
        keys = matmul(normed_low, key_full).astype(jnp.bfloat16).reshape(split_shape)
        values = (
            (
                matmul(normed_low, value_full).reshape(img_mb, tokens, model_width)
                + time_value[:, None, :]
            )
            .astype(jnp.bfloat16)
            .reshape(split_shape)
        )
        scores = (
            jnp.einsum("bqhd,bkhd->bhqk", query, keys, preferred_element_type=jnp.float32)
            * score_scale
            + bias_rows[None]
        )
        peak = jnp.max(scores, axis=-1, keepdims=True)
        expo = jnp.exp(scores - peak)
        total = jnp.sum(expo, axis=-1, keepdims=True)
        log_total = peak + jnp.log(total)
        probs_low = (expo / total).astype(jnp.bfloat16)
        mixed_low = (
            jnp.einsum("bhqk,bkhd->bqhd", probs_low, values, preferred_element_type=jnp.float32)
            .reshape(row_count, model_width)
            .astype(jnp.bfloat16)
        )
        hidden = x_rows + (matmul(mixed_low, proj_full) + proj_bias_full.astype(jnp.float32))
        second, unit_two, inv_two = normalize(hidden, gain_second, shift_second)
        second_low = second.astype(jnp.bfloat16)
        pre_act = matmul(second_low, up_full) + up_bias_full.astype(jnp.float32)
        activ_low = jax.nn.gelu(pre_act, approximate=False).astype(jnp.bfloat16)
        result = hidden + (matmul(activ_low, down_full) + down_bias_full.astype(jnp.float32))
        out_parts.append(result.astype(jnp.bfloat16).reshape(img_mb, tokens, model_width))
        up_back, down_back = (up_full, down_full)
        query_back, key_back, value_back, tquery_back, tvalue_back, proj_back = (
            query_full,
            key_full,
            value_full,
            tquery_full,
            tvalue_full,
            proj_full,
        )
        gain_first_back, gain_second_back = (gain_first, gain_second)
        grad_low = cotangent[first_img : first_img + img_mb].reshape(row_count, model_width)
        grad_rows = grad_low.astype(jnp.float32)
        totals["down_b"] = totals["down_b"] + jnp.sum(grad_rows, axis=0)
        d_pre = (times_transposed(grad_low, down_back) * gelu_slope(pre_act)).astype(jnp.bfloat16)
        totals["up_b"] = totals["up_b"] + jnp.sum(d_pre.astype(jnp.float32), axis=0)
        d_second = times_transposed(d_pre, up_back)
        totals["second_gain"] = totals["second_gain"] + jnp.sum(d_second * unit_two, axis=0)
        totals["second_shift"] = totals["second_shift"] + jnp.sum(d_second, axis=0)
        d_hidden = grad_rows + norm_back(d_second, unit_two, inv_two, gain_second_back)
        d_hidden_low = d_hidden.astype(jnp.bfloat16)
        totals["proj_bias"] = totals["proj_bias"] + jnp.sum(
            d_hidden_low.astype(jnp.float32), axis=0
        )
        d_mixed = (
            times_transposed(d_hidden_low, proj_back).astype(jnp.bfloat16).reshape(split_shape)
        )
        again_scores = (
            jnp.einsum("bqhd,bkhd->bhqk", query, keys, preferred_element_type=jnp.float32)
            * score_scale
            + bias_rows[None]
        )
        probs = jnp.exp(again_scores - log_total)
        probs_again = probs.astype(jnp.bfloat16)
        d_values = jnp.einsum(
            "bhqk,bqhd->bkhd", probs_again, d_mixed, preferred_element_type=jnp.float32
        ).astype(jnp.bfloat16)
        d_probs = jnp.einsum("bqhd,bkhd->bhqk", d_mixed, values, preferred_element_type=jnp.float32)
        d_scores = (probs * (d_probs - jnp.sum(probs * d_probs, axis=-1, keepdims=True))).astype(
            jnp.bfloat16
        )
        totals["pairs"] = totals["pairs"] + jnp.sum(d_scores.astype(jnp.float32), axis=0).reshape(
            head_count, tokens * tokens
        )
        d_query = (
            jnp.einsum("bhqk,bkhd->bqhd", d_scores, keys, preferred_element_type=jnp.float32)
            * score_scale
        ).astype(jnp.bfloat16)
        d_keys = (
            jnp.einsum("bhqk,bqhd->bkhd", d_scores, query, preferred_element_type=jnp.float32)
            * score_scale
        ).astype(jnp.bfloat16)
        d_query = d_query.reshape(row_count, model_width)
        d_keys = d_keys.reshape(row_count, model_width)
        d_values = d_values.reshape(row_count, model_width)
        d_tquery = jnp.sum(
            d_query.reshape(img_mb, tokens, model_width).astype(jnp.float32), axis=1
        ).astype(jnp.bfloat16)
        d_tvalue = jnp.sum(
            d_values.reshape(img_mb, tokens, model_width).astype(jnp.float32), axis=1
        ).astype(jnp.bfloat16)
        time_parts.append(
            times_transposed(d_tquery, tquery_back) + times_transposed(d_tvalue, tvalue_back)
        )
        d_normed = (
            times_transposed(d_query, query_back)
            + times_transposed(d_keys, key_back)
            + times_transposed(d_values, value_back)
        )
        totals["first_gain"] = totals["first_gain"] + jnp.sum(d_normed * unit_one, axis=0)
        totals["first_shift"] = totals["first_shift"] + jnp.sum(d_normed, axis=0)
        d_input = d_hidden + norm_back(d_normed, unit_one, inv_one, gain_first_back)
        input_parts.append(d_input.astype(jnp.bfloat16).reshape(img_mb, tokens, model_width))
        saved["normed"].append(normed_low)
        saved["mixed"].append(mixed_low)
        saved["second"].append(second_low)
        saved["activ"].append(activ_low)
        saved["time"].append(time_low)
        saved["query"].append(d_query)
        saved["keys"].append(d_keys)
        saved["values"].append(d_values)
        saved["hidden"].append(d_hidden_low)
        saved["grad"].append(grad_low)
        saved["pre"].append(d_pre)
        saved["tquery"].append(d_tquery)
        saved["tvalue"].append(d_tvalue)
    joined = {name: jnp.concatenate(parts, axis=0) for name, parts in saved.items()}
    left_normed, left_mixed, left_second, left_activ, left_time = (
        joined["normed"],
        joined["mixed"],
        joined["second"],
        joined["activ"],
        joined["time"],
    )
    (
        cols_query,
        cols_keys,
        cols_values,
        cols_hidden,
        cols_grad,
        cols_pre,
        cols_tquery,
        cols_tvalue,
    ) = (
        joined["query"],
        joined["keys"],
        joined["values"],
        joined["hidden"],
        joined["grad"],
        joined["pre"],
        joined["tquery"],
        joined["tvalue"],
    )
    grad_query = contract_rows(left_normed, cols_query)
    grad_keys = contract_rows(left_normed, cols_keys)
    grad_values = contract_rows(left_normed, cols_values)
    grad_proj = contract_rows(left_mixed, cols_hidden)
    grad_up = contract_rows(left_second, cols_pre)
    grad_down = contract_rows(left_activ, cols_grad)
    grad_tquery = contract_rows(left_time, cols_tquery)
    grad_tvalue = contract_rows(left_time, cols_tvalue)
    table_total = jax.ops.segment_sum(totals["pairs"].T, flat_index, num_segments=table_rows).T
    (
        query_grad,
        key_grad,
        value_grad,
        tquery_grad,
        tvalue_grad,
        proj_grad,
        up_grad,
        down_grad,
        first_gain_grad,
        first_shift_grad,
        proj_bias_grad,
        table_grad,
        second_gain_grad,
        second_shift_grad,
        up_bias_grad,
        down_bias_grad,
    ) = (
        lax.psum_scatter(
            grad_query.astype(jnp.bfloat16), "fsdp", scatter_dimension=1, tiled=True
        ).astype(jnp.float32),
        lax.psum_scatter(
            grad_keys.astype(jnp.bfloat16), "fsdp", scatter_dimension=1, tiled=True
        ).astype(jnp.float32),
        lax.psum_scatter(
            grad_values.astype(jnp.bfloat16), "fsdp", scatter_dimension=1, tiled=True
        ).astype(jnp.float32),
        lax.psum_scatter(
            grad_tquery.astype(jnp.bfloat16), "fsdp", scatter_dimension=1, tiled=True
        ).astype(jnp.float32),
        lax.psum_scatter(
            grad_tvalue.astype(jnp.bfloat16), "fsdp", scatter_dimension=1, tiled=True
        ).astype(jnp.float32),
        lax.psum_scatter(
            grad_proj.astype(jnp.bfloat16), "fsdp", scatter_dimension=1, tiled=True
        ).astype(jnp.float32),
        lax.psum_scatter(
            grad_up.astype(jnp.bfloat16), "fsdp", scatter_dimension=1, tiled=True
        ).astype(jnp.float32),
        lax.psum_scatter(
            grad_down.astype(jnp.bfloat16), "fsdp", scatter_dimension=1, tiled=True
        ).astype(jnp.float32),
        lax.psum_scatter(
            totals["first_gain"].astype(jnp.bfloat16), "fsdp", scatter_dimension=0, tiled=True
        ).astype(jnp.float32),
        lax.psum_scatter(
            totals["first_shift"].astype(jnp.bfloat16), "fsdp", scatter_dimension=0, tiled=True
        ).astype(jnp.float32),
        lax.psum_scatter(
            totals["proj_bias"].astype(jnp.bfloat16), "fsdp", scatter_dimension=0, tiled=True
        ).astype(jnp.float32),
        lax.psum_scatter(
            table_total.astype(jnp.bfloat16), "fsdp", scatter_dimension=0, tiled=True
        ).astype(jnp.float32),
        lax.psum_scatter(
            totals["second_gain"].astype(jnp.bfloat16), "fsdp", scatter_dimension=0, tiled=True
        ).astype(jnp.float32),
        lax.psum_scatter(
            totals["second_shift"].astype(jnp.bfloat16), "fsdp", scatter_dimension=0, tiled=True
        ).astype(jnp.float32),
        lax.psum_scatter(
            totals["up_b"].astype(jnp.bfloat16), "fsdp", scatter_dimension=0, tiled=True
        ).astype(jnp.float32),
        lax.psum_scatter(
            totals["down_b"].astype(jnp.bfloat16), "fsdp", scatter_dimension=0, tiled=True
        ).astype(jnp.float32),
    )
    query_grad, key_grad, value_grad, tquery_grad, tvalue_grad, proj_grad, up_grad, down_grad = (
        lax.psum_scatter(query_grad, "dp", scatter_dimension=0, tiled=True),
        lax.psum_scatter(key_grad, "dp", scatter_dimension=0, tiled=True),
        lax.psum_scatter(value_grad, "dp", scatter_dimension=0, tiled=True),
        lax.psum_scatter(tquery_grad, "dp", scatter_dimension=0, tiled=True),
        lax.psum_scatter(tvalue_grad, "dp", scatter_dimension=0, tiled=True),
        lax.psum_scatter(proj_grad, "dp", scatter_dimension=0, tiled=True),
        lax.psum_scatter(up_grad, "dp", scatter_dimension=0, tiled=True),
        lax.psum_scatter(down_grad, "dp", scatter_dimension=0, tiled=True),
    )
    (
        first_gain_grad,
        first_shift_grad,
        proj_bias_grad,
        table_grad,
        second_gain_grad,
        second_shift_grad,
        up_bias_grad,
        down_bias_grad,
    ) = lax.psum(
        (
            first_gain_grad,
            first_shift_grad,
            proj_bias_grad,
            table_grad,
            second_gain_grad,
            second_shift_grad,
            up_bias_grad,
            down_bias_grad,
        ),
        "dp",
    )
    layer_out = jnp.concatenate(out_parts, axis=0)
    images_grad = jnp.concatenate(input_parts, axis=0)
    time_grad = jnp.concatenate(time_parts, axis=0)
    return (
        layer_out,
        images_grad,
        time_grad,
        query_grad,
        key_grad,
        value_grad,
        tquery_grad,
        tvalue_grad,
        proj_grad,
        proj_bias_grad,
        first_gain_grad,
        first_shift_grad,
        second_gain_grad,
        second_shift_grad,
        up_grad,
        down_grad,
        up_bias_grad,
        down_bias_grad,
        table_grad,
    )


def solution(mesh):
    return jax.shard_map(
        body,
        mesh=mesh,
        in_specs=(
            P(("dp", "fsdp"), None, None),
            P(("dp", "fsdp"), None),
            P(("dp", "fsdp")),
            P(),
            P("dp", "fsdp"),
            P("dp", "fsdp"),
            P("dp", "fsdp"),
            P("dp", "fsdp"),
            P("dp", "fsdp"),
            P("dp", "fsdp"),
            P("fsdp"),
            P("fsdp"),
            P("fsdp"),
            P("fsdp"),
            P("fsdp"),
            P("dp", "fsdp"),
            P("dp", "fsdp"),
            P("fsdp"),
            P("fsdp"),
            P("fsdp", None),
            P(("dp", "fsdp"), None, None),
        ),
        out_specs=(
            P(("dp", "fsdp"), None, None),
            P(("dp", "fsdp"), None, None),
            P(("dp", "fsdp"), None),
            P("dp", "fsdp"),
            P("dp", "fsdp"),
            P("dp", "fsdp"),
            P("dp", "fsdp"),
            P("dp", "fsdp"),
            P("dp", "fsdp"),
            P("fsdp"),
            P("fsdp"),
            P("fsdp"),
            P("fsdp"),
            P("fsdp"),
            P("dp", "fsdp"),
            P("dp", "fsdp"),
            P("fsdp"),
            P("fsdp"),
            P("fsdp", None),
        ),
        check_vma=False,
    )
```

profile of v0, /device:TPU:0, one launch (start us, length us, event | category | flops | bytes accessed | tf_op | source)
XLA Modules:
  0.0 1675.9 jit_solution(1254166128935327157)
XLA Ops:
  8.7 18.4 %all-gather.1 = bf16[4,288,144]{1,2,0:T(8,128)(2,1)S(1)} all-gather(bf16[1,288,144]{1,2,0:T(8,128)(2,1)} %bitcast.354), channel_id=1, replica_groups=mesh['dp'=8,'fsdp'=4] {'fsdp'}, dimensions={0}, use_global_device_ids=true | all-gather | bytes 414720 | tf_op jit(solution)/shard_map/all_gather | solution.py:76
  28.5 21.7 %all-gather = bf16[4,288,144]{1,2,0:T(8,128)(2,1)S(1)} all-gather(bf16[1,288,144]{1,2,0:T(8,128)(2,1)S(1)} %bitcast.355), channel_id=1, replica_groups=mesh['dp'=8,'fsdp'=4] {'fsdp'}, dimensions={0}, use_global_device_ids=true | all-gather | bytes 414720 | tf_op jit(solution)/shard_map/all_gather | solution.py:74
  51.4 15.7 all-gather.3
  68.4 18.8 %all-gather.2 = bf16[4,288,144]{1,2,0:T(8,128)(2,1)S(1)} all-gather(bf16[1,288,144]{1,2,0:T(8,128)(2,1)S(1)} %bitcast.357), channel_id=1, replica_groups=mesh['dp'=8,'fsdp'=4] {'fsdp'}, dimensions={0}, use_global_device_ids=true | all-gather | bytes 414720 | tf_op jit(solution)/shard_map/all_gather | solution.py:72
  88.5 17.8 %all-gather.4 = bf16[4,288,144]{1,2,0:T(8,128)(2,1)S(1)} all-gather(bf16[1,288,144]{1,2,0:T(8,128)(2,1)S(1)} %bitcast.358), channel_id=1, replica_groups=mesh['dp'=8,'fsdp'=4] {'fsdp'}, dimensions={0}, use_global_device_ids=true | all-gather | bytes 414720 | tf_op jit(solution)/shard_map/all_gather | solution.py:73
  107.6 14.6 all-gather.6
  126.8 17.7 %all-reduce.16 = (bf16[1152]{0:T(1024)(128)(2,1)S(1)}, bf16[1152]{0:T(1024)(128)(2,1)S(1)}, bf16[1152]{0:T(1024)(128)(2,1)S(1)}, bf16[1152]{0:T(1024)(128)(2,1)S(1)}, bf16[1152]{0:T(1024)(128)(2,1)S(1)}) all-reduce(bf16[1152]{0:T(1024)(128)(2,1)S(1)} %dynamic-update-slice.1, ...), channel_id=1, replica_groups=mesh['dp'=8,'fsdp'=4] {'fsdp'}, use_global_device_ids=true, to_apply=%add.1 | all-reduce | flops 5760 | bytes 23040
  146.5 13.1 all-gather.5
  160.1 215.9 %gather_fusion = f32[65536,16]{1,0:T(8,128)} fusion(f32[16,961]{0,1:T(8,128)S(1)} %copy.149, s32[65536]{0:T(1024)S(1)} %broadcast_clamp_fusion), kind=kCustom, calls=%fused_computation | custom fusion | bytes 8650752 | tf_op jit(solution)/shard_map/gather | solution.py:212
  376.0 20.1 %copy.151 = f32[256,256,16]{0,1,2:T(8,128)} copy(f32[256,256,16]{2,1,0:T(8,128)} %bitcast.312) | data formatting | bytes 8388608 | tf_op jit(solution)/shard_map/gather | solution.py:212
  396.2 13.2 all-gather.7
  411.8 2.7 copy.154
  420.4 3.0 fusion.48
  426.8 2.7 fusion.49
  429.8 4.0 convolution_convert_fusion.10
  437.7 3.0 fusion.46
  444.0 4.5 fusion.47
  450.6 2.9 convolution_convert_fusion.11
  454.8 3.4 fusion.159
  461.9 3.2 fusion.160
  473.6 17.0 %fusion.7 = (bf16[256,4608]{1,0:T(8,128)(2,1)S(1)}, f32[256,4608]{1,0:T(8,128)}) fusion(f32[4608]{0:T(1024)} %reshape.570, bf16[256,1152]{1,0:T(8,128)(2,1)S(1)} %get-tuple-element.166, bf16[1152,4608]{1,0:T(8,128)(2,1)} %all-gather.33.cloned.1.call-done), kind=kOutput, calls=%fused_computation.25 | convolution fusion | flops 2795765760 | bytes 18302976 | tf_op jit(solution)/shard_map/dot_general | solution.py:21
  490.7 14.5 fusion.4
  506.6 8.4 convolution_convert_fusion
  517.2 9.1 convert_reduce_fusion.1
  526.3 6.8 fusion.162
  533.2 8.0 convert_reduce_fusion
  541.2 9.3 multiply_reduce_fusion.2
  550.6 3.1 convert_reduce_fusion.2
  556.0 2.9 convolution_convert_fusion.9
  559.1 3.4 multiply_reduce_fusion
  564.9 3.7 convert_add_fusion
  571.6 3.2 convolution_convert_fusion.6
  574.9 2.7 fusion.79
  579.1 3.4 convolution_convert_fusion.5
  582.6 3.2 bitcast_reduce_fusion
  587.3 3.2 convolution_convert_fusion.4
  596.9 4.3 convolution_convert_fusion.7
  602.5 10.3 convolution_convert_fusion.1
  612.8 14.5 copy.198
  627.4 66.2 %reduce-scatter.48.cloned.1.call-done = bf16[4608,288]{0,1:T(8,128)(2,1)} async-done(((bf16[4608,1152]{0,1:T(8,128)(2,1)}), bf16[4608,288]{0,1:T(8,128)(2,1)}) %reduce-scatter.48.cloned.1.call-update) | async-done | bytes 2654224 | tf_op jit(solution)/shard_map/reduce_scatter | solution.py:428
  693.6 5.5 copy.200
  699.1 50.4 %reduce-scatter.34.cloned.1.call-done = bf16[1152,288]{0,1:T(8,128)(2,1)} async-done(((bf16[1152,1152]{0,1:T(8,128)(2,1)}), bf16[1152,288]{0,1:T(8,128)(2,1)}) %reduce-scatter.34.cloned.1.call-update) | async-done | bytes 663568 | tf_op jit(solution)/shard_map/reduce_scatter | solution.py:407
  752.3 52.0 %reduce-scatter.36.cloned.1.call-done = bf16[1152,288]{0,1:T(8,128)(2,1)} async-done(((bf16[1152,1152]{0,1:T(8,128)(2,1)}), bf16[1152,288]{0,1:T(8,128)(2,1)}) %reduce-scatter.36.cloned.1.call-update) | async-done | bytes 663568 | tf_op jit(solution)/shard_map/reduce_scatter | solution.py:410
  804.3 2.7 copy.188
  807.0 51.8 %reduce-scatter.38.cloned.1.call-done = bf16[1152,288]{0,1:T(8,128)(2,1)} async-done(((bf16[1152,1152]{0,1:T(8,128)(2,1)}), bf16[1152,288]{0,1:T(8,128)(2,1)}) %reduce-scatter.38.cloned.1.call-update) | async-done | bytes 663568 | tf_op jit(solution)/shard_map/reduce_scatter | solution.py:413
  858.8 2.7 copy.190
  861.6 51.8 %reduce-scatter.40.cloned.1.call-done = bf16[1152,288]{0,1:T(8,128)(2,1)} async-done(((bf16[1152,1152]{0,1:T(8,128)(2,1)}), bf16[1152,288]{0,1:T(8,128)(2,1)}) %reduce-scatter.40.cloned.1.call-update) | async-done | bytes 663568 | tf_op jit(solution)/shard_map/reduce_scatter | solution.py:416
  913.4 2.6 copy.192
  916.1 51.8 %reduce-scatter.42.cloned.1.call-done = bf16[1152,288]{0,1:T(8,128)(2,1)} async-done(((bf16[1152,1152]{0,1:T(8,128)(2,1)}), bf16[1152,288]{0,1:T(8,128)(2,1)}) %reduce-scatter.42.cloned.1.call-update) | async-done | bytes 663568 | tf_op jit(solution)/shard_map/reduce_scatter | solution.py:419
  972.9 49.5 %reduce-scatter.44.cloned.1.call-done = bf16[1152,288]{0,1:T(8,128)(2,1)} async-done(((bf16[1152,1152]{0,1:T(8,128)(2,1)}), bf16[1152,288]{0,1:T(8,128)(2,1)}) %reduce-scatter.44.cloned.1.call-update) | async-done | bytes 663568 | tf_op jit(solution)/shard_map/reduce_scatter | solution.py:422
  1022.5 2.6 copy.196
  1025.3 2.9 fusion.164
  1035.3 3.4 fusion.102
  1038.7 165.7 %reduce-scatter.62.cloned.1.call-done = bf16[1152,1152]{1,0:T(8,128)(2,1)} async-done(((bf16[4608,1152]{1,0:T(8,128)(2,1)}), bf16[1152,1152]{1,0:T(8,128)(2,1)}) %reduce-scatter.62.cloned.1.call-update) | async-done | bytes 2654224
  1204.4 4.1 copy.199
  1208.5 2.6 convert_element_type.487
  1212.3 5.5 copy.206
  1217.8 17.2 %copy.168 = f32[65536,16]{1,0:T(8,128)} copy(f32[65536,16]{0,1:T(8,128)} %bitcast.314) | data formatting | bytes 8388608 | tf_op jit(solution)/shard_map/transpose | solution.py:388
  1235.0 347.8 %scatter_custom_fusion = f32[961,16]{1,0:T(8,128)S(1)} fusion(s32[65536]{0:T(1024)S(1)} %bitcast.353, f32[65536,16]{1,0:T(8,128)} %copy.168, f32[]{:T(128)} %constant.40.clone.1), kind=kCustom, calls=%fused_computation.235 | custom fusion | flops 1048576 | bytes 62016 | tf_op jit(solution)/shard_map/scatter-add | solution.py:388
  1585.8 25.0 %all-reduce.15 = (bf16[1152]{0:T(1024)(128)(2,1)S(1)}, bf16[1152]{0:T(1024)(128)(2,1)S(1)}, bf16[1152]{0:T(1024)(128)(2,1)S(1)}, bf16[1152]{0:T(1024)(128)(2,1)S...) all-reduce(bf16[1152]{0:T(1024)(128)(2,1)S(1)} %dynamic-update-slic, ...), channel_id=1, replica_groups=mesh['dp'=8,'fsdp'=4] {'fsdp'}, use_global_device_ids=true, to_apply=%add.5 | all-reduce | flops 28048 | bytes 112192
  1610.8 2.7 convolution_reduce_fusion.1
  1616.8 28.5 %all-reduce.14 = (f32[288]{0:T(512)}, f32[288]{0:T(512)}, f32[288]{0:T(512)}, f32[288]{0:T(512)}, f32[288]{0:T(512)}, /*index=5*/f32[1152]{0:T(1024)}, f32[288]{0:T(512)}, f32[4,961]{0,1:T(8,128)S(1)}) all-reduce(f32[288]{0:T(512)S(1)} %dynamic-slice_convert_fusion.7, ...), channel_id=1, replica_groups=mesh['dp'=8,'fsdp'=4] {'dp'}, use_global_device_ids=true, to_apply=%region_41.0 | all-reduce | flops 6724 | bytes 53792 | tf_op jit(solution)/shard_map/psum | solution.py:475
  1646.8 8.3 fusion.50
  1655.1 7.5 fusion.51
  (481 shorter events, 97.4 us)
Async XLA Ops:
  7.2 21.3 %copy-start.73 = (bf16[144,288]{1,0:T(8,128)(2,1)S(1)}, bf16[144,288]{1,0:T(8,128)(2,1)}, u32[]{:S(2)}) copy-start(bf16[144,288]{1,0:T(8,128)(2,1)} %param.27) | copy-start | bytes 248836
  7.2 116.3 %all-gather.31.cloned.1.call-start = ((), (), s32[]{:S(2)}) async-start(), calls=%async_computation.22 | async-start | bytes 1658880 | tf_op jit(solution)/shard_map/all_gather | solution.py:107
  7.9 43.5 %copy-start.74 = (bf16[144,288]{1,0:T(8,128)(2,1)S(1)}, bf16[144,288]{1,0:T(8,128)(2,1)}, u32[]{:S(2)}) copy-start(bf16[144,288]{1,0:T(8,128)(2,1)} %param.28) | copy-start | bytes 248836
  7.9 403.8 %all-gather.35.cloned.1.call-start = ((), (), s32[]{:S(2)}) async-start(), calls=%async_computation.24 | async-start | bytes 1843200 | tf_op jit(solution)/shard_map/all_gather | solution.py:108
  8.7 409.1 %all-gather.21.cloned.1.call-start = ((), (), s32[]{:S(2)}) async-start(), calls=%async_computation.17 | async-start | bytes 2985984 | tf_op jit(solution)/shard_map/all_gather | solution.py:88
  28.4 40.0 %copy-start.75 = (bf16[144,288]{1,0:T(8,128)(2,1)S(1)}, bf16[144,288]{1,0:T(8,128)(2,1)}, u32[]{:S(2)}) copy-start(bf16[144,288]{1,0:T(8,128)(2,1)} %param.25) | copy-start | bytes 248836
  28.4 392.0 %all-gather.19.cloned.1.call-start = ((), (), s32[]{:S(2)}) async-start(), calls=%async_computation.16 | async-start | bytes 2985984 | tf_op jit(solution)/shard_map/all_gather | solution.py:86
  51.3 37.1 %copy-start.76 = (bf16[144,288]{1,0:T(8,128)(2,1)S(1)}, bf16[144,288]{1,0:T(8,128)(2,1)}, u32[]{:S(2)}) copy-start(bf16[144,288]{1,0:T(8,128)(2,1)} %param.26) | copy-start | bytes 248836
  51.3 373.2 %all-gather.25.cloned.1.call-start = ((), (), s32[]{:S(2)}) async-start(), calls=%async_computation.19 | async-start | bytes 2985984 | tf_op jit(solution)/shard_map/all_gather | solution.py:87
  68.3 39.3 %copy-start.77 = (bf16[144,288]{1,0:T(8,128)(2,1)S(1)}, bf16[144,288]{1,0:T(8,128)(2,1)}, u32[]{:S(2)}) copy-start(bf16[144,288]{1,0:T(8,128)(2,1)} %param.30) | copy-start | bytes 248836
  68.3 358.5 %all-gather.23.cloned.1.call-start = ((), (), s32[]{:S(2)}) async-start(), calls=%async_computation.18 | async-start | bytes 2985984 | tf_op jit(solution)/shard_map/all_gather | solution.py:84
  88.4 341.4 %all-gather.27.cloned.1.call-start = ((), (), s32[]{:S(2)}) async-start(), calls=%async_computation.20 | async-start | bytes 2985984 | tf_op jit(solution)/shard_map/all_gather | solution.py:85
  106.4 17.8 %copy-start.114 = (u32[32]{0:T(128)S(1)}, u32[32]{0:T(128)}, u32[]{:S(2)}) copy-start(u32[32]{0:T(128)} %constant.114) | copy-start | bytes 388
  106.4 19.1 %copy-start.116 = (bf16[288]{0:T(512)(128)(2,1)S(1)}, bf16[288]{0:T(512)(128)(2,1)}, u32[]{:S(2)}) copy-start(bf16[288]{0:T(512)(128)(2,1)} %param.33) | copy-start | bytes 1732
  106.5 19.3 %copy-start.117 = (bf16[288]{0:T(512)(128)(2,1)S(1)}, bf16[288]{0:T(512)(128)(2,1)}, u32[]{:S(2)}) copy-start(bf16[288]{0:T(512)(128)(2,1)} %param.32) | copy-start | bytes 1732
  106.5 19.6 %copy-start.118 = (bf16[288]{0:T(512)(128)(2,1)S(1)}, bf16[288]{0:T(512)(128)(2,1)}, u32[]{:S(2)}) copy-start(bf16[288]{0:T(512)(128)(2,1)} %param.31) | copy-start | bytes 1732
  106.5 19.8 %copy-start.119 = (bf16[288]{0:T(512)(128)(2,1)S(1)}, bf16[288]{0:T(512)(128)(2,1)}, u32[]{:S(2)}) copy-start(bf16[288]{0:T(512)(128)(2,1)} %param.35) | copy-start | bytes 1732
  106.5 20.1 %copy-start.120 = (bf16[288]{0:T(512)(128)(2,1)S(1)}, bf16[288]{0:T(512)(128)(2,1)}, u32[]{:S(2)}) copy-start(bf16[288]{0:T(512)(128)(2,1)} %param.34) | copy-start | bytes 1732
  106.5 38.1 %copy-start.115 = (s32[2]{0:T(128)S(1)}, s32[2]{0:T(128)}, u32[]{:S(2)}) copy-start(s32[2]{0:T(128)} %param.23) | copy-start | bytes 28
  106.5 40.0 %copy-start.109 = (bf16[4,961]{1,0:T(4,128)(2,1)S(1)}, bf16[4,961]{1,0:T(4,128)(2,1)}, u32[]{:S(2)}) copy-start(bf16[4,961]{1,0:T(4,128)(2,1)} %param.40) | copy-start | bytes 23068
  107.6 52.3 %copy-start.43 = (s32[256,256]{1,0:T(8,128)S(1)}, s32[256,256]{1,0:T(8,128)}, u32[]{:S(2)}) copy-start(s32[256,256]{1,0:T(8,128)} %param.24) | copy-start | bytes 786436
  107.6 354.3 %all-gather.29.cloned.1.call-start = ((), (), s32[]{:S(2)}) async-start(), calls=%async_computation.21 | async-start | bytes 2985984 | tf_op jit(solution)/shard_map/all_gather | solution.py:89
  123.5 350.1 %all-gather.33.cloned.1.call-start = ((), (), s32[]{:S(2)}) async-start(), calls=%async_computation.23 | async-start | bytes 11943936 | tf_op jit(solution)/shard_map/all_gather | solution.py:115
  124.2 393.0 %all-gather.37.cloned.1.call-start = ((), (), s32[]{:S(2)}) async-start(), calls=%async_computation.25 | async-start | bytes 11943936 | tf_op jit(solution)/shard_map/all_gather | solution.py:116
  144.5 317.3 %copy-start.110 = (f32[1152]{0:T(1024)}, f32[1152]{0:T(1024)S(1)}, u32[]{:S(2)}) copy-start(f32[1152]{0:T(1024)S(1)} %convert_element_type.405) | copy-start | bytes 13828
  144.6 271.9 %copy-start.78 = (f32[1152]{0:T(1024)}, f32[1152]{0:T(1024)S(1)}, u32[]{:S(2)}) copy-start(f32[1152]{0:T(1024)S(1)} %convert_element_type.389) | copy-start | bytes 13828
  376.0 20.1 %copy-start.113 = (bf16[1152]{0:T(1024)(128)(2,1)S(1)}, bf16[1152]{0:T(1024)(128)(2,1)}, u32[]{:S(2)}) copy-start(bf16[1152]{0:T(1024)(128)(2,1)} %param.38) | copy-start | bytes 6916
  376.0 35.4 %copy-start.11 = (bf16[2,256,1152]{2,1,0:T(8,128)(2,1)S(1)}, bf16[2,256,1152]{2,1,0:T(8,128)(2,1)}, u32[]{:S(2)}) copy-start(bf16[2,256,1152]{2,1,0:T(8,128)(2,1)} %param.21) | copy-start | bytes 3538948
  414.5 279.1 %reduce-scatter.48.cloned.1.call-start = ((), (), s32[]{:S(2)}) async-start(), calls=%async_computation.33 | async-start | bytes 13271040 | tf_op jit(solution)/shard_map/reduce_scatter | solution.py:428
  415.3 27.6 %copy-start.69 = (bf16[1,1152]{1,0:T(2,128)(2,1)}, bf16[1,1152]{1,0:T(2,128)(2,1)S(1)}, u32[]{:S(2)}) copy-start(bf16[1,1152]{1,0:T(2,128)(2,1)S(1)} %get-tuple-element.171) | copy-start | bytes 6916
  429.8 36.0 %copy-start.20 = (bf16[256,1152]{0,1:T(8,128)(2,1)}, bf16[256,1152]{0,1:T(8,128)(2,1)S(1)}, u32[]{:S(2)}) copy-start(bf16[256,1152]{0,1:T(8,128)(2,1)S(1)} %copy.156) | copy-start | bytes 1769476
  465.1 85.5 %copy-start.15 = (f32[256,1152]{1,0:T(8,128)}, f32[256,1152]{1,0:T(8,128)S(1)}, u32[]{:S(2)}) copy-start(f32[256,1152]{1,0:T(8,128)S(1)} %get-tuple-element.182) | copy-start | bytes 3538948
  471.6 79.1 %copy-start.17 = (f32[256,1152]{1,0:T(8,128)}, f32[256,1152]{1,0:T(8,128)S(1)}, u32[]{:S(2)}) copy-start(f32[256,1152]{1,0:T(8,128)S(1)} %get-tuple-element.184) | copy-start | bytes 3538948
  473.5 17.1 %copy-start.63 = (bf16[256,1152]{1,0:T(8,128)(2,1)}, bf16[256,1152]{1,0:T(8,128)(2,1)S(1)}, u32[]{:S(2)}) copy-start(bf16[256,1152]{1,0:T(8,128)(2,1)S(1)} %get-tuple-element.166) | copy-start | bytes 1769476
  473.6 17.1 %copy-start.61 = (bf16[256,1152]{1,0:T(8,128)(2,1)}, bf16[256,1152]{1,0:T(8,128)(2,1)S(1)}, u32[]{:S(2)}) copy-start(bf16[256,1152]{1,0:T(8,128)(2,1)S(1)} %get-tuple-element.165) | copy-start | bytes 1769476
  473.6 17.0 %copy-start.91 = (f32[4608]{0:T(1024)S(1)}, f32[4608]{0:T(1024)}, u32[]{:S(2)}) copy-start(f32[4608]{0:T(1024)} %reshape.570) | copy-start | bytes 55300
  515.0 234.6 %reduce-scatter.34.cloned.1.call-start = ((), (), s32[]{:S(2)}) async-start(), calls=%async_computation.26 | async-start | bytes 3317760 | tf_op jit(solution)/shard_map/reduce_scatter | solution.py:407
  574.8 229.5 %reduce-scatter.36.cloned.1.call-start = ((), (), s32[]{:S(2)}) async-start(), calls=%async_computation.27 | async-start | bytes 3317760 | tf_op jit(solution)/shard_map/reduce_scatter | solution.py:410
  582.5 276.3 %reduce-scatter.38.cloned.1.call-start = ((), (), s32[]{:S(2)}) async-start(), calls=%async_computation.28 | async-start | bytes 3317760 | tf_op jit(solution)/shard_map/reduce_scatter | solution.py:413
  590.5 322.8 %reduce-scatter.40.cloned.1.call-start = ((), (), s32[]{:S(2)}) async-start(), calls=%async_computation.29 | async-start | bytes 3317760 | tf_op jit(solution)/shard_map/reduce_scatter | solution.py:416
  593.7 374.2 %reduce-scatter.42.cloned.1.call-start = ((), (), s32[]{:S(2)}) async-start(), calls=%async_computation.30 | async-start | bytes 3317760 | tf_op jit(solution)/shard_map/reduce_scatter | solution.py:419
  596.4 426.0 %reduce-scatter.44.cloned.1.call-start = ((), (), s32[]{:S(2)}) async-start(), calls=%async_computation.31 | async-start | bytes 3317760 | tf_op jit(solution)/shard_map/reduce_scatter | solution.py:422
  601.3 603.2 %reduce-scatter.62.cloned.1.call-start = ((), (), s32[]{:S(2)}) async-start(), calls=%async_computation.40 | async-start | bytes 13271040
  627.4 1039.4 %reduce-scatter.64.cloned.1.call-start = ((), (), s32[]{:S(2)}) async-start(), calls=%async_computation.41 | async-start | bytes 7962624
  699.1 970.0 %reduce-scatter.50.cloned.1.call-start = ((), (), s32[]{:S(2)}) async-start(), calls=%async_computation.34 | async-start | bytes 1990656
  752.2 916.8 %reduce-scatter.52.cloned.1.call-start = ((), (), s32[]{:S(2)}) async-start(), calls=%async_computation.35 | async-start | bytes 1990656
  807.0 862.1 %reduce-scatter.54.cloned.1.call-start = ((), (), s32[]{:S(2)}) async-start(), calls=%async_computation.36 | async-start | bytes 1990656
  861.5 807.5 %reduce-scatter.56.cloned.1.call-start = ((), (), s32[]{:S(2)}) async-start(), calls=%async_computation.37 | async-start | bytes 1990656
  916.0 54.6 %copy-start.44 = (s32[256,256]{1,0:T(8,128)S(1)}, s32[256,256]{1,0:T(8,128)}, u32[]{:S(2)}) copy-start(s32[256,256]{1,0:T(8,128)} %param.24) | copy-start | bytes 786436
  916.0 56.6 %copy-start.121 = (bf16[288]{0:T(512)(128)(2,1)S(1)}, bf16[288]{0:T(512)(128)(2,1)}, u32[]{:S(2)}) copy-start(bf16[288]{0:T(512)(128)(2,1)} %param.39) | copy-start | bytes 1732
  916.0 753.0 %reduce-scatter.58.cloned.1.call-start = ((), (), s32[]{:S(2)}) async-start(), calls=%async_computation.38 | async-start | bytes 1990656
  970.5 54.8 %copy-start.50 = (bf16[16,72,256]{2,1,0:T(8,128)(2,1)S(1)}, bf16[16,72,256]{2,1,0:T(8,128)(2,1)}, u32[]{:S(2)}) copy-start(bf16[16,72,256]{2,1,0:T(8,128)(2,1)} %copy-done.49) | copy-start | bytes 1769476
  970.5 698.6 %reduce-scatter.60.cloned.1.call-start = ((), (), s32[]{:S(2)}) async-start(), calls=%async_computation.39 | async-start | bytes 1990656
  1025.1 644.0 %reduce-scatter.46.cloned.1.call-start = ((), (), s32[]{:S(2)}) async-start(), calls=%async_computation.32 | async-start | bytes 5971968 | tf_op jit(solution)/shard_map/reduce_scatter | solution.py:463
  1217.8 366.5 %copy-start.112 = (f32[1152]{0:T(1024)S(1)}, f32[1152]{0:T(1024)}, u32[]{:S(2)}) copy-start(f32[1152]{0:T(1024)} %get-tuple-element.95) | copy-start | bytes 13828
  1217.8 367.9 %copy-start.84 = (f32[1152]{0:T(1024)S(1)}, f32[1152]{0:T(1024)}, u32[]{:S(2)}) copy-start(f32[1152]{0:T(1024)} %get-tuple-element.110) | copy-start | bytes 13828
  1217.8 367.9 %copy-start.85 = (f32[1152]{0:T(1024)S(1)}, f32[1152]{0:T(1024)}, u32[]{:S(2)}) copy-start(f32[1152]{0:T(1024)} %get-tuple-element.111) | copy-start | bytes 13828
  1217.8 367.9 %copy-start.89 = (f32[4608]{0:T(1024)S(1)}, f32[4608]{0:T(1024)}, u32[]{:S(2)}) copy-start(f32[4608]{0:T(1024)} %get-tuple-element.193) | copy-start | bytes 55300
  1217.8 367.9 %copy-start.90 = (f32[4608]{0:T(1024)S(1)}, f32[4608]{0:T(1024)}, u32[]{:S(2)}) copy-start(f32[4608]{0:T(1024)} %get-tuple-element.195) | copy-start | bytes 55300
  1235.0 378.5 %copy-start.6 = (bf16[1152,1152]{1,0:T(8,128)(2,1)S(1)}, bf16[1152,1152]{1,0:T(8,128)(2,1)}, u32[]{:S(2)}) copy-start(bf16[1152,1152]{1,0:T(8,128)(2,1)} %all-gather.21.cloned.1.call-done) | copy-start | bytes 7962628
  1615.2 30.9 %copy-start.125 = (f32[256]{0:T(256)S(1)}, f32[256]{0:T(256)}, u32[]{:S(2)}) copy-start(f32[256]{0:T(256)} %get-tuple-element.102) | copy-start | bytes 3076
  1615.2 30.9 %copy-start.124 = (f32[256]{0:T(256)S(1)}, f32[256]{0:T(256)}, u32[]{:S(2)}) copy-start(f32[256]{0:T(256)} %get-tuple-element.106) | copy-start | bytes 3076
  1615.2 30.9 %copy-start.123 = (f32[256]{0:T(256)S(1)}, f32[256]{0:T(256)}, u32[]{:S(2)}) copy-start(f32[256]{0:T(256)} %get-tuple-element.103) | copy-start | bytes 3076
  1615.2 30.9 %copy-start.122 = (f32[256]{0:T(256)S(1)}, f32[256]{0:T(256)}, u32[]{:S(2)}) copy-start(f32[256]{0:T(256)} %get-tuple-element.105) | copy-start | bytes 3076
  (99 other events, 379.4 us)
Sparse Core Ops, SparseCore 0:
  9.6 45.5 all-gather.30
  56.8 47.7 all-gather.34
  107.0 29.4 all-gather.20
  138.8 30.1 all-gather.18
  170.7 30.1 all-gather.24
  203.1 30.1 all-gather.22
  235.2 30.1 all-gather.26
  267.2 30.1 all-gather.28
  299.2 63.6 all-gather.32
  414.6 62.1 all-gather.36
  515.1 178.4 reduce-scatter.47
  695.7 53.7 reduce-scatter.33
  751.9 52.3 reduce-scatter.35
  806.4 52.3 reduce-scatter.37
  861.0 52.3 reduce-scatter.39
  915.5 52.3 reduce-scatter.41
  970.1 52.3 reduce-scatter.43
  1024.7 179.7 reduce-scatter.61
  1208.0 66.5 reduce-scatter.63
  1278.3 39.2 reduce-scatter.49
  1321.6 39.2 reduce-scatter.51
  1364.8 39.2 reduce-scatter.53
  1408.1 39.2 reduce-scatter.55
  1451.2 39.2 reduce-scatter.57
  1494.4 39.2 reduce-scatter.59
  1537.6 56.8 reduce-scatter.45
where the time goes:
time: 1690 us; the launch traced here: 1680 us
  waiting for transfers between devices  542 us (32%)
  other arithmetic  373 us (22%)
  local copies, waits for them, and re-layouts  346 us (20%)
  blocking collectives  204 us (12%)
  matrix products  188 us (11%)
  between operations  20.1 us (1%)
    scatter-add x1, other arithmetic, body(): jax.ops.segment_sum(totals['pairs'].T, flat_index, num_segments=table_rows)  348 us
    gather x2, local copies, waits for them, and re-layouts, body(): bias_rows = table_full.astype(jnp.float32)[:, offset_index]  236 us
    unnamed x34, waiting for transfers between devices  168 us
    dot_general x16, matrix products, matmul(): return jnp.dot(left, right, preferred_element_type=jnp.float32)  77.6 us
    unnamed x308, local copies, waits for them, and re-layouts  76.5 us
    reduce_scatter x1, waiting for transfers between devices, body(): lax.psum_scatter(grad_down.astype(jnp.bfloat16), 'fsdp', scatter_dimensio...  66.2 us
    dot_general x16, matrix products, times_transposed(): lax.dot_general(left, right, (((1,), (1,)), ((), ())), preferred_element_...  53 us
    reduce_scatter x1, waiting for transfers between devices, body(): lax.psum_scatter(grad_keys.astype(jnp.bfloat16), 'fsdp', scatter_dimensio...  52 us
  transfers between devices with their start and end apart: 26, of which 8 were waited for; matrix products, arithmetic and copies ran while one was open for 53% of the time, Pallas kernels for 0%

commit v1 on v0

v1 whole, which is shorter than its diff:
```python
import math

import jax
import jax.numpy as jnp
from jax import lax
from jax.experimental import pallas as pl
from jax.experimental.pallas import tpu as pltpu
from jax.sharding import PartitionSpec as P

LANES = 128
BOTH = ("dp", "fsdp")
VMEM_LIMIT = 58 * 1024 * 1024


def sinusoid(steps, model_width):
    half_width = model_width // 2
    frequency = jnp.exp(
        -math.log(10000.0) * jnp.arange(half_width).astype(jnp.float32) / half_width
    )
    angles = steps.astype(jnp.float32)[:, None] * frequency[None, :]
    return jnp.concatenate([jnp.sin(angles), jnp.cos(angles)], axis=1)


def matmul(left, right):
    return jnp.dot(left, right, preferred_element_type=jnp.float32)


def contract_rows(left, right):
    return lax.dot_general(
        left, right, (((0,), (0,)), ((), ())), preferred_element_type=jnp.float32
    )


def times_transposed(left, right):
    return lax.dot_general(
        left, right, (((1,), (1,)), ((), ())), preferred_element_type=jnp.float32
    )


def normalize(values, gain, shift):
    row_mean = jnp.mean(values, axis=-1, keepdims=True)
    centered = values - row_mean
    inv_std = lax.rsqrt(jnp.mean(centered * centered, axis=-1, keepdims=True) + 1e-06)
    unit_rows = centered * inv_std
    return (unit_rows * gain + shift, unit_rows, inv_std)


def norm_back(grad_rows, unit_rows, inv_std, gain):
    scaled = grad_rows * gain
    return inv_std * (
        scaled
        - jnp.mean(scaled, axis=-1, keepdims=True)
        - unit_rows * jnp.mean(scaled * unit_rows, axis=-1, keepdims=True)
    )


def gelu_slope(pre_act):
    return 0.5 * (1.0 + lax.erf(pre_act * (1.0 / math.sqrt(2.0)))) + pre_act * jnp.exp(
        -0.5 * pre_act * pre_act
    ) * (1.0 / math.sqrt(2.0 * math.pi))


def params(count=1):
    return pltpu.CompilerParams(
        dimension_semantics=("arbitrary",) * count, vmem_limit_bytes=VMEM_LIMIT
    )


def bias_kernel(index_ref, table_ref, bias_ref):
    chunks = table_ref.shape[2] // LANES
    rows = index_ref.shape[0]
    for head in range(table_ref.shape[0]):
        line = table_ref[head]
        pieces = [
            jnp.broadcast_to(line[:, c * LANES : (c + 1) * LANES], (8, LANES))
            for c in range(chunks)
        ]

        def some_rows(step, carry, head=head, pieces=pieces):
            for part in range(2):
                at = pl.multiple_of(step * 16 + part * 8, 8)
                for col in range(index_ref.shape[1] // LANES):
                    lanes = slice(col * LANES, (col + 1) * LANES)
                    index = index_ref[pl.ds(at, 8), lanes]
                    low = index & (LANES - 1)
                    high = index >> 7
                    found = jnp.take_along_axis(pieces[0], low, axis=1)
                    for c in range(1, chunks):
                        found = jnp.where(
                            high == c, jnp.take_along_axis(pieces[c], low, axis=1), found
                        )
                    bias_ref[head, pl.ds(at, 8), lanes] = found
            return carry

        lax.fori_loop(0, rows // 16, some_rows, 0)


def position_bias(index, table):
    heads, padded = table.shape
    tokens = index.shape[0]
    group = heads // 4
    return pl.pallas_call(
        bias_kernel,
        grid=(4,),
        in_specs=[
            pl.BlockSpec((tokens, tokens), lambda f: (0, 0)),
            pl.BlockSpec((group, 1, padded), lambda f: (f, 0, 0)),
        ],
        out_specs=pl.BlockSpec((group, tokens, tokens), lambda f: (f, 0, 0)),
        out_shape=jax.ShapeDtypeStruct((heads, tokens, tokens), jnp.float32),
        compiler_params=params(),
        name="position_bias",
    )(index, table.reshape(heads, 1, padded))


def table_kernel(index_ref, pairs_ref, out_ref):
    heads = pairs_ref.shape[0]
    tokens = index_ref.shape[1]
    rows = index_ref.shape[0]

    @pl.when(pl.program_id(0) == 0)
    def _():
        out_ref[...] = jnp.zeros_like(out_ref)

    sub = lax.broadcasted_iota(jnp.int32, (8, tokens), 0)
    lane_of = lax.broadcasted_iota(jnp.int32, (LANES, tokens), 0)

    def one_row(row, total):
        index = index_ref[pl.ds(row, 1), :]
        low = jnp.broadcast_to(index & (LANES - 1), (LANES, tokens))
        high = jnp.broadcast_to(index >> 7, (8, tokens))
        hit = sub == high
        left = jnp.concatenate(
            [
                jnp.where(hit, jnp.broadcast_to(pairs_ref[h, pl.ds(row, 1), :], (8, tokens)), 0.0)
                for h in range(heads)
            ],
            axis=0,
        ).astype(jnp.bfloat16)
        right = jnp.where(lane_of == low, 1.0, 0.0).astype(jnp.bfloat16)
        return total + times_transposed(left, right)

    def two_rows(step, total):
        return one_row(step * 2 + 1, one_row(step * 2, total))

    out_ref[...] += lax.fori_loop(
        0, rows // 2, two_rows, jnp.zeros((heads * 8, LANES), jnp.float32)
    )


def table_gradient(index, pairs):
    heads, tokens, _ = pairs.shape
    block = 64
    return pl.pallas_call(
        table_kernel,
        grid=(tokens // block,),
        in_specs=[
            pl.BlockSpec((block, tokens), lambda i: (i, 0)),
            pl.BlockSpec((heads, block, tokens), lambda i: (0, i, 0)),
        ],
        out_specs=pl.BlockSpec((heads * 8, LANES), lambda i: (0, 0)),
        out_shape=jax.ShapeDtypeStruct((heads * 8, LANES), jnp.float32),
        compiler_params=params(),
        name="table_gradient",
    )(index, pairs)


def attend_kernel(normed_ref, weight_ref, add_ref, bias_ref, qkv_ref, probs_ref, mixed_ref):
    images, heads = probs_ref.shape[1], probs_ref.shape[2]
    tokens = probs_ref.shape[3]
    width = mixed_ref.shape[2]
    size = width // heads
    scale = 1.0 / math.sqrt(size)
    kept = qkv_ref.shape[2]
    for image in range(images):
        rows = slice(image * tokens, (image + 1) * tokens)
        acc = matmul(normed_ref[rows, :], weight_ref[0, :, :kept])
        qkv_ref[0, rows, :] = (acc + add_ref[0, image : image + 1, :]).astype(jnp.bfloat16)
    for image in range(images):
        rows = slice(image * tokens, (image + 1) * tokens)
        both = qkv_ref[0, rows, :]
        outs = []
        for head in range(heads):
            at = head * size
            query = both[:, at : at + size]
            keys = both[:, width + at : width + at + size]
            values = both[:, 2 * width + at : 2 * width + at + size]
            scores = times_transposed(query, keys) * scale + bias_ref[head]
            peak = jnp.max(scores, axis=-1, keepdims=True)
            expo = jnp.exp(scores - peak)
            total = jnp.sum(expo, axis=-1, keepdims=True)
            probs = (expo / total).astype(jnp.bfloat16)
            probs_ref[0, image, head] = probs
            outs.append(matmul(probs, values))
        mixed_ref[0, rows, :] = jnp.concatenate(outs, axis=1).astype(jnp.bfloat16)


def attend(normed, weight, add, bias, images, tokens):
    groups, depth, packed = weight.shape
    heads = bias.shape[0] // groups
    width = packed // groups
    kept = add.shape[2]
    rows = images * tokens
    return pl.pallas_call(
        attend_kernel,
        grid=(groups,),
        in_specs=[
            pl.BlockSpec((rows, depth), lambda f: (0, 0)),
            pl.BlockSpec((1, depth, packed), lambda f: (f, 0, 0)),
            pl.BlockSpec((1, images, kept), lambda f: (f, 0, 0)),
            pl.BlockSpec((heads, tokens, tokens), lambda f: (f, 0, 0)),
        ],
        out_specs=[
            pl.BlockSpec((1, rows, kept), lambda f: (f, 0, 0)),
            pl.BlockSpec((1, images, heads, tokens, tokens), lambda f: (f, 0, 0, 0, 0)),
            pl.BlockSpec((1, rows, width), lambda f: (f, 0, 0)),
        ],
        out_shape=[
            jax.ShapeDtypeStruct((groups, rows, kept), jnp.bfloat16),
            jax.ShapeDtypeStruct((groups, images, heads, tokens, tokens), jnp.bfloat16),
            jax.ShapeDtypeStruct((groups, rows, width), jnp.bfloat16),
        ],
        compiler_params=params(),
        name="attend",
    )(normed, weight, add, bias)


def attend_back_kernel(grad_ref, qkv_ref, probs_ref, hidden_ref, out_ref, pairs_ref):
    images, heads = probs_ref.shape[1], probs_ref.shape[2]
    tokens = probs_ref.shape[3]
    width = grad_ref.shape[2]
    size = width // heads
    scale = 1.0 / math.sqrt(size)
    for image in range(images):
        rows = slice(image * tokens, (image + 1) * tokens)
        both = qkv_ref[0, rows, :]
        grads = grad_ref[0, rows, :]
        d_query, d_keys, d_values = [], [], []
        for head in range(heads):
            at = head * size
            query = both[:, at : at + size]
            keys = both[:, width + at : width + at + size]
            values = both[:, 2 * width + at : 2 * width + at + size]
            grad = grads[:, at : at + size]
            probs_low = probs_ref[0, image, head]
            probs = probs_low.astype(jnp.float32)
            d_values.append(contract_rows(probs_low, grad))
            d_probs = times_transposed(grad, values)
            moved = probs * d_probs
            d_scores = moved - probs * jnp.sum(moved, axis=-1, keepdims=True)
            d_low = d_scores.astype(jnp.bfloat16)
            if image == 0:
                pairs_ref[head] = d_low.astype(jnp.float32)
            else:
                pairs_ref[head] += d_low.astype(jnp.float32)
            d_query.append(matmul(d_low, keys) * scale)
            d_keys.append(contract_rows(d_low, query) * scale)
        out_ref[0, rows, :] = jnp.concatenate(
            d_query + d_keys + d_values + [hidden_ref[0, rows, :].astype(jnp.float32)], axis=1
        ).astype(jnp.bfloat16)


def attend_back(grad, qkv, probs, hidden):
    groups, rows, width = grad.shape
    kept = qkv.shape[2]
    _, images, heads, tokens, _ = probs.shape
    packed = 4 * width
    return pl.pallas_call(
        attend_back_kernel,
        grid=(groups,),
        in_specs=[
            pl.BlockSpec((1, rows, width), lambda f: (f, 0, 0)),
            pl.BlockSpec((1, rows, kept), lambda f: (f, 0, 0)),
            pl.BlockSpec((1, images, heads, tokens, tokens), lambda f: (f, 0, 0, 0, 0)),
            pl.BlockSpec((1, rows, width), lambda f: (f, 0, 0)),
        ],
        out_specs=[
            pl.BlockSpec((1, rows, packed), lambda f: (f, 0, 0)),
            pl.BlockSpec((heads, tokens, tokens), lambda f: (f, 0, 0)),
        ],
        out_shape=[
            jax.ShapeDtypeStruct((groups, rows, packed), jnp.bfloat16),
            jax.ShapeDtypeStruct((groups * heads, tokens, tokens), jnp.float32),
        ],
        compiler_params=params(),
        name="attend_back",
    )(grad, qkv, probs, hidden)


def pair_grad_kernel(one_ref, two_ref, right_ref, out_ref):
    cut = 3 * (right_ref.shape[2] // 4)
    below = cut // LANES * LANES
    above = below + LANES
    right = right_ref[0]
    first = matmul(one_ref[...], right[:, :above])
    last = matmul(two_ref[...], right[:, below:])
    lane = lax.broadcasted_iota(jnp.int32, (first.shape[0], LANES), 1)
    out_ref[0, :, :below] = first[:, :below].astype(jnp.bfloat16)
    out_ref[0, :, below:above] = jnp.where(
        lane < cut - below, first[:, below:], last[:, :LANES]
    ).astype(jnp.bfloat16)
    out_ref[0, :, above:] = last[:, LANES:].astype(jnp.bfloat16)


def pair_grad(normed_t, mixed_t, right):
    groups, rows, packed = right.shape
    depth = normed_t.shape[0]
    return pl.pallas_call(
        pair_grad_kernel,
        grid=(groups,),
        in_specs=[
            pl.BlockSpec((depth, rows), lambda f: (0, 0)),
            pl.BlockSpec((depth, rows), lambda f: (0, 0)),
            pl.BlockSpec((1, rows, packed), lambda f: (f, 0, 0)),
        ],
        out_specs=pl.BlockSpec((1, depth, packed), lambda f: (f, 0, 0)),
        out_shape=jax.ShapeDtypeStruct((groups, depth, packed), jnp.bfloat16),
        compiler_params=params(),
        name="pair_grad",
    )(normed_t, mixed_t, right)


def pack_down_kernel(in_ref, out_ref):
    groups, _, rows, packed = out_ref.shape
    width = packed // groups
    count = in_ref.shape[0] // rows
    for g in range(count):
        block = in_ref[g * rows : (g + 1) * rows, :]
        for f in range(groups):
            out_ref[f, 0, :, g * width : (g + 1) * width] = block[:, f * width : (f + 1) * width]


def unpack_down_kernel(in_ref, out_ref):
    groups, _, rows, packed = in_ref.shape
    width = packed // groups
    count = out_ref.shape[0] // rows
    for f in range(groups):
        block = in_ref[f, 0]
        for g in range(count):
            out_ref[g * rows : (g + 1) * rows, f * width : (f + 1) * width] = block[
                :, g * width : (g + 1) * width
            ]


def pack_down(natural, groups, parts, rows):
    total, width = natural.shape
    count = total // (parts * rows)
    if rows % 16:
        split = natural.reshape(parts, count, rows, groups, width // groups)
        return split.transpose(3, 0, 2, 1, 4).reshape(groups, parts, rows, width)
    return pl.pallas_call(
        pack_down_kernel,
        grid=(parts,),
        in_specs=[pl.BlockSpec((count * rows, width), lambda d: (d, 0))],
        out_specs=pl.BlockSpec((groups, 1, rows, width), lambda d: (0, d, 0, 0)),
        out_shape=jax.ShapeDtypeStruct((groups, parts, rows, width), natural.dtype),
        compiler_params=params(),
        name="pack_down",
    )(natural)


def unpack_down(packed):
    groups, parts, rows, width = packed.shape
    count = 4
    if rows % 16:
        split = packed.reshape(groups, parts, rows, count, width // count)
        return split.transpose(1, 3, 2, 0, 4).reshape(parts * count * rows, width)
    return pl.pallas_call(
        unpack_down_kernel,
        grid=(parts,),
        in_specs=[pl.BlockSpec((groups, 1, rows, width), lambda d: (0, d, 0, 0))],
        out_specs=pl.BlockSpec((count * rows, width), lambda d: (d, 0)),
        out_shape=jax.ShapeDtypeStruct((parts * count * rows, width), packed.dtype),
        compiler_params=params(),
        name="unpack_down",
    )(packed)


def take_proj_kernel(in_ref, out_ref):
    groups = in_ref.shape[0]
    width = out_ref.shape[1] // groups
    skip = in_ref.shape[2] - width
    for f in range(groups):
        out_ref[:, f * width : (f + 1) * width] = in_ref[f][:, skip:]


def take_proj(packed):
    groups, depth, width = packed.shape
    block = 288
    tail = width // 3
    return pl.pallas_call(
        take_proj_kernel,
        grid=(depth // block,),
        in_specs=[pl.BlockSpec((groups, block, tail), lambda d: (0, d, 2))],
        out_specs=pl.BlockSpec((block, width), lambda d: (d, 0)),
        out_shape=jax.ShapeDtypeStruct((depth, width), packed.dtype),
        compiler_params=params(),
        name="take_proj",
    )(packed)


def gather_shards(shard):
    rows, width = shard.shape
    groups, parts = lax.axis_size("fsdp"), lax.axis_size("dp")
    full = lax.all_gather(shard, ("fsdp", "dp"), axis=0, tiled=True)
    return full.reshape(groups, parts, rows, width)


def scatter_sum(terms):
    groups, parts, rows, width = terms.shape
    return lax.psum_scatter(
        terms.reshape(groups * parts * rows, width),
        ("fsdp", "dp"),
        scatter_dimension=0,
        tiled=True,
    )


def body(
    images,
    time_vector,
    timesteps,
    offset_index,
    query_weight,
    key_weight,
    value_weight,
    tquery_weight,
    tvalue_weight,
    proj_weight,
    proj_bias,
    first_gain,
    first_shift,
    second_gain,
    second_shift,
    up_weight,
    down_weight,
    up_bias,
    down_bias,
    bias_table,
    cotangent,
):
    low = jnp.bfloat16
    wide = jnp.float32
    count, tokens, width = images.shape
    rows = count * tokens
    groups, parts = lax.axis_size("fsdp"), lax.axis_size("dp")
    shard_rows, shard_cols = query_weight.shape
    group_heads, table_rows = bias_table.shape
    heads = group_heads * groups
    fold = down_weight.shape[0] // shard_rows
    own_part = lax.axis_index("dp")
    own_group = lax.axis_index("fsdp")

    wire_attn = jnp.concatenate([query_weight, key_weight, value_weight, proj_weight], axis=1)
    wire_down = jnp.concatenate(
        [down_weight[g * shard_rows : (g + 1) * shard_rows] for g in range(fold)], axis=1
    )
    small = jnp.concatenate(
        [
            proj_bias,
            first_gain,
            first_shift,
            second_gain,
            second_shift,
            down_bias,
            up_bias,
            bias_table.reshape(-1),
        ]
    )
    small = jnp.pad(small, (0, -small.shape[0] % 1024))
    small_all = lax.all_gather(small, "fsdp", axis=0, tiled=False)

    def vector_of(slot):
        return small_all[:, slot * shard_cols : (slot + 1) * shard_cols].reshape(-1).astype(wide)

    proj_b, gain_one, shift_one, gain_two, shift_two, down_b = (vector_of(i) for i in range(6))
    at = 6 * shard_cols
    up_b = small_all[:, at : at + up_bias.shape[0]].astype(wide)
    at = at + up_bias.shape[0]
    table = small_all[:, at : at + group_heads * table_rows].reshape(heads, table_rows)
    table = jnp.pad(table.astype(wide), ((0, 0), (0, -table_rows % LANES)))

    time_low = (time_vector.astype(wide) + sinusoid(timesteps, width)).astype(low)
    time_all = lax.all_gather(time_low, BOTH, axis=0, tiled=True)
    all_images = time_all.shape[0]
    time_cols = lax.dynamic_slice(
        time_all, (0, own_part * shard_rows), (all_images, shard_rows)
    )
    time_weight = jnp.concatenate([tquery_weight, tvalue_weight], axis=1)
    time_sum = lax.psum_scatter(
        matmul(time_cols, time_weight), "dp", scatter_dimension=0, tiled=True
    )
    time_part = lax.all_gather(time_sum, "fsdp", axis=0, tiled=False)
    time_own = lax.dynamic_slice(
        time_part, (0, own_group * count, 0), (groups, count, 2 * shard_cols)
    )
    gap = jnp.zeros((groups, count, shard_cols), wide)
    kept = -(-3 * shard_cols // LANES) * LANES
    time_add = jnp.concatenate(
        [
            time_own[:, :, :shard_cols],
            gap,
            time_own[:, :, shard_cols:],
            gap[:, :, : kept - 3 * shard_cols],
        ],
        axis=2,
    )

    attn_full = gather_shards(wire_attn).reshape(groups, width, width)
    up_full = gather_shards(up_weight).reshape(groups, width, width)
    down_full = unpack_down(gather_shards(wire_down))

    bias = position_bias(offset_index, table)

    x_rows = images.reshape(rows, width).astype(wide)
    normed, unit_one, inv_one = normalize(x_rows, gain_one, shift_one)
    normed_low = normed.astype(low)
    qkv, probs, mixed_split = attend(normed_low, attn_full, time_add, bias, count, tokens)
    proj_full = take_proj(attn_full)
    mixed = mixed_split.transpose(1, 0, 2).reshape(rows, width)
    hidden = x_rows + (matmul(mixed, proj_full) + proj_b)
    second, unit_two, inv_two = normalize(hidden, gain_two, shift_two)
    second_low = second.astype(low)
    grad_low = cotangent.reshape(rows, width)
    grad_rows = grad_low.astype(wide)
    result = hidden + down_b
    d_second = jnp.zeros((rows, width), wide)
    activ, d_pre = [], []
    for g in range(groups):
        pre_act = matmul(second_low, up_full[g]) + up_b[g]
        act = jax.nn.gelu(pre_act, approximate=False).astype(low)
        down_g = down_full[g * width : (g + 1) * width]
        result = result + matmul(act, down_g)
        d_g = (times_transposed(grad_low, down_g) * gelu_slope(pre_act)).astype(low)
        d_second = d_second + times_transposed(d_g, up_full[g])
        activ.append(act)
        d_pre.append(d_g)
    layer_out = result.astype(low).reshape(count, tokens, width)

    grad_down = jnp.concatenate([contract_rows(a, grad_low).astype(low) for a in activ], axis=0)
    grad_up = jnp.stack([contract_rows(second_low, d).astype(low) for d in d_pre])
    down_sum = scatter_sum(pack_down(grad_down, groups, parts, shard_rows))
    up_sum = scatter_sum(grad_up.reshape(groups, parts, shard_rows, width))

    d_hidden = grad_rows + norm_back(d_second, unit_two, inv_two, gain_two)
    d_hidden_low = d_hidden.astype(low)
    d_mixed = times_transposed(d_hidden_low, proj_full).astype(low)
    d_mixed_split = d_mixed.reshape(rows, groups, shard_cols).transpose(1, 0, 2)
    d_hidden_split = d_hidden_low.reshape(rows, groups, shard_cols).transpose(1, 0, 2)
    d_packed, pairs = attend_back(d_mixed_split, qkv, probs, d_hidden_split)
    attn_sum = scatter_sum(
        pair_grad(normed_low.T, mixed.T, d_packed).reshape(groups, parts, shard_rows, width)
    )

    d_time = jnp.sum(d_packed.reshape(groups, count, tokens, width).astype(wide), axis=2)
    d_time = jnp.concatenate(
        [d_time[:, :, :shard_cols], d_time[:, :, 2 * shard_cols : 3 * shard_cols]], axis=2
    ).astype(low)
    d_time_all = lax.all_gather(
        d_time.transpose(1, 0, 2).reshape(count, groups * 2 * shard_cols), BOTH, axis=0, tiled=True
    )
    d_time_cols = lax.dynamic_slice(
        d_time_all, (0, own_group * 2 * shard_cols), (all_images, 2 * shard_cols)
    )
    time_grads = contract_rows(time_cols, d_time_cols)
    tquery_grad = time_grads[:, :shard_cols]
    tvalue_grad = time_grads[:, shard_cols:]
    back = times_transposed(d_time_cols, time_weight)
    back = back.reshape(parts, groups, count, shard_rows).transpose(1, 0, 2, 3)
    back = lax.psum_scatter(back, "fsdp", scatter_dimension=0, tiled=False)
    back = lax.all_gather(back, "dp", axis=0, tiled=False)
    back = lax.dynamic_slice(
        back, (0, own_part, 0, 0), (parts, 1, count, shard_rows)
    ).reshape(parts, count, shard_rows)
    time_grad = back.transpose(1, 0, 2).reshape(count, width)

    lane = lax.broadcasted_iota(jnp.int32, (1, width), 1)
    d_normed = jnp.zeros((rows, width), wide)
    for g in range(groups):
        part = jnp.where(lane < 3 * shard_cols, d_packed[g], jnp.zeros((), low))
        d_normed = d_normed + times_transposed(part, attn_full[g])
    d_input = d_hidden + norm_back(d_normed, unit_one, inv_one, gain_one)
    images_grad = d_input.astype(low).reshape(count, tokens, width)

    table_sum = table_gradient(offset_index, pairs).reshape(heads, 8 * LANES)[:, :table_rows]

    def rows_sum(value):
        return jnp.sum(value, axis=0).reshape(groups, -1)

    vectors = [
        rows_sum(d_hidden_low.astype(wide)),
        rows_sum(d_normed * unit_one),
        rows_sum(d_normed),
        rows_sum(d_second * unit_two),
        rows_sum(d_second),
        rows_sum(grad_rows),
        jnp.stack([jnp.sum(d.astype(wide), axis=0) for d in d_pre]),
        table_sum.reshape(groups, group_heads * table_rows),
    ]
    flat = jnp.concatenate(vectors, axis=1)
    flat = jnp.pad(flat, ((0, 0), (0, -flat.shape[1] % 1024)))
    flat = lax.psum(flat, BOTH)
    own = lax.dynamic_slice(flat, (own_group, 0), (1, flat.shape[1]))[0]
    proj_bg, gain1_g, shift1_g, gain2_g, shift2_g, down_bg = (
        own[i * shard_cols : (i + 1) * shard_cols] for i in range(6)
    )
    at = 6 * shard_cols
    up_bg = own[at : at + up_bias.shape[0]]
    at = at + up_bias.shape[0]
    table_grad = own[at : at + group_heads * table_rows].reshape(group_heads, table_rows)

    attn_sum = attn_sum.astype(wide)
    query_grad, key_grad, value_grad, proj_grad = (
        attn_sum[:, i * shard_cols : (i + 1) * shard_cols] for i in range(4)
    )
    down_sum = down_sum.astype(wide)
    down_grad = jnp.concatenate(
        [down_sum[:, g * shard_cols : (g + 1) * shard_cols] for g in range(fold)], axis=0
    )
    return (
        layer_out,
        images_grad,
        time_grad,
        query_grad,
        key_grad,
        value_grad,
        tquery_grad,
        tvalue_grad,
        proj_grad,
        proj_bg,
        gain1_g,
        shift1_g,
        gain2_g,
        shift2_g,
        up_sum.astype(wide),
        down_grad,
        up_bg,
        down_bg,
        table_grad,
    )


def solution(mesh):
    rows = P(BOTH, None, None)
    matrix = P("dp", "fsdp")
    vector = P("fsdp")
    table = P("fsdp", None)
    return jax.shard_map(
        body,
        mesh=mesh,
        in_specs=(
            (rows, P(BOTH, None), P(BOTH), P())
            + (matrix,) * 6
            + (vector,) * 5
            + (matrix,) * 2
            + (vector,) * 2
            + (table, rows)
        ),
        out_specs=(
            (rows, rows, P(BOTH, None))
            + (matrix,) * 6
            + (vector,) * 5
            + (matrix,) * 2
            + (vector,) * 2
            + (table,)
        ),
        check_vma=False,
    )
```

time: 1690 us -> 1080 us (0.64)
  other arithmetic: 373 us -> 48.3 us
  local copies, waits for them, and re-layouts: 346 us -> 75.2 us
  Pallas kernels: 0 us -> 136 us
  matrix products: 188 us -> 122 us
  waiting for transfers between devices: 542 us -> 490 us
  blocking collectives: 204 us -> 181 us
    scatter-add x1 -> x0, other arithmetic: 348 us -> none  [body(): jax.ops.segment_sum(totals['pairs'].T, flat_index, num_segments=table_rows)]
    gather x2 -> x0, local copies, waits for them, and re-layouts: 236 us -> none  [body(): bias_rows = table_full.astype(jnp.float32)[:, offset_index]]
    pallas_call x0 -> x8, Pallas kernels: none -> 136 us  [the longest x1 33.8 us: position_bias(): pl.pallas_call(bias_kernel, grid=(4,), in_specs=[pl.BlockSpec((tokens, to...]
    unnamed x34 -> x11, waiting for transfers between devices: 168 us -> 35.6 us
    all_gather x10 -> x3, waiting for transfers between devices: 0.14 us -> 131 us  [gather_shards(): full = lax.all_gather(shard, ('fsdp', 'dp'), axis=0, tiled=True)]
    reduce_scatter x8 -> x3, waiting for transfers between devices: 374 us -> 290 us  [the longest x2 290 us: scatter_sum(): lax.psum_scatter(terms.reshape(groups * parts * rows, width), ('fsdp', 'd...]
    unnamed x308 -> x145, local copies, waits for them, and re-layouts: 76.5 us -> 15.8 us
    all_gather x8 -> x5, blocking collectives: 133 us -> 181 us  [the longest x1 73.4 us: body(): lax.all_gather(d_time.transpose(1, 0, 2).reshape(count, groups * 2 * shar...]
  transfers between devices with their start and end apart: 26 -> 9, of which waited for: 8 -> 6; matrix products, arithmetic and copies ran while one was open for 53% -> 12% of each run, Pallas kernels for 0% -> 9%
where the time goes in v1:
time: 1080 us; the launch traced here: 1070 us
  waiting for transfers between devices  490 us (45%)
  blocking collectives  181 us (17%)
  Pallas kernels  136 us (13%)
  matrix products  122 us (11%)
  local copies, waits for them, and re-layouts  75.2 us (7%)
  other arithmetic  48.3 us (4%)
  between operations  17.3 us (2%)
    reduce_scatter x2, waiting for transfers between devices, scatter_sum(): lax.psum_scatter(terms.reshape(groups * parts * rows, width), ('fsdp', 'd...  290 us
    all_gather x3, waiting for transfers between devices, gather_shards(): full = lax.all_gather(shard, ('fsdp', 'dp'), axis=0, tiled=True)  131 us
    all_gather x1, blocking collectives, body(): lax.all_gather(d_time.transpose(1, 0, 2).reshape(count, groups * 2 * shar...  73.4 us
    all_gather x1, blocking collectives, body(): time_all = lax.all_gather(time_low, BOTH, axis=0, tiled=True)  70.8 us
    dot_general x10, matrix products, matmul(): return jnp.dot(left, right, preferred_element_type=jnp.float32)  53.7 us
    dot_general x14, matrix products, times_transposed(): lax.dot_general(left, right, (((1,), (1,)), ((), ())), preferred_element_...  43.4 us
    unnamed x11, waiting for transfers between devices  35.6 us
    pallas_call x1, Pallas kernels, position_bias(): pl.pallas_call(bias_kernel, grid=(4,), in_specs=[pl.BlockSpec((tokens, to...  33.8 us
  transfers between devices with their start and end apart: 9, of which 6 were waited for; matrix products, arithmetic and copies ran while one was open for 12% of the time, Pallas kernels for 9%

profile of v1, /device:TPU:0, one launch (start us, length us, event | category | flops | bytes accessed | tf_op | source)
XLA Modules:
  0.0 1070.3 jit_solution(1938669777605317427)
XLA Ops:
  9.7 70.8 %all-gather.2 = bf16[32,2,1152]{2,1,0:T(2,128)(2,1)S(1)} all-gather(bf16[1,2,1152]{2,1,0:T(2,128)(2,1)S(1)} %fusion.120), channel_id=1, replica_groups=mesh['dp'=8,'fsdp'=4] {'dp','fsdp'}, dimensions={0}, use_global_device_ids=true | all-gather | bytes 152064 | tf_op jit(solution)/shard_map/all_gather | solution.py:484
  80.6 1.9 fusion.113
  82.7 2.1 concatenate.32
  87.5 13.2 %all-gather = bf16[28672]{0:T(1024)(128)(2,1)S(1)} all-gather(bf16[7168]{0:T(1024)(128)(2,1)S(1)} %pad.13), channel_id=2, replica_groups=mesh['dp'=8,'fsdp'=4] {'fsdp'}, dimensions={0}, use_global_device_ids=true | all-gather | bytes 71680 | tf_op jit(solution)/shard_map/all_gather | solution.py:471
  116.1 2.1 convert_reduce_fusion.4
  121.5 33.8 %position_bias.1.bias_ref = f32[16,256,256]{2,1,0:T(8,128)} custom-call(s32[256,256]{1,0:T(8,128)} %index_ref.3, f32[16,1,1024]{2,1,0:T(1,128)} %reshape.319.table_ref), custom_call_target="tpu_custom_call" | custom-call | tf_op jit(solution)/shard_map/position_bias/pallas_call | solution.py:102
  158.0 13.7 %all-gather.1 = f32[32,576]{1,0:T(8,128)S(1)} all-gather(f32[8,576]{1,0:T(8,128)S(1)} %constant_dynamic-slice_fusion.3), channel_id=3, replica_groups=mesh['dp'=8,'fsdp'=4] {'fsdp'}, dimensions={0}, use_global_device_ids=true | all-gather | bytes 92160 | tf_op jit(solution)/shard_map/all_gather | solution.py:493
  173.3 4.8 take_proj.1
  178.0 16.6 %attend.1 = (bf16[4,512,896]{2,1,0:T(8,128)(2,1)}, bf16[4,2,4,256,256]{4,3,2,1,0:T(8,128)(2,1)}, bf16[4,512,288]{2,1,0:T(8,128)(2,1)}) custom-call(bf16[512,1152]{1,0:T(8,128)(2,1)} %copy.88.normed_ref, bf16[4,1152,1152]{2,1,0:T(8,128)(2,1)} %bitcast.127, f32[4,2,896]{2,1,0:T(2,128)} %maximum_maximum_fusion.add_ref, f32[16,256,256]{2,1,0:T(8,128)} %position_bias.1.bias_ref), custom_call_target="tpu_custom_call" | custom-call | tf_op jit(solution)/shard_map/attend/pallas_call | solution.py:204
  194.6 2.5 copy.89
  197.1 62.2 %all-gather.12.cloned.1.call-done = bf16[4608,1152]{1,0:T(8,128)(2,1)} async-done(((bf16[144,1152]{1,0:T(8,128)(2,1)}), bf16[4608,1152]{1,0:T(8,128)(2,1)}) %all-gather.12.cloned.1.call-update) | async-done | bytes 10616848 | tf_op jit(solution)/shard_map/all_gather | solution.py:405
  259.3 12.3 %unpack_down.1 = bf16[4608,1152]{1,0:T(8,128)(2,1)} custom-call(bf16[4,8,144,1152]{3,2,1,0:T(8,128)(2,1)} %bitcast.140), custom_call_target="tpu_custom_call" | custom-call | tf_op jit(solution)/shard_map/unpack_down/pallas_call | solution.py:368
  271.6 3.6 fusion.138
  278.6 68.7 %all-gather.10.cloned.1.call-done = bf16[4608,1152]{1,0:T(8,128)(2,1)} async-done(((bf16[144,1152]{1,0:T(8,128)(2,1)}), bf16[4608,1152]{1,0:T(8,128)(2,1)}) %all-gather.10.cloned.1.call-update) | async-done | bytes 10616848 | tf_op jit(solution)/shard_map/all_gather | solution.py:405
  347.4 9.9 fusion.21
  357.3 4.5 convert_reduce_fusion.3
  362.5 8.5 fusion.24
  371.0 3.6 convert_reduce_fusion.2
  374.7 8.1 fusion.27
  382.8 3.6 convert_reduce_fusion.1
  386.4 8.1 fusion.30
  394.5 3.6 convert_reduce_fusion
  398.1 1.7 fusion.89
  401.7 1.8 convolution_add_fusion.4
  403.5 3.1 multiply_reduce_fusion
  409.3 3.0 convolution_convert_fusion.8
  412.2 2.4 copy.104
  414.6 2.5 copy.105
  417.1 2.5 copy.106
  419.7 17.4 %attend_back.1 = (bf16[4,512,1152]{2,1,0:T(8,128)(2,1)}, f32[16,256,256]{2,1,0:T(8,128)}) custom-call(bf16[4,512,288]{2,1,0:T(8,128)(2,1)} %bitcast.141, bf16[4,512,896]{2,1,0:T(8,128)(2,1)} %get-tuple-element.25.qkv_ref, bf16[4,2,4,256,256]{4,3,2,1,0:T(8,128)(2,1)} %get-tuple-element.26.probs_ref, bf16[4,512,288]{2,1,0:T(8,128)(2,1)} %bitcast.142), custom_call_target="tpu_custom_call" | custom-call | tf_op jit(solution)/shard_map/attend_back/pallas_call | solution.py:268
  437.1 3.0 bitcast_reduce_fusion
  442.3 73.4 %all-gather.3 = bf16[32,2,2304]{2,1,0:T(2,128)(2,1)} all-gather(bf16[1,2,2304]{2,1,0:T(2,128)(2,1)} %reshape.328), channel_id=1, replica_groups=mesh['dp'=8,'fsdp'=4] {'dp','fsdp'}, dimensions={0}, use_global_device_ids=true | all-gather | bytes 304128 | tf_op jit(solution)/shard_map/all_gather | solution.py:559
  515.6 1.8 reshape.329
  518.8 4.0 fusion.17
  522.9 4.7 convolution_add_fusion.2
  527.6 1.8 convolution_add_fusion.1
  529.4 4.5 multiply_reduce_fusion.1
  544.5 27.3 %table_gradient.1 = f32[128,128]{1,0:T(8,128)} custom-call(s32[256,256]{1,0:T(8,128)} %index_ref.3, f32[16,256,256]{2,1,0:T(8,128)} %get-tuple-element.28.pairs_ref), custom_call_target="tpu_custom_call" | custom-call | tf_op jit(solution)/shard_map/table_gradient/pallas_call | solution.py:154
  576.3 1.7 concatenate.38
  580.1 5.1 convolution_convert_fusion
  585.2 3.2 convolution_convert_fusion.1
  588.5 3.2 convolution_convert_fusion.2
  591.7 3.3 convolution_convert_fusion.3
  595.0 1.8 fusion.112
  599.8 14.6 %pad_maximum_fusion.1.in_ref = bf16[4608,1152]{1,0:T(8,128)(2,1)} fusion(bf16[1152,1152]{1,0:T(8,128)(2,1)} %convolution_convert_fusion, bf16[1152,1152]{1,0:T(8,128)(2,1)} %convolution_convert_fusion.1, bf16[1152,1152]{1,0:T(8,128)(2,1)} %convolution_convert_fusion.2, bf16[1152,1152]{1,0:T(8,128)(2,1)} %convolution_convert_fusion.3), kind=kLoop, calls=%fused_computation.1 | loop fusion | flops 42467328 | bytes 21233664 | tf_op jit(solution)/shard_map/concatenate | solution.py:540
  614.4 12.0 %pack_down.1 = bf16[4,8,144,1152]{3,2,1,0:T(8,128)(2,1)} custom-call(bf16[4608,1152]{1,0:T(8,128)(2,1)} %pad_maximum_fusion.1.in_ref), custom_call_target="tpu_custom_call" | custom-call | tf_op jit(solution)/shard_map/pack_down/pallas_call | solution.py:351
  626.5 2.1 fusion.175.one_ref
  628.6 11.9 %pair_grad.1 = bf16[4,1152,1152]{2,1,0:T(8,128)(2,1)} custom-call(bf16[1152,512]{1,0:T(8,128)(2,1)} %fusion.175.one_ref, bf16[1152,512]{1,0:T(8,128)(2,1)} %bitcast.143, bf16[4,512,1152]{2,1,0:T(8,128)(2,1)} %get-tuple-element.27.right_ref), custom_call_target="tpu_custom_call" | custom-call | tf_op jit(solution)/shard_map/pair_grad/pallas_call | solution.py:308
  640.8 3.6 fusion.3
  649.6 5.2 pad_maximum_fusion
  656.2 5.1 convolution_add_fusion.12
  661.2 4.1 convolution_add_fusion.10
  665.4 1.7 convolution_add_fusion.8
  667.1 2.8 fusion.13
  669.9 2.4 copy.131
  673.6 5.1 add_convert_fusion
  678.8 2.4 copy.133
  683.2 33.6 %all-reduce.7.cloned.1.call-done = f32[4,7168]{1,0:T(4,128)} async-done(((f32[4,7168]{1,0:T(4,128)}), f32[4,7168]{1,0:T(4,128)}) %all-reduce.7.cloned.1.call-update) | async-done | bytes 114704 | tf_op jit(solution)/shard_map/psum | solution.py:602
  721.3 9.6 all_gather.39
  731.7 34.9 %reduce-scatter.13.cloned.1.call-done = bf16[144,1152]{1,0:T(8,128)(2,1)} async-done(((bf16[4608,1152]{1,0:T(8,128)(2,1)}), bf16[144,1152]{1,0:T(8,128)(2,1)}) %reduce-scatter.13.cloned.1.call-update) | async-done | bytes 331792
  769.2 144.6 %reduce-scatter.9.cloned.1.call-done = bf16[144,1152]{1,0:T(8,128)(2,1)} async-done(((bf16[4608,1152]{1,0:T(8,128)(2,1)}), bf16[144,1152]{1,0:T(8,128)(2,1)}) %reduce-scatter.9.cloned.1.call-update) | async-done | bytes 331792 | tf_op jit(solution)/shard_map/reduce_scatter | solution.py:411
  913.8 2.1 fusion.136
  915.9 145.0 %reduce-scatter.11.cloned.1.call-done = bf16[144,1152]{1,0:T(8,128)(2,1)} async-done(((bf16[4608,1152]{1,0:T(8,128)(2,1)}), bf16[144,1152]{1,0:T(8,128)(2,1)}) %reduce-scatter.11.cloned.1.call-update) | async-done | bytes 331792 | tf_op jit(solution)/shard_map/reduce_scatter | solution.py:411
  1060.9 1.9 convert_element_type.251
  (246 shorter events, 76.8 us)
Async XLA Ops:
  8.0 76.9 %copy-start.11 = (bf16[576,288]{0,1:T(8,128)(2,1)S(1)}, bf16[576,288]{0,1:T(8,128)(2,1)}, u32[]{:S(2)}) copy-start(bf16[576,288]{0,1:T(8,128)(2,1)} %param.37) | copy-start | bytes 995332
  8.0 149.3 %all-reduce.9.cloned.1.call-start = ((), (), s32[]{:S(2)}) async-start(), calls=%async_computation.12 | async-start | bytes 327680
  80.6 4.2 copy-start.14
  82.6 4.7 copy-start.31
  82.6 4.8 copy-start.32
  82.6 4.7 copy-start.34
  82.6 4.7 copy-start.35
  82.6 4.7 copy-start.36
  82.6 4.7 copy-start.37
  82.7 4.7 copy-start.38
  82.7 4.7 copy-start.39
  82.7 18.6 %copy-start.2 = (bf16[2,256,1152]{2,1,0:T(8,128)(2,1)S(1)}, bf16[2,256,1152]{2,1,0:T(8,128)(2,1)}, u32[]{:S(2)}) copy-start(bf16[2,256,1152]{2,1,0:T(8,128)(2,1)} %param.21) | copy-start | bytes 3538948
  82.7 90.6 %all-gather.8.cloned.1.call-start = ((), (), s32[]{:S(2)}) async-start(), calls=%async_computation.4 | async-start | bytes 10948608 | tf_op jit(solution)/shard_map/all_gather | solution.py:405
  84.9 174.4 %all-gather.12.cloned.1.call-start = ((), (), s32[]{:S(2)}) async-start(), calls=%async_computation.6 | async-start | bytes 10948608 | tf_op jit(solution)/shard_map/all_gather | solution.py:405
  86.6 260.8 %all-gather.10.cloned.1.call-start = ((), (), s32[]{:S(2)}) async-start(), calls=%async_computation.5 | async-start | bytes 10948608 | tf_op jit(solution)/shard_map/all_gather | solution.py:405
  87.2 629.6 %all-reduce.7.cloned.1.call-start = ((), (), s32[]{:S(2)}) async-start(), calls=%async_computation.9 | async-start | bytes 229376 | tf_op jit(solution)/shard_map/psum | solution.py:602
  105.6 2.5 copy-start.15
  259.3 12.3 %copy-start.4 = (bf16[512,4,288]{0,2,1:T(8,128)(2,1)S(1)}, bf16[512,4,288]{0,2,1:T(8,128)(2,1)}, u32[]{:S(2)}) copy-start(bf16[512,4,288]{0,2,1:T(8,128)(2,1)} %copy.89) | copy-start | bytes 3538948
  259.3 12.3 %copy-start.30 = (f32[1152]{0:T(1024)S(1)}, f32[1152]{0:T(1024)}, u32[]{:S(2)}) copy-start(f32[1152]{0:T(1024)} %reshape.320) | copy-start | bytes 13828
  275.2 2.0 copy-start.22
  347.4 9.9 copy-start.5
  357.3 4.6 copy-start.9
  357.3 4.6 copy-start.29
  357.3 5.2 copy-start.40
  357.3 13.7 %slice-start.5 = ((s8[10616832]{0:T(1024)(128)(4,1)}), s8[4194304]{0:T(1024)(128)(4,1)S(1)}, s32[]{:S(2)}) async-start(s8[10616832]{0:T(1024)(128)(4,1)} %bitcast.136), calls=%async_computation.18 | async-start | bytes 8388608
  361.8 36.3 %copy-start.45 = (bf16[512,1152]{1,0:T(8,128)(2,1)}, bf16[512,1152]{1,0:T(8,128)(2,1)S(1)}, u32[]{:S(2)}) copy-start(bf16[512,1152]{1,0:T(8,128)(2,1)S(1)} %get-tuple-element.153) | copy-start | bytes 3538948
  362.5 8.5 slice-start.6
  362.5 8.5 slice-start.7
  371.0 3.7 copy-start.28
  374.7 25.2 %copy-start.41 = (bf16[512,1152]{1,0:T(8,128)(2,1)}, bf16[512,1152]{1,0:T(8,128)(2,1)S(1)}, u32[]{:S(2)}) copy-start(bf16[512,1152]{1,0:T(8,128)(2,1)S(1)} %get-tuple-element.151) | copy-start | bytes 3538948
  382.8 3.6 copy-start.27
  386.4 15.2 %copy-start.43 = (bf16[512,1152]{1,0:T(8,128)(2,1)}, bf16[512,1152]{1,0:T(8,128)(2,1)S(1)}, u32[]{:S(2)}) copy-start(bf16[512,1152]{1,0:T(8,128)(2,1)S(1)} %get-tuple-element.149) | copy-start | bytes 3538948
  398.1 5.3 copy-start.53
  401.6 1.8 copy-start.1
  401.6 1.8 copy-start.17
  401.6 1.8 copy-start.24
  406.6 2.7 copy-start.8
  518.8 8.7 slice-start
  518.8 8.7 slice-start.1
  518.8 8.7 slice-start.3
  522.8 4.7 slice-start.2
  522.8 4.7 slice-start.4
  522.8 4.7 copy-start.33
  527.6 1.8 copy-start.19
  527.6 1.8 copy-start.21
  579.6 141.7 %reduce-scatter.7.cloned.1.call-start = ((), (), s32[]{:S(2)}) async-start(), calls=%async_computation.7 | async-start | bytes 81920 | tf_op jit(solution)/shard_map/reduce_scatter | solution.py:570
  580.1 5.1 copy-start.6
  580.1 5.1 copy-start.49
  585.2 3.3 copy-start.47
  588.5 3.2 copy-start.51
  591.7 3.3 copy-start.12
  591.7 3.3 copy-start.13
  599.8 166.8 %reduce-scatter.13.cloned.1.call-start = ((), (), s32[]{:S(2)}) async-start(), calls=%async_computation.11 | async-start | bytes 10948608
  626.4 287.3 %reduce-scatter.9.cloned.1.call-start = ((), (), s32[]{:S(2)}) async-start(), calls=%async_computation.8 | async-start | bytes 10948608 | tf_op jit(solution)/shard_map/reduce_scatter | solution.py:411
  640.6 420.3 %reduce-scatter.11.cloned.1.call-start = ((), (), s32[]{:S(2)}) async-start(), calls=%async_computation.10 | async-start | bytes 10948608 | tf_op jit(solution)/shard_map/reduce_scatter | solution.py:411
  640.8 3.6 copy-start.10
  640.8 3.6 copy-start.44
  644.4 1.7 copy-start.42
  656.1 5.1 copy-start.48
  656.1 9.2 slice-start.8
  656.2 9.2 slice-start.9
  661.2 4.1 slice-start.10
  661.2 4.1 copy-start.50
  665.4 1.8 copy-start.52
  (10 other events, 12.2 us)
Sparse Core Ops, SparseCore 0:
  82.7 73.9 all-reduce.8
  599.9 16.4 reduce-scatter.6
  626.6 139.9 reduce-scatter.12
  772.5 141.1 reduce-scatter.8
  919.7 141.1 reduce-scatter.10
Sparse Core Ops, SparseCore 1:
  86.7 83.8 all-gather.7
  173.9 85.3 all-gather.11
  262.1 85.2 all-gather.9
  579.7 137.0 all-reduce.6

commit v2 on v1

--- a/solution.py
+++ b/solution.py
@@ -2,6 +2,7 @@
 
 import jax
 import jax.numpy as jnp
+import numpy as np
 from jax import lax
 from jax.experimental import pallas as pl
 from jax.experimental.pallas import tpu as pltpu
@@ -67,50 +68,50 @@
 
 
 def bias_kernel(index_ref, table_ref, bias_ref):
-    chunks = table_ref.shape[2] // LANES
-    rows = index_ref.shape[0]
-    for head in range(table_ref.shape[0]):
-        line = table_ref[head]
-        pieces = [
-            jnp.broadcast_to(line[:, c * LANES : (c + 1) * LANES], (8, LANES))
-            for c in range(chunks)
-        ]
-
-        def some_rows(step, carry, head=head, pieces=pieces):
-            for part in range(2):
-                at = pl.multiple_of(step * 16 + part * 8, 8)
-                for col in range(index_ref.shape[1] // LANES):
-                    lanes = slice(col * LANES, (col + 1) * LANES)
-                    index = index_ref[pl.ds(at, 8), lanes]
-                    low = index & (LANES - 1)
-                    high = index >> 7
-                    found = jnp.take_along_axis(pieces[0], low, axis=1)
-                    for c in range(1, chunks):
-                        found = jnp.where(
-                            high == c, jnp.take_along_axis(pieces[c], low, axis=1), found
-                        )
-                    bias_ref[head, pl.ds(at, 8), lanes] = found
-            return carry
-
-        lax.fori_loop(0, rows // 16, some_rows, 0)
+    heads, rows, tokens = bias_ref.shape
+    table = table_ref[...]
+    sub = lax.broadcasted_iota(jnp.int32, (8, tokens), 0)
+    lane_of = lax.broadcasted_iota(jnp.int32, (LANES, tokens), 0)
+    line = lax.broadcasted_iota(jnp.int32, (heads, heads * 8), 0)
+    column = lax.broadcasted_iota(jnp.int32, (heads, heads * 8), 1)
+    add_up = jnp.where(column >> 3 == line, 1.0, 0.0).astype(jnp.bfloat16)
+
+    def one_row(row):
+        index = index_ref[pl.ds(row, 1), :]
+        low = jnp.broadcast_to(index & (LANES - 1), (LANES, tokens))
+        hit = sub == jnp.broadcast_to(index >> 7, (8, tokens))
+        picked = matmul(table, jnp.where(lane_of == low, 1.0, 0.0).astype(jnp.bfloat16))
+        only = jnp.concatenate(
+            [jnp.where(hit, picked[h * 8 : (h + 1) * 8], 0.0) for h in range(heads)], axis=0
+        ).astype(jnp.bfloat16)
+        found = matmul(add_up, only)
+        for h in range(heads):
+            bias_ref[h, pl.ds(row, 1), :] = found[h : h + 1]
+
+    def some_rows(step, carry):
+        for part in range(4):
+            one_row(step * 4 + part)
+        return carry
+
+    lax.fori_loop(0, rows // 4, some_rows, 0)
 
 
 def position_bias(index, table):
     heads, padded = table.shape
     tokens = index.shape[0]
-    group = heads // 4
+    block = 64
     return pl.pallas_call(
         bias_kernel,
-        grid=(4,),
+        grid=(tokens // block,),
         in_specs=[
-            pl.BlockSpec((tokens, tokens), lambda f: (0, 0)),
-            pl.BlockSpec((group, 1, padded), lambda f: (f, 0, 0)),
+            pl.BlockSpec((block, tokens), lambda i: (i, 0)),
+            pl.BlockSpec((heads * 8, LANES), lambda i: (0, 0)),
         ],
-        out_specs=pl.BlockSpec((group, tokens, tokens), lambda f: (f, 0, 0)),
+        out_specs=pl.BlockSpec((heads, block, tokens), lambda i: (0, i, 0)),
         out_shape=jax.ShapeDtypeStruct((heads, tokens, tokens), jnp.float32),
         compiler_params=params(),
         name="position_bias",
-    )(index, table.reshape(heads, 1, padded))
+    )(index, table.reshape(heads * 8, LANES))
 
 
 def table_kernel(index_ref, pairs_ref, out_ref):
@@ -287,93 +288,195 @@
     )(grad, qkv, probs, hidden)
 
 
-def pair_grad_kernel(one_ref, two_ref, right_ref, out_ref):
+def store_slot(slot, own_ref, send_ref, at, value):
+    half = own_ref.shape[0]
+
+    @pl.when(slot < half)
+    def _():
+        own_ref[(slot,) + at] = value
+
+    @pl.when(slot >= half)
+    def _():
+        send_ref[(slot - half,) + at] = value
+
+
+def pair_grad_kernel(slot_ref, one_ref, two_ref, right_ref, own_ref, send_ref):
     cut = 3 * (right_ref.shape[2] // 4)
     below = cut // LANES * LANES
     above = below + LANES
+    rows = own_ref.shape[2]
     right = right_ref[0]
+    lane = lax.broadcasted_iota(jnp.int32, (rows, LANES), 1)
     first = matmul(one_ref[...], right[:, :above])
     last = matmul(two_ref[...], right[:, below:])
-    lane = lax.broadcasted_iota(jnp.int32, (first.shape[0], LANES), 1)
-    out_ref[0, :, :below] = first[:, :below].astype(jnp.bfloat16)
-    out_ref[0, :, below:above] = jnp.where(
-        lane < cut - below, first[:, below:], last[:, :LANES]
-    ).astype(jnp.bfloat16)
-    out_ref[0, :, above:] = last[:, LANES:].astype(jnp.bfloat16)
-
-
-def pair_grad(normed_t, mixed_t, right):
+    for part in range(2 * own_ref.shape[0]):
+        at = slice(part * rows, (part + 1) * rows)
+        value = jnp.concatenate(
+            [
+                first[at, :below],
+                jnp.where(lane < cut - below, first[at, below:], last[at, :LANES]),
+                last[at, LANES:],
+            ],
+            axis=1,
+        ).astype(jnp.bfloat16)
+        store_slot(slot_ref[part], own_ref, send_ref, (0,), value)
+
+
+def one_grad_kernel(slot_ref, one_ref, right_ref, own_ref, send_ref):
+    rows = own_ref.shape[2]
+    first = matmul(one_ref[...], right_ref[0])
+    for part in range(2 * own_ref.shape[0]):
+        value = first[part * rows : (part + 1) * rows].astype(jnp.bfloat16)
+        store_slot(slot_ref[part], own_ref, send_ref, (0,), value)
+
+
+def slot_grad(kernel, slots, lefts, right, parts, name):
     groups, rows, packed = right.shape
-    depth = normed_t.shape[0]
+    depth = lefts[0].shape[0]
+    half = jax.ShapeDtypeStruct((parts // 2, groups, depth // parts, packed), jnp.bfloat16)
+    out = pl.BlockSpec((parts // 2, 1, depth // parts, packed), lambda f, s: (0, f, 0, 0))
     return pl.pallas_call(
-        pair_grad_kernel,
+        kernel,
+        grid_spec=pltpu.PrefetchScalarGridSpec(
+            num_scalar_prefetch=1,
+            grid=(groups,),
+            in_specs=[pl.BlockSpec((depth, rows), lambda f, s: (0, 0)) for _ in lefts]
+            + [pl.BlockSpec((1, rows, packed), lambda f, s: (f, 0, 0))],
+            out_specs=[out, out],
+        ),
+        out_shape=[half, half],
+        compiler_params=params(),
+        name=name,
+    )(slots, *lefts, right)
+
+
+def down_grad_kernel(slot_ref, left_ref, right_ref, own_ref, send_ref):
+    half, groups, rows, packed = own_ref.shape
+    width = packed // groups
+    value = matmul(left_ref[...], right_ref[...]).astype(jnp.bfloat16)
+    slot = slot_ref[pl.program_id(0)]
+    for f in range(groups):
+        block = jnp.concatenate(
+            [
+                value[g * rows : (g + 1) * rows, f * width : (f + 1) * width]
+                for g in range(value.shape[0] // rows)
+            ],
+            axis=1,
+        )
+        store_slot(slot, own_ref, send_ref, (f,), block)
+
+
+def down_slot_grad(slots, left, right, groups, parts, rows):
+    hidden, tokens = left.shape
+    packed = right.shape[1]
+    half = jax.ShapeDtypeStruct((parts // 2, groups, rows, packed), jnp.bfloat16)
+    out = pl.BlockSpec((parts // 2, groups, rows, packed), lambda d, s: (0, 0, 0, 0))
+    return pl.pallas_call(
+        down_grad_kernel,
+        grid_spec=pltpu.PrefetchScalarGridSpec(
+            num_scalar_prefetch=1,
+            grid=(parts,),
+            in_specs=[
+                pl.BlockSpec((hidden // parts, tokens), lambda d, s: (d, 0)),
+                pl.BlockSpec((tokens, packed), lambda d, s: (0, 0)),
+            ],
+            out_specs=[out, out],
+        ),
+        out_shape=[half, half],
+        compiler_params=params(),
+        name="down_grad",
+    )(slots, left, right)
+
+
+def add_kernel(one_ref, two_ref, three_ref, four_ref, came_ref, *outs):
+    for k, (mine, out) in enumerate(zip((one_ref, two_ref, three_ref, four_ref), outs)):
+        total = mine[0, 0].astype(jnp.float32) + came_ref[k, 0].astype(jnp.float32)
+        out[0] = total.astype(jnp.bfloat16)
+
+
+def add_halves(own, came):
+    half, groups, rows, packed = own.shape
+    return pl.pallas_call(
+        add_kernel,
         grid=(groups,),
         in_specs=[
-            pl.BlockSpec((depth, rows), lambda f: (0, 0)),
-            pl.BlockSpec((depth, rows), lambda f: (0, 0)),
-            pl.BlockSpec((1, rows, packed), lambda f: (f, 0, 0)),
-        ],
-        out_specs=pl.BlockSpec((1, depth, packed), lambda f: (f, 0, 0)),
-        out_shape=jax.ShapeDtypeStruct((groups, depth, packed), jnp.bfloat16),
+            pl.BlockSpec((1, 1, rows, packed), lambda f, k=k: (k, f, 0, 0)) for k in range(half)
+        ]
+        + [pl.BlockSpec((half, 1, rows, packed), lambda f: (0, f, 0, 0))],
+        out_specs=[pl.BlockSpec((1, rows, packed), lambda f: (f, 0, 0))] * half,
+        out_shape=[jax.ShapeDtypeStruct((groups, rows, packed), jnp.bfloat16)] * half,
         compiler_params=params(),
-        name="pair_grad",
-    )(normed_t, mixed_t, right)
-
-
-def pack_down_kernel(in_ref, out_ref):
-    groups, _, rows, packed = out_ref.shape
+        name="add_halves",
+    )(*([own] * half), came)
+
+
+def place_kernel(part_ref, *refs):
+    *pieces, out_ref, sems = refs
+    copies = [
+        pltpu.make_async_copy(piece, out_ref.at[:, part_ref[j]], sems.at[j])
+        for j, piece in enumerate(pieces)
+    ]
+    for copy in copies:
+        copy.start()
+    for copy in copies:
+        copy.wait()
+
+
+def place_pieces(part_of, pieces):
+    groups, rows, width = pieces[0].shape
+    parts = len(pieces)
+    return pl.pallas_call(
+        place_kernel,
+        grid_spec=pltpu.PrefetchScalarGridSpec(
+            num_scalar_prefetch=1,
+            grid=(1,),
+            in_specs=[pl.BlockSpec(memory_space=pl.ANY)] * parts,
+            out_specs=pl.BlockSpec(memory_space=pl.ANY),
+            scratch_shapes=[pltpu.SemaphoreType.DMA((parts,))],
+        ),
+        out_shape=jax.ShapeDtypeStruct((groups, parts, rows, width), pieces[0].dtype),
+        compiler_params=params(),
+        name="place_pieces",
+    )(part_of, *pieces)
+
+
+def unpack_kernel(part_ref, *refs):
+    *pieces, out_ref, held, sems = refs
+    step = pl.program_id(0)
+    _, groups, rows, packed = held.shape
     width = packed // groups
-    count = in_ref.shape[0] // rows
-    for g in range(count):
-        block = in_ref[g * rows : (g + 1) * rows, :]
-        for f in range(groups):
-            out_ref[f, 0, :, g * width : (g + 1) * width] = block[:, f * width : (f + 1) * width]
-
-
-def unpack_down_kernel(in_ref, out_ref):
-    groups, _, rows, packed = in_ref.shape
-    width = packed // groups
-    count = out_ref.shape[0] // rows
-    for f in range(groups):
-        block = in_ref[f, 0]
-        for g in range(count):
-            out_ref[g * rows : (g + 1) * rows, f * width : (f + 1) * width] = block[
-                :, g * width : (g + 1) * width
-            ]
-
-
-def pack_down(natural, groups, parts, rows):
-    total, width = natural.shape
-    count = total // (parts * rows)
-    if rows % 16:
-        split = natural.reshape(parts, count, rows, groups, width // groups)
-        return split.transpose(3, 0, 2, 1, 4).reshape(groups, parts, rows, width)
+
+    @pl.when(step == 0)
+    def _():
+        for j, piece in enumerate(pieces):
+            pltpu.make_async_copy(piece, held.at[j], sems.at[j]).start()
+
+    pltpu.make_async_copy(pieces[0], held.at[step], sems.at[step]).wait()
+    for g in range(out_ref.shape[0] // rows):
+        out_ref[g * rows : (g + 1) * rows, :] = jnp.concatenate(
+            [held[step, f][:, g * width : (g + 1) * width] for f in range(groups)], axis=1
+        )
+
+
+def unpack_pieces(part_of, pieces, fold):
+    groups, rows, width = pieces[0].shape
+    parts = len(pieces)
     return pl.pallas_call(
-        pack_down_kernel,
-        grid=(parts,),
-        in_specs=[pl.BlockSpec((count * rows, width), lambda d: (d, 0))],
-        out_specs=pl.BlockSpec((groups, 1, rows, width), lambda d: (0, d, 0, 0)),
-        out_shape=jax.ShapeDtypeStruct((groups, parts, rows, width), natural.dtype),
+        unpack_kernel,
+        grid_spec=pltpu.PrefetchScalarGridSpec(
+            num_scalar_prefetch=1,
+            grid=(parts,),
+            in_specs=[pl.BlockSpec(memory_space=pl.ANY)] * parts,
+            out_specs=pl.BlockSpec((fold * rows, width), lambda j, p: (p[j], 0)),
+            scratch_shapes=[
+                pltpu.VMEM((parts, groups, rows, width), pieces[0].dtype),
+                pltpu.SemaphoreType.DMA((parts,)),
+            ],
+        ),
+        out_shape=jax.ShapeDtypeStruct((parts * fold * rows, width), pieces[0].dtype),
         compiler_params=params(),
-        name="pack_down",
-    )(natural)
-
-
-def unpack_down(packed):
-    groups, parts, rows, width = packed.shape
-    count = 4
-    if rows % 16:
-        split = packed.reshape(groups, parts, rows, count, width // count)
-        return split.transpose(1, 3, 2, 0, 4).reshape(parts * count * rows, width)
-    return pl.pallas_call(
-        unpack_down_kernel,
-        grid=(parts,),
-        in_specs=[pl.BlockSpec((groups, 1, rows, width), lambda d: (0, d, 0, 0))],
-        out_specs=pl.BlockSpec((count * rows, width), lambda d: (d, 0)),
-        out_shape=jax.ShapeDtypeStruct((parts * count * rows, width), packed.dtype),
-        compiler_params=params(),
-        name="unpack_down",
-    )(packed)
+        name="unpack_pieces",
+    )(part_of, *pieces)
 
 
 def take_proj_kernel(in_ref, out_ref):
@@ -399,6 +502,123 @@
     )(packed)
 
 
+NEAR = ((0, 2, 4, 6), (0, 4, 2, 6))
+
+
+def is_cube():
+    return lax.axis_size("dp") == 8 and lax.axis_size("fsdp") == 4
+
+
+def part_tables():
+    part_of = np.zeros((8, 8), np.int32)
+    slot_of = np.zeros((8, 8), np.int32)
+    for part in range(8):
+        core = part & 1
+        order = [part ^ m for m in NEAR[core]] + [part ^ 1 ^ m for m in NEAR[1 - core]]
+        part_of[part] = order
+        for slot, other in enumerate(order):
+            slot_of[part, other] = slot
+    own = lax.axis_index("dp")
+    pick = lambda table: lax.dynamic_slice(jnp.asarray(table), (own, 0), (1, 8))[0]
+    return pick(part_of), pick(slot_of)
+
+
+def swap(value, hop):
+    return lax.ppermute(value, "dp", [(i, i ^ NEAR[i & 1][hop]) for i in range(8)])
+
+
+def swap_core(value):
+    return lax.ppermute(value, "dp", [(i, i ^ 1) for i in range(8)])
+
+
+def after(value, *others):
+    return lax.optimization_barrier((value, *others))[0]
+
+
+class Gather:
+    def __init__(self, shard, behind=None, ready=None):
+        if behind is not None:
+            shard = after(shard, behind.own)
+        own = lax.all_gather(shard, "fsdp", axis=0, tiled=False)
+        if behind is not None:
+            own = after(own, behind.first)
+        if ready is not None:
+            own = after(own, ready)
+        self.own = own
+        self.first = swap(own, 1)
+        second = swap(own, 2)
+        third = swap(self.first, 2)
+        near = [own, self.first, second, third]
+        self.pieces = near + [swap_core(piece) for piece in near]
+
+
+class Scatter:
+    def __init__(self, own, send):
+        self.own = own
+        self.came = swap_core(send)
+
+    def near(self):
+        self.zero, self.one, two, three = add_halves(self.own, self.came)
+        self.far = swap(three, 2)
+        self.side = swap(two, 2)
+        return three
+
+    def back(self):
+        one = self.one.astype(jnp.float32) + self.far.astype(jnp.float32)
+        one = one.astype(jnp.bfloat16)
+        self.last = swap(one, 1)
+        return one
+
+    def total(self):
+        total = self.zero.astype(jnp.float32) + self.side.astype(jnp.float32)
+        self.sum = (total + self.last.astype(jnp.float32)).astype(jnp.bfloat16)
+        return self.sum
+
+    def end(self):
+        return lax.psum_scatter(self.sum, "fsdp", scatter_dimension=0, tiled=False)
+
+
+def swap_bit(value, axis, bit):
+    size = lax.axis_size(axis)
+    return lax.ppermute(value, axis, [(i, i ^ (1 << bit)) for i in range(size)])
+
+
+def bit_of(axis, bit):
+    return (lax.axis_index(axis) >> bit) & 1 == 1
+
+
+def small_gather(value, axis):
+    if not is_cube():
+        return lax.all_gather(value, axis, axis=0, tiled=True)
+    for bit in range(lax.axis_size(axis).bit_length() - 1):
+        other = swap_bit(value, axis, bit)
+        value = jnp.where(
+            bit_of(axis, bit),
+            jnp.concatenate([other, value], axis=0),
+            jnp.concatenate([value, other], axis=0),
+        )
+    return value
+
+
+def small_scatter(value, axis):
+    if not is_cube():
+        return lax.psum_scatter(value, axis, scatter_dimension=0, tiled=True)
+    for bit in reversed(range(lax.axis_size(axis).bit_length() - 1)):
+        half = value.shape[0] // 2
+        high = bit_of(axis, bit)
+        keep = jnp.where(high, value[half:], value[:half])
+        value = keep + swap_bit(jnp.where(high, value[:half], value[half:]), axis, bit)
+    return value
+
+
+def small_sum(value, axis):
+    if not is_cube():
+        return lax.psum(value, axis)
+    for bit in range(lax.axis_size(axis).bit_length() - 1):
+        value = value + swap_bit(value, axis, bit)
+    return value
+
+
 def gather_shards(shard):
     rows, width = shard.shape
     groups, parts = lax.axis_size("fsdp"), lax.axis_size("dp")
@@ -414,6 +634,18 @@
         scatter_dimension=0,
         tiled=True,
     )
+
+
+def pack_down(natural, groups, parts, rows):
+    total, width = natural.shape
+    split = natural.reshape(parts, total // (parts * rows), rows, groups, width // groups)
+    return split.transpose(3, 0, 2, 1, 4).reshape(groups, parts, rows, width)
+
+
+def unpack_down(packed, fold):
+    groups, parts, rows, width = packed.shape
+    split = packed.reshape(groups, parts, rows, fold, width // fold)
+    return split.transpose(1, 3, 2, 0, 4).reshape(parts * fold * rows, width)
 
 
 def body(
@@ -468,7 +700,7 @@
         ]
     )
     small = jnp.pad(small, (0, -small.shape[0] % 1024))
-    small_all = lax.all_gather(small, "fsdp", axis=0, tiled=False)
+    small_all = small_gather(small.reshape(1, -1, LANES), "fsdp").reshape(groups, -1)
 
     def vector_of(slot):
         return small_all[:, slot * shard_cols : (slot + 1) * shard_cols].reshape(-1).astype(wide)
@@ -478,19 +710,18 @@
     up_b = small_all[:, at : at + up_bias.shape[0]].astype(wide)
     at = at + up_bias.shape[0]
     table = small_all[:, at : at + group_heads * table_rows].reshape(heads, table_rows)
-    table = jnp.pad(table.astype(wide), ((0, 0), (0, -table_rows % LANES)))
+    table = jnp.pad(table, ((0, 0), (0, 8 * LANES - table_rows)))
+    bias = position_bias(offset_index, table)
 
     time_low = (time_vector.astype(wide) + sinusoid(timesteps, width)).astype(low)
-    time_all = lax.all_gather(time_low, BOTH, axis=0, tiled=True)
+    time_all = small_gather(small_gather(time_low, "fsdp"), "dp")
     all_images = time_all.shape[0]
     time_cols = lax.dynamic_slice(
         time_all, (0, own_part * shard_rows), (all_images, shard_rows)
     )
     time_weight = jnp.concatenate([tquery_weight, tvalue_weight], axis=1)
-    time_sum = lax.psum_scatter(
-        matmul(time_cols, time_weight), "dp", scatter_dimension=0, tiled=True
-    )
-    time_part = lax.all_gather(time_sum, "fsdp", axis=0, tiled=False)
+    time_sum = small_scatter(matmul(time_cols, time_weight), "dp")
+    time_part = small_gather(time_sum[None], "fsdp")
     time_own = lax.dynamic_slice(
         time_part, (0, own_group * count, 0), (groups, count, 2 * shard_cols)
     )
@@ -506,11 +737,20 @@
         axis=2,
     )
 
-    attn_full = gather_shards(wire_attn).reshape(groups, width, width)
-    up_full = gather_shards(up_weight).reshape(groups, width, width)
-    down_full = unpack_down(gather_shards(wire_down))
-
-    bias = position_bias(offset_index, table)
+    if is_cube():
+        part_of, slot_of = part_tables()
+        attn_move = Gather(wire_attn, ready=bias)
+        up_move = Gather(up_weight, behind=attn_move)
+        down_move = Gather(wire_down, behind=up_move)
+        attn_full = place_pieces(part_of, attn_move.pieces)
+        up_full = place_pieces(part_of, up_move.pieces)
+        down_full = unpack_pieces(part_of, down_move.pieces, fold)
+    else:
+        attn_full = gather_shards(wire_attn)
+        up_full = gather_shards(up_weight)
+        down_full = unpack_down(gather_shards(wire_down), fold)
+    attn_full = attn_full.reshape(groups, width, width)
+    up_full = up_full.reshape(groups, width, width)
 
     x_rows = images.reshape(rows, width).astype(wide)
     normed, unit_one, inv_one = normalize(x_rows, gain_one, shift_one)
@@ -523,42 +763,79 @@
     second_low = second.astype(low)
     grad_low = cotangent.reshape(rows, width)
     grad_rows = grad_low.astype(wide)
+    cube = is_cube()
+    wire = (groups, parts, shard_rows, width)
+    pre = [matmul(second_low, up_full[g]) + up_b[g] for g in range(groups)]
+    activ = [jax.nn.gelu(p, approximate=False).astype(low) for p in pre]
+    grad_cols = grad_low
+    if cube:
+        activ_t = jnp.concatenate([a.T for a in activ], axis=0)
+        own, send = down_slot_grad(slot_of, activ_t, grad_low, groups, parts, shard_rows)
+        down_move = Scatter(own, send)
+        grad_cols = after(grad_low, send)
     result = hidden + down_b
     d_second = jnp.zeros((rows, width), wide)
-    activ, d_pre = [], []
+    d_pre = []
     for g in range(groups):
-        pre_act = matmul(second_low, up_full[g]) + up_b[g]
-        act = jax.nn.gelu(pre_act, approximate=False).astype(low)
         down_g = down_full[g * width : (g + 1) * width]
-        result = result + matmul(act, down_g)
-        d_g = (times_transposed(grad_low, down_g) * gelu_slope(pre_act)).astype(low)
+        d_g = (times_transposed(grad_cols, down_g) * gelu_slope(pre[g])).astype(low)
         d_second = d_second + times_transposed(d_g, up_full[g])
-        activ.append(act)
         d_pre.append(d_g)
+    second_t = second_low.T
+    if cube:
+        second_t = after(second_t, down_move.near())
+        own, send = slot_grad(
+            one_grad_kernel, slot_of, [second_t], jnp.stack(d_pre), parts, "up_grad"
+        )
+        up_move = Scatter(own, send)
+        d_second = after(d_second, send)
+    else:
+        grad_down = jnp.concatenate([contract_rows(a, grad_low) for a in activ], axis=0)
+        down_sum = scatter_sum(pack_down(grad_down.astype(low), groups, parts, shard_rows))
+        grad_up = jnp.stack([contract_rows(second_low, d).astype(low) for d in d_pre])
+        up_sum = scatter_sum(grad_up.reshape(wire))
+    for g in range(groups):
+        down_g = down_full[g * width : (g + 1) * width]
+        result = result + matmul(activ[g], down_g)
     layer_out = result.astype(low).reshape(count, tokens, width)
-
-    grad_down = jnp.concatenate([contract_rows(a, grad_low).astype(low) for a in activ], axis=0)
-    grad_up = jnp.stack([contract_rows(second_low, d).astype(low) for d in d_pre])
-    down_sum = scatter_sum(pack_down(grad_down, groups, parts, shard_rows))
-    up_sum = scatter_sum(grad_up.reshape(groups, parts, shard_rows, width))
 
     d_hidden = grad_rows + norm_back(d_second, unit_two, inv_two, gain_two)
     d_hidden_low = d_hidden.astype(low)
-    d_mixed = times_transposed(d_hidden_low, proj_full).astype(low)
+    d_hidden_cols = after(d_hidden_low, down_move.back()) if cube else d_hidden_low
+    d_mixed = times_transposed(d_hidden_cols, proj_full).astype(low)
     d_mixed_split = d_mixed.reshape(rows, groups, shard_cols).transpose(1, 0, 2)
     d_hidden_split = d_hidden_low.reshape(rows, groups, shard_cols).transpose(1, 0, 2)
+    if cube:
+        d_mixed_split = after(d_mixed_split, up_move.near())
     d_packed, pairs = attend_back(d_mixed_split, qkv, probs, d_hidden_split)
-    attn_sum = scatter_sum(
-        pair_grad(normed_low.T, mixed.T, d_packed).reshape(groups, parts, shard_rows, width)
-    )
+    attn_back = attn_full
+    if cube:
+        normed_t = after(normed_low.T, up_move.back())
+        own, send = slot_grad(
+            pair_grad_kernel, slot_of, [normed_t, mixed.T], d_packed, parts, "pair_grad"
+        )
+        attn_move = Scatter(own, send)
+        attn_back = after(attn_full, send)
+        pairs = after(pairs, attn_move.near(), down_move.total())
+    else:
+        cut = 3 * shard_cols
+        grad_attn = jnp.stack(
+            [
+                jnp.concatenate(
+                    [contract_rows(normed_low, d[:, :cut]), contract_rows(mixed, d[:, cut:])],
+                    axis=1,
+                )
+                for d in d_packed
+            ]
+        )
+        attn_sum = scatter_sum(grad_attn.astype(low).reshape(wire))
 
     d_time = jnp.sum(d_packed.reshape(groups, count, tokens, width).astype(wide), axis=2)
     d_time = jnp.concatenate(
         [d_time[:, :, :shard_cols], d_time[:, :, 2 * shard_cols : 3 * shard_cols]], axis=2
     ).astype(low)
-    d_time_all = lax.all_gather(
-        d_time.transpose(1, 0, 2).reshape(count, groups * 2 * shard_cols), BOTH, axis=0, tiled=True
-    )
+    d_time = d_time.transpose(1, 0, 2).reshape(count, groups * 2 * shard_cols)
+    d_time_all = small_gather(small_gather(d_time, "fsdp"), "dp")
     d_time_cols = lax.dynamic_slice(
         d_time_all, (0, own_group * 2 * shard_cols), (all_images, 2 * shard_cols)
     )
@@ -567,8 +844,7 @@
     tvalue_grad = time_grads[:, shard_cols:]
     back = times_transposed(d_time_cols, time_weight)
     back = back.reshape(parts, groups, count, shard_rows).transpose(1, 0, 2, 3)
-    back = lax.psum_scatter(back, "fsdp", scatter_dimension=0, tiled=False)
-    back = lax.all_gather(back, "dp", axis=0, tiled=False)
+    back = small_gather(small_scatter(back, "fsdp"), "dp")
     back = lax.dynamic_slice(
         back, (0, own_part, 0, 0), (parts, 1, count, shard_rows)
     ).reshape(parts, count, shard_rows)
@@ -578,7 +854,7 @@
     d_normed = jnp.zeros((rows, width), wide)
     for g in range(groups):
         part = jnp.where(lane < 3 * shard_cols, d_packed[g], jnp.zeros((), low))
-        d_normed = d_normed + times_transposed(part, attn_full[g])
+        d_normed = d_normed + times_transposed(part, attn_back[g])
     d_input = d_hidden + norm_back(d_normed, unit_one, inv_one, gain_one)
     images_grad = d_input.astype(low).reshape(count, tokens, width)
 
@@ -599,8 +875,7 @@
     ]
     flat = jnp.concatenate(vectors, axis=1)
     flat = jnp.pad(flat, ((0, 0), (0, -flat.shape[1] % 1024)))
-    flat = lax.psum(flat, BOTH)
-    own = lax.dynamic_slice(flat, (own_group, 0), (1, flat.shape[1]))[0]
+    own = small_sum(small_scatter(flat.reshape(groups, -1, LANES), "fsdp"), "dp").reshape(-1)
     proj_bg, gain1_g, shift1_g, gain2_g, shift2_g, down_bg = (
         own[i * shard_cols : (i + 1) * shard_cols] for i in range(6)
     )
@@ -609,6 +884,13 @@
     at = at + up_bias.shape[0]
     table_grad = own[at : at + group_heads * table_rows].reshape(group_heads, table_rows)
 
+    if cube:
+        down_sum = down_move.end()
+        attn_move.back()
+        up_move.total()
+        up_sum = up_move.end()
+        attn_move.total()
+        attn_sum = attn_move.end()
     attn_sum = attn_sum.astype(wide)
     query_grad, key_grad, value_grad, proj_grad = (
         attn_sum[:, i * shard_cols : (i + 1) * shard_cols] for i in range(4)

time: 1080 us -> 1340 us (1.24)
  Pallas kernels: 136 us -> 840 us
  waiting for transfers between devices: 490 us -> 99.6 us
  blocking collectives: 181 us -> 0 us
  starting transfers between devices: 0.95 us -> 80.4 us
  other arithmetic: 48.3 us -> 75.9 us
  local copies, waits for them, and re-layouts: 75.2 us -> 89 us
    pallas_call x4 -> x10, Pallas kernels: 70 us -> 774 us  [the longest x2 647 us: place_pieces(): pl.pallas_call(place_kernel, grid_spec=pltpu.PrefetchScalarGridSpec(num_s...]
    reduce_scatter x3, waiting for transfers between devices: 290 us -> 12.6 us  [end(): return lax.psum_scatter(self.sum, 'fsdp', scatter_dimension=0, tiled=False)]
    all_gather x5 -> x0, blocking collectives: 181 us -> none  [the longest x1 73.4 us: body(): lax.all_gather(d_time.transpose(1, 0, 2).reshape(count, groups * 2 * shar...]
    all_gather x3, waiting for transfers between devices: 131 us -> 1.54 us  [__init__(): own = lax.all_gather(shard, 'fsdp', axis=0, tiled=False)]
    ppermute x0 -> x60, waiting for transfers between devices: none -> 85.3 us  [the longest x18 57.6 us: swap(): lax.ppermute(value, 'dp', [(i, i ^ NEAR[i & 1][hop]) for i in range(8)])]
    ppermute x0 -> x60, starting transfers between devices: none -> 79.7 us  [the longest x27 33.4 us: swap_bit(): return lax.ppermute(value, axis, [(i, i ^ 1 << bit) for i in range(size)])]
    unnamed x11 -> x6, waiting for transfers between devices: 35.6 us -> 0.1 us
    psum x1 -> x0, waiting for transfers between devices: 33.6 us -> none  [body(): flat = lax.psum(flat, BOTH)]
  transfers between devices with their start and end apart: 9 -> 66, of which waited for: 6 -> 19; matrix products, arithmetic and copies ran while one was open for 12% -> 22% of each run, Pallas kernels for 9% -> 62%
where the time goes in v2:
time: 1340 us; the launch traced here: 1330 us
  Pallas kernels  840 us (63%)
  matrix products  132 us (10%)
  waiting for transfers between devices  99.6 us (7%)
  local copies, waits for them, and re-layouts  89 us (7%)
  starting transfers between devices  80.4 us (6%)
  other arithmetic  75.9 us (6%)
  between operations  15.4 us (1%)
    pallas_call x2, Pallas kernels, place_pieces(): pl.pallas_call(place_kernel, grid_spec=pltpu.PrefetchScalarGridSpec(num_s...  647 us
    dot_general x10, matrix products, matmul(): return jnp.dot(left, right, preferred_element_type=jnp.float32)  77.2 us
    ppermute x18, waiting for transfers between devices, swap(): lax.ppermute(value, 'dp', [(i, i ^ NEAR[i & 1][hop]) for i in range(8)])  57.6 us
    dot_general x14, matrix products, times_transposed(): lax.dot_general(left, right, (((1,), (1,)), ((), ())), preferred_element_...  53.5 us
    pallas_call x1, Pallas kernels, position_bias(): pl.pallas_call(bias_kernel, grid=(tokens // block,), in_specs=[pl.BlockSp...  52.3 us
    ppermute x27, starting transfers between devices, swap_bit(): return lax.ppermute(value, axis, [(i, i ^ 1 << bit) for i in range(size)])  33.4 us
    ppermute x15, starting transfers between devices, swap_core(): return lax.ppermute(value, 'dp', [(i, i ^ 1) for i in range(8)])  28.3 us
    ppermute x27, waiting for transfers between devices, swap_bit(): return lax.ppermute(value, axis, [(i, i ^ 1 << bit) for i in range(size)])  27.7 us
  transfers between devices with their start and end apart: 66, of which 19 were waited for; matrix products, arithmetic and copies ran while one was open for 22% of the time, Pallas kernels for 62%

profile of v2, /device:TPU:0, one launch (start us, length us, event | category | flops | bytes accessed | tf_op | source)
XLA Modules:
  0.0 1331.6 jit_solution(12422961097253987083)
XLA Ops:
  9.0 3.1 collective-permute-start.9
  12.8 4.9 concatenate.147
  22.2 3.0 collective-permute-start.10
  27.0 3.0 collective-permute-start.1
  37.1 52.3 %position_bias.1.bias_ref = f32[16,256,256]{2,1,0:T(8,128)} custom-call(s32[256,256]{1,0:T(8,128)} %index_ref.3, bf16[128,128]{1,0:T(8,128)(2,1)} %reshape.303.table_ref), custom_call_target="tpu_custom_call" | custom-call | tf_op jit(solution)/shard_map/position_bias/pallas_call | solution.py:103
  92.6 4.2 collective-permute-done.14
  99.1 8.9 collective-permute-done.15
  108.0 24.8 %collective-permute-start.5 = (bf16[4,144,1152]{2,1,0:T(8,128)(2,1)}, bf16[4,144,1152]{2,1,0:T(8,128)(2,1)}, u32[]{:S(2)}, u32[]{:S(2)}) collective-permute-start(bf16[4,144,1152]{2,1,0:T(8,128)(2,1)} %bitcast.402), channel_id=1, source_target_pairs={{0,4},{4,0},{8,12},{12,8},{16,20},{20,16},{24,28},{28,24},{1,5},{5... | collective-permute-start | bytes 3981320 | tf_op jit(solution)/shard_map/ppermute | solution.py:531
  144.6 2.5 concatenate.175
  154.0 4.0 collective-permute-start.18
  168.9 2.8 copy.124.normed_ref
  176.9 11.0 collective-permute-done.19.refs_1_
  192.3 323.4 %place_pieces.2 = bf16[4,8,144,1152]{3,2,1,0:T(8,128)(2,1)} custom-call(s32[8]{0:T(128)} %fusion.312.part_ref, bf16[4,144,1152]{2,1,0:T(8,128)(2,1)} %bitcast.403, bf16[4,144,1152]{2,1,0:T(8,128)(2,1)} %collective-permute-done.2.refs_1_, bf16[4,144,1152]{2,1,0:T(8,128)(2,1)} %collective-permute-done.3.refs_2_, ...), custom_call_target="tpu_custom_call" | custom-call | tf_op jit(solution)/shard_map/place_pieces/pallas_call | solution.py:428
  515.7 4.7 take_proj.1
  520.5 16.7 %attend.1 = (bf16[4,512,896]{2,1,0:T(8,128)(2,1)}, bf16[4,2,4,256,256]{4,3,2,1,0:T(8,128)(2,1)}, bf16[4,512,288]{2,1,0:T(8,128)(2,1)}) custom-call(bf16[512,1152]{1,0:T(8,128)(2,1)} %copy.124.normed_ref, bf16[4,1152,1152]{2,1,0:T(8,128)(2,1)} %bitcast.376, f32[4,2,896]{2,1,0:T(2,128)} %maximum_maximum_fusion.add_ref, f32[16,256,256]{2,1,0:T(8,128)} %position_bias.1.bias_ref), custom_call_target="tpu_custom_call" | custom-call | tf_op jit(solution)/shard_map/attend/pallas_call | solution.py:205
  539.6 3.9 fusion.451
  549.7 14.0 %collective-permute-done.26.refs_1_ = bf16[4,144,1152]{2,1,0:T(8,128)(2,1)} collective-permute-done((bf16[4,144,1152]{2,1,0:T(8,128)(2,1)S(1)}, bf16[4,144,1152]{2,1,0:T(8,128)(2,1)}, u32[]{:S(2)}, u32[]{:S(2)}) %collective-permute-start.26) | collective-permute-done | bytes 1327136 | tf_op jit(solution)/shard_map/ppermute | solution.py:527
  566.4 323.4 %place_pieces.3 = bf16[4,8,144,1152]{3,2,1,0:T(8,128)(2,1)} custom-call(s32[8]{0:T(128)} %fusion.312.part_ref, bf16[4,144,1152]{2,1,0:T(8,128)(2,1)} %bitcast.8.refs_0_, bf16[4,144,1152]{2,1,0:T(8,128)(2,1)} %collective-permute-done.19.refs_1_, bf16[4,144,1152]{2,1,0:T(8,128)(2,1)} %collective-permute-done.20.refs_2_, ...), custom_call_target="tpu_custom_call" | custom-call | tf_op jit(solution)/shard_map/place_pieces/pallas_call | solution.py:428
  889.9 4.5 fusion.443
  894.4 8.3 fusion.43
  902.7 8.5 fusion.40
  911.2 8.2 fusion.37
  919.4 8.2 fusion.34
  929.9 6.7 copy.136.left_ref
  936.6 18.3 %down_grad.1 = (bf16[4,4,144,1152]{3,2,1,0:T(8,128)(2,1)}, bf16[4,4,144,1152]{3,2,1,0:T(8,128)(2,1)}) custom-call(s32[8]{0:T(128)} %fusion.313.slot_ref, bf16[4608,512]{1,0:T(8,128)(2,1)} %copy.136.left_ref, bf16[512,1152]{1,0:T(8,128)(2,1)} %bitcast.382), custom_call_target="tpu_custom_call" | custom-call | tf_op jit(solution)/shard_map/down_grad/pallas_call | solution.py:374
  955.4 9.1 unpack_pieces.1
  964.5 4.5 convert_reduce_fusion.2
  969.0 3.2 fusion.452
  972.2 3.7 convert_reduce_fusion
  975.9 3.7 convert_reduce_fusion.1
  979.5 3.7 convert_reduce_fusion.3
  983.2 2.8 pad_maximum_fusion.1.right_ref
  986.0 7.9 fusion.141
  994.0 6.9 add_halves.3
  1000.8 12.3 up_grad.1
  1013.5 4.0 fusion.453
  1019.3 9.8 fusion.144
  1034.5 2.5 convert_reduce_fusion.5
  1037.0 2.7 copy.144
  1039.7 7.5 collective-permute-done.34
  1047.2 3.1 add_convert_fusion.5
  1051.3 2.9 convolution_convert_fusion
  1056.6 2.5 copy.143
  1059.1 6.9 add_halves.4
  1066.1 17.2 %attend_back.1 = (bf16[4,512,1152]{2,1,0:T(8,128)(2,1)}, f32[16,256,256]{2,1,0:T(8,128)}) custom-call(bf16[4,512,288]{2,1,0:T(8,128)(2,1)} %bitcast.387, bf16[4,512,896]{2,1,0:T(8,128)(2,1)} %get-tuple-element.73.qkv_ref, bf16[4,2,4,256,256]{4,3,2,1,0:T(8,128)(2,1)} %get-tuple-element.74.probs_ref, bf16[4,512,288]{2,1,0:T(8,128)(2,1)} %bitcast.386), custom_call_target="tpu_custom_call" | custom-call | tf_op jit(solution)/shard_map/attend_back/pallas_call | solution.py:269
  1083.3 3.0 bitcast_reduce_fusion
  1089.6 10.5 fusion.147
  1103.0 3.4 add_convert_fusion.1
  1107.8 10.4 collective-permute-done.36
  1118.2 3.1 add_convert_fusion.4
  1121.3 13.8 %pair_grad.1 = (bf16[4,4,144,1152]{3,2,1,0:T(8,128)(2,1)}, bf16[4,4,144,1152]{3,2,1,0:T(8,128)(2,1)}) custom-call(s32[8]{0:T(128)} %fusion.313.slot_ref, bf16[1152,512]{1,0:T(8,128)(2,1)} %fusion.485.one_ref, bf16[1152,512]{1,0:T(8,128)(2,1)} %bitcast.390, bf16[4,512,1152]{2,1,0:T(8,128)(2,1)} %get-tuple-element.75.right_ref), custom_call_target="tpu_custom_call" | custom-call | tf_op jit(solution)/shard_map/pair_grad/pallas_call | solution.py:338
  1135.3 11.7 fusion.6
  1159.4 3.6 collective-permute-done.41
  1189.6 5.3 fusion.14
  1194.8 7.0 add_halves.5
  1203.2 4.6 convolution_add_fusion.2
  1207.8 5.4 convolution_add_fusion.1
  1215.8 14.7 %collective-permute-done.49 = bf16[4,144,1152]{2,1,0:T(8,128)(2,1)} collective-permute-done((bf16[4,144,1152]{2,1,0:T(8,128)(2,1)}, bf16[4,144,1152]{2,1,0:T(8,128)(2,1)}, u32[]{:S(2)}, u32[]{:S(2)}) %collective-permute-start.49) | collective-permute-done | bytes 1327136 | tf_op jit(solution)/shard_map/ppermute | solution.py:527
  1230.5 3.1 add_convert_fusion.3
  1234.9 7.2 multiply_reduce_fusion.1
  1244.8 27.3 %table_gradient.1 = f32[128,128]{1,0:T(8,128)} custom-call(s32[256,256]{1,0:T(8,128)} %index_ref.3, f32[16,256,256]{2,1,0:T(8,128)} %get-tuple-element.88.pairs_ref), custom_call_target="tpu_custom_call" | custom-call | tf_op jit(solution)/shard_map/table_gradient/pallas_call | solution.py:155
  1288.0 3.7 add_convert_fusion.2
  1295.9 4.9 add_convert_fusion.6
  1309.9 12.6 reduce-scatter.4.cloned.1.call-done
  (395 shorter events, 170.6 us)
Async XLA Ops:
  7.2 82.3 %all-gather.7.cloned.1.call-start = ((), (), s32[]{:S(2)}) async-start(), calls=%async_computation.6 | async-start | bytes 1658880 | tf_op jit(solution)/shard_map/all_gather | solution.py:542
  9.0 13.2 collective-permute-start.9
  17.8 9.2 collective-permute-start
  19.9 138.1 %all-gather.9.cloned.1.call-start = ((), (), s32[]{:S(2)}) async-start(), calls=%async_computation.7 | async-start | bytes 1658880 | tf_op jit(solution)/shard_map/all_gather | solution.py:542
  22.2 4.6 collective-permute-start.10
  26.9 3.1 collective-permute-start.11
  27.0 5.1 collective-permute-start.1
  30.0 4.0 collective-permute-start.12
  34.1 55.3 %collective-permute-start.13 = (bf16[32,1152]{1,0:T(8,128)(2,1)S(1)}, bf16[32,1152]{1,0:T(8,128)(2,1)S(1)}, u32[]{:S(2)}, u32[]{:S(2)}) collective-permute-start(bf16[32,1152]{1,0:T(8,128)(2,1)S(1)} %maximum_select_fusion.1), channel_id=1, source_target_pairs={{0,16},{4,20},{8,24},{12,28},{16,0},{20,4},{24,8},{28,12},{1,17},{... | collective-permute-start | bytes 221192 | tf_op jit(solution)/shard_map/ppermute | solution.py:583
  89.5 43.3 %collective-permute-start.2 = (bf16[4,144,1152]{2,1,0:T(8,128)(2,1)}, bf16[4,144,1152]{2,1,0:T(8,128)(2,1)}, u32[]{:S(2)}, u32[]{:S(2)}) collective-permute-start(bf16[4,144,1152]{2,1,0:T(8,128)(2,1)} %bitcast.400), channel_id=1, source_target_pairs={{0,8},{4,20},{8,0},{12,28},{16,24},{20,4},{24,16},{28,12},{1,9},{5... | collective-permute-start | bytes 3981320 | tf_op jit(solution)/shard_map/ppermute | solution.py:527
  91.3 98.9 %all-gather.11.cloned.1.call-start = ((), (), s32[]{:S(2)}) async-start(), calls=%async_computation.8 | async-start | bytes 1658880 | tf_op jit(solution)/shard_map/all_gather | solution.py:542
  91.4 5.4 collective-permute-start.14
  96.8 61.2 %collective-permute-start.3 = (bf16[4,144,1152]{2,1,0:T(8,128)(2,1)}, bf16[4,144,1152]{2,1,0:T(8,128)(2,1)}, u32[]{:S(2)}, u32[]{:S(2)}) collective-permute-start(bf16[4,144,1152]{2,1,0:T(8,128)(2,1)} %bitcast.401), channel_id=1, source_target_pairs={{0,16},{4,12},{8,24},{12,4},{16,0},{20,28},{24,8},{28,20},{1,17},{... | collective-permute-start | bytes 3981320 | tf_op jit(solution)/shard_map/ppermute | solution.py:527
  97.4 10.6 collective-permute-start.15
  108.0 53.0 %collective-permute-start.5 = (bf16[4,144,1152]{2,1,0:T(8,128)(2,1)}, bf16[4,144,1152]{2,1,0:T(8,128)(2,1)}, u32[]{:S(2)}, u32[]{:S(2)}) collective-permute-start(bf16[4,144,1152]{2,1,0:T(8,128)(2,1)} %bitcast.402), channel_id=1, source_target_pairs={{0,4},{4,0},{8,12},{12,8},{16,20},{20,16},{24,28},{28,24},{1,5},{5... | collective-permute-start | bytes 3981320 | tf_op jit(solution)/shard_map/ppermute | solution.py:531
  132.8 29.8 %collective-permute-start.4 = (bf16[4,144,1152]{2,1,0:T(8,128)(2,1)}, bf16[4,144,1152]{2,1,0:T(8,128)(2,1)}, u32[]{:S(2)}, u32[]{:S(2)}) collective-permute-start(bf16[4,144,1152]{2,1,0:T(8,128)(2,1)} %collective-permute-done.2.refs_1_), channel_id=1, source_target_pairs={{0,16},{4,12},{8,24},{12,4},{16,0},{20,28},{24,8},{28,20},{1,17},{... | collective-permute-start | bytes 3981320 | tf_op jit(solution)/shard_map/ppermute | solution.py:527
  133.9 13.2 collective-permute-start.16
  148.5 4.1 collective-permute-start.17
  154.0 7.1 collective-permute-start.18
  158.0 18.3 %collective-permute-start.7 = (bf16[4,144,1152]{2,1,0:T(8,128)(2,1)}, bf16[4,144,1152]{2,1,0:T(8,128)(2,1)}, u32[]{:S(2)}, u32[]{:S(2)}) collective-permute-start(bf16[4,144,1152]{2,1,0:T(8,128)(2,1)} %collective-permute-done.3.refs_2_), channel_id=1, source_target_pairs={{0,4},{4,0},{8,12},{12,8},{16,20},{20,16},{24,28},{28,24},{1,5},{5... | collective-permute-start | bytes 3981320 | tf_op jit(solution)/shard_map/ppermute | solution.py:531
  158.0 29.9 %collective-permute-start.19 = (bf16[4,144,1152]{2,1,0:T(8,128)(2,1)}, bf16[4,144,1152]{2,1,0:T(8,128)(2,1)}, u32[]{:S(2)}, u32[]{:S(2)}) collective-permute-start(bf16[4,144,1152]{2,1,0:T(8,128)(2,1)} %bitcast.8.refs_0_), channel_id=1, source_target_pairs={{0,8},{4,20},{8,0},{12,28},{16,24},{20,4},{24,16},{28,12},{1,9},{5... | collective-permute-start | bytes 3981320 | tf_op jit(solution)/shard_map/ppermute | solution.py:527
  158.9 998.6 %reduce-scatter.8.cloned.1.call-start = ((), (), s32[]{:S(2)}) async-start(), calls=%async_computation.5 | async-start | bytes 1658880 | tf_op jit(solution)/shard_map/reduce_scatter | solution.py:578
  161.1 29.2 %collective-permute-start.6 = (bf16[4,144,1152]{2,1,0:T(8,128)(2,1)}, bf16[4,144,1152]{2,1,0:T(8,128)(2,1)}, u32[]{:S(2)}, u32[]{:S(2)}) collective-permute-start(bf16[4,144,1152]{2,1,0:T(8,128)(2,1)} %collective-permute-done.2.refs_1_), channel_id=1, source_target_pairs={{0,4},{4,0},{8,12},{12,8},{16,20},{20,16},{24,28},{28,24},{1,5},{5... | collective-permute-start | bytes 3981320 | tf_op jit(solution)/shard_map/ppermute | solution.py:531
  161.1 29.2 %collective-permute-start.20 = (bf16[4,144,1152]{2,1,0:T(8,128)(2,1)}, bf16[4,144,1152]{2,1,0:T(8,128)(2,1)}, u32[]{:S(2)}, u32[]{:S(2)}) collective-permute-start(bf16[4,144,1152]{2,1,0:T(8,128)(2,1)} %bitcast.8.refs_0_), channel_id=1, source_target_pairs={{0,16},{4,12},{8,24},{12,4},{16,0},{20,28},{24,8},{28,20},{1,17},{... | collective-permute-start | bytes 3981320 | tf_op jit(solution)/shard_map/ppermute | solution.py:527
  162.6 28.2 %collective-permute-start.8 = (bf16[4,144,1152]{2,1,0:T(8,128)(2,1)}, bf16[4,144,1152]{2,1,0:T(8,128)(2,1)}, u32[]{:S(2)}, u32[]{:S(2)}) collective-permute-start(bf16[4,144,1152]{2,1,0:T(8,128)(2,1)} %collective-permute-done.4.refs_3_), channel_id=1, source_target_pairs={{0,4},{4,0},{8,12},{12,8},{16,20},{20,16},{24,28},{28,24},{1,5},{5... | collective-permute-start | bytes 3981320 | tf_op jit(solution)/shard_map/ppermute | solution.py:531
  176.3 367.6 %collective-permute-start.22 = (bf16[4,144,1152]{2,1,0:T(8,128)(2,1)}, bf16[4,144,1152]{2,1,0:T(8,128)(2,1)}, u32[]{:S(2)}, u32[]{:S(2)}) collective-permute-start(bf16[4,144,1152]{2,1,0:T(8,128)(2,1)} %bitcast.8.refs_0_), channel_id=1, source_target_pairs={{0,4},{4,0},{8,12},{12,8},{16,20},{20,16},{24,28},{28,24},{1,5},{5... | collective-permute-start | bytes 3981320 | tf_op jit(solution)/shard_map/ppermute | solution.py:531
  187.9 359.3 %collective-permute-start.21 = (bf16[4,144,1152]{2,1,0:T(8,128)(2,1)}, bf16[4,144,1152]{2,1,0:T(8,128)(2,1)}, u32[]{:S(2)}, u32[]{:S(2)}) collective-permute-start(bf16[4,144,1152]{2,1,0:T(8,128)(2,1)} %collective-permute-done.19.refs_1_), channel_id=1, source_target_pairs={{0,16},{4,12},{8,24},{12,4},{16,0},{20,28},{24,8},{28,20},{1,17},{... | collective-permute-start | bytes 3981320 | tf_op jit(solution)/shard_map/ppermute | solution.py:527
  190.3 373.4 %collective-permute-start.23 = (bf16[4,144,1152]{2,1,0:T(8,128)(2,1)}, bf16[4,144,1152]{2,1,0:T(8,128)(2,1)}, u32[]{:S(2)}, u32[]{:S(2)}) collective-permute-start(bf16[4,144,1152]{2,1,0:T(8,128)(2,1)} %collective-permute-done.19.refs_1_), channel_id=1, source_target_pairs={{0,4},{4,0},{8,12},{12,8},{16,20},{20,16},{24,28},{28,24},{1,5},{5... | collective-permute-start | bytes 3981320 | tf_op jit(solution)/shard_map/ppermute | solution.py:531
  190.3 358.9 %collective-permute-start.24 = (bf16[4,144,1152]{2,1,0:T(8,128)(2,1)}, bf16[4,144,1152]{2,1,0:T(8,128)(2,1)}, u32[]{:S(2)}, u32[]{:S(2)}) collective-permute-start(bf16[4,144,1152]{2,1,0:T(8,128)(2,1)} %collective-permute-done.20.refs_2_), channel_id=1, source_target_pairs={{0,4},{4,0},{8,12},{12,8},{16,20},{20,16},{24,28},{28,24},{1,5},{5... | collective-permute-start | bytes 3981320 | tf_op jit(solution)/shard_map/ppermute | solution.py:531
  190.8 373.4 %collective-permute-start.27 = (bf16[4,144,1152]{2,1,0:T(8,128)(2,1)}, bf16[4,144,1152]{2,1,0:T(8,128)(2,1)}, u32[]{:S(2)}, u32[]{:S(2)}) collective-permute-start(bf16[4,144,1152]{2,1,0:T(8,128)(2,1)} %bitcast.404), channel_id=1, source_target_pairs={{0,16},{4,12},{8,24},{12,4},{16,0},{20,28},{24,8},{28,20},{1,17},{... | collective-permute-start | bytes 3981320 | tf_op jit(solution)/shard_map/ppermute | solution.py:527
  545.8 17.9 %collective-permute-start.26 = (bf16[4,144,1152]{2,1,0:T(8,128)(2,1)S(1)}, bf16[4,144,1152]{2,1,0:T(8,128)(2,1)}, u32[]{:S(2)}, u32[]{:S(2)}) collective-permute-start(bf16[4,144,1152]{2,1,0:T(8,128)(2,1)S(1)} %bitcast.406), channel_id=1, source_target_pairs={{0,8},{4,20},{8,0},{12,28},{16,24},{20,4},{24,16},{28,12},{1,9},{5... | collective-permute-start | bytes 3981320 | tf_op jit(solution)/shard_map/ppermute | solution.py:527
  547.2 18.1 %collective-permute-start.25 = (bf16[4,144,1152]{2,1,0:T(8,128)(2,1)}, bf16[4,144,1152]{2,1,0:T(8,128)(2,1)S(1)}, u32[]{:S(2)}, u32[]{:S(2)}) collective-permute-start(bf16[4,144,1152]{2,1,0:T(8,128)(2,1)} %collective-permute-done.21.refs_3_), channel_id=1, source_target_pairs={{0,4},{4,0},{8,12},{12,8},{16,20},{20,16},{24,28},{28,24},{1,5},{5... | collective-permute-start | bytes 3981320 | tf_op jit(solution)/shard_map/ppermute | solution.py:531
  549.2 406.2 %collective-permute-start.29 = (bf16[4,144,1152]{2,1,0:T(8,128)(2,1)S(1)}, bf16[4,144,1152]{2,1,0:T(8,128)(2,1)}, u32[]{:S(2)}, u32[]{:S(2)}) collective-permute-start(bf16[4,144,1152]{2,1,0:T(8,128)(2,1)S(1)} %bitcast.407), channel_id=1, source_target_pairs={{0,4},{4,0},{8,12},{12,8},{16,20},{20,16},{24,28},{28,24},{1,5},{5... | collective-permute-start | bytes 3981320 | tf_op jit(solution)/shard_map/ppermute | solution.py:531
  563.6 391.7 %collective-permute-start.30 = (bf16[4,144,1152]{2,1,0:T(8,128)(2,1)}, bf16[4,144,1152]{2,1,0:T(8,128)(2,1)}, u32[]{:S(2)}, u32[]{:S(2)}) collective-permute-start(bf16[4,144,1152]{2,1,0:T(8,128)(2,1)} %collective-permute-done.26.refs_1_), channel_id=1, source_target_pairs={{0,4},{4,0},{8,12},{12,8},{16,20},{20,16},{24,28},{28,24},{1,5},{5... | collective-permute-start | bytes 3981320 | tf_op jit(solution)/shard_map/ppermute | solution.py:531
  563.6 355.8 %collective-permute-start.28 = (bf16[4,144,1152]{2,1,0:T(8,128)(2,1)}, bf16[4,144,1152]{2,1,0:T(8,128)(2,1)}, u32[]{:S(2)}, u32[]{:S(2)}) collective-permute-start(bf16[4,144,1152]{2,1,0:T(8,128)(2,1)} %collective-permute-done.26.refs_1_), channel_id=1, source_target_pairs={{0,16},{4,12},{8,24},{12,4},{16,0},{20,28},{24,8},{28,20},{1,17},{... | collective-permute-start | bytes 3981320 | tf_op jit(solution)/shard_map/ppermute | solution.py:527
  564.2 391.2 %collective-permute-start.31 = (bf16[4,144,1152]{2,1,0:T(8,128)(2,1)}, bf16[4,144,1152]{2,1,0:T(8,128)(2,1)}, u32[]{:S(2)}, u32[]{:S(2)}) collective-permute-start(bf16[4,144,1152]{2,1,0:T(8,128)(2,1)} %collective-permute-done.27.refs_2_), channel_id=1, source_target_pairs={{0,4},{4,0},{8,12},{12,8},{16,20},{20,16},{24,28},{28,24},{1,5},{5... | collective-permute-start | bytes 3981320 | tf_op jit(solution)/shard_map/ppermute | solution.py:531
  919.4 36.0 %collective-permute-start.32 = (bf16[4,144,1152]{2,1,0:T(8,128)(2,1)}, bf16[4,144,1152]{2,1,0:T(8,128)(2,1)}, u32[]{:S(2)}, u32[]{:S(2)}) collective-permute-start(bf16[4,144,1152]{2,1,0:T(8,128)(2,1)} %collective-permute-done.28.refs_3_), channel_id=1, source_target_pairs={{0,4},{4,0},{8,12},{12,8},{16,20},{20,16},{24,28},{28,24},{1,5},{5... | collective-permute-start | bytes 3981320 | tf_op jit(solution)/shard_map/ppermute | solution.py:531
  954.9 39.1 %collective-permute-start.33 = (bf16[4,4,144,1152]{3,2,1,0:T(8,128)(2,1)}, bf16[4,4,144,1152]{3,2,1,0:T(8,128)(2,1)}, u32[]{:S(2)}, u32[]{:S(2)}) collective-permute-start(bf16[4,4,144,1152]{3,2,1,0:T(8,128)(2,1)} %get-tuple-element.61), channel_id=1, source_target_pairs={{0,4},{4,0},{8,12},{12,8},{16,20},{20,16},{24,28},{28,24},{1,5},{5... | collective-permute-start | bytes 15925256 | tf_op jit(solution)/shard_map/ppermute | solution.py:531
  1013.2 45.9 %collective-permute-start.35 = (bf16[4,4,144,1152]{3,2,1,0:T(8,128)(2,1)}, bf16[4,4,144,1152]{3,2,1,0:T(8,128)(2,1)}, u32[]{:S(2)}, u32[]{:S(2)}) collective-permute-start(bf16[4,4,144,1152]{3,2,1,0:T(8,128)(2,1)} %get-tuple-element.66), channel_id=1, source_target_pairs={{0,4},{4,0},{8,12},{12,8},{16,20},{20,16},{24,28},{28,24},{1,5},{5... | collective-permute-start | bytes 15925256 | tf_op jit(solution)/shard_map/ppermute | solution.py:531
  1029.1 18.2 %collective-permute-start.34 = (bf16[4,144,1152]{2,1,0:T(8,128)(2,1)}, bf16[4,144,1152]{2,1,0:T(8,128)(2,1)}, u32[]{:S(2)}, u32[]{:S(2)}) collective-permute-start(bf16[4,144,1152]{2,1,0:T(8,128)(2,1)} %get-tuple-element.64), channel_id=1, source_target_pairs={{0,16},{4,12},{8,24},{12,4},{16,0},{20,28},{24,8},{28,20},{1,17},{... | collective-permute-start | bytes 3981320 | tf_op jit(solution)/shard_map/ppermute | solution.py:527
  1031.8 71.2 %collective-permute-start.51 = (bf16[4,144,1152]{2,1,0:T(8,128)(2,1)}, bf16[4,144,1152]{2,1,0:T(8,128)(2,1)}, u32[]{:S(2)}, u32[]{:S(2)}) collective-permute-start(bf16[4,144,1152]{2,1,0:T(8,128)(2,1)} %get-tuple-element.87), channel_id=1, source_target_pairs={{0,16},{4,12},{8,24},{12,4},{16,0},{20,28},{24,8},{28,20},{1,17},{... | collective-permute-start | bytes 3981320 | tf_op jit(solution)/shard_map/ppermute | solution.py:527
  1050.3 52.6 %collective-permute-start.52 = (bf16[4,144,1152]{2,1,0:T(8,128)(2,1)}, bf16[4,144,1152]{2,1,0:T(8,128)(2,1)}, u32[]{:S(2)}, u32[]{:S(2)}) collective-permute-start(bf16[4,144,1152]{2,1,0:T(8,128)(2,1)} %add_convert_fusion.5), channel_id=1, source_target_pairs={{0,8},{4,20},{8,0},{12,28},{16,24},{20,4},{24,16},{28,12},{1,9},{5... | collective-permute-start | bytes 3981320 | tf_op jit(solution)/shard_map/ppermute | solution.py:527
  1088.5 12.7 collective-permute-start.37
  1100.1 18.1 %collective-permute-start.36 = (bf16[4,144,1152]{2,1,0:T(8,128)(2,1)}, bf16[4,144,1152]{2,1,0:T(8,128)(2,1)}, u32[]{:S(2)}, u32[]{:S(2)}) collective-permute-start(bf16[4,144,1152]{2,1,0:T(8,128)(2,1)} %get-tuple-element.71), channel_id=1, source_target_pairs={{0,16},{4,12},{8,24},{12,4},{16,0},{20,28},{24,8},{28,20},{1,17},{... | collective-permute-start | bytes 3981320 | tf_op jit(solution)/shard_map/ppermute | solution.py:527
  1101.9 5.0 collective-permute-start.38
  1106.3 198.7 %reduce-scatter.6.cloned.1.call-start = ((), (), s32[]{:S(2)}) async-start(), calls=%async_computation.4 | async-start | bytes 1658880 | tf_op jit(solution)/shard_map/reduce_scatter | solution.py:578
  1107.7 39.3 %collective-permute-start.39 = (bf16[8,2304]{1,0:T(8,128)(2,1)S(1)}, bf16[8,2304]{1,0:T(8,128)(2,1)S(1)}, u32[]{:S(2)}, u32[]{:S(2)}) collective-permute-start(bf16[8,2304]{1,0:T(8,128)(2,1)S(1)} %maximum_select_fusion.7), channel_id=1, source_target_pairs={{0,4},{4,0},{8,12},{12,8},{16,20},{20,16},{24,28},{28,24},{1,5},{5... | collective-permute-start | bytes 110600 | tf_op jit(solution)/shard_map/ppermute | solution.py:583
  1135.2 59.7 %collective-permute-start.47 = (bf16[4,4,144,1152]{3,2,1,0:T(8,128)(2,1)}, bf16[4,4,144,1152]{3,2,1,0:T(8,128)(2,1)}, u32[]{:S(2)}, u32[]{:S(2)}) collective-permute-start(bf16[4,4,144,1152]{3,2,1,0:T(8,128)(2,1)} %get-tuple-element.78), channel_id=1, source_target_pairs={{0,4},{4,0},{8,12},{12,8},{16,20},{20,16},{24,28},{28,24},{1,5},{5... | collective-permute-start | bytes 15925256 | tf_op jit(solution)/shard_map/ppermute | solution.py:531
  1147.7 7.3 collective-permute-start.40
  1156.7 6.2 collective-permute-start.41
  1168.8 4.9 collective-permute-start.42
  1175.0 5.2 collective-permute-start.43
  1179.4 33.9 %collective-permute-start.58 = (bf16[4,144,1152]{2,1,0:T(8,128)(2,1)}, bf16[4,144,1152]{2,1,0:T(8,128)(2,1)S(1)}, u32[]{:S(2)}, u32[]{:S(2)}) collective-permute-start(bf16[4,144,1152]{2,1,0:T(8,128)(2,1)} %get-tuple-element.90), channel_id=1, source_target_pairs={{0,16},{4,12},{8,24},{12,4},{16,0},{20,28},{24,8},{28,20},{1,17},{... | collective-permute-start | bytes 3981320 | tf_op jit(solution)/shard_map/ppermute | solution.py:527
  1182.4 4.3 collective-permute-start.45
  1187.4 93.9 %collective-permute-start.46 = (f32[4,8,2,144]{3,0,2,1:T(4,128)}, f32[4,8,2,144]{3,0,2,1:T(4,128)}, u32[]{:S(2)}, u32[]{:S(2)}) collective-permute-start(f32[4,8,2,144]{3,0,2,1:T(4,128)} %maximum_select_fusion.3), channel_id=1, source_target_pairs={{0,16},{4,20},{8,24},{12,28},{16,0},{20,4},{24,8},{28,12},{1,17},{... | collective-permute-start | bytes 110600 | tf_op jit(solution)/shard_map/ppermute | solution.py:583
  1188.6 24.6 %collective-permute-start.59 = (bf16[4,144,1152]{2,1,0:T(8,128)(2,1)}, bf16[4,144,1152]{2,1,0:T(8,128)(2,1)S(1)}, u32[]{:S(2)}, u32[]{:S(2)}) collective-permute-start(bf16[4,144,1152]{2,1,0:T(8,128)(2,1)} %add_convert_fusion.4), channel_id=1, source_target_pairs={{0,8},{4,20},{8,0},{12,28},{16,24},{20,4},{24,16},{28,12},{1,9},{5... | collective-permute-start | bytes 3981320 | tf_op jit(solution)/shard_map/ppermute | solution.py:527
  1201.9 28.6 %collective-permute-start.49 = (bf16[4,144,1152]{2,1,0:T(8,128)(2,1)}, bf16[4,144,1152]{2,1,0:T(8,128)(2,1)}, u32[]{:S(2)}, u32[]{:S(2)}) collective-permute-start(bf16[4,144,1152]{2,1,0:T(8,128)(2,1)} %get-tuple-element.84), channel_id=1, source_target_pairs={{0,16},{4,12},{8,24},{12,4},{16,0},{20,28},{24,8},{28,20},{1,17},{... | collective-permute-start | bytes 3981320 | tf_op jit(solution)/shard_map/ppermute | solution.py:527
  1214.8 107.6 %reduce-scatter.4.cloned.1.call-start = ((), (), s32[]{:S(2)}) async-start(), calls=%async_computation.3 | async-start | bytes 1658880 | tf_op jit(solution)/shard_map/reduce_scatter | solution.py:578
  1214.9 73.1 %collective-permute-start.48 = (bf16[4,144,1152]{2,1,0:T(8,128)(2,1)}, bf16[4,144,1152]{2,1,0:T(8,128)(2,1)}, u32[]{:S(2)}, u32[]{:S(2)}) collective-permute-start(bf16[4,144,1152]{2,1,0:T(8,128)(2,1)} %get-tuple-element.82), channel_id=1, source_target_pairs={{0,16},{4,12},{8,24},{12,4},{16,0},{20,28},{24,8},{28,20},{1,17},{... | collective-permute-start | bytes 3981320 | tf_op jit(solution)/shard_map/ppermute | solution.py:527
  1233.6 54.4 %collective-permute-start.50 = (bf16[4,144,1152]{2,1,0:T(8,128)(2,1)}, bf16[4,144,1152]{2,1,0:T(8,128)(2,1)}, u32[]{:S(2)}, u32[]{:S(2)}) collective-permute-start(bf16[4,144,1152]{2,1,0:T(8,128)(2,1)} %add_convert_fusion.3), channel_id=1, source_target_pairs={{0,8},{4,20},{8,0},{12,28},{16,24},{20,4},{24,16},{28,12},{1,9},{5... | collective-permute-start | bytes 3981320 | tf_op jit(solution)/shard_map/ppermute | solution.py:527
  1279.4 6.0 collective-permute-start.53
  1287.5 4.9 collective-permute-start.54
  1295.0 8.1 collective-permute-start.56
  1303.9 3.9 collective-permute-start.57
  (69 other events, 1522.5 us)
Sparse Core Ops, SparseCore 0:
  20.1 34.8 all-gather.6
  91.5 32.5 all-gather.8
  159.0 31.2 all-gather.10
  1106.5 30.5 reduce-scatter.7
  1215.0 44.2 reduce-scatter.5
  1291.8 30.5 reduce-scatter.3

commit v3 on v2

--- a/solution.py
+++ b/solution.py
@@ -11,6 +11,7 @@
 LANES = 128
 BOTH = ("dp", "fsdp")
 VMEM_LIMIT = 58 * 1024 * 1024
+SHORT = pl.CostEstimate(flops=1, transcendentals=0, bytes_accessed=1)
 
 
 def sinusoid(steps, model_width):
@@ -69,49 +70,52 @@
 
 def bias_kernel(index_ref, table_ref, bias_ref):
     heads, rows, tokens = bias_ref.shape
-    table = table_ref[...]
-    sub = lax.broadcasted_iota(jnp.int32, (8, tokens), 0)
-    lane_of = lax.broadcasted_iota(jnp.int32, (LANES, tokens), 0)
-    line = lax.broadcasted_iota(jnp.int32, (heads, heads * 8), 0)
-    column = lax.broadcasted_iota(jnp.int32, (heads, heads * 8), 1)
-    add_up = jnp.where(column >> 3 == line, 1.0, 0.0).astype(jnp.bfloat16)
-
-    def one_row(row):
-        index = index_ref[pl.ds(row, 1), :]
-        low = jnp.broadcast_to(index & (LANES - 1), (LANES, tokens))
-        hit = sub == jnp.broadcast_to(index >> 7, (8, tokens))
-        picked = matmul(table, jnp.where(lane_of == low, 1.0, 0.0).astype(jnp.bfloat16))
-        only = jnp.concatenate(
-            [jnp.where(hit, picked[h * 8 : (h + 1) * 8], 0.0) for h in range(heads)], axis=0
-        ).astype(jnp.bfloat16)
-        found = matmul(add_up, only)
-        for h in range(heads):
-            bias_ref[h, pl.ds(row, 1), :] = found[h : h + 1]
+    chunks = table_ref.shape[2] // LANES
+    pieces = [
+        [
+            jnp.broadcast_to(table_ref[h, :, c * LANES : (c + 1) * LANES], (8, LANES))
+            for c in range(chunks)
+        ]
+        for h in range(heads)
+    ]
 
     def some_rows(step, carry):
-        for part in range(4):
-            one_row(step * 4 + part)
+        at = pl.multiple_of(step * 8, 8)
+        for col in range(tokens // LANES):
+            lanes = slice(col * LANES, (col + 1) * LANES)
+            index = index_ref[pl.ds(at, 8), lanes]
+            low = index & (LANES - 1)
+            high = index >> 7
+            hits = [high == c for c in range(chunks)]
+            for h in range(heads):
+                found = jnp.take_along_axis(pieces[h][0], low, axis=1)
+                for c in range(1, chunks):
+                    found = jnp.where(
+                        hits[c], jnp.take_along_axis(pieces[h][c], low, axis=1), found
+                    )
+                bias_ref[h, pl.ds(at, 8), lanes] = found
         return carry
 
-    lax.fori_loop(0, rows // 4, some_rows, 0)
+    lax.fori_loop(0, rows // 8, some_rows, 0)
 
 
 def position_bias(index, table):
     heads, padded = table.shape
     tokens = index.shape[0]
-    block = 64
+    group = heads // 4
     return pl.pallas_call(
         bias_kernel,
-        grid=(tokens // block,),
+        grid=(4,),
         in_specs=[
-            pl.BlockSpec((block, tokens), lambda i: (i, 0)),
-            pl.BlockSpec((heads * 8, LANES), lambda i: (0, 0)),
-        ],
-        out_specs=pl.BlockSpec((heads, block, tokens), lambda i: (0, i, 0)),
+            pl.BlockSpec((tokens, tokens), lambda f: (0, 0)),
+            pl.BlockSpec((group, 1, padded), lambda f: (f, 0, 0)),
+        ],
+        out_specs=pl.BlockSpec((group, tokens, tokens), lambda f: (f, 0, 0)),
         out_shape=jax.ShapeDtypeStruct((heads, tokens, tokens), jnp.float32),
         compiler_params=params(),
+        cost_estimate=SHORT,
         name="position_bias",
-    )(index, table.reshape(heads * 8, LANES))
+    )(index, table.astype(jnp.float32).reshape(heads, 1, padded))
 
 
 def table_kernel(index_ref, pairs_ref, out_ref):
@@ -162,20 +166,77 @@
         out_specs=pl.BlockSpec((heads * 8, LANES), lambda i: (0, 0)),
         out_shape=jax.ShapeDtypeStruct((heads * 8, LANES), jnp.float32),
         compiler_params=params(),
+        cost_estimate=SHORT,
         name="table_gradient",
     )(index, pairs)
 
 
-def attend_kernel(normed_ref, weight_ref, add_ref, bias_ref, qkv_ref, probs_ref, mixed_ref):
+def load_group(part_ref, pieces, held, in_sems, full_ref, out_sems):
+    step = pl.program_id(0)
+    rows = pieces[0].shape[1]
+
+    def copy(group, j):
+        at = pl.multiple_of(part_ref[j] * rows, 16)
+        return pltpu.make_async_copy(
+            pieces[j].at[group], held.at[group, pl.ds(at, rows)], in_sems.at[group, j]
+        )
+
+    @pl.when(step == 0)
+    def _():
+        for group in range(held.shape[0]):
+            for j in range(len(pieces)):
+                copy(group, j).start()
+
+    for j in range(len(pieces)):
+        copy(step, j).wait()
+    pltpu.make_async_copy(held.at[step], full_ref.at[step], out_sems.at[step]).start()
+
+
+def finish_groups(held, full_ref, out_sems):
+    @pl.when(pl.program_id(0) == held.shape[0] - 1)
+    def _():
+        for group in range(held.shape[0]):
+            pltpu.make_async_copy(held.at[group], full_ref.at[group], out_sems.at[group]).wait()
+
+
+def piece_call(kernel, name, part_of, pieces, inputs, in_specs, out_specs, out_shapes):
+    groups, rows, packed = pieces[0].shape
+    depth = rows * len(pieces)
+    full = jax.ShapeDtypeStruct((groups, depth, packed), pieces[0].dtype)
+    anywhere = pl.BlockSpec(memory_space=pl.ANY)
+    return pl.pallas_call(
+        kernel,
+        grid_spec=pltpu.PrefetchScalarGridSpec(
+            num_scalar_prefetch=1,
+            grid=(groups,),
+            in_specs=in_specs + [anywhere] * len(pieces),
+            out_specs=out_specs + [anywhere],
+            scratch_shapes=[
+                pltpu.VMEM((groups, depth, packed), pieces[0].dtype),
+                pltpu.SemaphoreType.DMA((groups, len(pieces))),
+                pltpu.SemaphoreType.DMA((groups,)),
+            ],
+        ),
+        out_shape=out_shapes + [full],
+        compiler_params=params(),
+        cost_estimate=SHORT,
+        name=name,
+    )(part_of, *inputs, *pieces)
+
+
+def attend_kernel(part_ref, normed_ref, add_ref, bias_ref, *refs):
+    *pieces, qkv_ref, probs_ref, mixed_ref, proj_ref, full_ref, held, in_sems, out_sems = refs
     images, heads = probs_ref.shape[1], probs_ref.shape[2]
     tokens = probs_ref.shape[3]
     width = mixed_ref.shape[2]
     size = width // heads
     scale = 1.0 / math.sqrt(size)
     kept = qkv_ref.shape[2]
+    step = pl.program_id(0)
+    load_group(part_ref, pieces, held, in_sems, full_ref, out_sems)
     for image in range(images):
         rows = slice(image * tokens, (image + 1) * tokens)
-        acc = matmul(normed_ref[rows, :], weight_ref[0, :, :kept])
+        acc = matmul(normed_ref[rows, :], held[step, :, :kept])
         qkv_ref[0, rows, :] = (acc + add_ref[0, image : image + 1, :]).astype(jnp.bfloat16)
     for image in range(images):
         rows = slice(image * tokens, (image + 1) * tokens)
@@ -194,36 +255,137 @@
             probs_ref[0, image, head] = probs
             outs.append(matmul(probs, values))
         mixed_ref[0, rows, :] = jnp.concatenate(outs, axis=1).astype(jnp.bfloat16)
-
-
-def attend(normed, weight, add, bias, images, tokens):
-    groups, depth, packed = weight.shape
+    for group in range(held.shape[0]):
+
+        @pl.when(step == group)
+        def _(group=group):
+            proj_ref[:, group * width : (group + 1) * width] = held[group, :, 3 * width :]
+
+    finish_groups(held, full_ref, out_sems)
+
+
+def attend(part_of, pieces, normed, add, bias, images, tokens):
+    groups, part_rows, packed = pieces[0].shape
+    depth = part_rows * len(pieces)
     heads = bias.shape[0] // groups
     width = packed // groups
     kept = add.shape[2]
     rows = images * tokens
+    low = jnp.bfloat16
+    return piece_call(
+        attend_kernel,
+        "attend",
+        part_of,
+        pieces,
+        [normed, add, bias],
+        [
+            pl.BlockSpec((rows, depth), lambda f, p: (0, 0)),
+            pl.BlockSpec((1, images, kept), lambda f, p: (f, 0, 0)),
+            pl.BlockSpec((heads, tokens, tokens), lambda f, p: (f, 0, 0)),
+        ],
+        [
+            pl.BlockSpec((1, rows, kept), lambda f, p: (f, 0, 0)),
+            pl.BlockSpec((1, images, heads, tokens, tokens), lambda f, p: (f, 0, 0, 0, 0)),
+            pl.BlockSpec((1, rows, width), lambda f, p: (f, 0, 0)),
+            pl.BlockSpec((depth, packed), lambda f, p: (0, 0)),
+        ],
+        [
+            jax.ShapeDtypeStruct((groups, rows, kept), low),
+            jax.ShapeDtypeStruct((groups, images, heads, tokens, tokens), low),
+            jax.ShapeDtypeStruct((groups, rows, width), low),
+            jax.ShapeDtypeStruct((depth, packed), low),
+        ],
+    )
+
+
+def up_kernel(part_ref, second_ref, bias_ref, *refs):
+    *pieces, activ_ref, slope_ref, full_ref, held, in_sems, out_sems = refs
+    load_group(part_ref, pieces, held, in_sems, full_ref, out_sems)
+    weight = held[pl.program_id(0)]
+    block = 256
+    for start in range(0, second_ref.shape[0], block):
+        rows = slice(start, start + block)
+        pre = matmul(second_ref[rows, :], weight) + bias_ref[0]
+        below = 0.5 * (1.0 + lax.erf(pre * (1.0 / math.sqrt(2.0))))
+        density = jnp.exp(-0.5 * pre * pre) * (1.0 / math.sqrt(2.0 * math.pi))
+        activ_ref[0, rows, :] = (pre * below).astype(jnp.bfloat16)
+        slope_ref[0, rows, :] = (below + pre * density).astype(jnp.bfloat16)
+    finish_groups(held, full_ref, out_sems)
+
+
+def up_forward(part_of, pieces, second, bias):
+    groups, part_rows, packed = pieces[0].shape
+    rows, depth = second.shape
+    wide = pl.BlockSpec((1, rows, packed), lambda f, p: (f, 0, 0))
+    shape = jax.ShapeDtypeStruct((groups, rows, packed), jnp.bfloat16)
+    return piece_call(
+        up_kernel,
+        "up_forward",
+        part_of,
+        pieces,
+        [second, bias.reshape(groups, 1, packed)],
+        [
+            pl.BlockSpec((rows, depth), lambda f, p: (0, 0)),
+            pl.BlockSpec((1, 1, packed), lambda f, p: (f, 0, 0)),
+        ],
+        [wide, wide],
+        [shape, shape],
+    )
+
+
+def down_back_kernel(
+    grad_ref, hidden_ref, activ_ref, slope_ref, up_ref, down_ref, pre_ref, second_ref, out_ref, total
+):
+    step = pl.program_id(0)
+    weight = down_ref[...]
+    d_activ = times_transposed(grad_ref[...], weight)
+    d_pre = (d_activ * slope_ref[0].astype(jnp.float32)).astype(jnp.bfloat16)
+    pre_ref[0] = d_pre
+    part = times_transposed(d_pre, up_ref[0])
+    more = matmul(activ_ref[0], weight)
+
+    @pl.when(step == 0)
+    def _():
+        second_ref[...] = part
+        total[...] = hidden_ref[...] + more
+
+    @pl.when(step > 0)
+    def _():
+        second_ref[...] += part
+        total[...] += more
+
+    @pl.when(step == pl.num_programs(0) - 1)
+    def _():
+        out_ref[...] = total[...].astype(jnp.bfloat16)
+
+
+def down_back(grad, hidden, activ, slope, up_full, down_full):
+    groups, rows, packed = activ.shape
+    depth = up_full.shape[1]
+    whole = pl.BlockSpec((rows, depth), lambda f: (0, 0))
+    mine = pl.BlockSpec((1, rows, packed), lambda f: (f, 0, 0))
     return pl.pallas_call(
-        attend_kernel,
+        down_back_kernel,
         grid=(groups,),
         in_specs=[
-            pl.BlockSpec((rows, depth), lambda f: (0, 0)),
+            whole,
+            whole,
+            mine,
+            mine,
             pl.BlockSpec((1, depth, packed), lambda f: (f, 0, 0)),
-            pl.BlockSpec((1, images, kept), lambda f: (f, 0, 0)),
-            pl.BlockSpec((heads, tokens, tokens), lambda f: (f, 0, 0)),
-        ],
-        out_specs=[
-            pl.BlockSpec((1, rows, kept), lambda f: (f, 0, 0)),
-            pl.BlockSpec((1, images, heads, tokens, tokens), lambda f: (f, 0, 0, 0, 0)),
-            pl.BlockSpec((1, rows, width), lambda f: (f, 0, 0)),
-        ],
+            pl.BlockSpec((packed, depth), lambda f: (f, 0)),
+        ],
+        out_specs=[mine, whole, whole],
         out_shape=[
-            jax.ShapeDtypeStruct((groups, rows, kept), jnp.bfloat16),
-            jax.ShapeDtypeStruct((groups, images, heads, tokens, tokens), jnp.bfloat16),
-            jax.ShapeDtypeStruct((groups, rows, width), jnp.bfloat16),
-        ],
+            jax.ShapeDtypeStruct((groups, rows, packed), jnp.bfloat16),
+            jax.ShapeDtypeStruct((rows, depth), jnp.float32),
+            jax.ShapeDtypeStruct((rows, depth), jnp.bfloat16),
+        ],
+        scratch_shapes=[pltpu.VMEM((rows, depth), jnp.float32)],
         compiler_params=params(),
-        name="attend",
-    )(normed, weight, add, bias)
+        cost_estimate=SHORT,
+        name="down_back",
+    )(grad, hidden, activ, slope, up_full, down_full)
 
 
 def attend_back_kernel(grad_ref, qkv_ref, probs_ref, hidden_ref, out_ref, pairs_ref):
@@ -284,6 +446,7 @@
             jax.ShapeDtypeStruct((groups * heads, tokens, tokens), jnp.float32),
         ],
         compiler_params=params(),
+        cost_estimate=SHORT,
         name="attend_back",
     )(grad, qkv, probs, hidden)
 
@@ -346,6 +509,7 @@
         ),
         out_shape=[half, half],
         compiler_params=params(),
+        cost_estimate=SHORT,
         name=name,
     )(slots, *lefts, right)
 
@@ -353,49 +517,58 @@
 def down_grad_kernel(slot_ref, left_ref, right_ref, own_ref, send_ref):
     half, groups, rows, packed = own_ref.shape
     width = packed // groups
-    value = matmul(left_ref[...], right_ref[...]).astype(jnp.bfloat16)
-    slot = slot_ref[pl.program_id(0)]
-    for f in range(groups):
-        block = jnp.concatenate(
-            [
-                value[g * rows : (g + 1) * rows, f * width : (f + 1) * width]
-                for g in range(value.shape[0] // rows)
-            ],
-            axis=1,
-        )
-        store_slot(slot, own_ref, send_ref, (f,), block)
-
-
-def down_slot_grad(slots, left, right, groups, parts, rows):
-    hidden, tokens = left.shape
-    packed = right.shape[1]
-    half = jax.ShapeDtypeStruct((parts // 2, groups, rows, packed), jnp.bfloat16)
-    out = pl.BlockSpec((parts // 2, groups, rows, packed), lambda d, s: (0, 0, 0, 0))
+    value = contract_rows(left_ref[0], right_ref[...]).astype(jnp.bfloat16)
+    each = 2 * half // groups
+    fold = value.shape[0] // (each * rows)
+    for part in range(each):
+        slot = slot_ref[pl.program_id(0) * each + part]
+        base = part * fold * rows
+        for f in range(groups):
+            block = jnp.concatenate(
+                [
+                    value[base + g * rows : base + (g + 1) * rows, f * width : (f + 1) * width]
+                    for g in range(fold)
+                ],
+                axis=1,
+            )
+            store_slot(slot, own_ref, send_ref, (f,), block)
+
+
+def down_slot_grad(slots, left, right, parts, part_rows):
+    groups, rows, packed = left.shape
+    half = jax.ShapeDtypeStruct((parts // 2, groups, part_rows, packed), jnp.bfloat16)
+    out = pl.BlockSpec((parts // 2, groups, part_rows, packed), lambda f, s: (0, 0, 0, 0))
     return pl.pallas_call(
         down_grad_kernel,
         grid_spec=pltpu.PrefetchScalarGridSpec(
             num_scalar_prefetch=1,
-            grid=(parts,),
+            grid=(groups,),
             in_specs=[
-                pl.BlockSpec((hidden // parts, tokens), lambda d, s: (d, 0)),
-                pl.BlockSpec((tokens, packed), lambda d, s: (0, 0)),
+                pl.BlockSpec((1, rows, packed), lambda f, s: (f, 0, 0)),
+                pl.BlockSpec((rows, packed), lambda f, s: (0, 0)),
             ],
             out_specs=[out, out],
         ),
         out_shape=[half, half],
         compiler_params=params(),
+        cost_estimate=SHORT,
         name="down_grad",
     )(slots, left, right)
 
 
 def add_kernel(one_ref, two_ref, three_ref, four_ref, came_ref, *outs):
-    for k, (mine, out) in enumerate(zip((one_ref, two_ref, three_ref, four_ref), outs)):
+    places = ((outs[0], (0,)), (outs[1], (0,)), (outs[2], (1, 0)), (outs[2], (0, 0)))
+    for k, (mine, (out, at)) in enumerate(
+        zip((one_ref, two_ref, three_ref, four_ref), places)
+    ):
         total = mine[0, 0].astype(jnp.float32) + came_ref[k, 0].astype(jnp.float32)
-        out[0] = total.astype(jnp.bfloat16)
+        out[at] = total.astype(jnp.bfloat16)
 
 
 def add_halves(own, came):
     half, groups, rows, packed = own.shape
+    single = pl.BlockSpec((1, rows, packed), lambda f: (f, 0, 0))
+    one = jax.ShapeDtypeStruct((groups, rows, packed), jnp.bfloat16)
     return pl.pallas_call(
         add_kernel,
         grid=(groups,),
@@ -403,41 +576,12 @@
             pl.BlockSpec((1, 1, rows, packed), lambda f, k=k: (k, f, 0, 0)) for k in range(half)
         ]
         + [pl.BlockSpec((half, 1, rows, packed), lambda f: (0, f, 0, 0))],
-        out_specs=[pl.BlockSpec((1, rows, packed), lambda f: (f, 0, 0))] * half,
-        out_shape=[jax.ShapeDtypeStruct((groups, rows, packed), jnp.bfloat16)] * half,
+        out_specs=[single, single, pl.BlockSpec((2, 1, rows, packed), lambda f: (0, f, 0, 0))],
+        out_shape=[one, one, jax.ShapeDtypeStruct((2, groups, rows, packed), jnp.bfloat16)],
         compiler_params=params(),
+        cost_estimate=SHORT,
         name="add_halves",
     )(*([own] * half), came)
-
-
-def place_kernel(part_ref, *refs):
-    *pieces, out_ref, sems = refs
-    copies = [
-        pltpu.make_async_copy(piece, out_ref.at[:, part_ref[j]], sems.at[j])
-        for j, piece in enumerate(pieces)
-    ]
-    for copy in copies:
-        copy.start()
-    for copy in copies:
-        copy.wait()
-
-
-def place_pieces(part_of, pieces):
-    groups, rows, width = pieces[0].shape
-    parts = len(pieces)
-    return pl.pallas_call(
-        place_kernel,
-        grid_spec=pltpu.PrefetchScalarGridSpec(
-            num_scalar_prefetch=1,
-            grid=(1,),
-            in_specs=[pl.BlockSpec(memory_space=pl.ANY)] * parts,
-            out_specs=pl.BlockSpec(memory_space=pl.ANY),
-            scratch_shapes=[pltpu.SemaphoreType.DMA((parts,))],
-        ),
-        out_shape=jax.ShapeDtypeStruct((groups, parts, rows, width), pieces[0].dtype),
-        compiler_params=params(),
-        name="place_pieces",
-    )(part_of, *pieces)
 
 
 def unpack_kernel(part_ref, *refs):
@@ -475,31 +619,9 @@
         ),
         out_shape=jax.ShapeDtypeStruct((parts * fold * rows, width), pieces[0].dtype),
         compiler_params=params(),
+        cost_estimate=SHORT,
         name="unpack_pieces",
     )(part_of, *pieces)
-
-
-def take_proj_kernel(in_ref, out_ref):
-    groups = in_ref.shape[0]
-    width = out_ref.shape[1] // groups
-    skip = in_ref.shape[2] - width
-    for f in range(groups):
-        out_ref[:, f * width : (f + 1) * width] = in_ref[f][:, skip:]
-
-
-def take_proj(packed):
-    groups, depth, width = packed.shape
-    block = 288
-    tail = width // 3
-    return pl.pallas_call(
-        take_proj_kernel,
-        grid=(depth // block,),
-        in_specs=[pl.BlockSpec((groups, block, tail), lambda d: (0, d, 2))],
-        out_specs=pl.BlockSpec((block, width), lambda d: (d, 0)),
-        out_shape=jax.ShapeDtypeStruct((depth, width), packed.dtype),
-        compiler_params=params(),
-        name="take_proj",
-    )(packed)
 
 
 NEAR = ((0, 2, 4, 6), (0, 4, 2, 6))
@@ -558,19 +680,18 @@
         self.came = swap_core(send)
 
     def near(self):
-        self.zero, self.one, two, three = add_halves(self.own, self.came)
-        self.far = swap(three, 2)
-        self.side = swap(two, 2)
-        return three
+        self.zero, self.one, pair = add_halves(self.own, self.came)
+        self.far = swap(pair, 2)
+        return pair
 
     def back(self):
-        one = self.one.astype(jnp.float32) + self.far.astype(jnp.float32)
+        one = self.one.astype(jnp.float32) + self.far[0].astype(jnp.float32)
         one = one.astype(jnp.bfloat16)
         self.last = swap(one, 1)
         return one
 
     def total(self):
-        total = self.zero.astype(jnp.float32) + self.side.astype(jnp.float32)
+        total = self.zero.astype(jnp.float32) + self.far[1].astype(jnp.float32)
         self.sum = (total + self.last.astype(jnp.float32)).astype(jnp.bfloat16)
         return self.sum
 
@@ -737,55 +858,48 @@
         axis=2,
     )
 
-    if is_cube():
+    cube = is_cube()
+    if cube:
         part_of, slot_of = part_tables()
-        attn_move = Gather(wire_attn, ready=bias)
+        attn_move = Gather(wire_attn)
         up_move = Gather(up_weight, behind=attn_move)
         down_move = Gather(wire_down, behind=up_move)
-        attn_full = place_pieces(part_of, attn_move.pieces)
-        up_full = place_pieces(part_of, up_move.pieces)
+        attn_pieces, up_pieces = attn_move.pieces, up_move.pieces
         down_full = unpack_pieces(part_of, down_move.pieces, fold)
     else:
-        attn_full = gather_shards(wire_attn)
-        up_full = gather_shards(up_weight)
+        part_of = jnp.zeros((1,), jnp.int32)
+        attn_pieces = [gather_shards(wire_attn).reshape(groups, width, width)]
+        up_pieces = [gather_shards(up_weight).reshape(groups, width, width)]
         down_full = unpack_down(gather_shards(wire_down), fold)
-    attn_full = attn_full.reshape(groups, width, width)
-    up_full = up_full.reshape(groups, width, width)
 
     x_rows = images.reshape(rows, width).astype(wide)
     normed, unit_one, inv_one = normalize(x_rows, gain_one, shift_one)
     normed_low = normed.astype(low)
-    qkv, probs, mixed_split = attend(normed_low, attn_full, time_add, bias, count, tokens)
-    proj_full = take_proj(attn_full)
+    qkv, probs, mixed_split, proj_full, attn_full = attend(
+        part_of, attn_pieces, normed_low, time_add, bias, count, tokens
+    )
     mixed = mixed_split.transpose(1, 0, 2).reshape(rows, width)
     hidden = x_rows + (matmul(mixed, proj_full) + proj_b)
     second, unit_two, inv_two = normalize(hidden, gain_two, shift_two)
     second_low = second.astype(low)
     grad_low = cotangent.reshape(rows, width)
     grad_rows = grad_low.astype(wide)
-    cube = is_cube()
     wire = (groups, parts, shard_rows, width)
-    pre = [matmul(second_low, up_full[g]) + up_b[g] for g in range(groups)]
-    activ = [jax.nn.gelu(p, approximate=False).astype(low) for p in pre]
+    if cube:
+        second_low = after(second_low, down_move.first)
+    activ, slope, up_full = up_forward(part_of, up_pieces, second_low, up_b)
     grad_cols = grad_low
     if cube:
-        activ_t = jnp.concatenate([a.T for a in activ], axis=0)
-        own, send = down_slot_grad(slot_of, activ_t, grad_low, groups, parts, shard_rows)
+        own, send = down_slot_grad(slot_of, activ, grad_low, parts, shard_rows)
         down_move = Scatter(own, send)
-        grad_cols = after(grad_low, send)
-    result = hidden + down_b
-    d_second = jnp.zeros((rows, width), wide)
-    d_pre = []
-    for g in range(groups):
-        down_g = down_full[g * width : (g + 1) * width]
-        d_g = (times_transposed(grad_cols, down_g) * gelu_slope(pre[g])).astype(low)
-        d_second = d_second + times_transposed(d_g, up_full[g])
-        d_pre.append(d_g)
-    second_t = second_low.T
+        grad_cols = after(grad_low, down_move.near())
+    d_pre, d_second, layer_out = down_back(
+        grad_cols, hidden + down_b, activ, slope, up_full, down_full
+    )
+    layer_out = layer_out.reshape(count, tokens, width)
     if cube:
-        second_t = after(second_t, down_move.near())
         own, send = slot_grad(
-            one_grad_kernel, slot_of, [second_t], jnp.stack(d_pre), parts, "up_grad"
+            one_grad_kernel, slot_of, [second_low.T], d_pre, parts, "up_grad"
         )
         up_move = Scatter(own, send)
         d_second = after(d_second, send)
@@ -794,29 +908,24 @@
         down_sum = scatter_sum(pack_down(grad_down.astype(low), groups, parts, shard_rows))
         grad_up = jnp.stack([contract_rows(second_low, d).astype(low) for d in d_pre])
         up_sum = scatter_sum(grad_up.reshape(wire))
-    for g in range(groups):
-        down_g = down_full[g * width : (g + 1) * width]
-        result = result + matmul(activ[g], down_g)
-    layer_out = result.astype(low).reshape(count, tokens, width)
 
     d_hidden = grad_rows + norm_back(d_second, unit_two, inv_two, gain_two)
     d_hidden_low = d_hidden.astype(low)
-    d_hidden_cols = after(d_hidden_low, down_move.back()) if cube else d_hidden_low
-    d_mixed = times_transposed(d_hidden_cols, proj_full).astype(low)
+    d_mixed = times_transposed(d_hidden_low, proj_full).astype(low)
     d_mixed_split = d_mixed.reshape(rows, groups, shard_cols).transpose(1, 0, 2)
     d_hidden_split = d_hidden_low.reshape(rows, groups, shard_cols).transpose(1, 0, 2)
     if cube:
-        d_mixed_split = after(d_mixed_split, up_move.near())
+        d_mixed_split = after(d_mixed_split, down_move.back(), up_move.near())
     d_packed, pairs = attend_back(d_mixed_split, qkv, probs, d_hidden_split)
     attn_back = attn_full
     if cube:
-        normed_t = after(normed_low.T, up_move.back())
+        normed_t = after(normed_low.T, down_move.total())
         own, send = slot_grad(
             pair_grad_kernel, slot_of, [normed_t, mixed.T], d_packed, parts, "pair_grad"
         )
         attn_move = Scatter(own, send)
-        attn_back = after(attn_full, send)
-        pairs = after(pairs, attn_move.near(), down_move.total())
+        attn_back = after(attn_full, send, up_move.back())
+        pairs = after(pairs, attn_move.near(), up_move.total())
     else:
         cut = 3 * shard_cols
         grad_attn = jnp.stack(
@@ -830,7 +939,8 @@
         )
         attn_sum = scatter_sum(grad_attn.astype(low).reshape(wire))
 
-    d_time = jnp.sum(d_packed.reshape(groups, count, tokens, width).astype(wide), axis=2)
+    d_time = after(d_packed, attn_back)
+    d_time = jnp.sum(d_time.reshape(groups, count, tokens, width).astype(wide), axis=2)
     d_time = jnp.concatenate(
         [d_time[:, :, :shard_cols], d_time[:, :, 2 * shard_cols : 3 * shard_cols]], axis=2
     ).astype(low)
@@ -870,7 +980,7 @@
         rows_sum(d_second * unit_two),
         rows_sum(d_second),
         rows_sum(grad_rows),
-        jnp.stack([jnp.sum(d.astype(wide), axis=0) for d in d_pre]),
+        jnp.sum(d_pre.astype(wide), axis=1),
         table_sum.reshape(groups, group_heads * table_rows),
     ]
     flat = jnp.concatenate(vectors, axis=1)
@@ -887,7 +997,6 @@
     if cube:
         down_sum = down_move.end()
         attn_move.back()
-        up_move.total()
         up_sum = up_move.end()
         attn_move.total()
         attn_sum = attn_move.end()

time: 1340 us -> 583 us (0.44)
  Pallas kernels: 840 us -> 205 us
  matrix products: 132 us -> 28.9 us
  waiting for transfers between devices: 99.6 us -> 145 us
  starting transfers between devices: 80.4 us -> 52.8 us
  local copies, waits for them, and re-layouts: 89 us -> 70.4 us
  other arithmetic: 75.9 us -> 59.6 us
    pallas_call x5 -> x4, Pallas kernels: 721 us -> 85.2 us  [the longest x2 35.6 us: piece_call(): pl.pallas_call(kernel, grid_spec=pltpu.PrefetchScalarGridSpec(num_scalar_...]
    dot_general x10 -> x2, matrix products: 77.2 us -> 5.41 us  [matmul(): return jnp.dot(left, right, preferred_element_type=jnp.float32)]
    ppermute x18 -> x15, waiting for transfers between devices: 57.6 us -> 108 us  [swap(): lax.ppermute(value, 'dp', [(i, i ^ NEAR[i & 1][hop]) for i in range(8)])]
    dot_general x14 -> x6, matrix products: 53.5 us -> 23.3 us  [times_transposed(): lax.dot_general(left, right, (((1,), (1,)), ((), ())), preferred_element_...]
    ppermute x15, starting transfers between devices: 28.3 us -> 2.96 us  [swap_core(): return lax.ppermute(value, 'dp', [(i, i ^ 1) for i in range(8)])]
  transfers between devices with their start and end apart: 66 -> 63, of which waited for: 19 -> 22; matrix products, arithmetic and copies ran while one was open for 22% -> 27% of each run, Pallas kernels for 62% -> 30%
where the time goes in v3:
time: 583 us; the launch traced here: 577 us
  Pallas kernels  205 us (35%)
  waiting for transfers between devices  145 us (25%)
  local copies, waits for them, and re-layouts  70.4 us (12%)
  other arithmetic  59.6 us (10%)
  starting transfers between devices  52.8 us (9%)
  matrix products  28.9 us (5%)
  between operations  15.4 us (3%)
    ppermute x15, waiting for transfers between devices, swap(): lax.ppermute(value, 'dp', [(i, i ^ NEAR[i & 1][hop]) for i in range(8)])  108 us
    pallas_call x2, Pallas kernels, piece_call(): pl.pallas_call(kernel, grid_spec=pltpu.PrefetchScalarGridSpec(num_scalar_...  35.6 us
    ppermute x27, waiting for transfers between devices, swap_bit(): return lax.ppermute(value, axis, [(i, i ^ 1 << bit) for i in range(size)])  34.2 us
    ppermute x27, starting transfers between devices, swap_bit(): return lax.ppermute(value, axis, [(i, i ^ 1 << bit) for i in range(size)])  33.9 us
    pallas_call x1, Pallas kernels, down_back(): pl.pallas_call(down_back_kernel, grid=(groups,), in_specs=[whole, whole,...  29.5 us
    pallas_call x1, Pallas kernels, table_gradient(): pl.pallas_call(table_kernel, grid=(tokens // block,), in_specs=[pl.BlockS...  27.4 us
    pallas_call x2, Pallas kernels, slot_grad(): pl.pallas_call(kernel, grid_spec=pltpu.PrefetchScalarGridSpec(num_scalar_...  26.7 us
    dot_general x6, matrix products, times_transposed(): lax.dot_general(left, right, (((1,), (1,)), ((), ())), preferred_element_...  23.3 us
  transfers between devices with their start and end apart: 63, of which 22 were waited for; matrix products, arithmetic and copies ran while one was open for 27% of the time, Pallas kernels for 30%

profile of v3, /device:TPU:0, one launch (start us, length us, event | category | flops | bytes accessed | tf_op | source)
XLA Modules:
  0.0 576.8 jit_solution(6082034506679053231)
XLA Ops:
  8.9 3.1 collective-permute-start.2
  12.8 4.9 concatenate.144
  18.3 2.0 concatenate.171
  20.4 2.1 fusion.70
  22.8 3.1 collective-permute-start.3
  52.2 2.8 all-gather.7.cloned.1.call-done
  59.9 3.0 collective-permute-done.1
  64.4 20.9 %collective-permute-done.12.refs_1_ = bf16[4,144,1152]{2,1,0:T(8,128)(2,1)} collective-permute-done((bf16[4,144,1152]{2,1,0:T(8,128)(2,1)}, bf16[4,144,1152]{2,1,0:T(8,128)(2,1)}, u32[]{:S(2)}, u32[]{:S(2)}) %collective-permute-start.12) | collective-permute-done | bytes 1327136 | tf_op jit(solution)/shard_map/ppermute | solution.py:649
  85.3 2.3 collective-permute-start.14
  93.4 3.3 collective-permute-done.11
  97.3 19.8 %collective-permute-done.14.refs_3_ = bf16[4,144,1152]{2,1,0:T(8,128)(2,1)} collective-permute-done((bf16[4,144,1152]{2,1,0:T(8,128)(2,1)}, bf16[4,144,1152]{2,1,0:T(8,128)(2,1)}, u32[]{:S(2)}, u32[]{:S(2)}) %collective-permute-start.14) | collective-permute-done | bytes 1327136 | tf_op jit(solution)/shard_map/ppermute | solution.py:649
  118.2 2.2 collective-permute-done.19.refs_1_
  122.8 20.1 %position_bias.1.bias_ref = f32[16,256,256]{2,1,0:T(8,128)} custom-call(s32[256,256]{1,0:T(8,128)} %index_ref.3, f32[16,1,1024]{2,1,0:T(1,128)} %reshape.338.table_ref), custom_call_target="tpu_custom_call" | custom-call | flops 1 | bytes 1 | tf_op jit(solution)/shard_map/position_bias/pallas_call | solution.py:106
  148.5 21.0 %attend.1 = (bf16[4,512,896]{2,1,0:T(8,128)(2,1)}, bf16[4,2,4,256,256]{4,3,2,1,0:T(8,128)(2,1)}, bf16[4,512,288]{2,1,0:T(8,128)(2,1)}, bf16[1152,1152]{1,0:T(8,128)(2,1)}, bf16[4,1152,1152]{2,1,0:T(8,128)(2,1)}) custom-call(s32[8]{0:T(128)} %fusion.57.part_ref, bf16[512,1152]{1,0:T(8,128)(2,1)} %copy.110.normed_ref, ...), custom_call_target="tpu_custom_call" | custom-call | flops 1 | bytes 1 | tf_op jit(solution)/shard_map/attend/pallas_call | solution.py:207
  172.8 4.2 fusion.74
  177.7 1.9 broadcast_add_fusion
  179.7 9.8 %collective-permute-done.20.refs_1_ = bf16[4,144,1152]{2,1,0:T(8,128)(2,1)} collective-permute-done((bf16[4,144,1152]{2,1,0:T(8,128)(2,1)}, bf16[4,144,1152]{2,1,0:T(8,128)(2,1)}, u32[]{:S(2)}, u32[]{:S(2)}) %collective-permute-start.20) | collective-permute-done | bytes 1327136 | tf_op jit(solution)/shard_map/ppermute | solution.py:649
  190.8 14.6 %up_forward.1 = (bf16[4,512,1152]{2,1,0:T(8,128)(2,1)}, bf16[4,512,1152]{2,1,0:T(8,128)(2,1)}, bf16[4,1152,1152]{2,1,0:T(8,128)(2,1)}) custom-call(s32[8]{0:T(128)} %fusion.57.part_ref, bf16[512,1152]{1,0:T(8,128)(2,1)} %copy.117.second_ref, f32[4,1,1152]{2,1,0:T(1,128)} %reshape.343.bias_ref, bf16[4,144,1152]{2,1,0:T(8,128)(2,1)} %bitcast.9.refs_0_, ...), custom_call_target="tpu_custom_call" | custom-call | flops 1 | bytes 1 | tf_op jit(solution)/shard_map/up_forward/pallas_call | solution.py:207
  205.4 18.5 %down_grad.1 = (bf16[4,4,144,1152]{3,2,1,0:T(8,128)(2,1)}, bf16[4,4,144,1152]{3,2,1,0:T(8,128)(2,1)}) custom-call(s32[8]{0:T(128)} %fusion.56.slot_ref, bf16[4,512,1152]{2,1,0:T(8,128)(2,1)} %get-tuple-element.66.left_ref.activ_ref, bf16[512,1152]{1,0:T(8,128)(2,1)} %bitcast.141), custom_call_target="tpu_custom_call" | custom-call | flops 1 | bytes 1 | tf_op jit(solution)/shard_map/down_grad/pallas_call | solution.py:541
  226.5 15.6 %collective-permute-done.28.refs_2_ = bf16[4,144,1152]{2,1,0:T(8,128)(2,1)} collective-permute-done((bf16[4,144,1152]{2,1,0:T(8,128)(2,1)}, bf16[4,144,1152]{2,1,0:T(8,128)(2,1)}, u32[]{:S(2)}, u32[]{:S(2)}) %collective-permute-start.28) | collective-permute-done | bytes 1327136 | tf_op jit(solution)/shard_map/ppermute | solution.py:649
  242.0 14.2 %collective-permute-done.29.refs_3_ = bf16[4,144,1152]{2,1,0:T(8,128)(2,1)} collective-permute-done((bf16[4,144,1152]{2,1,0:T(8,128)(2,1)}, bf16[4,144,1152]{2,1,0:T(8,128)(2,1)}, u32[]{:S(2)}, u32[]{:S(2)}) %collective-permute-start.29) | collective-permute-done | bytes 1327136 | tf_op jit(solution)/shard_map/ppermute | solution.py:649
  256.3 6.6 %add_halves.3 = (bf16[4,144,1152]{2,1,0:T(8,128)(2,1)}, bf16[4,144,1152]{2,1,0:T(8,128)(2,1)}, bf16[2,4,144,1152]{3,2,1,0:T(8,128)(2,1)}) custom-call(bf16[4,4,144,1152]{3,2,1,0:T(8,128)(2,1)} %get-tuple-element.67.one_ref.two_ref.three_ref.four_ref, bf16[4,4,144,1152]{3,2,1,0:T(8,128)(2,1)} %get-tuple-element.67.one_ref.two_ref.three_ref.four_ref, ...), custom_call_target="tpu_custom_call" | custom-call | flops 1 | bytes 1 | tf_op jit(solution)/shard_map/add_halves/pallas_call | solution.py:572
  265.1 3.1 copy.120.hidden_ref
  268.2 8.9 %unpack_pieces.1.down_ref = bf16[4608,1152]{1,0:T(8,128)(2,1)} custom-call(s32[8]{0:T(128)} %fusion.57.part_ref, bf16[4,144,1152]{2,1,0:T(8,128)(2,1)} %bitcast.10.refs_0_, bf16[4,144,1152]{2,1,0:T(8,128)(2,1)} %collective-permute-done.20.refs_1_, bf16[4,144,1152]{2,1,0:T(8,128)(2,1)} %collective-permute-done.28.refs_2_, ...), custom_call_target="tpu_custom_call" | custom-call | flops 1 | bytes 1 | tf_op jit(solution)/shard_map/unpack_pieces/pallas_call | solution.py:608
  278.4 29.5 %down_back.1 = (bf16[4,512,1152]{2,1,0:T(8,128)(2,1)}, f32[512,1152]{1,0:T(8,128)}, bf16[512,1152]{1,0:T(8,128)(2,1)}) custom-call(bf16[512,1152]{1,0:T(8,128)(2,1)} %copy.119.grad_ref, f32[512,1152]{1,0:T(8,128)} %copy.120.hidden_ref, bf16[4,512,1152]{2,1,0:T(8,128)(2,1)} %get-tuple-element.66.left_ref.activ_ref, ...), custom_call_target="tpu_custom_call" | custom-call | flops 1 | bytes 1 | tf_op jit(solution)/shard_map/down_back/pallas_call | solution.py:367
  308.0 12.5 %up_grad.1 = (bf16[4,4,144,1152]{3,2,1,0:T(8,128)(2,1)}, bf16[4,4,144,1152]{3,2,1,0:T(8,128)(2,1)}) custom-call(s32[8]{0:T(128)} %fusion.56.slot_ref, bf16[1152,512]{1,0:T(8,128)(2,1)} %bitcast.140, bf16[4,512,1152]{2,1,0:T(8,128)(2,1)} %get-tuple-element.75.right_ref), custom_call_target="tpu_custom_call" | custom-call | flops 1 | bytes 1 | tf_op jit(solution)/shard_map/up_grad/pallas_call | solution.py:501
  321.8 2.7 fusion.9
  326.6 3.1 copy.121
  329.7 12.9 %collective-permute-done.36 = bf16[4,144,1152]{2,1,0:T(8,128)(2,1)} collective-permute-done((bf16[4,144,1152]{2,1,0:T(8,128)(2,1)}, bf16[4,144,1152]{2,1,0:T(8,128)(2,1)}, u32[]{:S(2)}, u32[]{:S(2)}) %collective-permute-start.36) | collective-permute-done | bytes 1327136 | tf_op jit(solution)/shard_map/ppermute | solution.py:649
  342.6 3.6 fusion.8
  346.3 3.1 multiply_reduce_fusion
  349.5 7.3 %add_halves.4 = (bf16[4,144,1152]{2,1,0:T(8,128)(2,1)}, bf16[4,144,1152]{2,1,0:T(8,128)(2,1)}, bf16[2,4,144,1152]{3,2,1,0:T(8,128)(2,1)}) custom-call(bf16[4,4,144,1152]{3,2,1,0:T(8,128)(2,1)} %get-tuple-element.79.one_ref.two_ref.three_ref.four_ref, bf16[4,4,144,1152]{3,2,1,0:T(8,128)(2,1)} %get-tuple-element.79.one_ref.two_ref.three_ref.four_ref, ...), custom_call_target="tpu_custom_call" | custom-call | flops 1 | bytes 1 | tf_op jit(solution)/shard_map/add_halves/pallas_call | solution.py:572
  359.9 2.9 convolution_convert_fusion
  362.8 2.4 copy.122
  365.2 2.5 copy.123
  367.7 2.6 copy.124
  370.3 17.3 %attend_back.1 = (bf16[4,512,1152]{2,1,0:T(8,128)(2,1)}, f32[16,256,256]{2,1,0:T(8,128)}) custom-call(bf16[4,512,288]{2,1,0:T(8,128)(2,1)} %bitcast.143, bf16[4,512,896]{2,1,0:T(8,128)(2,1)} %get-tuple-element.82.qkv_ref, bf16[4,2,4,256,256]{4,3,2,1,0:T(8,128)(2,1)} %get-tuple-element.83.probs_ref, bf16[4,512,288]{2,1,0:T(8,128)(2,1)} %bitcast.144), custom_call_target="tpu_custom_call" | custom-call | flops 1 | bytes 1 | tf_op jit(solution)/shard_map/attend_back/pallas_call | solution.py:431
  387.6 14.2 %pair_grad.1 = (bf16[4,4,144,1152]{3,2,1,0:T(8,128)(2,1)}, bf16[4,4,144,1152]{3,2,1,0:T(8,128)(2,1)}) custom-call(s32[8]{0:T(128)} %fusion.56.slot_ref, bf16[1152,512]{1,0:T(8,128)(2,1)} %fusion.84.one_ref, bf16[1152,512]{1,0:T(8,128)(2,1)} %bitcast.146, bf16[4,512,1152]{2,1,0:T(8,128)(2,1)} %get-tuple-element.91.right_ref), custom_call_target="tpu_custom_call" | custom-call | flops 1 | bytes 1 | tf_op jit(solution)/shard_map/pair_grad/pallas_call | solution.py:501
  404.6 2.4 reduce_sum.157
  411.1 3.6 convert_reduce_fusion
  416.9 2.3 copy.133
  419.3 3.1 fusion.6
  423.5 3.0 bitcast_reduce_fusion
  430.3 3.9 fusion.13
  434.2 3.9 convolution_add_fusion.2
  438.0 5.3 convolution_add_fusion.1
  444.7 7.0 %add_halves.5 = (bf16[4,144,1152]{2,1,0:T(8,128)(2,1)}, bf16[4,144,1152]{2,1,0:T(8,128)(2,1)}, bf16[2,4,144,1152]{3,2,1,0:T(8,128)(2,1)}) custom-call(bf16[4,4,144,1152]{3,2,1,0:T(8,128)(2,1)} %get-tuple-element.92.one_ref.two_ref.three_ref.four_ref, bf16[4,4,144,1152]{3,2,1,0:T(8,128)(2,1)} %get-tuple-element.92.one_ref.two_ref.three_ref.four_ref, ...), custom_call_target="tpu_custom_call" | custom-call | flops 1 | bytes 1 | tf_op jit(solution)/shard_map/add_halves/pallas_call | solution.py:572
  452.6 7.1 %multiply_reduce_fusion.1 = (f32[1152]{0:T(1024)}, f32[512]{0:T(512)S(1)}, f32[512]{0:T(512)S(1)}, f32[1152]{0:T(1024)}, f32[512,1152]{0,1:T(8,128)}) fusion(f32[512,1152]{0,1:T(8,128)S(1)} %copy-done.2, f32[512]{0:T(512)S(1)} %bitcast.164, f32[512]{0:T(512)S(1)} %bitcast.168, f32[1152]{0:T(1024)S(1)} %reshape.335, f32[512,1152]{0,1:T(8,128)} %convolution_add_fusion.1, ...), kind=kOutput, calls=%fused_computation.34 | convolution fusion | flops 1365439232 | bytes 10934912 | tf_op jit(solution)/shard_map/dot_general | solution.py:37
  463.0 3.3 collective-permute-done.41
  468.2 3.3 fusion.2
  471.7 12.4 %collective-permute-done.49 = bf16[2,4,144,1152]{3,2,1,0:T(8,128)(2,1)} collective-permute-done((bf16[2,4,144,1152]{3,2,1,0:T(8,128)(2,1)}, bf16[2,4,144,1152]{3,2,1,0:T(8,128)(2,1)}, u32[]{:S(2)}, u32[]{:S(2)}) %collective-permute-start.49) | collective-permute-done | bytes 2654240 | tf_op jit(solution)/shard_map/ppermute | solution.py:649
  484.1 3.1 fusion.3
  488.0 4.4 add_convert_fusion
  494.2 2.4 copy.141
  497.9 1.9 collective-permute-start.43
  500.1 5.3 collective-permute-done.43
  505.4 3.4 fusion.5
  510.2 27.4 %table_gradient.1 = f32[128,128]{1,0:T(8,128)} custom-call(s32[256,256]{1,0:T(8,128)} %index_ref.3, f32[16,256,256]{2,1,0:T(8,128)} %get-tuple-element.98.pairs_ref), custom_call_target="tpu_custom_call" | custom-call | flops 1 | bytes 1 | tf_op jit(solution)/shard_map/table_gradient/pallas_call | solution.py:159
  540.0 3.7 collective-permute-start.45
  543.7 5.7 collective-permute-done.52
  549.6 3.8 collective-permute-done.53
  557.7 2.1 collective-permute-done.55
  561.2 2.5 collective-permute-done.56
  565.8 1.9 bitcast_convert_fusion
  (353 shorter events, 108.8 us)
Async XLA Ops:
  7.2 47.8 %all-gather.7.cloned.1.call-start = ((), (), s32[]{:S(2)}) async-start(), calls=%async_computation.6 | async-start | bytes 1658880 | tf_op jit(solution)/shard_map/all_gather | solution.py:664
  8.9 13.8 %collective-permute-start.2 = (bf16[2,1152]{1,0:T(2,128)(2,1)S(1)}, bf16[2,1152]{1,0:T(2,128)(2,1)S(1)}, u32[]{:S(2)}, u32[]{:S(2)}) collective-permute-start(bf16[2,1152]{1,0:T(2,128)(2,1)S(1)} %fusion.55), channel_id=1, source_target_pairs={{0,1},{1,0},{2,3},{3,2},{4,5},{5,4},{6,7},{7,6},{8,9},{9,8},{10,11... | collective-permute-start | bytes 13832 | tf_op jit(solution)/shard_map/ppermute | solution.py:704
  18.3 38.9 %collective-permute-start = (bf16[1,56,128]{2,1,0:T(8,128)(2,1)}, bf16[1,56,128]{2,1,0:T(8,128)(2,1)S(1)}, u32[]{:S(2)}, u32[]{:S(2)}) collective-permute-start(bf16[1,56,128]{2,1,0:T(8,128)(2,1)} %get-tuple-element.218), channel_id=1, source_target_pairs={{0,1},{1,0},{2,3},{3,2},{4,5},{5,4},{6,7},{7,6},{8,9},{9,8},{10,11... | collective-permute-start | bytes 43016 | tf_op jit(solution)/shard_map/ppermute | solution.py:704
  20.3 67.7 %all-gather.9.cloned.1.call-start = ((), (), s32[]{:S(2)}) async-start(), calls=%async_computation.7 | async-start | bytes 1658880 | tf_op jit(solution)/shard_map/all_gather | solution.py:664
  22.8 4.7 collective-permute-start.3
  27.6 1.3 collective-permute-start.4
  29.5 12.7 %collective-permute-start.5 = (bf16[16,1152]{1,0:T(8,128)(2,1)}, bf16[16,1152]{1,0:T(8,128)(2,1)}, u32[]{:S(2)}, u32[]{:S(2)}) collective-permute-start(bf16[16,1152]{1,0:T(8,128)(2,1)} %maximum_select_fusion.6), channel_id=1, source_target_pairs={{0,8},{4,12},{8,0},{12,4},{16,24},{20,28},{24,16},{28,20},{1,9},{5... | collective-permute-start | bytes 110600 | tf_op jit(solution)/shard_map/ppermute | solution.py:704
  34.4 82.6 %copy-start = (f32[512,1152]{0,1:T(8,128)}, f32[512,1152]{0,1:T(8,128)S(1)}, u32[]{:S(2)}) copy-start(f32[512,1152]{0,1:T(8,128)S(1)} %copy.140) | copy-start | bytes 7077892
  43.0 4.4 collective-permute-start.6
  49.4 5.7 collective-permute-start.7
  55.0 116.2 %all-gather.11.cloned.1.call-start = ((), (), s32[]{:S(2)}) async-start(), calls=%async_computation.8 | async-start | bytes 1658880 | tf_op jit(solution)/shard_map/all_gather | solution.py:664
  55.1 4.5 collective-permute-start.8
  56.6 28.7 %collective-permute-start.12 = (bf16[4,144,1152]{2,1,0:T(8,128)(2,1)}, bf16[4,144,1152]{2,1,0:T(8,128)(2,1)}, u32[]{:S(2)}, u32[]{:S(2)}) collective-permute-start(bf16[4,144,1152]{2,1,0:T(8,128)(2,1)} %bitcast.150), channel_id=1, source_target_pairs={{0,8},{4,20},{8,0},{12,28},{16,24},{20,4},{24,16},{28,12},{1,9},{5... | collective-permute-start | bytes 3981320 | tf_op jit(solution)/shard_map/ppermute | solution.py:649
  58.0 4.8 collective-permute-start.1
  59.6 27.9 %collective-permute-start.9 = (f32[8,576]{1,0:T(8,128)S(1)}, f32[8,576]{1,0:T(8,128)S(1)}, u32[]{:S(2)}, u32[]{:S(2)}) collective-permute-start(f32[8,576]{1,0:T(8,128)S(1)} %slice_select_fusion.3), channel_id=1, source_target_pairs={{0,4},{4,0},{8,12},{12,8},{16,20},{20,16},{24,28},{28,24},{1,5},{5... | collective-permute-start | bytes 55304 | tf_op jit(solution)/shard_map/ppermute | solution.py:704
  62.8 33.9 %collective-permute-start.13 = (bf16[4,144,1152]{2,1,0:T(8,128)(2,1)}, bf16[4,144,1152]{2,1,0:T(8,128)(2,1)}, u32[]{:S(2)}, u32[]{:S(2)}) collective-permute-start(bf16[4,144,1152]{2,1,0:T(8,128)(2,1)} %bitcast.151), channel_id=1, source_target_pairs={{0,16},{4,12},{8,24},{12,4},{16,0},{20,28},{24,8},{28,20},{1,17},{... | collective-permute-start | bytes 3981320 | tf_op jit(solution)/shard_map/ppermute | solution.py:649
  64.4 32.9 %collective-permute-start.15 = (bf16[4,144,1152]{2,1,0:T(8,128)(2,1)}, bf16[4,144,1152]{2,1,0:T(8,128)(2,1)}, u32[]{:S(2)}, u32[]{:S(2)}) collective-permute-start(bf16[4,144,1152]{2,1,0:T(8,128)(2,1)} %bitcast.152), channel_id=1, source_target_pairs={{0,4},{4,0},{8,12},{12,8},{16,20},{20,16},{24,28},{28,24},{1,5},{5... | collective-permute-start | bytes 3981320 | tf_op jit(solution)/shard_map/ppermute | solution.py:653
  85.3 31.7 %collective-permute-start.14 = (bf16[4,144,1152]{2,1,0:T(8,128)(2,1)}, bf16[4,144,1152]{2,1,0:T(8,128)(2,1)}, u32[]{:S(2)}, u32[]{:S(2)}) collective-permute-start(bf16[4,144,1152]{2,1,0:T(8,128)(2,1)} %collective-permute-done.12.refs_1_), channel_id=1, source_target_pairs={{0,16},{4,12},{8,24},{12,4},{16,0},{20,28},{24,8},{28,20},{1,17},{... | collective-permute-start | bytes 3981320 | tf_op jit(solution)/shard_map/ppermute | solution.py:649
  87.6 3.8 collective-permute-start.10
  88.1 32.3 %collective-permute-start.19 = (bf16[4,144,1152]{2,1,0:T(8,128)(2,1)}, bf16[4,144,1152]{2,1,0:T(8,128)(2,1)}, u32[]{:S(2)}, u32[]{:S(2)}) collective-permute-start(bf16[4,144,1152]{2,1,0:T(8,128)(2,1)} %bitcast.9.refs_0_), channel_id=1, source_target_pairs={{0,8},{4,20},{8,0},{12,28},{16,24},{20,4},{24,16},{28,12},{1,9},{5... | collective-permute-start | bytes 3981320 | tf_op jit(solution)/shard_map/ppermute | solution.py:649
  89.7 325.0 %reduce-scatter.8.cloned.1.call-start = ((), (), s32[]{:S(2)}) async-start(), calls=%async_computation.5 | async-start | bytes 1658880 | tf_op jit(solution)/shard_map/reduce_scatter | solution.py:699
  91.4 5.3 collective-permute-start.11
  96.7 51.2 %collective-permute-start.16 = (bf16[4,144,1152]{2,1,0:T(8,128)(2,1)}, bf16[4,144,1152]{2,1,0:T(8,128)(2,1)}, u32[]{:S(2)}, u32[]{:S(2)}) collective-permute-start(bf16[4,144,1152]{2,1,0:T(8,128)(2,1)} %collective-permute-done.12.refs_1_), channel_id=1, source_target_pairs={{0,4},{4,0},{8,12},{12,8},{16,20},{20,16},{24,28},{28,24},{1,5},{5... | collective-permute-start | bytes 3981320 | tf_op jit(solution)/shard_map/ppermute | solution.py:653
  96.8 51.2 %collective-permute-start.17 = (bf16[4,144,1152]{2,1,0:T(8,128)(2,1)}, bf16[4,144,1152]{2,1,0:T(8,128)(2,1)}, u32[]{:S(2)}, u32[]{:S(2)}) collective-permute-start(bf16[4,144,1152]{2,1,0:T(8,128)(2,1)} %collective-permute-done.13.refs_2_), channel_id=1, source_target_pairs={{0,4},{4,0},{8,12},{12,8},{16,20},{20,16},{24,28},{28,24},{1,5},{5... | collective-permute-start | bytes 3981320 | tf_op jit(solution)/shard_map/ppermute | solution.py:653
  97.3 51.2 %collective-permute-start.21 = (bf16[4,144,1152]{2,1,0:T(8,128)(2,1)}, bf16[4,144,1152]{2,1,0:T(8,128)(2,1)}, u32[]{:S(2)}, u32[]{:S(2)}) collective-permute-start(bf16[4,144,1152]{2,1,0:T(8,128)(2,1)} %bitcast.9.refs_0_), channel_id=1, source_target_pairs={{0,16},{4,12},{8,24},{12,4},{16,0},{20,28},{24,8},{28,20},{1,17},{... | collective-permute-start | bytes 3981320 | tf_op jit(solution)/shard_map/ppermute | solution.py:649
  117.0 31.5 %collective-permute-start.18 = (bf16[4,144,1152]{2,1,0:T(8,128)(2,1)}, bf16[4,144,1152]{2,1,0:T(8,128)(2,1)}, u32[]{:S(2)}, u32[]{:S(2)}) collective-permute-start(bf16[4,144,1152]{2,1,0:T(8,128)(2,1)} %collective-permute-done.14.refs_3_), channel_id=1, source_target_pairs={{0,4},{4,0},{8,12},{12,8},{16,20},{20,16},{24,28},{28,24},{1,5},{5... | collective-permute-start | bytes 3981320 | tf_op jit(solution)/shard_map/ppermute | solution.py:653
  120.4 56.6 %collective-permute-start.22 = (bf16[4,144,1152]{2,1,0:T(8,128)(2,1)}, bf16[4,144,1152]{2,1,0:T(8,128)(2,1)}, u32[]{:S(2)}, u32[]{:S(2)}) collective-permute-start(bf16[4,144,1152]{2,1,0:T(8,128)(2,1)} %collective-permute-done.19.refs_1_), channel_id=1, source_target_pairs={{0,16},{4,12},{8,24},{12,4},{16,0},{20,28},{24,8},{28,20},{1,17},{... | collective-permute-start | bytes 3981320 | tf_op jit(solution)/shard_map/ppermute | solution.py:649
  147.9 42.9 %collective-permute-start.23 = (bf16[4,144,1152]{2,1,0:T(8,128)(2,1)}, bf16[4,144,1152]{2,1,0:T(8,128)(2,1)}, u32[]{:S(2)}, u32[]{:S(2)}) collective-permute-start(bf16[4,144,1152]{2,1,0:T(8,128)(2,1)} %bitcast.9.refs_0_), channel_id=1, source_target_pairs={{0,4},{4,0},{8,12},{12,8},{16,20},{20,16},{24,28},{28,24},{1,5},{5... | collective-permute-start | bytes 3981320 | tf_op jit(solution)/shard_map/ppermute | solution.py:653
  147.9 42.9 %collective-permute-start.24 = (bf16[4,144,1152]{2,1,0:T(8,128)(2,1)}, bf16[4,144,1152]{2,1,0:T(8,128)(2,1)}, u32[]{:S(2)}, u32[]{:S(2)}) collective-permute-start(bf16[4,144,1152]{2,1,0:T(8,128)(2,1)} %collective-permute-done.19.refs_1_), channel_id=1, source_target_pairs={{0,4},{4,0},{8,12},{12,8},{16,20},{20,16},{24,28},{28,24},{1,5},{5... | collective-permute-start | bytes 3981320 | tf_op jit(solution)/shard_map/ppermute | solution.py:653
  148.4 42.4 %collective-permute-start.25 = (bf16[4,144,1152]{2,1,0:T(8,128)(2,1)}, bf16[4,144,1152]{2,1,0:T(8,128)(2,1)}, u32[]{:S(2)}, u32[]{:S(2)}) collective-permute-start(bf16[4,144,1152]{2,1,0:T(8,128)(2,1)} %collective-permute-done.21.refs_2_), channel_id=1, source_target_pairs={{0,4},{4,0},{8,12},{12,8},{16,20},{20,16},{24,28},{28,24},{1,5},{5... | collective-permute-start | bytes 3981320 | tf_op jit(solution)/shard_map/ppermute | solution.py:653
  171.2 18.2 %collective-permute-start.20 = (bf16[4,144,1152]{2,1,0:T(8,128)(2,1)}, bf16[4,144,1152]{2,1,0:T(8,128)(2,1)}, u32[]{:S(2)}, u32[]{:S(2)}) collective-permute-start(bf16[4,144,1152]{2,1,0:T(8,128)(2,1)} %bitcast.10.refs_0_), channel_id=1, source_target_pairs={{0,8},{4,20},{8,0},{12,28},{16,24},{20,4},{24,16},{28,12},{1,9},{5... | collective-permute-start | bytes 3981320 | tf_op jit(solution)/shard_map/ppermute | solution.py:649
  177.1 13.8 %collective-permute-start.26 = (bf16[4,144,1152]{2,1,0:T(8,128)(2,1)}, bf16[4,144,1152]{2,1,0:T(8,128)(2,1)}, u32[]{:S(2)}, u32[]{:S(2)}) collective-permute-start(bf16[4,144,1152]{2,1,0:T(8,128)(2,1)} %collective-permute-done.22.refs_3_), channel_id=1, source_target_pairs={{0,4},{4,0},{8,12},{12,8},{16,20},{20,16},{24,28},{28,24},{1,5},{5... | collective-permute-start | bytes 3981320 | tf_op jit(solution)/shard_map/ppermute | solution.py:653
  223.9 32.3 %collective-permute-start.27 = (bf16[4,4,144,1152]{3,2,1,0:T(8,128)(2,1)}, bf16[4,4,144,1152]{3,2,1,0:T(8,128)(2,1)}, u32[]{:S(2)}, u32[]{:S(2)}) collective-permute-start(bf16[4,4,144,1152]{3,2,1,0:T(8,128)(2,1)} %get-tuple-element.68), channel_id=1, source_target_pairs={{0,4},{4,0},{8,12},{12,8},{16,20},{20,16},{24,28},{28,24},{1,5},{5... | collective-permute-start | bytes 15925256 | tf_op jit(solution)/shard_map/ppermute | solution.py:653
  223.9 18.1 %collective-permute-start.28 = (bf16[4,144,1152]{2,1,0:T(8,128)(2,1)}, bf16[4,144,1152]{2,1,0:T(8,128)(2,1)}, u32[]{:S(2)}, u32[]{:S(2)}) collective-permute-start(bf16[4,144,1152]{2,1,0:T(8,128)(2,1)} %bitcast.10.refs_0_), channel_id=1, source_target_pairs={{0,16},{4,12},{8,24},{12,4},{16,0},{20,28},{24,8},{28,20},{1,17},{... | collective-permute-start | bytes 3981320 | tf_op jit(solution)/shard_map/ppermute | solution.py:649
  224.5 31.7 %collective-permute-start.29 = (bf16[4,144,1152]{2,1,0:T(8,128)(2,1)}, bf16[4,144,1152]{2,1,0:T(8,128)(2,1)}, u32[]{:S(2)}, u32[]{:S(2)}) collective-permute-start(bf16[4,144,1152]{2,1,0:T(8,128)(2,1)} %collective-permute-done.20.refs_1_), channel_id=1, source_target_pairs={{0,16},{4,12},{8,24},{12,4},{16,0},{20,28},{24,8},{28,20},{1,17},{... | collective-permute-start | bytes 3981320 | tf_op jit(solution)/shard_map/ppermute | solution.py:649
  226.0 42.2 %collective-permute-start.30 = (bf16[4,144,1152]{2,1,0:T(8,128)(2,1)}, bf16[4,144,1152]{2,1,0:T(8,128)(2,1)}, u32[]{:S(2)}, u32[]{:S(2)}) collective-permute-start(bf16[4,144,1152]{2,1,0:T(8,128)(2,1)} %bitcast.10.refs_0_), channel_id=1, source_target_pairs={{0,4},{4,0},{8,12},{12,8},{16,20},{20,16},{24,28},{28,24},{1,5},{5... | collective-permute-start | bytes 3981320 | tf_op jit(solution)/shard_map/ppermute | solution.py:653
  226.0 42.2 %collective-permute-start.31 = (bf16[4,144,1152]{2,1,0:T(8,128)(2,1)}, bf16[4,144,1152]{2,1,0:T(8,128)(2,1)}, u32[]{:S(2)}, u32[]{:S(2)}) collective-permute-start(bf16[4,144,1152]{2,1,0:T(8,128)(2,1)} %collective-permute-done.20.refs_1_), channel_id=1, source_target_pairs={{0,4},{4,0},{8,12},{12,8},{16,20},{20,16},{24,28},{28,24},{1,5},{5... | collective-permute-start | bytes 3981320 | tf_op jit(solution)/shard_map/ppermute | solution.py:653
  242.0 26.1 %collective-permute-start.32 = (bf16[4,144,1152]{2,1,0:T(8,128)(2,1)}, bf16[4,144,1152]{2,1,0:T(8,128)(2,1)}, u32[]{:S(2)}, u32[]{:S(2)}) collective-permute-start(bf16[4,144,1152]{2,1,0:T(8,128)(2,1)} %collective-permute-done.28.refs_2_), channel_id=1, source_target_pairs={{0,4},{4,0},{8,12},{12,8},{16,20},{20,16},{24,28},{28,24},{1,5},{5... | collective-permute-start | bytes 3981320 | tf_op jit(solution)/shard_map/ppermute | solution.py:653
  256.3 11.9 %collective-permute-start.33 = (bf16[4,144,1152]{2,1,0:T(8,128)(2,1)}, bf16[4,144,1152]{2,1,0:T(8,128)(2,1)}, u32[]{:S(2)}, u32[]{:S(2)}) collective-permute-start(bf16[4,144,1152]{2,1,0:T(8,128)(2,1)} %collective-permute-done.29.refs_3_), channel_id=1, source_target_pairs={{0,4},{4,0},{8,12},{12,8},{16,20},{20,16},{24,28},{28,24},{1,5},{5... | collective-permute-start | bytes 3981320 | tf_op jit(solution)/shard_map/ppermute | solution.py:653
  262.9 58.9 %collective-permute-start.34 = (bf16[2,4,144,1152]{3,2,1,0:T(8,128)(2,1)}, bf16[2,4,144,1152]{3,2,1,0:T(8,128)(2,1)}, u32[]{:S(2)}, u32[]{:S(2)}) collective-permute-start(bf16[2,4,144,1152]{3,2,1,0:T(8,128)(2,1)} %get-tuple-element.69), channel_id=1, source_target_pairs={{0,16},{4,12},{8,24},{12,4},{16,0},{20,28},{24,8},{28,20},{1,17},{... | collective-permute-start | bytes 7962632 | tf_op jit(solution)/shard_map/ppermute | solution.py:649
  320.5 28.9 %collective-permute-start.35 = (bf16[4,4,144,1152]{3,2,1,0:T(8,128)(2,1)}, bf16[4,4,144,1152]{3,2,1,0:T(8,128)(2,1)}, u32[]{:S(2)}, u32[]{:S(2)}) collective-permute-start(bf16[4,4,144,1152]{3,2,1,0:T(8,128)(2,1)} %get-tuple-element.76), channel_id=1, source_target_pairs={{0,4},{4,0},{8,12},{12,8},{16,20},{20,16},{24,28},{28,24},{1,5},{5... | collective-permute-start | bytes 15925256 | tf_op jit(solution)/shard_map/ppermute | solution.py:653
  324.5 18.1 %collective-permute-start.36 = (bf16[4,144,1152]{2,1,0:T(8,128)(2,1)}, bf16[4,144,1152]{2,1,0:T(8,128)(2,1)}, u32[]{:S(2)}, u32[]{:S(2)}) collective-permute-start(bf16[4,144,1152]{2,1,0:T(8,128)(2,1)} %fusion.9), channel_id=1, source_target_pairs={{0,8},{4,20},{8,0},{12,28},{16,24},{20,4},{24,16},{28,12},{1,9},{5... | collective-permute-start | bytes 3981320 | tf_op jit(solution)/shard_map/ppermute | solution.py:649
  346.2 219.6 %reduce-scatter.6.cloned.1.call-start = ((), (), s32[]{:S(2)}) async-start(), calls=%async_computation.4 | async-start | bytes 1658880 | tf_op jit(solution)/shard_map/reduce_scatter | solution.py:699
  356.8 62.5 %collective-permute-start.37 = (bf16[2,4,144,1152]{3,2,1,0:T(8,128)(2,1)}, bf16[2,4,144,1152]{3,2,1,0:T(8,128)(2,1)}, u32[]{:S(2)}, u32[]{:S(2)}) collective-permute-start(bf16[2,4,144,1152]{3,2,1,0:T(8,128)(2,1)} %get-tuple-element.80), channel_id=1, source_target_pairs={{0,16},{4,12},{8,24},{12,4},{16,0},{20,28},{24,8},{28,20},{1,17},{... | collective-permute-start | bytes 7962632 | tf_op jit(solution)/shard_map/ppermute | solution.py:649
  401.7 43.0 %collective-permute-start.48 = (bf16[4,4,144,1152]{3,2,1,0:T(8,128)(2,1)}, bf16[4,4,144,1152]{3,2,1,0:T(8,128)(2,1)}, u32[]{:S(2)}, u32[]{:S(2)}) collective-permute-start(bf16[4,4,144,1152]{3,2,1,0:T(8,128)(2,1)} %get-tuple-element.88), channel_id=1, source_target_pairs={{0,4},{4,0},{8,12},{12,8},{16,20},{20,16},{24,28},{28,24},{1,5},{5... | collective-permute-start | bytes 15925256 | tf_op jit(solution)/shard_map/ppermute | solution.py:653
  422.4 45.8 %collective-permute-start.51 = (bf16[4,144,1152]{2,1,0:T(8,128)(2,1)}, bf16[4,144,1152]{2,1,0:T(8,128)(2,1)}, u32[]{:S(2)}, u32[]{:S(2)}) collective-permute-start(bf16[4,144,1152]{2,1,0:T(8,128)(2,1)} %fusion.6), channel_id=1, source_target_pairs={{0,8},{4,20},{8,0},{12,28},{16,24},{20,4},{24,16},{28,12},{1,9},{5... | collective-permute-start | bytes 3981320 | tf_op jit(solution)/shard_map/ppermute | solution.py:649
  428.7 14.7 %collective-permute-start.38 = (bf16[2,2304]{1,0:T(2,128)(2,1)}, bf16[2,2304]{1,0:T(2,128)(2,1)S(1)}, u32[]{:S(2)}, u32[]{:S(2)}) collective-permute-start(bf16[2,2304]{1,0:T(2,128)(2,1)} %reshape.320), channel_id=1, source_target_pairs={{0,1},{1,0},{2,3},{3,2},{4,5},{5,4},{6,7},{7,6},{8,9},{9,8},{10,11... | collective-permute-start | bytes 27656 | tf_op jit(solution)/shard_map/ppermute | solution.py:704
  443.4 16.4 %collective-permute-start.39 = (bf16[4,2304]{1,0:T(4,128)(2,1)S(1)}, bf16[4,2304]{1,0:T(4,128)(2,1)S(1)}, u32[]{:S(2)}, u32[]{:S(2)}) collective-permute-start(bf16[4,2304]{1,0:T(4,128)(2,1)S(1)} %maximum_select_fusion.11), channel_id=1, source_target_pairs={{0,2},{1,3},{2,0},{3,1},{4,6},{5,7},{6,4},{7,5},{8,10},{9,11},{10,... | collective-permute-start | bytes 55304 | tf_op jit(solution)/shard_map/ppermute | solution.py:704
  451.8 32.3 %collective-permute-start.49 = (bf16[2,4,144,1152]{3,2,1,0:T(8,128)(2,1)}, bf16[2,4,144,1152]{3,2,1,0:T(8,128)(2,1)}, u32[]{:S(2)}, u32[]{:S(2)}) collective-permute-start(bf16[2,4,144,1152]{3,2,1,0:T(8,128)(2,1)} %get-tuple-element.94), channel_id=1, source_target_pairs={{0,16},{4,12},{8,24},{12,4},{16,0},{20,28},{24,8},{28,20},{1,17},{... | collective-permute-start | bytes 7962632 | tf_op jit(solution)/shard_map/ppermute | solution.py:649
  459.8 1.3 collective-permute-start.40
  461.1 5.2 collective-permute-start.41
  467.0 29.5 %collective-permute-start.42 = (bf16[32,2304]{1,0:T(8,128)(2,1)}, bf16[32,2304]{1,0:T(8,128)(2,1)}, u32[]{:S(2)}, u32[]{:S(2)}) collective-permute-start(bf16[32,2304]{1,0:T(8,128)(2,1)} %maximum_select_fusion), channel_id=1, source_target_pairs={{0,16},{4,20},{8,24},{12,28},{16,0},{20,4},{24,8},{28,12},{1,17},{... | collective-permute-start | bytes 442376 | tf_op jit(solution)/shard_map/ppermute | solution.py:704
  471.5 96.1 %reduce-scatter.4.cloned.1.call-start = ((), (), s32[]{:S(2)}) async-start(), calls=%async_computation.3 | async-start | bytes 1658880 | tf_op jit(solution)/shard_map/reduce_scatter | solution.py:699
  487.2 18.2 %collective-permute-start.50 = (bf16[4,144,1152]{2,1,0:T(8,128)(2,1)}, bf16[4,144,1152]{2,1,0:T(8,128)(2,1)}, u32[]{:S(2)}, u32[]{:S(2)}) collective-permute-start(bf16[4,144,1152]{2,1,0:T(8,128)(2,1)} %fusion.3), channel_id=1, source_target_pairs={{0,8},{4,20},{8,0},{12,28},{16,24},{20,4},{24,16},{28,12},{1,9},{5... | collective-permute-start | bytes 3981320 | tf_op jit(solution)/shard_map/ppermute | solution.py:649
  497.9 7.5 %collective-permute-start.43 = (f32[2,8,2,144]{3,0,2,1:T(2,128)S(1)}, f32[2,8,2,144]{3,0,2,1:T(2,128)S(1)}, u32[]{:S(2)}, u32[]{:S(2)}) collective-permute-start(f32[2,8,2,144]{3,0,2,1:T(2,128)S(1)} %broadcast_select_fusion.1), channel_id=1, source_target_pairs={{0,2},{1,3},{2,0},{3,1},{4,6},{5,7},{6,4},{7,5},{8,10},{9,11},{10,... | collective-permute-start | bytes 55304 | tf_op jit(solution)/shard_map/ppermute | solution.py:704
  508.8 31.1 %collective-permute-start.44 = (f32[1,8,2,144]{3,0,2,1:T(1,128)S(1)}, f32[1,8,2,144]{3,0,2,1:T(1,128)S(1)}, u32[]{:S(2)}, u32[]{:S(2)}) collective-permute-start(f32[1,8,2,144]{3,0,2,1:T(1,128)S(1)} %broadcast_select_fusion.2), channel_id=1, source_target_pairs={{0,1},{1,0},{2,3},{3,2},{4,5},{5,4},{6,7},{7,6},{8,9},{9,8},{10,11... | collective-permute-start | bytes 27656 | tf_op jit(solution)/shard_map/ppermute | solution.py:704
  538.9 10.5 %collective-permute-start.52 = (f32[2,56,128]{2,1,0:T(8,128)S(1)}, f32[2,56,128]{2,1,0:T(8,128)S(1)}, u32[]{:S(2)}, u32[]{:S(2)}) collective-permute-start(f32[2,56,128]{2,1,0:T(8,128)S(1)} %bitcast.160), channel_id=1, source_target_pairs={{0,2},{1,3},{2,0},{3,1},{4,6},{5,7},{6,4},{7,5},{8,10},{9,11},{10,... | collective-permute-start | bytes 172040 | tf_op jit(solution)/shard_map/ppermute | solution.py:704
  540.0 9.5 %collective-permute-start.45 = (f32[1,8,2,144]{3,0,2,1:T(1,128)S(1)}, f32[1,8,2,144]{3,0,2,1:T(1,128)S(1)}, u32[]{:S(2)}, u32[]{:S(2)}) collective-permute-start(f32[1,8,2,144]{3,0,2,1:T(1,128)S(1)} %fusion.50), channel_id=1, source_target_pairs={{0,4},{4,0},{8,12},{12,8},{16,20},{20,16},{24,28},{28,24},{1,5},{5... | collective-permute-start | bytes 27656 | tf_op jit(solution)/shard_map/ppermute | solution.py:704
  549.4 4.0 collective-permute-start.53
  549.5 4.8 collective-permute-start.46
  553.4 2.4 collective-permute-start.54
  554.4 6.0 %collective-permute-start.47 = (f32[4,8,2,144]{3,0,2,1:T(4,128)S(1)}, f32[4,8,2,144]{3,0,2,1:T(4,128)S(1)}, u32[]{:S(2)}, u32[]{:S(2)}) collective-permute-start(f32[4,8,2,144]{3,0,2,1:T(4,128)S(1)} %maximum_select_fusion.3), channel_id=1, source_target_pairs={{0,16},{4,20},{8,24},{12,28},{16,0},{20,4},{24,8},{28,12},{1,17},{... | collective-permute-start | bytes 110600 | tf_op jit(solution)/shard_map/ppermute | solution.py:704
  555.9 3.9 collective-permute-start.55
  559.8 3.9 collective-permute-start.56
  (59 other events, 772.3 us)
Sparse Core Ops, SparseCore 0:
  20.5 34.4 all-gather.6
  56.5 31.4 all-gather.8
  90.2 32.6 all-gather.10
  346.3 30.4 reduce-scatter.7
  471.7 48.6 reduce-scatter.5
  522.5 31.8 reduce-scatter.3

commit v4 on v3

--- a/solution.py
+++ b/solution.py
@@ -113,7 +113,7 @@
         out_specs=pl.BlockSpec((group, tokens, tokens), lambda f: (f, 0, 0)),
         out_shape=jax.ShapeDtypeStruct((heads, tokens, tokens), jnp.float32),
         compiler_params=params(),
-        cost_estimate=SHORT,
+        cost_estimate=pl.CostEstimate(flops=1 << 34, transcendentals=0, bytes_accessed=1 << 22),
         name="position_bias",
     )(index, table.astype(jnp.float32).reshape(heads, 1, padded))
 
@@ -130,7 +130,7 @@
     sub = lax.broadcasted_iota(jnp.int32, (8, tokens), 0)
     lane_of = lax.broadcasted_iota(jnp.int32, (LANES, tokens), 0)
 
-    def one_row(row, total):
+    def row_terms(row):
         index = index_ref[pl.ds(row, 1), :]
         low = jnp.broadcast_to(index & (LANES - 1), (LANES, tokens))
         high = jnp.broadcast_to(index >> 7, (8, tokens))
@@ -143,13 +143,16 @@
             axis=0,
         ).astype(jnp.bfloat16)
         right = jnp.where(lane_of == low, 1.0, 0.0).astype(jnp.bfloat16)
+        return left, right
+
+    def some_rows(step, total):
+        terms = [row_terms(step * 4 + k) for k in range(4)]
+        left = jnp.concatenate([t[0] for t in terms], axis=1)
+        right = jnp.concatenate([t[1] for t in terms], axis=1)
         return total + times_transposed(left, right)
 
-    def two_rows(step, total):
-        return one_row(step * 2 + 1, one_row(step * 2, total))
-
     out_ref[...] += lax.fori_loop(
-        0, rows // 2, two_rows, jnp.zeros((heads * 8, LANES), jnp.float32)
+        0, rows // 4, some_rows, jnp.zeros((heads * 8, LANES), jnp.float32)
     )
 
 
@@ -658,19 +661,19 @@
 
 
 class Gather:
-    def __init__(self, shard, behind=None, ready=None):
-        if behind is not None:
-            shard = after(shard, behind.own)
-        own = lax.all_gather(shard, "fsdp", axis=0, tiled=False)
+    def __init__(self, shard, queue=None, behind=None, ready=None, between=None):
+        if queue is not None:
+            shard = after(shard, queue.group)
+        self.group = own = lax.all_gather(shard, "fsdp", axis=0, tiled=False)
         if behind is not None:
             own = after(own, behind.first)
         if ready is not None:
             own = after(own, ready)
-        self.own = own
         self.first = swap(own, 1)
-        second = swap(own, 2)
-        third = swap(self.first, 2)
-        near = [own, self.first, second, third]
+        self.second = swap(own, 2)
+        third = self.first if between is None else after(self.first, between)
+        self.third = swap(third, 2)
+        near = [own, self.first, self.second, self.third]
         self.pieces = near + [swap_core(piece) for piece in near]
 
 
@@ -679,8 +682,8 @@
         self.own = own
         self.came = swap_core(send)
 
-    def near(self):
-        self.zero, self.one, pair = add_halves(self.own, self.came)
+    def near(self, *gates):
+        self.zero, self.one, pair = add_halves(after(self.own, *gates), self.came)
         self.far = swap(pair, 2)
         return pair
 
@@ -690,8 +693,9 @@
         self.last = swap(one, 1)
         return one
 
-    def total(self):
-        total = self.zero.astype(jnp.float32) + self.far[1].astype(jnp.float32)
+    def total(self, *gates):
+        zero = after(self.zero, *gates)
+        total = zero.astype(jnp.float32) + self.far[1].astype(jnp.float32)
         self.sum = (total + self.last.astype(jnp.float32)).astype(jnp.bfloat16)
         return self.sum
 
@@ -820,8 +824,12 @@
             bias_table.reshape(-1),
         ]
     )
-    small = jnp.pad(small, (0, -small.shape[0] % 1024))
-    small_all = small_gather(small.reshape(1, -1, LANES), "fsdp").reshape(groups, -1)
+    small = jnp.pad(small, (0, -small.shape[0] % 1024)).reshape(-1, LANES)
+    time_low = (time_vector.astype(wide) + sinusoid(timesteps, width)).astype(low)
+    both = jnp.concatenate([small, time_low.reshape(-1, LANES)], axis=0)
+    both = small_gather(both[None], "fsdp")
+    small_all = both[:, : small.shape[0]].reshape(groups, -1)
+    time_all = small_gather(both[:, small.shape[0] :].reshape(groups * count, width), "dp")
 
     def vector_of(slot):
         return small_all[:, slot * shard_cols : (slot + 1) * shard_cols].reshape(-1).astype(wide)
@@ -834,8 +842,6 @@
     table = jnp.pad(table, ((0, 0), (0, 8 * LANES - table_rows)))
     bias = position_bias(offset_index, table)
 
-    time_low = (time_vector.astype(wide) + sinusoid(timesteps, width)).astype(low)
-    time_all = small_gather(small_gather(time_low, "fsdp"), "dp")
     all_images = time_all.shape[0]
     time_cols = lax.dynamic_slice(
         time_all, (0, own_part * shard_rows), (all_images, shard_rows)
@@ -861,9 +867,9 @@
     cube = is_cube()
     if cube:
         part_of, slot_of = part_tables()
-        attn_move = Gather(wire_attn)
-        up_move = Gather(up_weight, behind=attn_move)
-        down_move = Gather(wire_down, behind=up_move)
+        attn_move = Gather(wire_attn, ready=time_own, between=bias)
+        up_move = Gather(up_weight, queue=attn_move, behind=attn_move)
+        down_move = Gather(wire_down, queue=attn_move, behind=up_move)
         attn_pieces, up_pieces = attn_move.pieces, up_move.pieces
         down_full = unpack_pieces(part_of, down_move.pieces, fold)
     else:
@@ -878,6 +884,8 @@
     qkv, probs, mixed_split, proj_full, attn_full = attend(
         part_of, attn_pieces, normed_low, time_add, bias, count, tokens
     )
+    if cube:
+        mixed_split = after(mixed_split, down_move.first)
     mixed = mixed_split.transpose(1, 0, 2).reshape(rows, width)
     hidden = x_rows + (matmul(mixed, proj_full) + proj_b)
     second, unit_two, inv_two = normalize(hidden, gain_two, shift_two)
@@ -885,24 +893,33 @@
     grad_low = cotangent.reshape(rows, width)
     grad_rows = grad_low.astype(wide)
     wire = (groups, parts, shard_rows, width)
-    if cube:
-        second_low = after(second_low, down_move.first)
     activ, slope, up_full = up_forward(part_of, up_pieces, second_low, up_b)
     grad_cols = grad_low
     if cube:
-        own, send = down_slot_grad(slot_of, activ, grad_low, parts, shard_rows)
+        own, send = down_slot_grad(
+            slot_of,
+            after(activ, down_move.third, *down_move.pieces[4:7]),
+            grad_low,
+            parts,
+            shard_rows,
+        )
         down_move = Scatter(own, send)
-        grad_cols = after(grad_low, down_move.near())
+        grad_cols = after(grad_low, down_move.near(down_full))
     d_pre, d_second, layer_out = down_back(
         grad_cols, hidden + down_b, activ, slope, up_full, down_full
     )
     layer_out = layer_out.reshape(count, tokens, width)
     if cube:
         own, send = slot_grad(
-            one_grad_kernel, slot_of, [second_low.T], d_pre, parts, "up_grad"
+            one_grad_kernel,
+            slot_of,
+            [after(second_low.T, down_move.back())],
+            d_pre,
+            parts,
+            "up_grad",
         )
         up_move = Scatter(own, send)
-        d_second = after(d_second, send)
+        d_second = after(d_second, send, down_move.total())
     else:
         grad_down = jnp.concatenate([contract_rows(a, grad_low) for a in activ], axis=0)
         down_sum = scatter_sum(pack_down(grad_down.astype(low), groups, parts, shard_rows))
@@ -915,17 +932,19 @@
     d_mixed_split = d_mixed.reshape(rows, groups, shard_cols).transpose(1, 0, 2)
     d_hidden_split = d_hidden_low.reshape(rows, groups, shard_cols).transpose(1, 0, 2)
     if cube:
-        d_mixed_split = after(d_mixed_split, down_move.back(), up_move.near())
+        d_mixed_split = after(d_mixed_split, up_move.near())
     d_packed, pairs = attend_back(d_mixed_split, qkv, probs, d_hidden_split)
     attn_back = attn_full
     if cube:
-        normed_t = after(normed_low.T, down_move.total())
+        normed_t = normed_low.T
         own, send = slot_grad(
             pair_grad_kernel, slot_of, [normed_t, mixed.T], d_packed, parts, "pair_grad"
         )
-        attn_move = Scatter(own, send)
-        attn_back = after(attn_full, send, up_move.back())
-        pairs = after(pairs, attn_move.near(), up_move.total())
+        down_sum = down_move.end()
+        attn_move = Scatter(own, after(send, up_move.back(), down_sum))
+        attn_pair = attn_move.near()
+        attn_back = after(attn_full, attn_pair)
+        pairs = after(pairs, attn_pair, up_move.total(attn_pair))
     else:
         cut = 3 * shard_cols
         grad_attn = jnp.stack(
@@ -954,11 +973,7 @@
     tvalue_grad = time_grads[:, shard_cols:]
     back = times_transposed(d_time_cols, time_weight)
     back = back.reshape(parts, groups, count, shard_rows).transpose(1, 0, 2, 3)
-    back = small_gather(small_scatter(back, "fsdp"), "dp")
-    back = lax.dynamic_slice(
-        back, (0, own_part, 0, 0), (parts, 1, count, shard_rows)
-    ).reshape(parts, count, shard_rows)
-    time_grad = back.transpose(1, 0, 2).reshape(count, width)
+    back = back.reshape(groups, -1, LANES)
 
     lane = lax.broadcasted_iota(jnp.int32, (1, width), 1)
     d_normed = jnp.zeros((rows, width), wide)
@@ -984,8 +999,19 @@
         table_sum.reshape(groups, group_heads * table_rows),
     ]
     flat = jnp.concatenate(vectors, axis=1)
-    flat = jnp.pad(flat, ((0, 0), (0, -flat.shape[1] % 1024)))
-    own = small_sum(small_scatter(flat.reshape(groups, -1, LANES), "fsdp"), "dp").reshape(-1)
+    flat = jnp.pad(flat, ((0, 0), (0, -flat.shape[1] % 1024))).reshape(groups, -1, LANES)
+    lines = flat.shape[1]
+    own = small_scatter(jnp.concatenate([flat, back], axis=1), "fsdp")[0]
+    slots = jnp.where(
+        lax.broadcasted_iota(jnp.int32, (parts, 1, 1), 0) == own_part, own[None, lines:], 0.0
+    )
+    own = small_sum(
+        jnp.concatenate([own[:lines], slots.reshape(-1, LANES)], axis=0), "dp"
+    )
+    back = own[lines:].reshape(parts, parts, count, shard_rows)
+    back = lax.dynamic_slice(back, (0, own_part, 0, 0), (parts, 1, count, shard_rows))
+    time_grad = back.reshape(parts, count, shard_rows).transpose(1, 0, 2).reshape(count, width)
+    own = own[:lines].reshape(-1)
     proj_bg, gain1_g, shift1_g, gain2_g, shift2_g, down_bg = (
         own[i * shard_cols : (i + 1) * shard_cols] for i in range(6)
     )
@@ -995,10 +1021,10 @@
     table_grad = own[at : at + group_heads * table_rows].reshape(group_heads, table_rows)
 
     if cube:
-        down_sum = down_move.end()
         attn_move.back()
-        up_sum = up_move.end()
-        attn_move.total()
+        attn_total = attn_move.total()
+        down_sum = after(down_sum, attn_total)
+        up_sum = after(up_move.end(), attn_total)
         attn_sum = attn_move.end()
     attn_sum = attn_sum.astype(wide)
     query_grad, key_grad, value_grad, proj_grad = (

time: 583 us -> 575 us (0.986)
  starting transfers between devices: 52.8 us -> 34.1 us
  local copies, waits for them, and re-layouts: 70.4 us -> 84.9 us
  Pallas kernels: 205 us -> 195 us
    ppermute x15, waiting for transfers between devices: 108 us -> 67.1 us  [swap(): lax.ppermute(value, 'dp', [(i, i ^ NEAR[i & 1][hop]) for i in range(8)])]
    ppermute x15, waiting for transfers between devices: 0.04 us -> 22 us  [swap_core(): return lax.ppermute(value, 'dp', [(i, i ^ 1) for i in range(8)])]
    ppermute x27 -> x20, starting transfers between devices: 33.9 us -> 17.9 us  [swap_bit(): return lax.ppermute(value, axis, [(i, i ^ 1 << bit) for i in range(size)])]
    ppermute x27 -> x20, waiting for transfers between devices: 34.2 us -> 48.2 us  [swap_bit(): return lax.ppermute(value, axis, [(i, i ^ 1 << bit) for i in range(size)])]
    pallas_call x1, Pallas kernels: 27.4 us -> 17.9 us  [table_gradient(): pl.pallas_call(table_kernel, grid=(tokens // block,), in_specs=[pl.BlockS...]
    reduce_scatter x3, waiting for transfers between devices: 0.01 us -> 5.9 us  [end(): return lax.psum_scatter(self.sum, 'fsdp', scatter_dimension=0, tiled=False)]
    unnamed x131 -> x96, local copies, waits for them, and re-layouts: 13.7 us -> 11.8 us
  transfers between devices with their start and end apart: 63 -> 56, of which waited for: 22 -> 26; matrix products, arithmetic and copies ran while one was open for 27% -> 29% of each run, Pallas kernels for 30% -> 28%
where the time goes in v4:
time: 575 us; the launch traced here: 569 us
  Pallas kernels  195 us (34%)
  waiting for transfers between devices  149 us (26%)
  local copies, waits for them, and re-layouts  84.9 us (15%)
  other arithmetic  63.3 us (11%)
  starting transfers between devices  34.1 us (6%)
  matrix products  28.6 us (5%)
  between operations  15.3 us (3%)
    ppermute x15, waiting for transfers between devices, swap(): lax.ppermute(value, 'dp', [(i, i ^ NEAR[i & 1][hop]) for i in range(8)])  67.1 us
    ppermute x20, waiting for transfers between devices, swap_bit(): return lax.ppermute(value, axis, [(i, i ^ 1 << bit) for i in range(size)])  48.2 us
    pallas_call x2, Pallas kernels, piece_call(): pl.pallas_call(kernel, grid_spec=pltpu.PrefetchScalarGridSpec(num_scalar_...  35.9 us
    pallas_call x1, Pallas kernels, down_back(): pl.pallas_call(down_back_kernel, grid=(groups,), in_specs=[whole, whole,...  29.6 us
    pallas_call x2, Pallas kernels, slot_grad(): pl.pallas_call(kernel, grid_spec=pltpu.PrefetchScalarGridSpec(num_scalar_...  26 us
    dot_general x6, matrix products, times_transposed(): lax.dot_general(left, right, (((1,), (1,)), ((), ())), preferred_element_...  22.5 us
    ppermute x15, waiting for transfers between devices, swap_core(): return lax.ppermute(value, 'dp', [(i, i ^ 1) for i in range(8)])  22 us
    pallas_call x3, Pallas kernels, add_halves(): pl.pallas_call(add_kernel, grid=(groups,), in_specs=[pl.BlockSpec((1, 1,...  20.3 us
  transfers between devices with their start and end apart: 56, of which 26 were waited for; matrix products, arithmetic and copies ran while one was open for 29% of the time, Pallas kernels for 28%

profile of v4, /device:TPU:0, one launch (start us, length us, event | category | flops | bytes accessed | tf_op | source)
XLA Modules:
  0.0 569.4 jit_solution(11512337067085335168)
XLA Ops:
  7.2 2.0 concatenate.128
  11.8 4.9 concatenate.109
  16.7 3.1 collective-permute-start
  21.6 3.1 collective-permute-start.1
  24.7 4.4 collective-permute-done.1
  32.3 2.2 collective-permute-done.3
  34.5 1.9 collective-permute-start.4
  36.4 2.5 collective-permute-done.4
  40.3 1.9 collective-permute-start.5
  42.2 5.5 all-gather.7.cloned.1.call-done
  49.3 2.5 collective-permute-done.6
  54.6 2.9 collective-permute-done.8
  58.6 6.3 %collective-permute-done.9 = f32[2,8,576]{2,1,0:T(8,128)S(1)} collective-permute-done((f32[2,8,576]{2,1,0:T(8,128)S(1)}, f32[2,8,576]{2,1,0:T(8,128)S(1)}, u32[]{:S(2)}, u32[]{:S(2)}) %collective-permute-start.9) | collective-permute-done | bytes 36896 | tf_op jit(solution)/shard_map/ppermute | solution.py:708
  67.3 20.2 %position_bias.1.bias_ref = f32[16,256,256]{2,1,0:T(8,128)} custom-call(s32[256,256]{1,0:T(8,128)} %index_ref.3, f32[16,1,1024]{2,1,0:T(1,128)} %reshape.351.table_ref), custom_call_target="tpu_custom_call" | custom-call | flops 17179869184 | bytes 4194304 | tf_op jit(solution)/shard_map/position_bias/pallas_call | solution.py:106
  90.9 28.5 %collective-permute-done.11.refs_2_ = bf16[4,144,1152]{2,1,0:T(8,128)(2,1)} collective-permute-done((bf16[4,144,1152]{2,1,0:T(8,128)(2,1)S(1)}, bf16[4,144,1152]{2,1,0:T(8,128)(2,1)}, u32[]{:S(2)}, u32[]{:S(2)}) %collective-permute-start.11) | collective-permute-done | bytes 1327136 | tf_op jit(solution)/shard_map/ppermute | solution.py:652
  119.4 14.4 %collective-permute-done.12.refs_3_ = bf16[4,144,1152]{2,1,0:T(8,128)(2,1)} collective-permute-done((bf16[4,144,1152]{2,1,0:T(8,128)(2,1)}, bf16[4,144,1152]{2,1,0:T(8,128)(2,1)}, u32[]{:S(2)}, u32[]{:S(2)}) %collective-permute-start.12) | collective-permute-done | bytes 1327136 | tf_op jit(solution)/shard_map/ppermute | solution.py:652
  152.0 13.9 %collective-permute-done.19.refs_2_ = bf16[4,144,1152]{2,1,0:T(8,128)(2,1)} collective-permute-done((bf16[4,144,1152]{2,1,0:T(8,128)(2,1)}, bf16[4,144,1152]{2,1,0:T(8,128)(2,1)}, u32[]{:S(2)}, u32[]{:S(2)}) %collective-permute-start.19) | collective-permute-done | bytes 1327136 | tf_op jit(solution)/shard_map/ppermute | solution.py:652
  170.6 21.0 %attend.1 = (bf16[4,512,896]{2,1,0:T(8,128)(2,1)}, bf16[4,2,4,256,256]{4,3,2,1,0:T(8,128)(2,1)}, bf16[4,512,288]{2,1,0:T(8,128)(2,1)}, bf16[1152,1152]{1,0:T(8,128)(2,1)}, bf16[4,1152,1152]{2,1,0:T(8,128)(2,1)}) custom-call(s32[8]{0:T(128)} %fusion.52.part_ref, bf16[512,1152]{1,0:T(8,128)(2,1)} %copy.134.normed_ref, ...), custom_call_target="tpu_custom_call" | custom-call | flops 1 | bytes 1 | tf_op jit(solution)/shard_map/attend/pallas_call | solution.py:210
  193.3 4.7 fusion.70
  204.2 3.1 collective-permute-done.24.refs_7_
  207.3 14.9 %up_forward.1 = (bf16[4,512,1152]{2,1,0:T(8,128)(2,1)}, bf16[4,512,1152]{2,1,0:T(8,128)(2,1)}, bf16[4,1152,1152]{2,1,0:T(8,128)(2,1)}) custom-call(s32[8]{0:T(128)} %fusion.52.part_ref, bf16[512,1152]{1,0:T(8,128)(2,1)} %copy.141.second_ref, f32[4,1,1152]{2,1,0:T(1,128)} %reshape.356.bias_ref, bf16[4,144,1152]{2,1,0:T(8,128)(2,1)} %bitcast.151, ...), custom_call_target="tpu_custom_call" | custom-call | flops 1 | bytes 1 | tf_op jit(solution)/shard_map/up_forward/pallas_call | solution.py:210
  222.2 18.4 %down_grad.1 = (bf16[4,4,144,1152]{3,2,1,0:T(8,128)(2,1)}, bf16[4,4,144,1152]{3,2,1,0:T(8,128)(2,1)}) custom-call(s32[8]{0:T(128)} %fusion.51.slot_ref, bf16[4,512,1152]{2,1,0:T(8,128)(2,1)} %get-tuple-element.77.left_ref.activ_ref, bf16[512,1152]{1,0:T(8,128)(2,1)} %bitcast.138), custom_call_target="tpu_custom_call" | custom-call | flops 1 | bytes 1 | tf_op jit(solution)/shard_map/down_grad/pallas_call | solution.py:544
  241.1 10.4 %collective-permute-done.30.refs_7_ = bf16[4,144,1152]{2,1,0:T(8,128)(2,1)S(1)} collective-permute-done((bf16[4,144,1152]{2,1,0:T(8,128)(2,1)}, bf16[4,144,1152]{2,1,0:T(8,128)(2,1)S(1)}, u32[]{:S(2)}, u32[]{:S(2)}) %collective-permute-start.30) | collective-permute-done | bytes 1327136 | tf_op jit(solution)/shard_map/ppermute | solution.py:656
  252.5 9.0 %unpack_pieces.1.down_ref = bf16[4608,1152]{1,0:T(8,128)(2,1)} custom-call(s32[8]{0:T(128)} %fusion.52.part_ref, bf16[4,144,1152]{2,1,0:T(8,128)(2,1)} %bitcast.8.refs_0_, bf16[4,144,1152]{2,1,0:T(8,128)(2,1)} %collective-permute-done.18.refs_1_, bf16[4,144,1152]{2,1,0:T(8,128)(2,1)} %collective-permute-done.28.refs_2_, ...), custom_call_target="tpu_custom_call" | custom-call | flops 1 | bytes 1 | tf_op jit(solution)/shard_map/unpack_pieces/pallas_call | solution.py:611
  261.5 6.7 %add_halves.3 = (bf16[4,144,1152]{2,1,0:T(8,128)(2,1)}, bf16[4,144,1152]{2,1,0:T(8,128)(2,1)}, bf16[2,4,144,1152]{3,2,1,0:T(8,128)(2,1)}) custom-call(bf16[4,4,144,1152]{3,2,1,0:T(8,128)(2,1)} %get-tuple-element.79.one_ref.two_ref.three_ref.four_ref, bf16[4,4,144,1152]{3,2,1,0:T(8,128)(2,1)} %get-tuple-element.79.one_ref.two_ref.three_ref.four_ref, ...), custom_call_target="tpu_custom_call" | custom-call | flops 1 | bytes 1 | tf_op jit(solution)/shard_map/add_halves/pallas_call | solution.py:575
  271.1 3.1 copy.144.hidden_ref
  275.6 29.6 %down_back.1 = (bf16[4,512,1152]{2,1,0:T(8,128)(2,1)}, f32[512,1152]{1,0:T(8,128)}, bf16[512,1152]{1,0:T(8,128)(2,1)}) custom-call(bf16[512,1152]{1,0:T(8,128)(2,1)} %copy.143.grad_ref, f32[512,1152]{1,0:T(8,128)} %copy.144.hidden_ref, bf16[4,512,1152]{2,1,0:T(8,128)(2,1)} %get-tuple-element.77.left_ref.activ_ref, ...), custom_call_target="tpu_custom_call" | custom-call | flops 1 | bytes 1 | tf_op jit(solution)/shard_map/down_back/pallas_call | solution.py:370
  306.9 12.2 %up_grad.1 = (bf16[4,4,144,1152]{3,2,1,0:T(8,128)(2,1)}, bf16[4,4,144,1152]{3,2,1,0:T(8,128)(2,1)}) custom-call(s32[8]{0:T(128)} %fusion.51.slot_ref, bf16[1152,512]{1,0:T(8,128)(2,1)} %bitcast.137, bf16[4,512,1152]{2,1,0:T(8,128)(2,1)} %get-tuple-element.89.right_ref), custom_call_target="tpu_custom_call" | custom-call | flops 1 | bytes 1 | tf_op jit(solution)/shard_map/up_grad/pallas_call | solution.py:504
  319.7 8.5 %collective-permute-done.34.came_ref = bf16[4,4,144,1152]{3,2,1,0:T(8,128)(2,1)} collective-permute-done((bf16[4,4,144,1152]{3,2,1,0:T(8,128)(2,1)}, bf16[4,4,144,1152]{3,2,1,0:T(8,128)(2,1)}, u32[]{:S(2)}, u32[]{:S(2)}) %collective-permute-start.34) | collective-permute-done | bytes 5308448 | tf_op jit(solution)/shard_map/ppermute | solution.py:656
  328.2 6.7 %add_halves.4 = (bf16[4,144,1152]{2,1,0:T(8,128)(2,1)}, bf16[4,144,1152]{2,1,0:T(8,128)(2,1)}, bf16[2,4,144,1152]{3,2,1,0:T(8,128)(2,1)}) custom-call(bf16[4,4,144,1152]{3,2,1,0:T(8,128)(2,1)} %get-tuple-element.93.one_ref.two_ref.three_ref.four_ref, bf16[4,4,144,1152]{3,2,1,0:T(8,128)(2,1)} %get-tuple-element.93.one_ref.two_ref.three_ref.four_ref, ...), custom_call_target="tpu_custom_call" | custom-call | flops 1 | bytes 1 | tf_op jit(solution)/shard_map/add_halves/pallas_call | solution.py:575
  337.0 3.3 fusion.8
  340.4 3.1 fusion.80.one_ref
  343.5 3.3 copy.145
  346.8 3.3 multiply_reduce_fusion
  352.7 2.9 convolution_convert_fusion
  355.6 2.4 copy.146
  358.0 2.6 copy.147
  360.6 2.5 copy.148
  363.1 17.3 %attend_back.1 = (bf16[4,512,1152]{2,1,0:T(8,128)(2,1)}, f32[16,256,256]{2,1,0:T(8,128)}) custom-call(bf16[4,512,288]{2,1,0:T(8,128)(2,1)} %bitcast.140, bf16[4,512,896]{2,1,0:T(8,128)(2,1)} %get-tuple-element.96.qkv_ref, bf16[4,2,4,256,256]{4,3,2,1,0:T(8,128)(2,1)} %get-tuple-element.97.probs_ref, bf16[4,512,288]{2,1,0:T(8,128)(2,1)} %bitcast.141), custom_call_target="tpu_custom_call" | custom-call | flops 1 | bytes 1 | tf_op jit(solution)/shard_map/attend_back/pallas_call | solution.py:434
  380.4 13.8 %pair_grad.1 = (bf16[4,4,144,1152]{3,2,1,0:T(8,128)(2,1)}, bf16[4,4,144,1152]{3,2,1,0:T(8,128)(2,1)}) custom-call(s32[8]{0:T(128)} %fusion.51.slot_ref, bf16[1152,512]{1,0:T(8,128)(2,1)} %fusion.80.one_ref, bf16[1152,512]{1,0:T(8,128)(2,1)} %bitcast.143, bf16[4,512,1152]{2,1,0:T(8,128)(2,1)} %get-tuple-element.110.right_ref), custom_call_target="tpu_custom_call" | custom-call | flops 1 | bytes 1 | tf_op jit(solution)/shard_map/pair_grad/pallas_call | solution.py:504
  394.2 2.7 fusion.6
  397.7 2.1 convert_reduce_fusion.1
  403.7 3.6 convert_reduce_fusion
  407.3 2.4 reduce_sum.156
  413.8 7.0 %add_halves.5 = (bf16[4,144,1152]{2,1,0:T(8,128)(2,1)}, bf16[4,144,1152]{2,1,0:T(8,128)(2,1)}, bf16[2,4,144,1152]{3,2,1,0:T(8,128)(2,1)}) custom-call(bf16[4,4,144,1152]{3,2,1,0:T(8,128)(2,1)} %get-tuple-element.100.one_ref.two_ref.three_ref.four_ref, bf16[4,4,144,1152]{3,2,1,0:T(8,128)(2,1)} %get-tuple-element.100.one_ref.two_ref.three_ref.four_ref, ...), custom_call_target="tpu_custom_call" | custom-call | flops 1 | bytes 1 | tf_op jit(solution)/shard_map/add_halves/pallas_call | solution.py:575
  422.1 3.3 fusion.5
  425.5 3.0 bitcast_reduce_fusion
  430.7 4.0 fusion.13
  434.8 4.0 convolution_add_fusion.2
  440.2 3.5 convolution_add_fusion.1
  445.8 6.3 %multiply_reduce_fusion.1 = (f32[1152]{0:T(1024)}, f32[512]{0:T(512)}, f32[512]{0:T(512)}, f32[1152]{0:T(1024)}, f32[512,1152]{0,1:T(8,128)}) fusion(f32[512,1152]{0,1:T(8,128)S(1)} %copy-done.1, f32[512]{0:T(512)S(1)} %bitcast.167, f32[512]{0:T(512)S(1)} %bitcast.171, f32[1152]{0:T(1024)S(1)} %reshape.348, f32[512,1152]{0,1:T(8,128)S(1)} %convolution_add_fusion.1, ...), kind=kOutput, calls=%fused_computation.34 | convolution fusion | flops 1365439232 | bytes 10939392 | tf_op jit(solution)/shard_map/dot_general | solution.py:37
  452.1 17.9 %table_gradient.1 = f32[128,128]{1,0:T(8,128)} custom-call(s32[256,256]{1,0:T(8,128)} %index_ref.3, f32[16,256,256]{2,1,0:T(8,128)} %get-tuple-element.109.pairs_ref), custom_call_target="tpu_custom_call" | custom-call | flops 1 | bytes 1 | tf_op jit(solution)/shard_map/table_gradient/pallas_call | solution.py:162
  479.5 3.6 collective-permute-done.41
  484.0 4.6 collective-permute-done.42
  499.8 4.7 collective-permute-done.43
  505.4 3.1 fusion.1
  510.0 2.9 collective-permute-done.44
  518.8 7.8 %collective-permute-done.49 = bf16[4,144,1152]{2,1,0:T(8,128)(2,1)} collective-permute-done((bf16[4,144,1152]{2,1,0:T(8,128)(2,1)}, bf16[4,144,1152]{2,1,0:T(8,128)(2,1)}, u32[]{:S(2)}, u32[]{:S(2)}) %collective-permute-start.49) | collective-permute-done | bytes 1327136 | tf_op jit(solution)/shard_map/ppermute | solution.py:652
  526.6 3.7 fusion.3
  530.3 4.7 add_convert_fusion
  535.1 2.4 copy.166
  539.3 3.8 collective-permute-done.46
  544.5 3.4 collective-permute-done.47
  554.3 5.9 %reduce-scatter.6.cloned.1.call-done = bf16[1,144,1152]{2,1,0:T(8,128)(2,1)} async-done(((bf16[4,144,1152]{2,1,0:T(8,128)(2,1)}), bf16[1,144,1152]{2,1,0:T(8,128)(2,1)}) %reduce-scatter.6.cloned.1.call-update) | async-done | bytes 331792 | tf_op jit(solution)/shard_map/reduce_scatter | solution.py:703
  (313 shorter events, 120.9 us)
Async XLA Ops:
  7.2 44.8 %copy-start.14 = (bf16[576,288]{0,1:T(8,128)(2,1)S(1)}, bf16[576,288]{0,1:T(8,128)(2,1)}, u32[]{:S(2)}) copy-start(bf16[576,288]{0,1:T(8,128)(2,1)} %param.39) | copy-start | bytes 995332
  7.2 40.5 %all-gather.7.cloned.1.call-start = ((), (), s32[]{:S(2)}) async-start(), calls=%async_computation.6 | async-start | bytes 1658880 | tf_op jit(solution)/shard_map/all_gather | solution.py:667
  9.3 80.2 %all-gather.11.cloned.1.call-start = ((), (), s32[]{:S(2)}) async-start(), calls=%async_computation.8 | async-start | bytes 1658880 | tf_op jit(solution)/shard_map/all_gather | solution.py:667
  16.7 4.9 collective-permute-start
  21.6 7.5 %collective-permute-start.1 = (bf16[2,74,128]{2,1,0:T(8,128)(2,1)S(1)}, bf16[2,74,128]{2,1,0:T(8,128)(2,1)S(1)}, u32[]{:S(2)}, u32[]{:S(2)}) collective-permute-start(bf16[2,74,128]{2,1,0:T(8,128)(2,1)S(1)} %maximum_select_fusion.4), channel_id=1, source_target_pairs={{0,2},{1,3},{2,0},{3,1},{4,6},{5,7},{6,4},{7,5},{8,10},{9,11},{10,... | collective-permute-start | bytes 113672 | tf_op jit(solution)/shard_map/ppermute | solution.py:708
  29.2 1.3 collective-permute-start.2
  30.5 4.0 collective-permute-start.3
  34.5 4.4 collective-permute-start.4
  40.3 7.4 %collective-permute-start.5 = (f32[32,576]{1,0:T(8,128)S(1)}, f32[32,576]{1,0:T(8,128)S(1)}, u32[]{:S(2)}, u32[]{:S(2)}) collective-permute-start(f32[32,576]{1,0:T(8,128)S(1)} %slice_select_fusion.1), channel_id=1, source_target_pairs={{0,16},{4,20},{8,24},{12,28},{16,0},{20,4},{24,8},{28,12},{1,17},{... | collective-permute-start | bytes 221192 | tf_op jit(solution)/shard_map/ppermute | solution.py:708
  47.7 17.9 %copy-start.12 = (bf16[576,1152]{1,0:T(8,128)(2,1)S(1)}, bf16[576,1152]{1,0:T(8,128)(2,1)}, u32[]{:S(2)}) copy-start(bf16[576,1152]{1,0:T(8,128)(2,1)} %all-gather.7.cloned.1.call-done) | copy-start | bytes 3981316
  47.7 86.8 %all-gather.9.cloned.1.call-start = ((), (), s32[]{:S(2)}) async-start(), calls=%async_computation.7 | async-start | bytes 1658880 | tf_op jit(solution)/shard_map/all_gather | solution.py:667
  47.8 4.1 collective-permute-start.6
  51.9 1.8 collective-permute-start.7
  53.7 3.8 collective-permute-start.8
  57.5 7.4 %collective-permute-start.9 = (f32[2,8,576]{2,1,0:T(8,128)S(1)}, f32[2,8,576]{2,1,0:T(8,128)S(1)}, u32[]{:S(2)}, u32[]{:S(2)}) collective-permute-start(f32[2,8,576]{2,1,0:T(8,128)S(1)} %maximum_select_fusion.5), channel_id=1, source_target_pairs={{0,2},{1,3},{2,0},{3,1},{4,6},{5,7},{6,4},{7,5},{8,10},{9,11},{10,... | collective-permute-start | bytes 110600 | tf_op jit(solution)/shard_map/ppermute | solution.py:708
  65.6 23.4 %collective-permute-start.10 = (bf16[4,144,1152]{2,1,0:T(8,128)(2,1)S(1)}, bf16[4,144,1152]{2,1,0:T(8,128)(2,1)}, u32[]{:S(2)}, u32[]{:S(2)}) collective-permute-start(bf16[4,144,1152]{2,1,0:T(8,128)(2,1)S(1)} %bitcast.153), channel_id=1, source_target_pairs={{0,8},{4,20},{8,0},{12,28},{16,24},{20,4},{24,16},{28,12},{1,9},{5... | collective-permute-start | bytes 3981320 | tf_op jit(solution)/shard_map/ppermute | solution.py:652
  67.0 23.1 %copy-start.3 = (bf16[2,256,1152]{2,1,0:T(8,128)(2,1)S(1)}, bf16[2,256,1152]{2,1,0:T(8,128)(2,1)}, u32[]{:S(2)}) copy-start(bf16[2,256,1152]{2,1,0:T(8,128)(2,1)} %param.23) | copy-start | bytes 3538948
  67.1 329.9 %reduce-scatter.4.cloned.1.call-start = ((), (), s32[]{:S(2)}) async-start(), calls=%async_computation.3 | async-start | bytes 1658880 | tf_op jit(solution)/shard_map/reduce_scatter | solution.py:703
  87.5 31.9 %collective-permute-start.11 = (bf16[4,144,1152]{2,1,0:T(8,128)(2,1)S(1)}, bf16[4,144,1152]{2,1,0:T(8,128)(2,1)}, u32[]{:S(2)}, u32[]{:S(2)}) collective-permute-start(bf16[4,144,1152]{2,1,0:T(8,128)(2,1)S(1)} %bitcast.154), channel_id=1, source_target_pairs={{0,16},{4,12},{8,24},{12,4},{16,0},{20,28},{24,8},{28,20},{1,17},{... | collective-permute-start | bytes 3981320 | tf_op jit(solution)/shard_map/ppermute | solution.py:652
  89.0 44.9 %collective-permute-start.12 = (bf16[4,144,1152]{2,1,0:T(8,128)(2,1)}, bf16[4,144,1152]{2,1,0:T(8,128)(2,1)}, u32[]{:S(2)}, u32[]{:S(2)}) collective-permute-start(bf16[4,144,1152]{2,1,0:T(8,128)(2,1)} %collective-permute-done.10.refs_1_), channel_id=1, source_target_pairs={{0,16},{4,12},{8,24},{12,4},{16,0},{20,28},{24,8},{28,20},{1,17},{... | collective-permute-start | bytes 3981320 | tf_op jit(solution)/shard_map/ppermute | solution.py:652
  89.5 45.0 %collective-permute-start.17 = (bf16[4,144,1152]{2,1,0:T(8,128)(2,1)}, bf16[4,144,1152]{2,1,0:T(8,128)(2,1)}, u32[]{:S(2)}, u32[]{:S(2)}) collective-permute-start(bf16[4,144,1152]{2,1,0:T(8,128)(2,1)} %bitcast.148), channel_id=1, source_target_pairs={{0,8},{4,20},{8,0},{12,28},{16,24},{20,4},{24,16},{28,12},{1,9},{5... | collective-permute-start | bytes 3981320 | tf_op jit(solution)/shard_map/ppermute | solution.py:652
  90.1 44.4 %collective-permute-start.13 = (bf16[4,144,1152]{2,1,0:T(8,128)(2,1)S(1)}, bf16[4,144,1152]{2,1,0:T(8,128)(2,1)}, u32[]{:S(2)}, u32[]{:S(2)}) collective-permute-start(bf16[4,144,1152]{2,1,0:T(8,128)(2,1)S(1)} %bitcast.155), channel_id=1, source_target_pairs={{0,4},{4,0},{8,12},{12,8},{16,20},{20,16},{24,28},{28,24},{1,5},{5... | collective-permute-start | bytes 3981320 | tf_op jit(solution)/shard_map/ppermute | solution.py:656
  90.3 60.8 %collective-permute-start.14 = (bf16[4,144,1152]{2,1,0:T(8,128)(2,1)}, bf16[4,144,1152]{2,1,0:T(8,128)(2,1)}, u32[]{:S(2)}, u32[]{:S(2)}) collective-permute-start(bf16[4,144,1152]{2,1,0:T(8,128)(2,1)} %collective-permute-done.10.refs_1_), channel_id=1, source_target_pairs={{0,4},{4,0},{8,12},{12,8},{16,20},{20,16},{24,28},{28,24},{1,5},{5... | collective-permute-start | bytes 3981320 | tf_op jit(solution)/shard_map/ppermute | solution.py:656
  119.4 31.9 %collective-permute-start.15 = (bf16[4,144,1152]{2,1,0:T(8,128)(2,1)}, bf16[4,144,1152]{2,1,0:T(8,128)(2,1)}, u32[]{:S(2)}, u32[]{:S(2)}) collective-permute-start(bf16[4,144,1152]{2,1,0:T(8,128)(2,1)} %collective-permute-done.11.refs_2_), channel_id=1, source_target_pairs={{0,4},{4,0},{8,12},{12,8},{16,20},{20,16},{24,28},{28,24},{1,5},{5... | collective-permute-start | bytes 3981320 | tf_op jit(solution)/shard_map/ppermute | solution.py:656
  133.8 32.1 %collective-permute-start.19 = (bf16[4,144,1152]{2,1,0:T(8,128)(2,1)}, bf16[4,144,1152]{2,1,0:T(8,128)(2,1)}, u32[]{:S(2)}, u32[]{:S(2)}) collective-permute-start(bf16[4,144,1152]{2,1,0:T(8,128)(2,1)} %bitcast.149), channel_id=1, source_target_pairs={{0,16},{4,12},{8,24},{12,4},{16,0},{20,28},{24,8},{28,20},{1,17},{... | collective-permute-start | bytes 3981320 | tf_op jit(solution)/shard_map/ppermute | solution.py:652
  134.5 31.4 %collective-permute-start.16 = (bf16[4,144,1152]{2,1,0:T(8,128)(2,1)}, bf16[4,144,1152]{2,1,0:T(8,128)(2,1)}, u32[]{:S(2)}, u32[]{:S(2)}) collective-permute-start(bf16[4,144,1152]{2,1,0:T(8,128)(2,1)} %collective-permute-done.12.refs_3_), channel_id=1, source_target_pairs={{0,4},{4,0},{8,12},{12,8},{16,20},{20,16},{24,28},{28,24},{1,5},{5... | collective-permute-start | bytes 3981320 | tf_op jit(solution)/shard_map/ppermute | solution.py:656
  134.5 32.4 %collective-permute-start.18 = (bf16[4,144,1152]{2,1,0:T(8,128)(2,1)}, bf16[4,144,1152]{2,1,0:T(8,128)(2,1)}, u32[]{:S(2)}, u32[]{:S(2)}) collective-permute-start(bf16[4,144,1152]{2,1,0:T(8,128)(2,1)} %bitcast.8.refs_0_), channel_id=1, source_target_pairs={{0,8},{4,20},{8,0},{12,28},{16,24},{20,4},{24,16},{28,12},{1,9},{5... | collective-permute-start | bytes 3981320 | tf_op jit(solution)/shard_map/ppermute | solution.py:652
  151.1 46.8 %collective-permute-start.21 = (bf16[4,144,1152]{2,1,0:T(8,128)(2,1)}, bf16[4,144,1152]{2,1,0:T(8,128)(2,1)}, u32[]{:S(2)}, u32[]{:S(2)}) collective-permute-start(bf16[4,144,1152]{2,1,0:T(8,128)(2,1)} %bitcast.150), channel_id=1, source_target_pairs={{0,4},{4,0},{8,12},{12,8},{16,20},{20,16},{24,28},{28,24},{1,5},{5... | collective-permute-start | bytes 3981320 | tf_op jit(solution)/shard_map/ppermute | solution.py:656
  151.3 47.3 %collective-permute-start.28 = (bf16[4,144,1152]{2,1,0:T(8,128)(2,1)}, bf16[4,144,1152]{2,1,0:T(8,128)(2,1)}, u32[]{:S(2)}, u32[]{:S(2)}) collective-permute-start(bf16[4,144,1152]{2,1,0:T(8,128)(2,1)} %bitcast.8.refs_0_), channel_id=1, source_target_pairs={{0,16},{4,12},{8,24},{12,4},{16,0},{20,28},{24,8},{28,20},{1,17},{... | collective-permute-start | bytes 3981320 | tf_op jit(solution)/shard_map/ppermute | solution.py:652
  165.9 34.0 %collective-permute-start.20 = (bf16[4,144,1152]{2,1,0:T(8,128)(2,1)}, bf16[4,144,1152]{2,1,0:T(8,128)(2,1)}, u32[]{:S(2)}, u32[]{:S(2)}) collective-permute-start(bf16[4,144,1152]{2,1,0:T(8,128)(2,1)} %collective-permute-done.17.refs_1_), channel_id=1, source_target_pairs={{0,16},{4,12},{8,24},{12,4},{16,0},{20,28},{24,8},{28,20},{1,17},{... | collective-permute-start | bytes 3981320 | tf_op jit(solution)/shard_map/ppermute | solution.py:652
  166.0 34.0 %collective-permute-start.22 = (bf16[4,144,1152]{2,1,0:T(8,128)(2,1)}, bf16[4,144,1152]{2,1,0:T(8,128)(2,1)}, u32[]{:S(2)}, u32[]{:S(2)}) collective-permute-start(bf16[4,144,1152]{2,1,0:T(8,128)(2,1)} %collective-permute-done.17.refs_1_), channel_id=1, source_target_pairs={{0,4},{4,0},{8,12},{12,8},{16,20},{20,16},{24,28},{28,24},{1,5},{5... | collective-permute-start | bytes 3981320 | tf_op jit(solution)/shard_map/ppermute | solution.py:656
  166.9 33.5 %collective-permute-start.23 = (bf16[4,144,1152]{2,1,0:T(8,128)(2,1)}, bf16[4,144,1152]{2,1,0:T(8,128)(2,1)}, u32[]{:S(2)}, u32[]{:S(2)}) collective-permute-start(bf16[4,144,1152]{2,1,0:T(8,128)(2,1)} %collective-permute-done.19.refs_2_), channel_id=1, source_target_pairs={{0,4},{4,0},{8,12},{12,8},{16,20},{20,16},{24,28},{28,24},{1,5},{5... | collective-permute-start | bytes 3981320 | tf_op jit(solution)/shard_map/ppermute | solution.py:656
  198.0 24.2 %collective-permute-start.26 = (bf16[4,144,1152]{2,1,0:T(8,128)(2,1)}, bf16[4,144,1152]{2,1,0:T(8,128)(2,1)}, u32[]{:S(2)}, u32[]{:S(2)}) collective-permute-start(bf16[4,144,1152]{2,1,0:T(8,128)(2,1)} %bitcast.8.refs_0_), channel_id=1, source_target_pairs={{0,4},{4,0},{8,12},{12,8},{16,20},{20,16},{24,28},{28,24},{1,5},{5... | collective-permute-start | bytes 3981320 | tf_op jit(solution)/shard_map/ppermute | solution.py:656
  198.6 23.6 %collective-permute-start.25 = (bf16[4,144,1152]{2,1,0:T(8,128)(2,1)}, bf16[4,144,1152]{2,1,0:T(8,128)(2,1)}, u32[]{:S(2)}, u32[]{:S(2)}) collective-permute-start(bf16[4,144,1152]{2,1,0:T(8,128)(2,1)} %collective-permute-done.18.refs_1_), channel_id=1, source_target_pairs={{0,16},{4,12},{8,24},{12,4},{16,0},{20,28},{24,8},{28,20},{1,17},{... | collective-permute-start | bytes 3981320 | tf_op jit(solution)/shard_map/ppermute | solution.py:652
  199.9 22.3 %collective-permute-start.27 = (bf16[4,144,1152]{2,1,0:T(8,128)(2,1)}, bf16[4,144,1152]{2,1,0:T(8,128)(2,1)}, u32[]{:S(2)}, u32[]{:S(2)}) collective-permute-start(bf16[4,144,1152]{2,1,0:T(8,128)(2,1)} %collective-permute-done.18.refs_1_), channel_id=1, source_target_pairs={{0,4},{4,0},{8,12},{12,8},{16,20},{20,16},{24,28},{28,24},{1,5},{5... | collective-permute-start | bytes 3981320 | tf_op jit(solution)/shard_map/ppermute | solution.py:656
  200.0 22.2 %collective-permute-start.29 = (bf16[4,144,1152]{2,1,0:T(8,128)(2,1)}, bf16[4,144,1152]{2,1,0:T(8,128)(2,1)}, u32[]{:S(2)}, u32[]{:S(2)}) collective-permute-start(bf16[4,144,1152]{2,1,0:T(8,128)(2,1)} %collective-permute-done.28.refs_2_), channel_id=1, source_target_pairs={{0,4},{4,0},{8,12},{12,8},{16,20},{20,16},{24,28},{28,24},{1,5},{5... | collective-permute-start | bytes 3981320 | tf_op jit(solution)/shard_map/ppermute | solution.py:656
  200.4 6.9 %collective-permute-start.24 = (bf16[4,144,1152]{2,1,0:T(8,128)(2,1)}, bf16[4,144,1152]{2,1,0:T(8,128)(2,1)}, u32[]{:S(2)}, u32[]{:S(2)}) collective-permute-start(bf16[4,144,1152]{2,1,0:T(8,128)(2,1)} %collective-permute-done.20.refs_3_), channel_id=1, source_target_pairs={{0,4},{4,0},{8,12},{12,8},{16,20},{20,16},{24,28},{28,24},{1,5},{5... | collective-permute-start | bytes 3981320 | tf_op jit(solution)/shard_map/ppermute | solution.py:656
  202.7 19.4 %copy-start.4 = (bf16[512,1152]{0,1:T(8,128)(2,1)}, bf16[512,1152]{0,1:T(8,128)(2,1)S(1)}, u32[]{:S(2)}) copy-start(bf16[512,1152]{0,1:T(8,128)(2,1)S(1)} %get-tuple-element.220) | copy-start | bytes 3538948
  240.6 20.9 %collective-permute-start.31 = (bf16[4,4,144,1152]{3,2,1,0:T(8,128)(2,1)}, bf16[4,4,144,1152]{3,2,1,0:T(8,128)(2,1)}, u32[]{:S(2)}, u32[]{:S(2)}) collective-permute-start(bf16[4,4,144,1152]{3,2,1,0:T(8,128)(2,1)} %get-tuple-element.80), channel_id=1, source_target_pairs={{0,4},{4,0},{8,12},{12,8},{16,20},{20,16},{24,28},{28,24},{1,5},{5... | collective-permute-start | bytes 15925256 | tf_op jit(solution)/shard_map/ppermute | solution.py:656
  241.0 10.5 %collective-permute-start.30 = (bf16[4,144,1152]{2,1,0:T(8,128)(2,1)}, bf16[4,144,1152]{2,1,0:T(8,128)(2,1)S(1)}, u32[]{:S(2)}, u32[]{:S(2)}) collective-permute-start(bf16[4,144,1152]{2,1,0:T(8,128)(2,1)} %collective-permute-done.25.refs_3_), channel_id=1, source_target_pairs={{0,4},{4,0},{8,12},{12,8},{16,20},{20,16},{24,28},{28,24},{1,5},{5... | collective-permute-start | bytes 3981320 | tf_op jit(solution)/shard_map/ppermute | solution.py:656
  268.2 37.1 %collective-permute-start.32 = (bf16[2,4,144,1152]{3,2,1,0:T(8,128)(2,1)}, bf16[2,4,144,1152]{3,2,1,0:T(8,128)(2,1)}, u32[]{:S(2)}, u32[]{:S(2)}) collective-permute-start(bf16[2,4,144,1152]{3,2,1,0:T(8,128)(2,1)} %get-tuple-element.81), channel_id=1, source_target_pairs={{0,16},{4,12},{8,24},{12,4},{16,0},{20,28},{24,8},{28,20},{1,17},{... | collective-permute-start | bytes 7962632 | tf_op jit(solution)/shard_map/ppermute | solution.py:652
  275.6 29.6 %copy-start.11 = (bf16[4,144,1152]{2,1,0:T(8,128)(2,1)S(1)}, bf16[4,144,1152]{2,1,0:T(8,128)(2,1)}, u32[]{:S(2)}) copy-start(bf16[4,144,1152]{2,1,0:T(8,128)(2,1)} %get-tuple-element.87) | copy-start | bytes 3981316
  319.1 9.1 %collective-permute-start.34 = (bf16[4,4,144,1152]{3,2,1,0:T(8,128)(2,1)}, bf16[4,4,144,1152]{3,2,1,0:T(8,128)(2,1)}, u32[]{:S(2)}, u32[]{:S(2)}) collective-permute-start(bf16[4,4,144,1152]{3,2,1,0:T(8,128)(2,1)} %get-tuple-element.90), channel_id=1, source_target_pairs={{0,4},{4,0},{8,12},{12,8},{16,20},{20,16},{24,28},{28,24},{1,5},{5... | collective-permute-start | bytes 15925256 | tf_op jit(solution)/shard_map/ppermute | solution.py:656
  319.1 17.9 %collective-permute-start.33 = (bf16[4,144,1152]{2,1,0:T(8,128)(2,1)S(1)}, bf16[4,144,1152]{2,1,0:T(8,128)(2,1)}, u32[]{:S(2)}, u32[]{:S(2)}) collective-permute-start(bf16[4,144,1152]{2,1,0:T(8,128)(2,1)S(1)} %fusion.9), channel_id=1, source_target_pairs={{0,8},{4,20},{8,0},{12,28},{16,24},{20,4},{24,16},{28,12},{1,9},{5... | collective-permute-start | bytes 3981320 | tf_op jit(solution)/shard_map/ppermute | solution.py:652
  319.7 17.3 %copy-start.10 = (bf16[4,144,1152]{2,1,0:T(8,128)(2,1)S(1)}, bf16[4,144,1152]{2,1,0:T(8,128)(2,1)}, u32[]{:S(2)}) copy-start(bf16[4,144,1152]{2,1,0:T(8,128)(2,1)} %get-tuple-element.91) | copy-start | bytes 3981316
  334.8 59.4 %collective-permute-start.35 = (bf16[2,4,144,1152]{3,2,1,0:T(8,128)(2,1)}, bf16[2,4,144,1152]{3,2,1,0:T(8,128)(2,1)}, u32[]{:S(2)}, u32[]{:S(2)}) collective-permute-start(bf16[2,4,144,1152]{3,2,1,0:T(8,128)(2,1)} %get-tuple-element.94), channel_id=1, source_target_pairs={{0,16},{4,12},{8,24},{12,4},{16,0},{20,28},{24,8},{28,20},{1,17},{... | collective-permute-start | bytes 7962632 | tf_op jit(solution)/shard_map/ppermute | solution.py:652
  340.3 212.1 %reduce-scatter.8.cloned.1.call-start = ((), (), s32[]{:S(2)}) async-start(), calls=%async_computation.5 | async-start | bytes 1658880 | tf_op jit(solution)/shard_map/reduce_scatter | solution.py:703
  380.4 13.8 %copy-start.9 = (bf16[4,144,1152]{2,1,0:T(8,128)(2,1)S(1)}, bf16[4,144,1152]{2,1,0:T(8,128)(2,1)}, u32[]{:S(2)}) copy-start(bf16[4,144,1152]{2,1,0:T(8,128)(2,1)} %get-tuple-element.102) | copy-start | bytes 3981316
  397.0 16.8 %collective-permute-start.36 = (bf16[4,4,144,1152]{3,2,1,0:T(8,128)(2,1)}, bf16[4,4,144,1152]{3,2,1,0:T(8,128)(2,1)}, u32[]{:S(2)}, u32[]{:S(2)}) collective-permute-start(bf16[4,4,144,1152]{3,2,1,0:T(8,128)(2,1)} %get-tuple-element.103), channel_id=1, source_target_pairs={{0,4},{4,0},{8,12},{12,8},{16,20},{20,16},{24,28},{28,24},{1,5},{5... | collective-permute-start | bytes 15925256 | tf_op jit(solution)/shard_map/ppermute | solution.py:656
  397.0 25.2 %collective-permute-start.37 = (bf16[4,144,1152]{2,1,0:T(8,128)(2,1)}, bf16[4,144,1152]{2,1,0:T(8,128)(2,1)}, u32[]{:S(2)}, u32[]{:S(2)}) collective-permute-start(bf16[4,144,1152]{2,1,0:T(8,128)(2,1)} %fusion.6), channel_id=1, source_target_pairs={{0,8},{4,20},{8,0},{12,28},{16,24},{20,4},{24,16},{28,12},{1,9},{5... | collective-permute-start | bytes 3981320 | tf_op jit(solution)/shard_map/ppermute | solution.py:652
  420.8 84.6 %collective-permute-start.48 = (bf16[2,4,144,1152]{3,2,1,0:T(8,128)(2,1)}, bf16[2,4,144,1152]{3,2,1,0:T(8,128)(2,1)}, u32[]{:S(2)}, u32[]{:S(2)}) collective-permute-start(bf16[2,4,144,1152]{3,2,1,0:T(8,128)(2,1)} %get-tuple-element.104), channel_id=1, source_target_pairs={{0,16},{4,12},{8,24},{12,4},{16,0},{20,28},{24,8},{28,20},{1,17},{... | collective-permute-start | bytes 7962632 | tf_op jit(solution)/shard_map/ppermute | solution.py:652
  425.5 134.7 %reduce-scatter.6.cloned.1.call-start = ((), (), s32[]{:S(2)}) async-start(), calls=%async_computation.4 | async-start | bytes 1658880 | tf_op jit(solution)/shard_map/reduce_scatter | solution.py:703
  430.7 8.0 %collective-permute-start.38 = (bf16[2,2304]{1,0:T(2,128)(2,1)}, bf16[2,2304]{1,0:T(2,128)(2,1)S(1)}, u32[]{:S(2)}, u32[]{:S(2)}) collective-permute-start(bf16[2,2304]{1,0:T(2,128)(2,1)} %reshape.339), channel_id=1, source_target_pairs={{0,1},{1,0},{2,3},{3,2},{4,5},{5,4},{6,7},{7,6},{8,9},{9,8},{10,11... | collective-permute-start | bytes 27656 | tf_op jit(solution)/shard_map/ppermute | solution.py:708
  438.8 6.3 %collective-permute-start.39 = (bf16[4,2304]{1,0:T(4,128)(2,1)S(1)}, bf16[4,2304]{1,0:T(4,128)(2,1)S(1)}, u32[]{:S(2)}, u32[]{:S(2)}) collective-permute-start(bf16[4,2304]{1,0:T(4,128)(2,1)S(1)} %maximum_select_fusion.8), channel_id=1, source_target_pairs={{0,2},{1,3},{2,0},{3,1},{4,6},{5,7},{6,4},{7,5},{8,10},{9,11},{10,... | collective-permute-start | bytes 55304 | tf_op jit(solution)/shard_map/ppermute | solution.py:708
  445.8 31.7 %collective-permute-start.40 = (bf16[8,2304]{1,0:T(8,128)(2,1)}, bf16[8,2304]{1,0:T(8,128)(2,1)}, u32[]{:S(2)}, u32[]{:S(2)}) collective-permute-start(bf16[8,2304]{1,0:T(8,128)(2,1)} %maximum_select_fusion.7), channel_id=1, source_target_pairs={{0,4},{4,0},{8,12},{12,8},{16,20},{20,16},{24,28},{28,24},{1,5},{5... | collective-permute-start | bytes 110600 | tf_op jit(solution)/shard_map/ppermute | solution.py:708
  478.4 4.7 collective-permute-start.41
  483.1 5.4 collective-permute-start.42
  498.2 6.3 %collective-permute-start.43 = (f32[2,74,128]{2,1,0:T(8,128)S(1)}, f32[2,74,128]{2,1,0:T(8,128)S(1)}, u32[]{:S(2)}, u32[]{:S(2)}) collective-permute-start(f32[2,74,128]{2,1,0:T(8,128)S(1)} %slice_select_fusion), channel_id=1, source_target_pairs={{0,2},{1,3},{2,0},{3,1},{4,6},{5,7},{6,4},{7,5},{8,10},{9,11},{10,... | collective-permute-start | bytes 227336 | tf_op jit(solution)/shard_map/ppermute | solution.py:708
  508.5 18.1 %collective-permute-start.49 = (bf16[4,144,1152]{2,1,0:T(8,128)(2,1)}, bf16[4,144,1152]{2,1,0:T(8,128)(2,1)}, u32[]{:S(2)}, u32[]{:S(2)}) collective-permute-start(bf16[4,144,1152]{2,1,0:T(8,128)(2,1)} %fusion.1), channel_id=1, source_target_pairs={{0,8},{4,20},{8,0},{12,28},{16,24},{20,4},{24,16},{28,12},{1,9},{5... | collective-permute-start | bytes 3981320 | tf_op jit(solution)/shard_map/ppermute | solution.py:652
  508.9 4.0 collective-permute-start.44
  518.8 18.8 %collective-permute-start.45 = (f32[200,128]{1,0:T(8,128)}, f32[200,128]{1,0:T(8,128)}, u32[]{:S(2)}, u32[]{:S(2)}) collective-permute-start(f32[200,128]{1,0:T(8,128)} %pad_maximum_fusion.2), channel_id=1, source_target_pairs={{0,4},{4,0},{8,12},{12,8},{16,20},{20,16},{24,28},{28,24},{1,5},{5... | collective-permute-start | bytes 307208 | tf_op jit(solution)/shard_map/ppermute | solution.py:708
  535.1 16.0 %copy-start.7 = (bf16[1,144,1152]{2,1,0:T(8,128)(2,1)S(1)}, bf16[1,144,1152]{2,1,0:T(8,128)(2,1)}, u32[]{:S(2)}) copy-start(bf16[1,144,1152]{2,1,0:T(8,128)(2,1)} %reduce-scatter.4.cloned.1.call-done) | copy-start | bytes 995332
  538.4 4.7 collective-permute-start.46
  543.2 4.7 collective-permute-start.47
  (34 other events, 138.1 us)
Sparse Core Ops, SparseCore 0:
  10.2 37.4 all-gather.6
  49.2 33.5 all-gather.10
  85.0 31.5 all-gather.8
  340.4 29.0 reduce-scatter.3
  425.6 29.6 reduce-scatter.7
  530.4 29.7 reduce-scatter.5

commit v5 on v4

--- a/solution.py
+++ b/solution.py
@@ -11,7 +11,12 @@
 LANES = 128
 BOTH = ("dp", "fsdp")
 VMEM_LIMIT = 58 * 1024 * 1024
-SHORT = pl.CostEstimate(flops=1, transcendentals=0, bytes_accessed=1)
+
+
+def lasting(microseconds):
+    return pl.CostEstimate(
+        flops=int(microseconds * 1e9), transcendentals=0, bytes_accessed=1
+    )
 
 
 def sinusoid(steps, model_width):
@@ -113,7 +118,7 @@
         out_specs=pl.BlockSpec((group, tokens, tokens), lambda f: (f, 0, 0)),
         out_shape=jax.ShapeDtypeStruct((heads, tokens, tokens), jnp.float32),
         compiler_params=params(),
-        cost_estimate=pl.CostEstimate(flops=1 << 34, transcendentals=0, bytes_accessed=1 << 22),
+        cost_estimate=lasting(20),
         name="position_bias",
     )(index, table.astype(jnp.float32).reshape(heads, 1, padded))
 
@@ -169,13 +174,26 @@
         out_specs=pl.BlockSpec((heads * 8, LANES), lambda i: (0, 0)),
         out_shape=jax.ShapeDtypeStruct((heads * 8, LANES), jnp.float32),
         compiler_params=params(),
-        cost_estimate=SHORT,
+        cost_estimate=lasting(18),
         name="table_gradient",
     )(index, pairs)
 
 
-def load_group(part_ref, pieces, held, in_sems, full_ref, out_sems):
+def piece_list(refs):
+    out = []
+    for ref in refs:
+        out.extend([ref] if len(ref.shape) == 3 else [ref.at[k] for k in range(ref.shape[0])])
+    return out
+
+
+def piece_shape(refs):
+    count = sum(1 if len(ref.shape) == 3 else ref.shape[0] for ref in refs)
+    return (count, *refs[0].shape)
+
+
+def load_group(part_ref, refs, held, in_sems, full_ref, out_sems):
     step = pl.program_id(0)
+    pieces = piece_list(refs)
     rows = pieces[0].shape[1]
 
     def copy(group, j):
@@ -203,8 +221,8 @@
 
 
 def piece_call(kernel, name, part_of, pieces, inputs, in_specs, out_specs, out_shapes):
-    groups, rows, packed = pieces[0].shape
-    depth = rows * len(pieces)
+    parts, groups, rows, packed = piece_shape(pieces)
+    depth = rows * parts
     full = jax.ShapeDtypeStruct((groups, depth, packed), pieces[0].dtype)
     anywhere = pl.BlockSpec(memory_space=pl.ANY)
     return pl.pallas_call(
@@ -216,13 +234,13 @@
             out_specs=out_specs + [anywhere],
             scratch_shapes=[
                 pltpu.VMEM((groups, depth, packed), pieces[0].dtype),
-                pltpu.SemaphoreType.DMA((groups, len(pieces))),
+                pltpu.SemaphoreType.DMA((groups, parts)),
                 pltpu.SemaphoreType.DMA((groups,)),
             ],
         ),
         out_shape=out_shapes + [full],
         compiler_params=params(),
-        cost_estimate=SHORT,
+        cost_estimate=lasting(13),
         name=name,
     )(part_of, *inputs, *pieces)
 
@@ -268,8 +286,8 @@
 
 
 def attend(part_of, pieces, normed, add, bias, images, tokens):
-    groups, part_rows, packed = pieces[0].shape
-    depth = part_rows * len(pieces)
+    parts, groups, part_rows, packed = piece_shape(pieces)
+    depth = part_rows * parts
     heads = bias.shape[0] // groups
     width = packed // groups
     kept = add.shape[2]
@@ -317,7 +335,7 @@
 
 
 def up_forward(part_of, pieces, second, bias):
-    groups, part_rows, packed = pieces[0].shape
+    _, groups, _, packed = piece_shape(pieces)
     rows, depth = second.shape
     wide = pl.BlockSpec((1, rows, packed), lambda f, p: (f, 0, 0))
     shape = jax.ShapeDtypeStruct((groups, rows, packed), jnp.bfloat16)
@@ -336,71 +354,128 @@
     )
 
 
+def column_sum(value):
+    return jnp.sum(value, axis=0, keepdims=True)
+
+
 def down_back_kernel(
-    grad_ref, hidden_ref, activ_ref, slope_ref, up_ref, down_ref, pre_ref, second_ref, out_ref, total
+    grad_ref,
+    hidden_ref,
+    row_ref,
+    activ_ref,
+    slope_ref,
+    up_ref,
+    down_ref,
+    pre_ref,
+    out_ref,
+    d_hidden_ref,
+    d_low_ref,
+    sum_ref,
+    up_sum_ref,
+    total,
+    second,
 ):
     step = pl.program_id(0)
     weight = down_ref[...]
     d_activ = times_transposed(grad_ref[...], weight)
     d_pre = (d_activ * slope_ref[0].astype(jnp.float32)).astype(jnp.bfloat16)
     pre_ref[0] = d_pre
+    up_sum_ref[0] = column_sum(d_pre.astype(jnp.float32))
     part = times_transposed(d_pre, up_ref[0])
     more = matmul(activ_ref[0], weight)
 
     @pl.when(step == 0)
     def _():
-        second_ref[...] = part
-        total[...] = hidden_ref[...] + more
+        second[...] = part
+        total[...] = more
 
     @pl.when(step > 0)
     def _():
-        second_ref[...] += part
+        second[...] += part
         total[...] += more
 
     @pl.when(step == pl.num_programs(0) - 1)
     def _():
-        out_ref[...] = total[...].astype(jnp.bfloat16)
-
-
-def down_back(grad, hidden, activ, slope, up_full, down_full):
+        block = 64
+        gain, shift = row_ref[0:1, :], row_ref[1:2, :]
+        sum_ref[...] = jnp.zeros_like(sum_ref)
+
+        def some_rows(at, carry):
+            rows = pl.ds(pl.multiple_of(at * block, block), block)
+            hidden = hidden_ref[rows, :]
+            out_ref[rows, :] = (hidden + shift + total[rows, :]).astype(jnp.bfloat16)
+            _, unit, inv = normalize(hidden, gain, 0.0)
+            d_second = second[rows, :]
+            grad = grad_ref[rows, :].astype(jnp.float32)
+            d_hidden = grad + norm_back(d_second, unit, inv, gain)
+            d_low = d_hidden.astype(jnp.bfloat16)
+            d_hidden_ref[rows, :] = d_hidden
+            d_low_ref[rows, :] = d_low
+            sum_ref[0:1, :] += column_sum(d_low.astype(jnp.float32))
+            sum_ref[1:2, :] += column_sum(d_second * unit)
+            sum_ref[2:3, :] += column_sum(d_second)
+            sum_ref[3:4, :] += column_sum(grad)
+            return carry
+
+        lax.fori_loop(0, hidden_ref.shape[0] // block, some_rows, 0)
+
+
+def down_back(grad, hidden, lines, activ, slope, up_full, down_full):
     groups, rows, packed = activ.shape
     depth = up_full.shape[1]
     whole = pl.BlockSpec((rows, depth), lambda f: (0, 0))
     mine = pl.BlockSpec((1, rows, packed), lambda f: (f, 0, 0))
+    few = pl.BlockSpec((8, depth), lambda f: (0, 0))
     return pl.pallas_call(
         down_back_kernel,
         grid=(groups,),
         in_specs=[
             whole,
             whole,
+            few,
             mine,
             mine,
             pl.BlockSpec((1, depth, packed), lambda f: (f, 0, 0)),
             pl.BlockSpec((packed, depth), lambda f: (f, 0)),
         ],
-        out_specs=[mine, whole, whole],
+        out_specs=[
+            mine,
+            whole,
+            whole,
+            whole,
+            few,
+            pl.BlockSpec((1, 1, packed), lambda f: (f, 0, 0)),
+        ],
         out_shape=[
             jax.ShapeDtypeStruct((groups, rows, packed), jnp.bfloat16),
+            jax.ShapeDtypeStruct((rows, depth), jnp.bfloat16),
             jax.ShapeDtypeStruct((rows, depth), jnp.float32),
             jax.ShapeDtypeStruct((rows, depth), jnp.bfloat16),
-        ],
-        scratch_shapes=[pltpu.VMEM((rows, depth), jnp.float32)],
+            jax.ShapeDtypeStruct((8, depth), jnp.float32),
+            jax.ShapeDtypeStruct((groups, 1, packed), jnp.float32),
+        ],
+        scratch_shapes=[
+            pltpu.VMEM((rows, depth), jnp.float32),
+            pltpu.VMEM((rows, depth), jnp.float32),
+        ],
         compiler_params=params(),
-        cost_estimate=SHORT,
+        cost_estimate=lasting(33),
         name="down_back",
-    )(grad, hidden, activ, slope, up_full, down_full)
-
-
-def attend_back_kernel(grad_ref, qkv_ref, probs_ref, hidden_ref, out_ref, pairs_ref):
+    )(grad, hidden, lines, activ, slope, up_full, down_full)
+
+
+def attend_back_kernel(
+    hidden_ref, proj_ref, qkv_ref, probs_ref, out_ref, pairs_ref, time_ref
+):
     images, heads = probs_ref.shape[1], probs_ref.shape[2]
     tokens = probs_ref.shape[3]
-    width = grad_ref.shape[2]
+    width = proj_ref.shape[0]
     size = width // heads
     scale = 1.0 / math.sqrt(size)
     for image in range(images):
         rows = slice(image * tokens, (image + 1) * tokens)
         both = qkv_ref[0, rows, :]
-        grads = grad_ref[0, rows, :]
+        grads = times_transposed(hidden_ref[rows, :], proj_ref[...]).astype(jnp.bfloat16)
         d_query, d_keys, d_values = [], [], []
         for head in range(heads):
             at = head * size
@@ -421,37 +496,108 @@
                 pairs_ref[head] += d_low.astype(jnp.float32)
             d_query.append(matmul(d_low, keys) * scale)
             d_keys.append(contract_rows(d_low, query) * scale)
-        out_ref[0, rows, :] = jnp.concatenate(
-            d_query + d_keys + d_values + [hidden_ref[0, rows, :].astype(jnp.float32)], axis=1
-        ).astype(jnp.bfloat16)
-
-
-def attend_back(grad, qkv, probs, hidden):
-    groups, rows, width = grad.shape
+        packed = jnp.concatenate(d_query + d_keys + d_values, axis=1).astype(jnp.bfloat16)
+        out_ref[0, rows, : 3 * width] = packed
+        time_ref[0, image : image + 1, :] = column_sum(packed.astype(jnp.float32))
+    for group in range(hidden_ref.shape[1] // width):
+
+        @pl.when(pl.program_id(0) == group)
+        def _(group=group):
+            out_ref[0, :, 3 * width :] = hidden_ref[:, group * width : (group + 1) * width]
+
+
+def attend_back(hidden, proj, qkv, probs):
+    rows, packed = hidden.shape
+    groups, images, heads, tokens, _ = probs.shape
     kept = qkv.shape[2]
-    _, images, heads, tokens, _ = probs.shape
-    packed = 4 * width
+    width = packed // groups
     return pl.pallas_call(
         attend_back_kernel,
         grid=(groups,),
         in_specs=[
-            pl.BlockSpec((1, rows, width), lambda f: (f, 0, 0)),
+            pl.BlockSpec((rows, packed), lambda f: (0, 0)),
+            pl.BlockSpec((width, packed), lambda f: (f, 0)),
             pl.BlockSpec((1, rows, kept), lambda f: (f, 0, 0)),
             pl.BlockSpec((1, images, heads, tokens, tokens), lambda f: (f, 0, 0, 0, 0)),
-            pl.BlockSpec((1, rows, width), lambda f: (f, 0, 0)),
         ],
         out_specs=[
             pl.BlockSpec((1, rows, packed), lambda f: (f, 0, 0)),
             pl.BlockSpec((heads, tokens, tokens), lambda f: (f, 0, 0)),
+            pl.BlockSpec((1, images, 3 * width), lambda f: (f, 0, 0)),
         ],
         out_shape=[
             jax.ShapeDtypeStruct((groups, rows, packed), jnp.bfloat16),
             jax.ShapeDtypeStruct((groups * heads, tokens, tokens), jnp.float32),
+            jax.ShapeDtypeStruct((groups, images, 3 * width), jnp.float32),
         ],
         compiler_params=params(),
-        cost_estimate=SHORT,
+        cost_estimate=lasting(19),
         name="attend_back",
-    )(grad, qkv, probs, hidden)
+    )(hidden, proj, qkv, probs)
+
+
+def input_grad_kernel(
+    right_ref, weight_ref, image_ref, d_hidden_ref, row_ref, out_ref, sum_ref, total
+):
+    step = pl.program_id(0)
+    cut = 3 * (right_ref.shape[2] // 4)
+    kept = -(-cut // LANES) * LANES
+    lane = lax.broadcasted_iota(jnp.int32, (1, kept), 1)
+    right = right_ref[0, :, :kept]
+    right = jnp.where(lane < cut, right.astype(jnp.float32), 0.0).astype(jnp.bfloat16)
+    part = times_transposed(right, weight_ref[0, :, :kept])
+
+    @pl.when(step == 0)
+    def _():
+        total[...] = part
+
+    @pl.when(step > 0)
+    def _():
+        total[...] += part
+
+    @pl.when(step == pl.num_programs(0) - 1)
+    def _():
+        block = 64
+        gain = row_ref[0:1, :]
+        sum_ref[...] = jnp.zeros_like(sum_ref)
+
+        def some_rows(at, carry):
+            rows = pl.ds(pl.multiple_of(at * block, block), block)
+            _, unit, inv = normalize(image_ref[rows, :].astype(jnp.float32), gain, 0.0)
+            d_normed = total[rows, :]
+            d_input = d_hidden_ref[rows, :] + norm_back(d_normed, unit, inv, gain)
+            out_ref[rows, :] = d_input.astype(jnp.bfloat16)
+            sum_ref[0:1, :] += column_sum(d_normed * unit)
+            sum_ref[1:2, :] += column_sum(d_normed)
+            return carry
+
+        lax.fori_loop(0, image_ref.shape[0] // block, some_rows, 0)
+
+
+def input_grad(right, weight, images, d_hidden, lines):
+    groups, rows, packed = right.shape
+    whole = pl.BlockSpec((rows, packed), lambda f: (0, 0))
+    few = pl.BlockSpec((8, packed), lambda f: (0, 0))
+    return pl.pallas_call(
+        input_grad_kernel,
+        grid=(groups,),
+        in_specs=[
+            pl.BlockSpec((1, rows, packed), lambda f: (f, 0, 0)),
+            pl.BlockSpec((1, packed, packed), lambda f: (f, 0, 0)),
+            whole,
+            whole,
+            few,
+        ],
+        out_specs=[whole, few],
+        out_shape=[
+            jax.ShapeDtypeStruct((rows, packed), jnp.bfloat16),
+            jax.ShapeDtypeStruct((8, packed), jnp.float32),
+        ],
+        scratch_shapes=[pltpu.VMEM((rows, packed), jnp.float32)],
+        compiler_params=params(),
+        cost_estimate=lasting(13),
+        name="input_grad",
+    )(right, weight, images, d_hidden, lines)
 
 
 def store_slot(slot, own_ref, send_ref, at, value):
@@ -512,7 +658,7 @@
         ),
         out_shape=[half, half],
         compiler_params=params(),
-        cost_estimate=SHORT,
+        cost_estimate=lasting(18),
         name=name,
     )(slots, *lefts, right)
 
@@ -554,7 +700,7 @@
         ),
         out_shape=[half, half],
         compiler_params=params(),
-        cost_estimate=SHORT,
+        cost_estimate=lasting(18),
         name="down_grad",
     )(slots, left, right)
 
@@ -582,13 +728,14 @@
         out_specs=[single, single, pl.BlockSpec((2, 1, rows, packed), lambda f: (0, f, 0, 0))],
         out_shape=[one, one, jax.ShapeDtypeStruct((2, groups, rows, packed), jnp.bfloat16)],
         compiler_params=params(),
-        cost_estimate=SHORT,
+        cost_estimate=lasting(7),
         name="add_halves",
     )(*([own] * half), came)
 
 
 def unpack_kernel(part_ref, *refs):
     *pieces, out_ref, held, sems = refs
+    pieces = piece_list(pieces)
     step = pl.program_id(0)
     _, groups, rows, packed = held.shape
     width = packed // groups
@@ -606,14 +753,13 @@
 
 
 def unpack_pieces(part_of, pieces, fold):
-    groups, rows, width = pieces[0].shape
-    parts = len(pieces)
+    parts, groups, rows, width = piece_shape(pieces)
     return pl.pallas_call(
         unpack_kernel,
         grid_spec=pltpu.PrefetchScalarGridSpec(
             num_scalar_prefetch=1,
             grid=(parts,),
-            in_specs=[pl.BlockSpec(memory_space=pl.ANY)] * parts,
+            in_specs=[pl.BlockSpec(memory_space=pl.ANY)] * len(pieces),
             out_specs=pl.BlockSpec((fold * rows, width), lambda j, p: (p[j], 0)),
             scratch_shapes=[
                 pltpu.VMEM((parts, groups, rows, width), pieces[0].dtype),
@@ -622,7 +768,7 @@
         ),
         out_shape=jax.ShapeDtypeStruct((parts * fold * rows, width), pieces[0].dtype),
         compiler_params=params(),
-        cost_estimate=SHORT,
+        cost_estimate=lasting(9),
         name="unpack_pieces",
     )(part_of, *pieces)
 
@@ -661,20 +807,19 @@
 
 
 class Gather:
-    def __init__(self, shard, queue=None, behind=None, ready=None, between=None):
-        if queue is not None:
-            shard = after(shard, queue.group)
-        self.group = own = lax.all_gather(shard, "fsdp", axis=0, tiled=False)
-        if behind is not None:
-            own = after(own, behind.first)
-        if ready is not None:
-            own = after(own, ready)
+    def __init__(self, group, ahead=None, *gates):
+        own, again = group, group
+        if ahead is not None:
+            own = after(own, ahead.second)
+            again = after(again, ahead.third, *gates)
         self.first = swap(own, 1)
-        self.second = swap(own, 2)
-        third = self.first if between is None else after(self.first, between)
-        self.third = swap(third, 2)
-        near = [own, self.first, self.second, self.third]
-        self.pieces = near + [swap_core(piece) for piece in near]
+        self.second = swap(again, 2)
+        self.third = swap(self.first, 2)
+        self.near = [group, self.first, self.second, self.third]
+
+    def pieces(self, *gates):
+        late = [after(piece, *gates) if gates else piece for piece in self.near[2:]]
+        return self.near + [swap_core(piece) for piece in self.near[:2] + late]
 
 
 class Scatter:
@@ -829,7 +974,6 @@
     both = jnp.concatenate([small, time_low.reshape(-1, LANES)], axis=0)
     both = small_gather(both[None], "fsdp")
     small_all = both[:, : small.shape[0]].reshape(groups, -1)
-    time_all = small_gather(both[:, small.shape[0] :].reshape(groups * count, width), "dp")
 
     def vector_of(slot):
         return small_all[:, slot * shard_cols : (slot + 1) * shard_cols].reshape(-1).astype(wide)
@@ -842,13 +986,9 @@
     table = jnp.pad(table, ((0, 0), (0, 8 * LANES - table_rows)))
     bias = position_bias(offset_index, table)
 
-    all_images = time_all.shape[0]
-    time_cols = lax.dynamic_slice(
-        time_all, (0, own_part * shard_rows), (all_images, shard_rows)
-    )
-    time_weight = jnp.concatenate([tquery_weight, tvalue_weight], axis=1)
-    time_sum = small_scatter(matmul(time_cols, time_weight), "dp")
-    time_part = small_gather(time_sum[None], "fsdp")
+    time_rows = both[:, small.shape[0] :].reshape(groups * count, width)
+    time_weight = small_gather(jnp.concatenate([tquery_weight, tvalue_weight], axis=1), "dp")
+    time_part = small_gather(matmul(time_rows, time_weight)[None], "fsdp")
     time_own = lax.dynamic_slice(
         time_part, (0, own_group * count, 0), (groups, count, 2 * shard_cols)
     )
@@ -867,11 +1007,12 @@
     cube = is_cube()
     if cube:
         part_of, slot_of = part_tables()
-        attn_move = Gather(wire_attn, ready=time_own, between=bias)
-        up_move = Gather(up_weight, queue=attn_move, behind=attn_move)
-        down_move = Gather(wire_down, queue=attn_move, behind=up_move)
-        attn_pieces, up_pieces = attn_move.pieces, up_move.pieces
-        down_full = unpack_pieces(part_of, down_move.pieces, fold)
+        attn_group = lax.all_gather(wire_attn, "fsdp", axis=0, tiled=False)
+        wire_rest = after(jnp.stack([up_weight, wire_down]), both)
+        rest = lax.all_gather(wire_rest, "fsdp", axis=1, tiled=False)
+        attn_move = Gather(after(attn_group, time_weight))
+        up_move = Gather(after(rest[0], bias), attn_move)
+        attn_pieces = attn_move.pieces()
     else:
         part_of = jnp.zeros((1,), jnp.int32)
         attn_pieces = [gather_shards(wire_attn).reshape(groups, width, width)]
@@ -879,36 +1020,43 @@
         down_full = unpack_down(gather_shards(wire_down), fold)
 
     x_rows = images.reshape(rows, width).astype(wide)
-    normed, unit_one, inv_one = normalize(x_rows, gain_one, shift_one)
+    normed, _, _ = normalize(x_rows, gain_one, shift_one)
     normed_low = normed.astype(low)
     qkv, probs, mixed_split, proj_full, attn_full = attend(
         part_of, attn_pieces, normed_low, time_add, bias, count, tokens
     )
     if cube:
+        up_pieces = up_move.pieces(mixed_split)
+        down_move = Gather(rest[1], up_move, mixed_split)
         mixed_split = after(mixed_split, down_move.first)
     mixed = mixed_split.transpose(1, 0, 2).reshape(rows, width)
     hidden = x_rows + (matmul(mixed, proj_full) + proj_b)
-    second, unit_two, inv_two = normalize(hidden, gain_two, shift_two)
+    second, _, _ = normalize(hidden, gain_two, shift_two)
     second_low = second.astype(low)
     grad_low = cotangent.reshape(rows, width)
-    grad_rows = grad_low.astype(wide)
     wire = (groups, parts, shard_rows, width)
     activ, slope, up_full = up_forward(part_of, up_pieces, second_low, up_b)
     grad_cols = grad_low
     if cube:
+        down_pieces = down_move.pieces(activ)
+        down_full = unpack_pieces(part_of, down_pieces, fold)
         own, send = down_slot_grad(
             slot_of,
-            after(activ, down_move.third, *down_move.pieces[4:7]),
+            after(activ, *down_pieces),
             grad_low,
             parts,
             shard_rows,
         )
         down_move = Scatter(own, send)
         grad_cols = after(grad_low, down_move.near(down_full))
-    d_pre, d_second, layer_out = down_back(
-        grad_cols, hidden + down_b, activ, slope, up_full, down_full
+    def lines_of(*values):
+        return jnp.concatenate([jnp.stack(values), jnp.zeros((8 - len(values), width), wide)])
+
+    d_pre, layer_out, d_hidden, d_hidden_low, down_sums, up_sums = down_back(
+        grad_cols, hidden, lines_of(gain_two, down_b), activ, slope, up_full, down_full
     )
     layer_out = layer_out.reshape(count, tokens, width)
+    d_hidden_cols = d_hidden_low
     if cube:
         own, send = slot_grad(
             one_grad_kernel,
@@ -918,33 +1066,30 @@
             parts,
             "up_grad",
         )
-        up_move = Scatter(own, send)
-        d_second = after(d_second, send, down_move.total())
+        up_move = Scatter(own, after(send, down_move.last))
+        d_hidden_cols = after(d_hidden_low, send, down_move.total())
     else:
         grad_down = jnp.concatenate([contract_rows(a, grad_low) for a in activ], axis=0)
         down_sum = scatter_sum(pack_down(grad_down.astype(low), groups, parts, shard_rows))
         grad_up = jnp.stack([contract_rows(second_low, d).astype(low) for d in d_pre])
         up_sum = scatter_sum(grad_up.reshape(wire))
 
-    d_hidden = grad_rows + norm_back(d_second, unit_two, inv_two, gain_two)
-    d_hidden_low = d_hidden.astype(low)
-    d_mixed = times_transposed(d_hidden_low, proj_full).astype(low)
-    d_mixed_split = d_mixed.reshape(rows, groups, shard_cols).transpose(1, 0, 2)
-    d_hidden_split = d_hidden_low.reshape(rows, groups, shard_cols).transpose(1, 0, 2)
     if cube:
-        d_mixed_split = after(d_mixed_split, up_move.near())
-    d_packed, pairs = attend_back(d_mixed_split, qkv, probs, d_hidden_split)
+        d_hidden_cols = after(d_hidden_cols, up_move.near())
+    d_packed, pairs, d_time = attend_back(d_hidden_cols, proj_full, qkv, probs)
     attn_back = attn_full
     if cube:
-        normed_t = normed_low.T
+        normed_t = after(normed_low.T, up_move.back())
         own, send = slot_grad(
             pair_grad_kernel, slot_of, [normed_t, mixed.T], d_packed, parts, "pair_grad"
         )
         down_sum = down_move.end()
-        attn_move = Scatter(own, after(send, up_move.back(), down_sum))
-        attn_pair = attn_move.near()
+        attn_move = Scatter(own, after(send, up_move.last))
+        up_total = up_move.total()
+        attn_pair = attn_move.near(up_total)
         attn_back = after(attn_full, attn_pair)
-        pairs = after(pairs, attn_pair, up_move.total(attn_pair))
+        pairs = after(pairs, attn_move.back())
+        attn_total = attn_move.total()
     else:
         cut = 3 * shard_cols
         grad_attn = jnp.stack(
@@ -958,74 +1103,49 @@
         )
         attn_sum = scatter_sum(grad_attn.astype(low).reshape(wire))
 
-    d_time = after(d_packed, attn_back)
-    d_time = jnp.sum(d_time.reshape(groups, count, tokens, width).astype(wide), axis=2)
+    images_grad, input_sums = input_grad(
+        d_packed, attn_back, images.reshape(rows, width), d_hidden, lines_of(gain_one)
+    )
+    images_grad = images_grad.reshape(count, tokens, width)
+
+    d_time = after(d_time, images_grad)
     d_time = jnp.concatenate(
         [d_time[:, :, :shard_cols], d_time[:, :, 2 * shard_cols : 3 * shard_cols]], axis=2
     ).astype(low)
     d_time = d_time.transpose(1, 0, 2).reshape(count, groups * 2 * shard_cols)
-    d_time_all = small_gather(small_gather(d_time, "fsdp"), "dp")
+    d_time_rows = small_gather(d_time, "fsdp")
     d_time_cols = lax.dynamic_slice(
-        d_time_all, (0, own_group * 2 * shard_cols), (all_images, 2 * shard_cols)
-    )
-    time_grads = contract_rows(time_cols, d_time_cols)
-    tquery_grad = time_grads[:, :shard_cols]
-    tvalue_grad = time_grads[:, shard_cols:]
-    back = times_transposed(d_time_cols, time_weight)
-    back = back.reshape(parts, groups, count, shard_rows).transpose(1, 0, 2, 3)
-    back = back.reshape(groups, -1, LANES)
-
-    lane = lax.broadcasted_iota(jnp.int32, (1, width), 1)
-    d_normed = jnp.zeros((rows, width), wide)
-    for g in range(groups):
-        part = jnp.where(lane < 3 * shard_cols, d_packed[g], jnp.zeros((), low))
-        d_normed = d_normed + times_transposed(part, attn_back[g])
-    d_input = d_hidden + norm_back(d_normed, unit_one, inv_one, gain_one)
-    images_grad = d_input.astype(low).reshape(count, tokens, width)
-
-    table_sum = table_gradient(offset_index, pairs).reshape(heads, 8 * LANES)[:, :table_rows]
-
-    def rows_sum(value):
-        return jnp.sum(value, axis=0).reshape(groups, -1)
-
-    vectors = [
-        rows_sum(d_hidden_low.astype(wide)),
-        rows_sum(d_normed * unit_one),
-        rows_sum(d_normed),
-        rows_sum(d_second * unit_two),
-        rows_sum(d_second),
-        rows_sum(grad_rows),
-        jnp.sum(d_pre.astype(wide), axis=1),
-        table_sum.reshape(groups, group_heads * table_rows),
-    ]
-    flat = jnp.concatenate(vectors, axis=1)
-    flat = jnp.pad(flat, ((0, 0), (0, -flat.shape[1] % 1024))).reshape(groups, -1, LANES)
-    lines = flat.shape[1]
-    own = small_scatter(jnp.concatenate([flat, back], axis=1), "fsdp")[0]
-    slots = jnp.where(
-        lax.broadcasted_iota(jnp.int32, (parts, 1, 1), 0) == own_part, own[None, lines:], 0.0
-    )
-    own = small_sum(
-        jnp.concatenate([own[:lines], slots.reshape(-1, LANES)], axis=0), "dp"
-    )
-    back = own[lines:].reshape(parts, parts, count, shard_rows)
-    back = lax.dynamic_slice(back, (0, own_part, 0, 0), (parts, 1, count, shard_rows))
-    time_grad = back.reshape(parts, count, shard_rows).transpose(1, 0, 2).reshape(count, width)
-    own = own[:lines].reshape(-1)
-    proj_bg, gain1_g, shift1_g, gain2_g, shift2_g, down_bg = (
-        own[i * shard_cols : (i + 1) * shard_cols] for i in range(6)
-    )
-    at = 6 * shard_cols
-    up_bg = own[at : at + up_bias.shape[0]]
-    at = at + up_bias.shape[0]
-    table_grad = own[at : at + group_heads * table_rows].reshape(group_heads, table_rows)
+        d_time_rows, (0, own_group * 2 * shard_cols), (groups * count, 2 * shard_cols)
+    )
+    time_grads = small_scatter(contract_rows(time_rows, d_time_cols).astype(low), "dp")
+    back = times_transposed(d_time_cols, time_weight).reshape(-1, LANES)
+
+    table_sum = table_gradient(offset_index, pairs)
+    vectors = jnp.concatenate(
+        [down_sums[:4], input_sums[:2], up_sums.reshape(groups, width)]
+    ).reshape(-1, LANES)
+    flat = jnp.concatenate([vectors, table_sum, back], axis=0)
+    ends = (vectors.shape[0], vectors.shape[0] + table_sum.shape[0])
+    flat = small_sum(flat, "fsdp")
+    time_grad = lax.dynamic_slice(
+        flat[ends[1] :].reshape(groups * count, width), (own_group * count, 0), (count, width)
+    )
+    flat = small_sum(flat[: ends[1]], "dp")
+    vectors = flat[: ends[0]].reshape(-1, width)
+    own = lax.dynamic_slice(vectors, (0, own_group * shard_cols), (6, shard_cols))
+    proj_bg, gain2_g, shift2_g, down_bg, gain1_g, shift1_g = (own[i] for i in range(6))
+    up_bg = lax.dynamic_slice(vectors, (6 + own_group, 0), (1, width))[0]
+    table_grad = lax.dynamic_slice(
+        flat[ends[0] : ends[1]], (own_group * group_heads * 8, 0), (group_heads * 8, LANES)
+    )
+    table_grad = table_grad.reshape(group_heads, 8 * LANES)[:, :table_rows]
 
     if cube:
-        attn_move.back()
-        attn_total = attn_move.total()
         down_sum = after(down_sum, attn_total)
         up_sum = after(up_move.end(), attn_total)
         attn_sum = attn_move.end()
+    time_grads = time_grads.astype(wide)
+    tquery_grad, tvalue_grad = time_grads[:, :shard_cols], time_grads[:, shard_cols:]
     attn_sum = attn_sum.astype(wide)
     query_grad, key_grad, value_grad, proj_grad = (
         attn_sum[:, i * shard_cols : (i + 1) * shard_cols] for i in range(4)

time: 575 us -> 540 us (0.939)
  local copies, waits for them, and re-layouts: 84.9 us -> 54.9 us
  other arithmetic: 63.3 us -> 36.3 us
  Pallas kernels: 195 us -> 217 us
  matrix products: 28.6 us -> 7.07 us
  waiting for transfers between devices: 149 us -> 167 us
    ppermute x20 -> x17, waiting for transfers between devices: 48.2 us -> 84.9 us  [swap_bit(): return lax.ppermute(value, axis, [(i, i ^ 1 << bit) for i in range(size)])]
    reshape x19 -> x6, local copies, waits for them, and re-layouts: 24.2 us -> 2.97 us  [the longest x1 1.51 us: body(): vectors = jnp.concatenate([down_sums[:4], input_sums[:2], up_sums.reshape...]
    dot_general x6 -> x1, matrix products: 22.5 us -> 1.92 us  [times_transposed(): lax.dot_general(left, right, (((1,), (1,)), ((), ())), preferred_element_...]
    ppermute x15, waiting for transfers between devices: 67.1 us -> 49.9 us  [swap(): lax.ppermute(value, 'dp', [(i, i ^ NEAR[i & 1][hop]) for i in range(8)])]
    reduce_sum x6 -> x0, other arithmetic: 16 us -> none  [the longest x4 9.36 us: rows_sum(): return jnp.sum(value, axis=0).reshape(groups, -1)]
    pallas_call x0 -> x1, Pallas kernels: none -> 14.2 us  [input_grad(): pl.pallas_call(input_grad_kernel, grid=(groups,), in_specs=[pl.BlockSpec(...]
    all_gather x3 -> x2, waiting for transfers between devices: 5.47 us -> 15.6 us  [the longest x1 15.5 us: body(): rest = lax.all_gather(wire_rest, 'fsdp', axis=1, tiled=False)]
    slice x7 -> x10, local copies, waits for them, and re-layouts: 2.98 us -> 9.64 us  [the longest x1 7.98 us: body(): up_move = Gather(after(rest[0], bias), attn_move)]
  transfers between devices with their start and end apart: 56 -> 52, of which waited for: 26 -> 27; matrix products, arithmetic and copies ran while one was open for 29% -> 15% of each run, Pallas kernels for 28% -> 35%
where the time goes in v5:
time: 540 us; the launch traced here: 535 us
  Pallas kernels  217 us (40%)
  waiting for transfers between devices  167 us (31%)
  local copies, waits for them, and re-layouts  54.9 us (10%)
  starting transfers between devices  38.1 us (7%)
  other arithmetic  36.3 us (7%)
  between operations  14.8 us (3%)
  matrix products  7.07 us (1%)
    ppermute x17, waiting for transfers between devices, swap_bit(): return lax.ppermute(value, axis, [(i, i ^ 1 << bit) for i in range(size)])  84.9 us
    ppermute x15, waiting for transfers between devices, swap(): lax.ppermute(value, 'dp', [(i, i ^ NEAR[i & 1][hop]) for i in range(8)])  49.9 us
    pallas_call x2, Pallas kernels, piece_call(): pl.pallas_call(kernel, grid_spec=pltpu.PrefetchScalarGridSpec(num_scalar_...  35.7 us
    pallas_call x1, Pallas kernels, down_back(): pl.pallas_call(down_back_kernel, grid=(groups,), in_specs=[whole, whole,...  32.9 us
    pallas_call x2, Pallas kernels, slot_grad(): pl.pallas_call(kernel, grid_spec=pltpu.PrefetchScalarGridSpec(num_scalar_...  26.4 us
    pallas_call x1, Pallas kernels, attend_back(): pl.pallas_call(attend_back_kernel, grid=(groups,), in_specs=[pl.BlockSpec...  21.7 us
    pallas_call x1, Pallas kernels, position_bias(): pl.pallas_call(bias_kernel, grid=(4,), in_specs=[pl.BlockSpec((tokens, to...  20.3 us
    pallas_call x3, Pallas kernels, add_halves(): pl.pallas_call(add_kernel, grid=(groups,), in_specs=[pl.BlockSpec((1, 1,...  20.2 us
  transfers between devices with their start and end apart: 52, of which 27 were waited for; matrix products, arithmetic and copies ran while one was open for 15% of the time, Pallas kernels for 35%

profile of v5, /device:TPU:0, one launch (start us, length us, event | category | flops | bytes accessed | tf_op | source)
XLA Modules:
  0.0 534.9 jit_solution(6990126207951060524)
XLA Ops:
  7.2 2.0 concatenate.115
  11.8 4.9 concatenate.96
  16.7 3.1 collective-permute-start
  22.1 2.7 collective-permute-start.1
  24.8 5.5 %collective-permute-done.1 = bf16[2,74,128]{2,1,0:T(8,128)(2,1)S(1)} collective-permute-done((bf16[2,74,128]{2,1,0:T(8,128)(2,1)S(1)}, bf16[2,74,128]{2,1,0:T(8,128)(2,1)S(1)}, u32[]{:S(2)}, u32[]{:S(2)}) %collective-permute-start.1) | collective-permute-done | bytes 37920 | tf_op jit(solution)/shard_map/ppermute | solution.py:853
  33.6 1.6 collective-permute-start.3
  35.2 9.1 %collective-permute-done.3 = bf16[288,576]{1,0:T(8,128)(2,1)S(1)} collective-permute-done((bf16[288,576]{1,0:T(8,128)(2,1)S(1)}, bf16[288,576]{1,0:T(8,128)(2,1)S(1)}, u32[]{:S(2)}, u32[]{:S(2)}) %collective-permute-start.3) | collective-permute-done | bytes 331808 | tf_op jit(solution)/shard_map/ppermute | solution.py:853
  44.6 1.6 collective-permute-start.4
  47.4 15.2 %collective-permute-done.4 = bf16[576,576]{1,0:T(8,128)(2,1)} collective-permute-done((bf16[576,576]{1,0:T(8,128)(2,1)S(1)}, bf16[576,576]{1,0:T(8,128)(2,1)}, u32[]{:S(2)}, u32[]{:S(2)}) %collective-permute-start.4) | collective-permute-done | bytes 663584 | tf_op jit(solution)/shard_map/ppermute | solution.py:853
  62.6 2.0 maximum_select_fusion
  64.6 1.6 collective-permute-start.7
  66.1 20.3 %position_bias.1.bias_ref = f32[16,256,256]{2,1,0:T(8,128)} custom-call(s32[256,256]{1,0:T(8,128)} %index_ref.3, f32[16,1,1024]{2,1,0:T(1,128)} %reshape.262.table_ref), custom_call_target="tpu_custom_call" | custom-call | flops 20000000000 | bytes 1 | tf_op jit(solution)/shard_map/position_bias/pallas_call | solution.py:111
  88.4 15.5 %all-gather.7.cloned.1.call-done = bf16[2,576,1152]{2,0,1:T(2,128)(2,1)} async-done(((bf16[2,144,1152]{2,0,1:T(2,128)(2,1)}), bf16[2,576,1152]{2,0,1:T(2,128)(2,1)}) %all-gather.7.cloned.1.call-update) | async-done | bytes 2654224 | tf_op jit(solution)/shard_map/all_gather | solution.py:1012
  104.0 8.0 %fusion.28 = (bf16[1,576,1152]{2,0,1:T(2,128)(2,1)S(1)}, bf16[1,576,1152]{2,0,1:T(2,128)(2,1)}) fusion(bf16[2,576,1152]{2,0,1:T(2,128)(2,1)} %all-gather.7.cloned.1.call-done), kind=kLoop, calls=%fused_computation.112 | loop fusion | bytes 5308416 | tf_op jit(solution)/shard_map/slice | solution.py:1014
  116.9 2.4 collective-permute-done.5
  121.7 1.5 collective-permute-start.14
  124.2 14.4 %collective-permute-done.16.refs_1_ = bf16[4,144,1152]{2,1,0:T(8,128)(2,1)} collective-permute-done((bf16[4,144,1152]{2,1,0:T(8,128)(2,1)}, bf16[4,144,1152]{2,1,0:T(8,128)(2,1)}, u32[]{:S(2)}, u32[]{:S(2)}) %collective-permute-start.16) | collective-permute-done | bytes 1327136 | tf_op jit(solution)/shard_map/ppermute | solution.py:798
  138.6 1.8 collective-permute-start.13
  142.7 1.5 fusion.13.normed_ref
  144.4 3.0 copy.91
  147.4 1.5 collective-permute-start.17
  151.6 21.0 %attend.1 = (bf16[4,512,896]{2,1,0:T(8,128)(2,1)}, bf16[4,2,4,256,256]{4,3,2,1,0:T(8,128)(2,1)}, bf16[4,512,288]{2,1,0:T(8,128)(2,1)}, bf16[1152,1152]{1,0:T(8,128)(2,1)}, bf16[4,1152,1152]{2,1,0:T(8,128)(2,1)}) custom-call(s32[8]{0:T(128)} %fusion.25.part_ref, bf16[512,1152]{1,0:T(8,128)(2,1)} %fusion.13.normed_ref, ...), custom_call_target="tpu_custom_call" | custom-call | flops 12999999488 | bytes 1 | tf_op jit(solution)/shard_map/attend/pallas_call | solution.py:228
  172.8 6.8 %collective-permute-done.17.refs_3_ = bf16[4,144,1152]{2,1,0:T(8,128)(2,1)} collective-permute-done((bf16[4,144,1152]{2,1,0:T(8,128)(2,1)}, bf16[4,144,1152]{2,1,0:T(8,128)(2,1)}, u32[]{:S(2)}, u32[]{:S(2)}) %collective-permute-start.17) | collective-permute-done | bytes 1327136 | tf_op jit(solution)/shard_map/ppermute | solution.py:798
  179.5 1.5 collective-permute-start.22
  181.1 2.5 copy.79
  183.5 4.2 fusion.36
  188.2 1.7 copy-done.33
  192.5 14.7 %up_forward.1 = (bf16[4,512,1152]{2,1,0:T(8,128)(2,1)}, bf16[4,512,1152]{2,1,0:T(8,128)(2,1)}, bf16[4,1152,1152]{2,1,0:T(8,128)(2,1)}) custom-call(s32[8]{0:T(128)} %fusion.25.part_ref, bf16[512,1152]{1,0:T(8,128)(2,1)} %add_convert_fusion.second_ref, f32[4,1,1152]{2,1,0:T(1,128)} %reshape.267.bias_ref, bf16[4,144,1152]{2,1,0:T(8,128)(2,1)} %bitcast.11.refs_0_, ...), custom_call_target="tpu_custom_call" | custom-call | flops 12999999488 | bytes 1 | tf_op jit(solution)/shard_map/up_forward/pallas_call | solution.py:228
  207.4 4.5 collective-permute-done.23.refs_3_
  213.1 1.8 collective-permute-done.27.refs_7_
  216.0 18.5 %down_grad.1 = (bf16[4,4,144,1152]{3,2,1,0:T(8,128)(2,1)}, bf16[4,4,144,1152]{3,2,1,0:T(8,128)(2,1)}) custom-call(s32[8]{0:T(128)} %fusion.24.slot_ref, bf16[4,512,1152]{2,1,0:T(8,128)(2,1)} %get-tuple-element.95.left_ref.activ_ref, bf16[512,1152]{1,0:T(8,128)(2,1)} %bitcast.102), custom_call_target="tpu_custom_call" | custom-call | flops 17999998976 | bytes 1 | tf_op jit(solution)/shard_map/down_grad/pallas_call | solution.py:690
  236.7 9.0 %unpack_pieces.1.down_ref = bf16[4608,1152]{1,0:T(8,128)(2,1)} custom-call(s32[8]{0:T(128)} %fusion.25.part_ref, bf16[4,144,1152]{2,1,0:T(8,128)(2,1)} %bitcast.10.refs_0_, bf16[4,144,1152]{2,1,0:T(8,128)(2,1)} %copy-done.32, bf16[4,144,1152]{2,1,0:T(8,128)(2,1)} %collective-permute-done.22.refs_2_, bf16[4,144,1152]{2,1,0:T(8,128)(2,1)} %copy-done.34, ...), custom_call_target="tpu_custom_call" | custom-call | flops 8999999488 | bytes 1 | tf_op jit(solution)/shard_map/unpack_pieces/pallas_call | solution.py:757
  245.8 6.6 %add_halves.3 = (bf16[4,144,1152]{2,1,0:T(8,128)(2,1)}, bf16[4,144,1152]{2,1,0:T(8,128)(2,1)}, bf16[2,4,144,1152]{3,2,1,0:T(8,128)(2,1)}) custom-call(bf16[4,4,144,1152]{3,2,1,0:T(8,128)(2,1)} %get-tuple-element.97.one_ref.two_ref.three_ref.four_ref, bf16[4,4,144,1152]{3,2,1,0:T(8,128)(2,1)} %get-tuple-element.97.one_ref.two_ref.three_ref.four_ref, ...), custom_call_target="tpu_custom_call" | custom-call | flops 7000000000 | bytes 1 | tf_op jit(solution)/shard_map/add_halves/pallas_call | solution.py:721
  253.9 32.9 %down_back.1 = (bf16[4,512,1152]{2,1,0:T(8,128)(2,1)}, bf16[512,1152]{1,0:T(8,128)(2,1)}, f32[512,1152]{1,0:T(8,128)}, bf16[512,1152]{1,0:T(8,128)(2,1)}, f32[8,1152]{1,0:T(8,128)}, /*index=5*/f32[4,1,1152]{2,1,0:T(1,128)}) custom-call(bf16[512,1152]{1,0:T(8,128)(2,1)} %bitcast.103, f32[512,1152]{1,0:T(8,128)} %copy-done, ...), custom_call_target="tpu_custom_call" | custom-call | flops 32999999488 | bytes 1 | tf_op jit(solution)/shard_map/down_back/pallas_call | solution.py:429
  291.9 12.6 %up_grad.1 = (bf16[4,4,144,1152]{3,2,1,0:T(8,128)(2,1)}, bf16[4,4,144,1152]{3,2,1,0:T(8,128)(2,1)}) custom-call(s32[8]{0:T(128)} %fusion.24.slot_ref, bf16[1152,512]{1,0:T(8,128)(2,1)} %copy.80.one_ref, bf16[4,512,1152]{2,1,0:T(8,128)(2,1)} %get-tuple-element.107.right_ref), custom_call_target="tpu_custom_call" | custom-call | flops 17999998976 | bytes 1 | tf_op jit(solution)/shard_map/up_grad/pallas_call | solution.py:650
  304.6 3.2 collective-permute-done.30
  308.8 9.0 %collective-permute-done.31.came_ref = bf16[4,4,144,1152]{3,2,1,0:T(8,128)(2,1)S(1)} collective-permute-done((bf16[4,4,144,1152]{3,2,1,0:T(8,128)(2,1)}, bf16[4,4,144,1152]{3,2,1,0:T(8,128)(2,1)S(1)}, u32[]{:S(2)}, u32[]{:S(2)}) %collective-permute-start.31) | collective-permute-done | bytes 5308448 | tf_op jit(solution)/shard_map/ppermute | solution.py:802
  317.8 2.4 copy-done.4
  320.1 6.7 %add_halves.4 = (bf16[4,144,1152]{2,1,0:T(8,128)(2,1)}, bf16[4,144,1152]{2,1,0:T(8,128)(2,1)}, bf16[2,4,144,1152]{3,2,1,0:T(8,128)(2,1)}) custom-call(bf16[4,4,144,1152]{3,2,1,0:T(8,128)(2,1)} %get-tuple-element.111.one_ref.two_ref.three_ref.four_ref, bf16[4,4,144,1152]{3,2,1,0:T(8,128)(2,1)} %get-tuple-element.111.one_ref.two_ref.three_ref.four_ref, ...), custom_call_target="tpu_custom_call" | custom-call | flops 7000000000 | bytes 1 | tf_op jit(solution)/shard_map/add_halves/pallas_call | solution.py:721
  327.3 3.7 fusion.8
  331.0 21.7 %attend_back.1 = (bf16[4,512,1152]{2,1,0:T(8,128)(2,1)}, f32[16,256,256]{2,1,0:T(8,128)}, f32[4,2,864]{2,1,0:T(2,128)}) custom-call(bf16[512,1152]{1,0:T(8,128)(2,1)} %get-tuple-element.114.hidden_ref, bf16[1152,1152]{1,0:T(8,128)(2,1)} %get-tuple-element.87.proj_ref, bf16[4,512,896]{2,1,0:T(8,128)(2,1)} %get-tuple-element.115.qkv_ref, ...), custom_call_target="tpu_custom_call" | custom-call | flops 19000000512 | bytes 1 | tf_op jit(solution)/shard_map/attend_back/pallas_call | solution.py:514
  352.7 6.4 %collective-permute-done.32 = bf16[2,4,144,1152]{3,2,1,0:T(8,128)(2,1)} collective-permute-done((bf16[2,4,144,1152]{3,2,1,0:T(8,128)(2,1)}, bf16[2,4,144,1152]{3,2,1,0:T(8,128)(2,1)}, u32[]{:S(2)}, u32[]{:S(2)}) %collective-permute-start.32) | collective-permute-done | bytes 2654240 | tf_op jit(solution)/shard_map/ppermute | solution.py:798
  359.1 2.7 fusion.6
  364.0 13.8 %pair_grad.1 = (bf16[4,4,144,1152]{3,2,1,0:T(8,128)(2,1)}, bf16[4,4,144,1152]{3,2,1,0:T(8,128)(2,1)}) custom-call(s32[8]{0:T(128)} %fusion.24.slot_ref, bf16[1152,512]{1,0:T(8,128)(2,1)} %copy.81.one_ref, bf16[1152,512]{1,0:T(8,128)(2,1)} %bitcast.89, bf16[4,512,1152]{2,1,0:T(8,128)(2,1)} %get-tuple-element.117.right_ref), custom_call_target="tpu_custom_call" | custom-call | flops 17999998976 | bytes 1 | tf_op jit(solution)/shard_map/pair_grad/pallas_call | solution.py:650
  377.8 2.0 collective-permute-done.33
  380.0 2.9 fusion.5
  382.9 6.0 %collective-permute-done.34.came_ref = bf16[4,4,144,1152]{3,2,1,0:T(8,128)(2,1)} collective-permute-done((bf16[4,4,144,1152]{3,2,1,0:T(8,128)(2,1)}, bf16[4,4,144,1152]{3,2,1,0:T(8,128)(2,1)}, u32[]{:S(2)}, u32[]{:S(2)}) %collective-permute-start.34) | collective-permute-done | bytes 5308448 | tf_op jit(solution)/shard_map/ppermute | solution.py:802
  388.9 6.9 %add_halves.5 = (bf16[4,144,1152]{2,1,0:T(8,128)(2,1)}, bf16[4,144,1152]{2,1,0:T(8,128)(2,1)}, bf16[2,4,144,1152]{3,2,1,0:T(8,128)(2,1)}) custom-call(bf16[4,4,144,1152]{3,2,1,0:T(8,128)(2,1)} %get-tuple-element.123.one_ref.two_ref.three_ref.four_ref, bf16[4,4,144,1152]{3,2,1,0:T(8,128)(2,1)} %get-tuple-element.123.one_ref.two_ref.three_ref.four_ref, ...), custom_call_target="tpu_custom_call" | custom-call | flops 7000000000 | bytes 1 | tf_op jit(solution)/shard_map/add_halves/pallas_call | solution.py:721
  397.0 14.2 %input_grad.1 = (bf16[512,1152]{1,0:T(8,128)(2,1)}, f32[8,1152]{1,0:T(8,128)}) custom-call(bf16[4,512,1152]{2,1,0:T(8,128)(2,1)} %get-tuple-element.117.right_ref, bf16[4,1152,1152]{2,1,0:T(8,128)(2,1)} %get-tuple-element.127.weight_ref, bf16[512,1152]{1,0:T(8,128)(2,1)} %bitcast.85, f32[512,1152]{1,0:T(8,128)} %get-tuple-element.128.d_hidden_ref, ...), custom_call_target="tpu_custom_call" | custom-call | flops 12999999488 | bytes 1 | tf_op jit(solution)/shard_map/input_grad/pallas_call | solution.py:581
  411.6 3.6 collective-permute-done.36
  416.9 3.3 collective-permute-done.37
  422.6 11.6 %collective-permute-done.35 = bf16[2,4,144,1152]{3,2,1,0:T(8,128)(2,1)S(1)} collective-permute-done((bf16[2,4,144,1152]{3,2,1,0:T(8,128)(2,1)}, bf16[2,4,144,1152]{3,2,1,0:T(8,128)(2,1)S(1)}, u32[]{:S(2)}, u32[]{:S(2)}) %collective-permute-start.35) | collective-permute-done | bytes 2654240 | tf_op jit(solution)/shard_map/ppermute | solution.py:798
  438.3 11.6 %collective-permute-done.41 = bf16[576,576]{0,1:T(8,128)(2,1)S(1)} collective-permute-done((bf16[576,576]{0,1:T(8,128)(2,1)S(1)}, bf16[576,576]{0,1:T(8,128)(2,1)S(1)}, u32[]{:S(2)}, u32[]{:S(2)}) %collective-permute-start.41) | collective-permute-done | bytes 663584 | tf_op jit(solution)/shard_map/ppermute | solution.py:853
  453.7 1.9 fusion.37
  456.4 8.3 %collective-permute-done.42 = bf16[288,576]{0,1:T(8,128)(2,1)} collective-permute-done((bf16[288,576]{0,1:T(8,128)(2,1)}, bf16[288,576]{0,1:T(8,128)(2,1)}, u32[]{:S(2)}, u32[]{:S(2)}) %collective-permute-start.42) | collective-permute-done | bytes 331808 | tf_op jit(solution)/shard_map/ppermute | solution.py:853
  465.9 3.3 fusion.2
  469.3 17.7 %table_gradient.1 = f32[128,128]{1,0:T(8,128)} custom-call(s32[256,256]{1,0:T(8,128)} %index_ref.3, f32[16,256,256]{2,1,0:T(8,128)} %get-tuple-element.135.pairs_ref), custom_call_target="tpu_custom_call" | custom-call | flops 17999998976 | bytes 1 | tf_op jit(solution)/shard_map/table_gradient/pallas_call | solution.py:167
  488.1 11.4 %collective-permute-done.38 = f32[290,128]{1,0:T(8,128)S(1)} collective-permute-done((f32[290,128]{1,0:T(8,128)S(1)}, f32[290,128]{1,0:T(8,128)S(1)}, u32[]{:S(2)}, u32[]{:S(2)}) %collective-permute-start.38) | collective-permute-done | bytes 148512 | tf_op jit(solution)/shard_map/ppermute | solution.py:853
  500.3 2.3 collective-permute-start.39
  502.6 5.5 %collective-permute-done.39 = f32[290,128]{1,0:T(8,128)S(1)} collective-permute-done((f32[290,128]{1,0:T(8,128)S(1)}, f32[290,128]{1,0:T(8,128)S(1)}, u32[]{:S(2)}, u32[]{:S(2)}) %collective-permute-start.39) | collective-permute-done | bytes 148512 | tf_op jit(solution)/shard_map/ppermute | solution.py:853
  511.9 2.9 collective-permute-done.45
  514.8 1.8 collective-permute-start.46
  517.2 2.5 collective-permute-done.46
  524.2 1.9 convert_element_type.268
  (262 shorter events, 71.6 us)
Async XLA Ops:
  7.2 17.6 %copy-start.17 = (bf16[144,1152]{1,0:T(8,128)(2,1)S(1)}, bf16[144,1152]{1,0:T(8,128)(2,1)}, u32[]{:S(2)}) copy-start(bf16[144,1152]{1,0:T(8,128)(2,1)} %param.38) | copy-start | bytes 995332
  7.2 57.4 %all-gather.5.cloned.1.call-start = ((), (), s32[]{:S(2)}) async-start(), calls=%async_computation.6 | async-start | bytes 1658880 | tf_op jit(solution)/shard_map/all_gather | solution.py:1010
  9.3 94.7 %all-gather.7.cloned.1.call-start = ((), (), s32[]{:S(2)}) async-start(), calls=%async_computation.7 | async-start | bytes 3317760 | tf_op jit(solution)/shard_map/all_gather | solution.py:1012
  16.7 5.3 collective-permute-start
  22.1 8.3 %collective-permute-start.1 = (bf16[2,74,128]{2,1,0:T(8,128)(2,1)S(1)}, bf16[2,74,128]{2,1,0:T(8,128)(2,1)S(1)}, u32[]{:S(2)}, u32[]{:S(2)}) collective-permute-start(bf16[2,74,128]{2,1,0:T(8,128)(2,1)S(1)} %maximum_select_fusion.4), channel_id=1, source_target_pairs={{0,2},{1,3},{2,0},{3,1},{4,6},{5,7},{6,4},{7,5},{8,10},{9,11},{10,... | collective-permute-start | bytes 113672 | tf_op jit(solution)/shard_map/ppermute | solution.py:853
  31.8 489.9 %reduce-scatter.8.cloned.1.call-start = ((), (), s32[]{:S(2)}) async-start(), calls=%async_computation.5 | async-start | bytes 1658880 | tf_op jit(solution)/shard_map/reduce_scatter | solution.py:848
  32.0 1.5 collective-permute-start.2
  33.6 10.7 %collective-permute-start.3 = (bf16[288,576]{1,0:T(8,128)(2,1)S(1)}, bf16[288,576]{1,0:T(8,128)(2,1)S(1)}, u32[]{:S(2)}, u32[]{:S(2)}) collective-permute-start(bf16[288,576]{1,0:T(8,128)(2,1)S(1)} %maximum_select_fusion.2), channel_id=1, source_target_pairs={{0,8},{4,12},{8,0},{12,4},{16,24},{20,28},{24,16},{28,20},{1,9},{5... | collective-permute-start | bytes 995336 | tf_op jit(solution)/shard_map/ppermute | solution.py:853
  44.6 18.0 %collective-permute-start.4 = (bf16[576,576]{1,0:T(8,128)(2,1)S(1)}, bf16[576,576]{1,0:T(8,128)(2,1)}, u32[]{:S(2)}, u32[]{:S(2)}) collective-permute-start(bf16[576,576]{1,0:T(8,128)(2,1)S(1)} %maximum_select_fusion.1), channel_id=1, source_target_pairs={{0,16},{4,20},{8,24},{12,28},{16,0},{20,4},{24,8},{28,12},{1,17},{... | collective-permute-start | bytes 1990664 | tf_op jit(solution)/shard_map/ppermute | solution.py:853
  64.5 50.7 %copy-start.2 = (bf16[1152,576]{1,0:T(8,128)(2,1)}, bf16[1152,576]{1,0:T(8,128)(2,1)S(1)}, u32[]{:S(2)}) copy-start(bf16[1152,576]{1,0:T(8,128)(2,1)S(1)} %maximum_select_fusion) | copy-start | bytes 3981316
  64.6 23.3 %collective-permute-start.7 = (bf16[4,144,1152]{2,1,0:T(8,128)(2,1)}, bf16[4,144,1152]{2,1,0:T(8,128)(2,1)}, u32[]{:S(2)}, u32[]{:S(2)}) collective-permute-start(bf16[4,144,1152]{2,1,0:T(8,128)(2,1)} %bitcast.7.refs_0_), channel_id=1, source_target_pairs={{0,8},{4,20},{8,0},{12,28},{16,24},{20,4},{24,16},{28,12},{1,9},{5... | collective-permute-start | bytes 3981320 | tf_op jit(solution)/shard_map/ppermute | solution.py:798
  86.4 26.8 %collective-permute-start.8 = (bf16[4,144,1152]{2,1,0:T(8,128)(2,1)}, bf16[4,144,1152]{2,1,0:T(8,128)(2,1)}, u32[]{:S(2)}, u32[]{:S(2)}) collective-permute-start(bf16[4,144,1152]{2,1,0:T(8,128)(2,1)} %bitcast.7.refs_0_), channel_id=1, source_target_pairs={{0,16},{4,12},{8,24},{12,4},{16,0},{20,28},{24,8},{28,20},{1,17},{... | collective-permute-start | bytes 3981320 | tf_op jit(solution)/shard_map/ppermute | solution.py:798
  87.9 33.8 %collective-permute-start.9 = (bf16[4,144,1152]{2,1,0:T(8,128)(2,1)}, bf16[4,144,1152]{2,1,0:T(8,128)(2,1)}, u32[]{:S(2)}, u32[]{:S(2)}) collective-permute-start(bf16[4,144,1152]{2,1,0:T(8,128)(2,1)} %collective-permute-done.7.refs_1_), channel_id=1, source_target_pairs={{0,16},{4,12},{8,24},{12,4},{16,0},{20,28},{24,8},{28,20},{1,17},{... | collective-permute-start | bytes 3981320 | tf_op jit(solution)/shard_map/ppermute | solution.py:798
  113.2 25.4 %collective-permute-start.16 = (bf16[4,144,1152]{2,1,0:T(8,128)(2,1)}, bf16[4,144,1152]{2,1,0:T(8,128)(2,1)}, u32[]{:S(2)}, u32[]{:S(2)}) collective-permute-start(bf16[4,144,1152]{2,1,0:T(8,128)(2,1)} %bitcast.11.refs_0_), channel_id=1, source_target_pairs={{0,8},{4,20},{8,0},{12,28},{16,24},{20,4},{24,16},{28,12},{1,9},{5... | collective-permute-start | bytes 3981320 | tf_op jit(solution)/shard_map/ppermute | solution.py:798
  115.2 32.2 %copy-start.19 = (bf16[8,1152]{1,0:T(8,128)(2,1)}, bf16[8,1152]{1,0:T(8,128)(2,1)S(1)}, u32[]{:S(2)}) copy-start(bf16[8,1152]{1,0:T(8,128)(2,1)S(1)} %reshape.243) | copy-start | bytes 55300
  115.5 3.8 collective-permute-start.5
  119.3 4.9 collective-permute-start.6
  120.5 28.4 %collective-permute-start.10 = (bf16[4,144,1152]{2,1,0:T(8,128)(2,1)}, bf16[4,144,1152]{2,1,0:T(8,128)(2,1)}, u32[]{:S(2)}, u32[]{:S(2)}) collective-permute-start(bf16[4,144,1152]{2,1,0:T(8,128)(2,1)} %bitcast.7.refs_0_), channel_id=1, source_target_pairs={{0,4},{4,0},{8,12},{12,8},{16,20},{20,16},{24,28},{28,24},{1,5},{5... | collective-permute-start | bytes 3981320 | tf_op jit(solution)/shard_map/ppermute | solution.py:802
  121.7 25.7 %collective-permute-start.14 = (bf16[4,144,1152]{2,1,0:T(8,128)(2,1)}, bf16[4,144,1152]{2,1,0:T(8,128)(2,1)}, u32[]{:S(2)}, u32[]{:S(2)}) collective-permute-start(bf16[4,144,1152]{2,1,0:T(8,128)(2,1)} %bitcast.11.refs_0_), channel_id=1, source_target_pairs={{0,16},{4,12},{8,24},{12,4},{16,0},{20,28},{24,8},{28,20},{1,17},{... | collective-permute-start | bytes 3981320 | tf_op jit(solution)/shard_map/ppermute | solution.py:798
  123.3 27.8 %collective-permute-start.11 = (bf16[4,144,1152]{2,1,0:T(8,128)(2,1)}, bf16[4,144,1152]{2,1,0:T(8,128)(2,1)}, u32[]{:S(2)}, u32[]{:S(2)}) collective-permute-start(bf16[4,144,1152]{2,1,0:T(8,128)(2,1)} %collective-permute-done.7.refs_1_), channel_id=1, source_target_pairs={{0,4},{4,0},{8,12},{12,8},{16,20},{20,16},{24,28},{28,24},{1,5},{5... | collective-permute-start | bytes 3981320 | tf_op jit(solution)/shard_map/ppermute | solution.py:802
  124.2 26.9 %collective-permute-start.12 = (bf16[4,144,1152]{2,1,0:T(8,128)(2,1)}, bf16[4,144,1152]{2,1,0:T(8,128)(2,1)}, u32[]{:S(2)}, u32[]{:S(2)}) collective-permute-start(bf16[4,144,1152]{2,1,0:T(8,128)(2,1)} %collective-permute-done.8.refs_2_), channel_id=1, source_target_pairs={{0,4},{4,0},{8,12},{12,8},{16,20},{20,16},{24,28},{28,24},{1,5},{5... | collective-permute-start | bytes 3981320 | tf_op jit(solution)/shard_map/ppermute | solution.py:802
  138.6 13.0 %collective-permute-start.13 = (bf16[4,144,1152]{2,1,0:T(8,128)(2,1)}, bf16[4,144,1152]{2,1,0:T(8,128)(2,1)}, u32[]{:S(2)}, u32[]{:S(2)}) collective-permute-start(bf16[4,144,1152]{2,1,0:T(8,128)(2,1)} %collective-permute-done.9.refs_3_), channel_id=1, source_target_pairs={{0,4},{4,0},{8,12},{12,8},{16,20},{20,16},{24,28},{28,24},{1,5},{5... | collective-permute-start | bytes 3981320 | tf_op jit(solution)/shard_map/ppermute | solution.py:802
  147.4 32.2 %collective-permute-start.17 = (bf16[4,144,1152]{2,1,0:T(8,128)(2,1)}, bf16[4,144,1152]{2,1,0:T(8,128)(2,1)}, u32[]{:S(2)}, u32[]{:S(2)}) collective-permute-start(bf16[4,144,1152]{2,1,0:T(8,128)(2,1)} %collective-permute-done.16.refs_1_), channel_id=1, source_target_pairs={{0,16},{4,12},{8,24},{12,4},{16,0},{20,28},{24,8},{28,20},{1,17},{... | collective-permute-start | bytes 3981320 | tf_op jit(solution)/shard_map/ppermute | solution.py:798
  148.9 30.6 %collective-permute-start.15 = (bf16[4,144,1152]{2,1,0:T(8,128)(2,1)}, bf16[4,144,1152]{2,1,0:T(8,128)(2,1)S(1)}, u32[]{:S(2)}, u32[]{:S(2)}) collective-permute-start(bf16[4,144,1152]{2,1,0:T(8,128)(2,1)} %bitcast.10.refs_0_), channel_id=1, source_target_pairs={{0,8},{4,20},{8,0},{12,28},{16,24},{20,4},{24,16},{28,12},{1,9},{5... | collective-permute-start | bytes 3981320 | tf_op jit(solution)/shard_map/ppermute | solution.py:798
  151.1 37.1 %collective-permute-start.18 = (bf16[4,144,1152]{2,1,0:T(8,128)(2,1)}, bf16[4,144,1152]{2,1,0:T(8,128)(2,1)}, u32[]{:S(2)}, u32[]{:S(2)}) collective-permute-start(bf16[4,144,1152]{2,1,0:T(8,128)(2,1)} %bitcast.11.refs_0_), channel_id=1, source_target_pairs={{0,4},{4,0},{8,12},{12,8},{16,20},{20,16},{24,28},{28,24},{1,5},{5... | collective-permute-start | bytes 3981320 | tf_op jit(solution)/shard_map/ppermute | solution.py:802
  151.1 40.8 %collective-permute-start.19 = (bf16[4,144,1152]{2,1,0:T(8,128)(2,1)}, bf16[4,144,1152]{2,1,0:T(8,128)(2,1)}, u32[]{:S(2)}, u32[]{:S(2)}) collective-permute-start(bf16[4,144,1152]{2,1,0:T(8,128)(2,1)} %collective-permute-done.16.refs_1_), channel_id=1, source_target_pairs={{0,4},{4,0},{8,12},{12,8},{16,20},{20,16},{24,28},{28,24},{1,5},{5... | collective-permute-start | bytes 3981320 | tf_op jit(solution)/shard_map/ppermute | solution.py:802
  172.6 19.4 %collective-permute-start.20 = (bf16[4,144,1152]{2,1,0:T(8,128)(2,1)}, bf16[4,144,1152]{2,1,0:T(8,128)(2,1)}, u32[]{:S(2)}, u32[]{:S(2)}) collective-permute-start(bf16[4,144,1152]{2,1,0:T(8,128)(2,1)} %collective-permute-done.14.refs_2_), channel_id=1, source_target_pairs={{0,4},{4,0},{8,12},{12,8},{16,20},{20,16},{24,28},{28,24},{1,5},{5... | collective-permute-start | bytes 3981320 | tf_op jit(solution)/shard_map/ppermute | solution.py:802
  179.5 13.0 %collective-permute-start.21 = (bf16[4,144,1152]{2,1,0:T(8,128)(2,1)}, bf16[4,144,1152]{2,1,0:T(8,128)(2,1)}, u32[]{:S(2)}, u32[]{:S(2)}) collective-permute-start(bf16[4,144,1152]{2,1,0:T(8,128)(2,1)} %collective-permute-done.17.refs_3_), channel_id=1, source_target_pairs={{0,4},{4,0},{8,12},{12,8},{16,20},{20,16},{24,28},{28,24},{1,5},{5... | collective-permute-start | bytes 3981320 | tf_op jit(solution)/shard_map/ppermute | solution.py:802
  179.5 27.6 %collective-permute-start.22 = (bf16[4,144,1152]{2,1,0:T(8,128)(2,1)}, bf16[4,144,1152]{2,1,0:T(8,128)(2,1)}, u32[]{:S(2)}, u32[]{:S(2)}) collective-permute-start(bf16[4,144,1152]{2,1,0:T(8,128)(2,1)} %bitcast.10.refs_0_), channel_id=1, source_target_pairs={{0,16},{4,12},{8,24},{12,4},{16,0},{20,28},{24,8},{28,20},{1,17},{... | collective-permute-start | bytes 3981320 | tf_op jit(solution)/shard_map/ppermute | solution.py:798
  187.7 47.9 %copy-start = (f32[512,1152]{1,0:T(8,128)}, f32[512,1152]{1,0:T(8,128)S(1)}, u32[]{:S(2)}) copy-start(f32[512,1152]{1,0:T(8,128)S(1)} %get-tuple-element.255.hidden_ref) | copy-start | bytes 7077892
  189.9 21.9 %collective-permute-start.23 = (bf16[4,144,1152]{2,1,0:T(8,128)(2,1)S(1)}, bf16[4,144,1152]{2,1,0:T(8,128)(2,1)S(1)}, u32[]{:S(2)}, u32[]{:S(2)}) collective-permute-start(bf16[4,144,1152]{2,1,0:T(8,128)(2,1)S(1)} %copy-done.33), channel_id=1, source_target_pairs={{0,16},{4,12},{8,24},{12,4},{16,0},{20,28},{24,8},{28,20},{1,17},{... | collective-permute-start | bytes 3981320 | tf_op jit(solution)/shard_map/ppermute | solution.py:798
  191.9 21.1 %collective-permute-start.24 = (bf16[4,144,1152]{2,1,0:T(8,128)(2,1)}, bf16[4,144,1152]{2,1,0:T(8,128)(2,1)}, u32[]{:S(2)}, u32[]{:S(2)}) collective-permute-start(bf16[4,144,1152]{2,1,0:T(8,128)(2,1)} %bitcast.10.refs_0_), channel_id=1, source_target_pairs={{0,4},{4,0},{8,12},{12,8},{16,20},{20,16},{24,28},{28,24},{1,5},{5... | collective-permute-start | bytes 3981320 | tf_op jit(solution)/shard_map/ppermute | solution.py:802
  192.0 21.0 %collective-permute-start.25 = (bf16[4,144,1152]{2,1,0:T(8,128)(2,1)S(1)}, bf16[4,144,1152]{2,1,0:T(8,128)(2,1)}, u32[]{:S(2)}, u32[]{:S(2)}) collective-permute-start(bf16[4,144,1152]{2,1,0:T(8,128)(2,1)S(1)} %copy-done.33), channel_id=1, source_target_pairs={{0,4},{4,0},{8,12},{12,8},{16,20},{20,16},{24,28},{28,24},{1,5},{5... | collective-permute-start | bytes 3981320 | tf_op jit(solution)/shard_map/ppermute | solution.py:802
  207.2 5.9 %collective-permute-start.26 = (bf16[4,144,1152]{2,1,0:T(8,128)(2,1)}, bf16[4,144,1152]{2,1,0:T(8,128)(2,1)S(1)}, u32[]{:S(2)}, u32[]{:S(2)}) collective-permute-start(bf16[4,144,1152]{2,1,0:T(8,128)(2,1)} %collective-permute-done.22.refs_2_), channel_id=1, source_target_pairs={{0,4},{4,0},{8,12},{12,8},{16,20},{20,16},{24,28},{28,24},{1,5},{5... | collective-permute-start | bytes 3981320 | tf_op jit(solution)/shard_map/ppermute | solution.py:802
  211.8 22.6 %copy-start.34 = (bf16[4,144,1152]{2,1,0:T(8,128)(2,1)}, bf16[4,144,1152]{2,1,0:T(8,128)(2,1)S(1)}, u32[]{:S(2)}) copy-start(bf16[4,144,1152]{2,1,0:T(8,128)(2,1)S(1)} %collective-permute-done.23.refs_3_) | copy-start | bytes 3981316
  211.8 3.1 collective-permute-start.27
  216.0 18.7 %copy-start.24 = (f32[4,288]{1,0:T(4,128)S(1)}, f32[4,288]{1,0:T(4,128)}, u32[]{:S(2)}) copy-start(f32[4,288]{1,0:T(4,128)} %copy-done.23) | copy-start | bytes 13828
  216.0 18.8 %copy-start.27 = (f32[4,288]{1,0:T(4,128)S(1)}, f32[4,288]{1,0:T(4,128)}, u32[]{:S(2)}) copy-start(f32[4,288]{1,0:T(4,128)} %get-tuple-element.241) | copy-start | bytes 13828
  234.5 11.3 %collective-permute-start.28 = (bf16[4,4,144,1152]{3,2,1,0:T(8,128)(2,1)}, bf16[4,4,144,1152]{3,2,1,0:T(8,128)(2,1)}, u32[]{:S(2)}, u32[]{:S(2)}) collective-permute-start(bf16[4,4,144,1152]{3,2,1,0:T(8,128)(2,1)} %get-tuple-element.98), channel_id=1, source_target_pairs={{0,4},{4,0},{8,12},{12,8},{16,20},{20,16},{24,28},{28,24},{1,5},{5... | collective-permute-start | bytes 15925256 | tf_op jit(solution)/shard_map/ppermute | solution.py:802
  252.4 34.4 %collective-permute-start.29 = (bf16[2,4,144,1152]{3,2,1,0:T(8,128)(2,1)}, bf16[2,4,144,1152]{3,2,1,0:T(8,128)(2,1)S(1)}, u32[]{:S(2)}, u32[]{:S(2)}) collective-permute-start(bf16[2,4,144,1152]{3,2,1,0:T(8,128)(2,1)} %get-tuple-element.99), channel_id=1, source_target_pairs={{0,16},{4,12},{8,24},{12,4},{16,0},{20,28},{24,8},{28,20},{1,17},{... | collective-permute-start | bytes 7962632 | tf_op jit(solution)/shard_map/ppermute | solution.py:798
  253.9 34.5 %copy-start.13 = (bf16[4,144,1152]{2,1,0:T(8,128)(2,1)S(1)}, bf16[4,144,1152]{2,1,0:T(8,128)(2,1)}, u32[]{:S(2)}) copy-start(bf16[4,144,1152]{2,1,0:T(8,128)(2,1)} %get-tuple-element.105) | copy-start | bytes 3981316
  289.7 18.0 %collective-permute-start.30 = (bf16[4,144,1152]{2,1,0:T(8,128)(2,1)}, bf16[4,144,1152]{2,1,0:T(8,128)(2,1)S(1)}, u32[]{:S(2)}, u32[]{:S(2)}) collective-permute-start(bf16[4,144,1152]{2,1,0:T(8,128)(2,1)} %fusion.9), channel_id=1, source_target_pairs={{0,8},{4,20},{8,0},{12,28},{16,24},{20,4},{24,16},{28,12},{1,9},{5... | collective-permute-start | bytes 3981320 | tf_op jit(solution)/shard_map/ppermute | solution.py:798
  308.8 9.0 %collective-permute-start.31 = (bf16[4,4,144,1152]{3,2,1,0:T(8,128)(2,1)}, bf16[4,4,144,1152]{3,2,1,0:T(8,128)(2,1)S(1)}, u32[]{:S(2)}, u32[]{:S(2)}) collective-permute-start(bf16[4,4,144,1152]{3,2,1,0:T(8,128)(2,1)} %get-tuple-element.112), channel_id=1, source_target_pairs={{0,4},{4,0},{8,12},{12,8},{16,20},{20,16},{24,28},{28,24},{1,5},{5... | collective-permute-start | bytes 15925256 | tf_op jit(solution)/shard_map/ppermute | solution.py:802
  326.8 32.3 %collective-permute-start.32 = (bf16[2,4,144,1152]{3,2,1,0:T(8,128)(2,1)}, bf16[2,4,144,1152]{3,2,1,0:T(8,128)(2,1)}, u32[]{:S(2)}, u32[]{:S(2)}) collective-permute-start(bf16[2,4,144,1152]{3,2,1,0:T(8,128)(2,1)} %get-tuple-element.113), channel_id=1, source_target_pairs={{0,16},{4,12},{8,24},{12,4},{16,0},{20,28},{24,8},{28,20},{1,17},{... | collective-permute-start | bytes 7962632 | tf_op jit(solution)/shard_map/ppermute | solution.py:798
  331.0 28.1 %copy-start.12 = (bf16[4,144,1152]{2,1,0:T(8,128)(2,1)S(1)}, bf16[4,144,1152]{2,1,0:T(8,128)(2,1)}, u32[]{:S(2)}) copy-start(bf16[4,144,1152]{2,1,0:T(8,128)(2,1)} %get-tuple-element.119) | copy-start | bytes 3981316
  361.8 18.0 %collective-permute-start.33 = (bf16[4,144,1152]{2,1,0:T(8,128)(2,1)}, bf16[4,144,1152]{2,1,0:T(8,128)(2,1)S(1)}, u32[]{:S(2)}, u32[]{:S(2)}) collective-permute-start(bf16[4,144,1152]{2,1,0:T(8,128)(2,1)} %fusion.6), channel_id=1, source_target_pairs={{0,8},{4,20},{8,0},{12,28},{16,24},{20,4},{24,16},{28,12},{1,9},{5... | collective-permute-start | bytes 3981320 | tf_op jit(solution)/shard_map/ppermute | solution.py:798
  379.8 9.1 %collective-permute-start.34 = (bf16[4,4,144,1152]{3,2,1,0:T(8,128)(2,1)}, bf16[4,4,144,1152]{3,2,1,0:T(8,128)(2,1)}, u32[]{:S(2)}, u32[]{:S(2)}) collective-permute-start(bf16[4,4,144,1152]{3,2,1,0:T(8,128)(2,1)} %get-tuple-element.125), channel_id=1, source_target_pairs={{0,4},{4,0},{8,12},{12,8},{16,20},{20,16},{24,28},{28,24},{1,5},{5... | collective-permute-start | bytes 15925256 | tf_op jit(solution)/shard_map/ppermute | solution.py:802
  379.9 144.3 %reduce-scatter.6.cloned.1.call-start = ((), (), s32[]{:S(2)}) async-start(), calls=%async_computation.4 | async-start | bytes 1658880 | tf_op jit(solution)/shard_map/reduce_scatter | solution.py:848
  395.8 38.4 %collective-permute-start.35 = (bf16[2,4,144,1152]{3,2,1,0:T(8,128)(2,1)}, bf16[2,4,144,1152]{3,2,1,0:T(8,128)(2,1)S(1)}, u32[]{:S(2)}, u32[]{:S(2)}) collective-permute-start(bf16[2,4,144,1152]{3,2,1,0:T(8,128)(2,1)} %get-tuple-element.126), channel_id=1, source_target_pairs={{0,16},{4,12},{8,24},{12,4},{16,0},{20,28},{24,8},{28,20},{1,17},{... | collective-permute-start | bytes 7962632 | tf_op jit(solution)/shard_map/ppermute | solution.py:798
  396.9 23.2 %copy-start.20 = (bf16[8,1152]{1,0:T(8,128)(2,1)S(1)}, bf16[8,1152]{1,0:T(8,128)(2,1)}, u32[]{:S(2)}) copy-start(bf16[8,1152]{1,0:T(8,128)(2,1)} %copy-done.19) | copy-start | bytes 55300
  411.5 3.7 collective-permute-start.36
  415.3 4.9 collective-permute-start.37
  416.8 109.3 %reduce-scatter.4.cloned.1.call-start = ((), (), s32[]{:S(2)}) async-start(), calls=%async_computation.3 | async-start | bytes 1658880 | tf_op jit(solution)/shard_map/reduce_scatter | solution.py:848
  416.9 18.8 %copy-start.9 = (bf16[4,144,1152]{2,1,0:T(8,128)(2,1)S(1)}, bf16[4,144,1152]{2,1,0:T(8,128)(2,1)}, u32[]{:S(2)}) copy-start(bf16[4,144,1152]{2,1,0:T(8,128)(2,1)} %get-tuple-element.134) | copy-start | bytes 3981316
  421.2 28.8 %collective-permute-start.41 = (bf16[576,576]{0,1:T(8,128)(2,1)S(1)}, bf16[576,576]{0,1:T(8,128)(2,1)S(1)}, u32[]{:S(2)}, u32[]{:S(2)}) collective-permute-start(bf16[576,576]{0,1:T(8,128)(2,1)S(1)} %broadcast_select_fusion), channel_id=1, source_target_pairs={{0,16},{4,20},{8,24},{12,28},{16,0},{20,4},{24,8},{28,12},{1,17},{... | collective-permute-start | bytes 1990664 | tf_op jit(solution)/shard_map/ppermute | solution.py:853
  437.1 28.8 %collective-permute-start.40 = (bf16[4,144,1152]{2,1,0:T(8,128)(2,1)}, bf16[4,144,1152]{2,1,0:T(8,128)(2,1)}, u32[]{:S(2)}, u32[]{:S(2)}) collective-permute-start(bf16[4,144,1152]{2,1,0:T(8,128)(2,1)} %fusion.3), channel_id=1, source_target_pairs={{0,8},{4,20},{8,0},{12,28},{16,24},{20,4},{24,16},{28,12},{1,9},{5... | collective-permute-start | bytes 3981320 | tf_op jit(solution)/shard_map/ppermute | solution.py:798
  451.2 13.4 %collective-permute-start.42 = (bf16[288,576]{0,1:T(8,128)(2,1)}, bf16[288,576]{0,1:T(8,128)(2,1)}, u32[]{:S(2)}, u32[]{:S(2)}) collective-permute-start(bf16[288,576]{0,1:T(8,128)(2,1)} %broadcast_select_fusion.1), channel_id=1, source_target_pairs={{0,8},{4,12},{8,0},{12,4},{16,24},{20,28},{24,16},{28,20},{1,9},{5... | collective-permute-start | bytes 995336 | tf_op jit(solution)/shard_map/ppermute | solution.py:853
  469.3 17.7 %copy-start.14 = (f32[90,128]{1,0:T(8,128)S(1)}, f32[90,128]{1,0:T(8,128)}, u32[]{:S(2)}) copy-start(f32[90,128]{1,0:T(8,128)} %reshape.253) | copy-start | bytes 138244
  487.8 11.7 %collective-permute-start.38 = (f32[290,128]{1,0:T(8,128)S(1)}, f32[290,128]{1,0:T(8,128)S(1)}, u32[]{:S(2)}, u32[]{:S(2)}) collective-permute-start(f32[290,128]{1,0:T(8,128)S(1)} %pad_maximum_fusion.3), channel_id=1, source_target_pairs={{0,1},{1,0},{2,3},{3,2},{4,5},{5,4},{6,7},{7,6},{8,9},{9,8},{10,11... | collective-permute-start | bytes 445448 | tf_op jit(solution)/shard_map/ppermute | solution.py:853
  488.0 20.2 %collective-permute-start.43 = (bf16[144,576]{0,1:T(8,128)(2,1)S(1)}, bf16[144,576]{0,1:T(8,128)(2,1)S(1)}, u32[]{:S(2)}, u32[]{:S(2)}) collective-permute-start(bf16[144,576]{0,1:T(8,128)(2,1)S(1)} %broadcast_select_fusion.2), channel_id=1, source_target_pairs={{0,4},{4,0},{8,12},{12,8},{16,20},{20,16},{24,28},{28,24},{1,5},{5... | collective-permute-start | bytes 497672 | tf_op jit(solution)/shard_map/ppermute | solution.py:853
  500.3 7.8 %collective-permute-start.39 = (f32[290,128]{1,0:T(8,128)S(1)}, f32[290,128]{1,0:T(8,128)S(1)}, u32[]{:S(2)}, u32[]{:S(2)}) collective-permute-start(f32[290,128]{1,0:T(8,128)S(1)} %fusion.27), channel_id=1, source_target_pairs={{0,2},{1,3},{2,0},{3,1},{4,6},{5,7},{6,4},{7,5},{8,10},{9,11},{10,... | collective-permute-start | bytes 445448 | tf_op jit(solution)/shard_map/ppermute | solution.py:853
  508.1 1.4 collective-permute-start.44
  509.6 5.3 collective-permute-start.45
  514.8 4.9 collective-permute-start.46
  (25 other events, 212.1 us)
Sparse Core Ops, SparseCore 0:
  10.2 37.4 all-gather.4
  49.8 54.1 all-gather.6
  380.0 30.5 reduce-scatter.7
  416.9 30.1 reduce-scatter.5
  469.4 35.7 reduce-scatter.3

commit v6 on v5

--- a/solution.py
+++ b/solution.py
@@ -828,12 +828,15 @@
         self.came = swap_core(send)
 
     def near(self, *gates):
-        self.zero, self.one, pair = add_halves(after(self.own, *gates), self.came)
-        self.far = swap(pair, 2)
-        return pair
-
-    def back(self):
-        one = self.one.astype(jnp.float32) + self.far[0].astype(jnp.float32)
+        self.zero, self.one, self.sent = add_halves(after(self.own, *gates), self.came)
+        return self.sent
+
+    def send(self, *gates):
+        self.far = swap(after(self.sent, *gates), 2)
+
+    def back(self, *gates):
+        one = after(self.one, *gates) if gates else self.one
+        one = one.astype(jnp.float32) + self.far[0].astype(jnp.float32)
         one = one.astype(jnp.bfloat16)
         self.last = swap(one, 1)
         return one
@@ -868,6 +871,21 @@
             jnp.concatenate([value, other], axis=0),
         )
     return value
+
+
+def gather_links_first(value, axis):
+    if not is_cube():
+        return lax.all_gather(value, axis, axis=0, tiled=True)
+    bits = lax.axis_size(axis).bit_length() - 1
+    rest = value.shape
+    for done, bit in enumerate(reversed(range(bits))):
+        other = swap_bit(value, axis, bit)
+        value = jnp.where(
+            bit_of(axis, bit),
+            jnp.stack([other, value], axis=done),
+            jnp.stack([value, other], axis=done),
+        )
+    return value.reshape(-1, *rest[1:])
 
 
 def small_scatter(value, axis):
@@ -987,7 +1005,9 @@
     bias = position_bias(offset_index, table)
 
     time_rows = both[:, small.shape[0] :].reshape(groups * count, width)
-    time_weight = small_gather(jnp.concatenate([tquery_weight, tvalue_weight], axis=1), "dp")
+    time_weight = gather_links_first(
+        jnp.concatenate([tquery_weight, tvalue_weight], axis=1), "dp"
+    )
     time_part = small_gather(matmul(time_rows, time_weight)[None], "fsdp")
     time_own = lax.dynamic_slice(
         time_part, (0, own_group * count, 0), (groups, count, 2 * shard_cols)
@@ -1008,10 +1028,10 @@
     if cube:
         part_of, slot_of = part_tables()
         attn_group = lax.all_gather(wire_attn, "fsdp", axis=0, tiled=False)
-        wire_rest = after(jnp.stack([up_weight, wire_down]), both)
-        rest = lax.all_gather(wire_rest, "fsdp", axis=1, tiled=False)
+        up_group = lax.all_gather(after(up_weight, both), "fsdp", axis=0, tiled=False)
+        down_group = lax.all_gather(after(wire_down, both), "fsdp", axis=0, tiled=False)
         attn_move = Gather(after(attn_group, time_weight))
-        up_move = Gather(after(rest[0], bias), attn_move)
+        up_move = Gather(after(up_group, bias), attn_move)
         attn_pieces = attn_move.pieces()
     else:
         part_of = jnp.zeros((1,), jnp.int32)
@@ -1027,7 +1047,7 @@
     )
     if cube:
         up_pieces = up_move.pieces(mixed_split)
-        down_move = Gather(rest[1], up_move, mixed_split)
+        down_move = Gather(down_group, up_move, mixed_split)
         mixed_split = after(mixed_split, down_move.first)
     mixed = mixed_split.transpose(1, 0, 2).reshape(rows, width)
     hidden = x_rows + (matmul(mixed, proj_full) + proj_b)
@@ -1049,6 +1069,7 @@
         )
         down_move = Scatter(own, send)
         grad_cols = after(grad_low, down_move.near(down_full))
+        down_move.send()
     def lines_of(*values):
         return jnp.concatenate([jnp.stack(values), jnp.zeros((8 - len(values), width), wide)])
 
@@ -1058,39 +1079,27 @@
     layer_out = layer_out.reshape(count, tokens, width)
     d_hidden_cols = d_hidden_low
     if cube:
+        d_hidden_cols = after(d_hidden_low, down_move.back())
+    d_packed, pairs, d_time = attend_back(d_hidden_cols, proj_full, qkv, probs)
+    attn_back = attn_full
+    if cube:
+        normed_t = after(normed_low.T, down_move.last)
         own, send = slot_grad(
-            one_grad_kernel,
-            slot_of,
-            [after(second_low.T, down_move.back())],
-            d_pre,
-            parts,
-            "up_grad",
+            pair_grad_kernel, slot_of, [normed_t, mixed.T], d_packed, parts, "pair_grad"
         )
-        up_move = Scatter(own, after(send, down_move.last))
-        d_hidden_cols = after(d_hidden_low, send, down_move.total())
+        attn_move = Scatter(own, after(send, down_move.total()))
+        down_sum = down_move.end()
+        second_t = after(second_low.T, send)
+        own, send = slot_grad(one_grad_kernel, slot_of, [second_t], d_pre, parts, "up_grad")
+        up_move = Scatter(own, send)
+        attn_pair = attn_move.near(send)
+        attn_move.send()
+        attn_back = after(attn_full, up_move.near(attn_pair))
     else:
         grad_down = jnp.concatenate([contract_rows(a, grad_low) for a in activ], axis=0)
         down_sum = scatter_sum(pack_down(grad_down.astype(low), groups, parts, shard_rows))
         grad_up = jnp.stack([contract_rows(second_low, d).astype(low) for d in d_pre])
         up_sum = scatter_sum(grad_up.reshape(wire))
-
-    if cube:
-        d_hidden_cols = after(d_hidden_cols, up_move.near())
-    d_packed, pairs, d_time = attend_back(d_hidden_cols, proj_full, qkv, probs)
-    attn_back = attn_full
-    if cube:
-        normed_t = after(normed_low.T, up_move.back())
-        own, send = slot_grad(
-            pair_grad_kernel, slot_of, [normed_t, mixed.T], d_packed, parts, "pair_grad"
-        )
-        down_sum = down_move.end()
-        attn_move = Scatter(own, after(send, up_move.last))
-        up_total = up_move.total()
-        attn_pair = attn_move.near(up_total)
-        attn_back = after(attn_full, attn_pair)
-        pairs = after(pairs, attn_move.back())
-        attn_total = attn_move.total()
-    else:
         cut = 3 * shard_cols
         grad_attn = jnp.stack(
             [
@@ -1108,7 +1117,16 @@
     )
     images_grad = images_grad.reshape(count, tokens, width)
 
-    d_time = after(d_time, images_grad)
+    if cube:
+        attn_one = attn_move.back(images_grad)
+        up_move.send(attn_one)
+        pairs = after(pairs, attn_one)
+    table_sum = table_gradient(offset_index, pairs)
+    if cube:
+        d_time = after(d_time, table_sum)
+        attn_total = attn_move.total(table_sum)
+        up_one = up_move.back()
+        up_total = up_move.total()
     d_time = jnp.concatenate(
         [d_time[:, :, :shard_cols], d_time[:, :, 2 * shard_cols : 3 * shard_cols]], axis=2
     ).astype(low)
@@ -1117,10 +1135,12 @@
     d_time_cols = lax.dynamic_slice(
         d_time_rows, (0, own_group * 2 * shard_cols), (groups * count, 2 * shard_cols)
     )
-    time_grads = small_scatter(contract_rows(time_rows, d_time_cols).astype(low), "dp")
+    time_grads = contract_rows(time_rows, d_time_cols).astype(low)
+    if cube:
+        time_grads = after(time_grads, up_total)
+    time_grads = small_scatter(time_grads, "dp")
     back = times_transposed(d_time_cols, time_weight).reshape(-1, LANES)
 
-    table_sum = table_gradient(offset_index, pairs)
     vectors = jnp.concatenate(
         [down_sums[:4], input_sums[:2], up_sums.reshape(groups, width)]
     ).reshape(-1, LANES)
@@ -1130,7 +1150,10 @@
     time_grad = lax.dynamic_slice(
         flat[ends[1] :].reshape(groups * count, width), (own_group * count, 0), (count, width)
     )
-    flat = small_sum(flat[: ends[1]], "dp")
+    flat = flat[: ends[1]]
+    if cube:
+        flat = after(flat, attn_total, up_one)
+    flat = small_sum(flat, "dp")
     vectors = flat[: ends[0]].reshape(-1, width)
     own = lax.dynamic_slice(vectors, (0, own_group * shard_cols), (6, shard_cols))
     proj_bg, gain2_g, shift2_g, down_bg, gain1_g, shift1_g = (own[i] for i in range(6))
@@ -1141,9 +1164,9 @@
     table_grad = table_grad.reshape(group_heads, 8 * LANES)[:, :table_rows]
 
     if cube:
-        down_sum = after(down_sum, attn_total)
-        up_sum = after(up_move.end(), attn_total)
-        attn_sum = attn_move.end()
+        down_sum = after(down_sum, up_total)
+        attn_sum = after(attn_move.end(), up_total)
+        up_sum = up_move.end()
     time_grads = time_grads.astype(wide)
     tquery_grad, tvalue_grad = time_grads[:, :shard_cols], time_grads[:, shard_cols:]
     attn_sum = attn_sum.astype(wide)

time: 540 us -> 483 us (0.89)
  local copies, waits for them, and re-layouts: 54.9 us -> 27.1 us
  waiting for transfers between devices: 167 us -> 140 us
    ppermute x17, waiting for transfers between devices: 84.9 us -> 64.5 us  [swap_bit(): return lax.ppermute(value, axis, [(i, i ^ 1 << bit) for i in range(size)])]
    ppermute x15, waiting for transfers between devices: 16.8 us -> 1.84 us  [swap_core(): return lax.ppermute(value, 'dp', [(i, i ^ 1) for i in range(8)])]
    all_gather x1, waiting for transfers between devices: 0.02 us -> 14.6 us  [body(): attn_group = lax.all_gather(wire_attn, 'fsdp', axis=0, tiled=False)]
    unnamed x88 -> x106, local copies, waits for them, and re-layouts: 16.9 us -> 6.88 us
    all_gather x1 -> x2, waiting for transfers between devices: 15.5 us -> 5.57 us  [the longest x1 5.57 us: body(): lax.all_gather(after(wire_down, both), 'fsdp', axis=0, tiled=False)]
    slice x2 -> x1, local copies, waits for them, and re-layouts: 7.99 us -> 0.01 us  [body(): flat = flat[:ends[1]]]
  transfers between devices with their start and end apart: 52 -> 53, of which waited for: 27 -> 25; matrix products, arithmetic and copies ran while one was open for 15% -> 11% of each run, Pallas kernels for 35% -> 37%
where the time goes in v6:
time: 483 us; the launch traced here: 478 us
  Pallas kernels  217 us (45%)
  waiting for transfers between devices  140 us (29%)
  starting transfers between devices  41.2 us (9%)
  other arithmetic  32 us (7%)
  local copies, waits for them, and re-layouts  27.1 us (6%)
  between operations  15.3 us (3%)
  matrix products  5.66 us (1%)
    ppermute x17, waiting for transfers between devices, swap_bit(): return lax.ppermute(value, axis, [(i, i ^ 1 << bit) for i in range(size)])  64.5 us
    ppermute x15, waiting for transfers between devices, swap(): lax.ppermute(value, 'dp', [(i, i ^ NEAR[i & 1][hop]) for i in range(8)])  53.4 us
    pallas_call x2, Pallas kernels, piece_call(): pl.pallas_call(kernel, grid_spec=pltpu.PrefetchScalarGridSpec(num_scalar_...  35.5 us
    pallas_call x1, Pallas kernels, down_back(): pl.pallas_call(down_back_kernel, grid=(groups,), in_specs=[whole, whole,...  33.1 us
    pallas_call x2, Pallas kernels, slot_grad(): pl.pallas_call(kernel, grid_spec=pltpu.PrefetchScalarGridSpec(num_scalar_...  26.3 us
    pallas_call x1, Pallas kernels, attend_back(): pl.pallas_call(attend_back_kernel, grid=(groups,), in_specs=[pl.BlockSpec...  21.9 us
    pallas_call x3, Pallas kernels, add_halves(): pl.pallas_call(add_kernel, grid=(groups,), in_specs=[pl.BlockSpec((1, 1,...  20.3 us
    pallas_call x1, Pallas kernels, position_bias(): pl.pallas_call(bias_kernel, grid=(4,), in_specs=[pl.BlockSpec((tokens, to...  20.1 us
  transfers between devices with their start and end apart: 53, of which 25 were waited for; matrix products, arithmetic and copies ran while one was open for 11% of the time, Pallas kernels for 37%

profile of v6, /device:TPU:0, one launch (start us, length us, event | category | flops | bytes accessed | tf_op | source)
XLA Modules:
  0.0 478.0 jit_solution(14217072730377997934)
XLA Ops:
  7.3 2.0 concatenate.137
  10.4 3.1 collective-permute-start.2
  14.5 3.6 collective-permute-done.2
  18.2 1.8 collective-permute-start.3
  20.2 7.8 %collective-permute-done.3 = bf16[2,144,576]{2,1,0:T(8,128)(2,1)S(1)} collective-permute-done((bf16[2,144,576]{2,1,0:T(8,128)(2,1)S(1)}, bf16[2,144,576]{2,1,0:T(8,128)(2,1)S(1)}, u32[]{:S(2)}, u32[]{:S(2)}) %collective-permute-start.3) | collective-permute-done | bytes 331808 | tf_op jit(solution)/shard_map/ppermute | solution.py:856
  28.7 1.8 collective-permute-done.4
  31.1 14.6 %all-gather.7.cloned.1.call-done = bf16[576,1152]{1,0:T(8,128)(2,1)} async-done(((bf16[144,1152]{1,0:T(8,128)(2,1)}), bf16[576,1152]{1,0:T(8,128)(2,1)}) %all-gather.7.cloned.1.call-update) | async-done | bytes 1327120 | tf_op jit(solution)/shard_map/all_gather | solution.py:1030
  45.7 1.5 collective-permute-start.7
  49.4 2.0 collective-permute-done
  51.4 1.6 collective-permute-start.1
  53.3 3.2 collective-permute-done.1
  58.0 1.5 collective-permute-start.8
  59.5 10.8 %collective-permute-done.7.refs_1_ = bf16[4,144,1152]{2,1,0:T(8,128)(2,1)} collective-permute-done((bf16[4,144,1152]{2,1,0:T(8,128)(2,1)}, bf16[4,144,1152]{2,1,0:T(8,128)(2,1)}, u32[]{:S(2)}, u32[]{:S(2)}) %collective-permute-start.7) | collective-permute-done | bytes 1327136 | tf_op jit(solution)/shard_map/ppermute | solution.py:798
  70.2 2.5 collective-permute-start.9
  72.7 20.1 %position_bias.1.bias_ref = f32[16,256,256]{2,1,0:T(8,128)} custom-call(s32[256,256]{1,0:T(8,128)} %index_ref.3, f32[16,1,1024]{2,1,0:T(1,128)} %reshape.453.table_ref), custom_call_target="tpu_custom_call" | custom-call | flops 20000000000 | bytes 1 | tf_op jit(solution)/shard_map/position_bias/pallas_call | solution.py:111
  99.3 1.7 collective-permute-done.5
  103.5 5.1 %collective-permute-done.6 = f32[2,8,576]{2,1,0:T(8,128)S(1)} collective-permute-done((f32[2,8,576]{2,1,0:T(8,128)S(1)}, f32[2,8,576]{2,1,0:T(8,128)S(1)}, u32[]{:S(2)}, u32[]{:S(2)}) %collective-permute-start.6) | collective-permute-done | bytes 36896 | tf_op jit(solution)/shard_map/ppermute | solution.py:856
  108.6 7.9 %collective-permute-done.16.refs_1_ = bf16[4,144,1152]{2,1,0:T(8,128)(2,1)} collective-permute-done((bf16[4,144,1152]{2,1,0:T(8,128)(2,1)}, bf16[4,144,1152]{2,1,0:T(8,128)(2,1)}, u32[]{:S(2)}, u32[]{:S(2)}) %collective-permute-start.16) | collective-permute-done | bytes 1327136 | tf_op jit(solution)/shard_map/ppermute | solution.py:798
  116.6 1.4 fusion.34
  119.6 1.5 fusion.13.normed_ref
  121.3 5.6 %all-gather.9.cloned.1.call-done = bf16[576,1152]{1,0:T(8,128)(2,1)} async-done(((bf16[144,1152]{1,0:T(8,128)(2,1)}), bf16[576,1152]{1,0:T(8,128)(2,1)}) %all-gather.9.cloned.1.call-update) | async-done | bytes 1327120 | tf_op jit(solution)/shard_map/all_gather | solution.py:1032
  126.9 1.5 collective-permute-start.15
  129.6 21.0 %attend.1 = (bf16[4,512,896]{2,1,0:T(8,128)(2,1)}, bf16[4,2,4,256,256]{4,3,2,1,0:T(8,128)(2,1)}, bf16[4,512,288]{2,1,0:T(8,128)(2,1)}, bf16[1152,1152]{1,0:T(8,128)(2,1)}, bf16[4,1152,1152]{2,1,0:T(8,128)(2,1)}) custom-call(s32[8]{0:T(128)} %fusion.27.part_ref, bf16[512,1152]{1,0:T(8,128)(2,1)} %fusion.13.normed_ref, ...), custom_call_target="tpu_custom_call" | custom-call | flops 12999999488 | bytes 1 | tf_op jit(solution)/shard_map/attend/pallas_call | solution.py:228
  150.6 3.4 collective-permute-start.21
  154.0 2.5 collective-permute-done.15.refs_1_
  156.5 3.0 copy.69
  159.5 4.2 fusion.37
  164.1 1.7 copy-done.41
  165.9 1.5 collective-permute-start.23
  167.4 1.5 add_convert_fusion.second_ref
  169.0 14.5 %up_forward.1 = (bf16[4,512,1152]{2,1,0:T(8,128)(2,1)}, bf16[4,512,1152]{2,1,0:T(8,128)(2,1)}, bf16[4,1152,1152]{2,1,0:T(8,128)(2,1)}) custom-call(s32[8]{0:T(128)} %fusion.27.part_ref, bf16[512,1152]{1,0:T(8,128)(2,1)} %add_convert_fusion.second_ref, f32[4,1,1152]{2,1,0:T(1,128)} %reshape.458.bias_ref, bf16[4,144,1152]{2,1,0:T(8,128)(2,1)} %bitcast.20.refs_0_, ...), custom_call_target="tpu_custom_call" | custom-call | flops 12999999488 | bytes 1 | tf_op jit(solution)/shard_map/up_forward/pallas_call | solution.py:228
  184.1 4.6 collective-permute-done.23.refs_3_
  190.0 1.8 collective-permute-done.27.refs_7_
  192.9 18.6 %down_grad.1 = (bf16[4,4,144,1152]{3,2,1,0:T(8,128)(2,1)}, bf16[4,4,144,1152]{3,2,1,0:T(8,128)(2,1)}) custom-call(s32[8]{0:T(128)} %fusion.26.slot_ref, bf16[4,512,1152]{2,1,0:T(8,128)(2,1)} %get-tuple-element.101.left_ref.activ_ref, bf16[512,1152]{1,0:T(8,128)(2,1)} %bitcast.124), custom_call_target="tpu_custom_call" | custom-call | flops 17999998976 | bytes 1 | tf_op jit(solution)/shard_map/down_grad/pallas_call | solution.py:690
  213.8 8.9 %unpack_pieces.1.down_ref = bf16[4608,1152]{1,0:T(8,128)(2,1)} custom-call(s32[8]{0:T(128)} %fusion.27.part_ref, bf16[4,144,1152]{2,1,0:T(8,128)(2,1)} %bitcast.19.refs_0_, bf16[4,144,1152]{2,1,0:T(8,128)(2,1)} %copy-done.40, bf16[4,144,1152]{2,1,0:T(8,128)(2,1)} %collective-permute-done.22.refs_2_, bf16[4,144,1152]{2,1,0:T(8,128)(2,1)} %copy-done.42, ...), custom_call_target="tpu_custom_call" | custom-call | flops 8999999488 | bytes 1 | tf_op jit(solution)/shard_map/unpack_pieces/pallas_call | solution.py:757
  222.7 6.6 %add_halves.3 = (bf16[4,144,1152]{2,1,0:T(8,128)(2,1)}, bf16[4,144,1152]{2,1,0:T(8,128)(2,1)}, bf16[2,4,144,1152]{3,2,1,0:T(8,128)(2,1)}) custom-call(bf16[4,4,144,1152]{3,2,1,0:T(8,128)(2,1)} %get-tuple-element.103.one_ref.two_ref.three_ref.four_ref, bf16[4,4,144,1152]{3,2,1,0:T(8,128)(2,1)} %get-tuple-element.103.one_ref.two_ref.three_ref.four_ref, ...), custom_call_target="tpu_custom_call" | custom-call | flops 7000000000 | bytes 1 | tf_op jit(solution)/shard_map/add_halves/pallas_call | solution.py:721
  229.4 33.1 %down_back.1 = (bf16[4,512,1152]{2,1,0:T(8,128)(2,1)}, bf16[512,1152]{1,0:T(8,128)(2,1)}, f32[512,1152]{1,0:T(8,128)}, bf16[512,1152]{1,0:T(8,128)(2,1)}, f32[8,1152]{1,0:T(8,128)}, /*index=5*/f32[4,1,1152]{2,1,0:T(1,128)}) custom-call(bf16[512,1152]{1,0:T(8,128)(2,1)} %bitcast.125, f32[512,1152]{1,0:T(8,128)} %copy-done, ...), custom_call_target="tpu_custom_call" | custom-call | flops 32999999488 | bytes 1 | tf_op jit(solution)/shard_map/down_back/pallas_call | solution.py:429
  262.5 1.6 fusion.9
  265.3 21.9 %attend_back.1 = (bf16[4,512,1152]{2,1,0:T(8,128)(2,1)}, f32[16,256,256]{2,1,0:T(8,128)}, f32[4,2,864]{2,1,0:T(2,128)}) custom-call(bf16[512,1152]{1,0:T(8,128)(2,1)} %get-tuple-element.112.hidden_ref, bf16[1152,1152]{1,0:T(8,128)(2,1)} %get-tuple-element.93.proj_ref, bf16[4,512,896]{2,1,0:T(8,128)(2,1)} %get-tuple-element.113.qkv_ref, ...), custom_call_target="tpu_custom_call" | custom-call | flops 19000000512 | bytes 1 | tf_op jit(solution)/shard_map/attend_back/pallas_call | solution.py:514
  287.2 1.4 copy.70.one_ref
  288.6 14.1 %pair_grad.1 = (bf16[4,4,144,1152]{3,2,1,0:T(8,128)(2,1)}, bf16[4,4,144,1152]{3,2,1,0:T(8,128)(2,1)}) custom-call(s32[8]{0:T(128)} %fusion.26.slot_ref, bf16[1152,512]{1,0:T(8,128)(2,1)} %copy.70.one_ref, bf16[1152,512]{1,0:T(8,128)(2,1)} %bitcast.104, bf16[4,512,1152]{2,1,0:T(8,128)(2,1)} %get-tuple-element.115.right_ref), custom_call_target="tpu_custom_call" | custom-call | flops 17999998976 | bytes 1 | tf_op jit(solution)/shard_map/pair_grad/pallas_call | solution.py:650
  302.7 2.9 fusion.8
  307.2 12.2 %up_grad.1 = (bf16[4,4,144,1152]{3,2,1,0:T(8,128)(2,1)}, bf16[4,4,144,1152]{3,2,1,0:T(8,128)(2,1)}) custom-call(s32[8]{0:T(128)} %fusion.26.slot_ref, bf16[1152,512]{1,0:T(8,128)(2,1)} %copy.71.one_ref, bf16[4,512,1152]{2,1,0:T(8,128)(2,1)} %get-tuple-element.120.right_ref), custom_call_target="tpu_custom_call" | custom-call | flops 17999998976 | bytes 1 | tf_op jit(solution)/shard_map/up_grad/pallas_call | solution.py:650
  319.6 6.7 %add_halves.4 = (bf16[4,144,1152]{2,1,0:T(8,128)(2,1)}, bf16[4,144,1152]{2,1,0:T(8,128)(2,1)}, bf16[2,4,144,1152]{3,2,1,0:T(8,128)(2,1)}) custom-call(bf16[4,4,144,1152]{3,2,1,0:T(8,128)(2,1)} %get-tuple-element.124.one_ref.two_ref.three_ref.four_ref, bf16[4,4,144,1152]{3,2,1,0:T(8,128)(2,1)} %get-tuple-element.124.one_ref.two_ref.three_ref.four_ref, ...), custom_call_target="tpu_custom_call" | custom-call | flops 7000000000 | bytes 1 | tf_op jit(solution)/shard_map/add_halves/pallas_call | solution.py:721
  326.3 2.0 collective-permute-start.33
  329.1 7.0 %add_halves.5 = (bf16[4,144,1152]{2,1,0:T(8,128)(2,1)}, bf16[4,144,1152]{2,1,0:T(8,128)(2,1)}, bf16[2,4,144,1152]{3,2,1,0:T(8,128)(2,1)}) custom-call(bf16[4,4,144,1152]{3,2,1,0:T(8,128)(2,1)} %get-tuple-element.128.one_ref.two_ref.three_ref.four_ref, bf16[4,4,144,1152]{3,2,1,0:T(8,128)(2,1)} %get-tuple-element.128.one_ref.two_ref.three_ref.four_ref, ...), custom_call_target="tpu_custom_call" | custom-call | flops 7000000000 | bytes 1 | tf_op jit(solution)/shard_map/add_halves/pallas_call | solution.py:721
  336.1 14.4 %input_grad.1 = (bf16[512,1152]{1,0:T(8,128)(2,1)}, f32[8,1152]{1,0:T(8,128)}) custom-call(bf16[4,512,1152]{2,1,0:T(8,128)(2,1)} %get-tuple-element.115.right_ref, bf16[4,1152,1152]{2,1,0:T(8,128)(2,1)} %get-tuple-element.130.weight_ref, bf16[512,1152]{1,0:T(8,128)(2,1)} %bitcast.98, f32[512,1152]{1,0:T(8,128)} %get-tuple-element.131.d_hidden_ref, ...), custom_call_target="tpu_custom_call" | custom-call | flops 12999999488 | bytes 1 | tf_op jit(solution)/shard_map/input_grad/pallas_call | solution.py:581
  351.3 7.2 %collective-permute-done.33 = bf16[2,4,144,1152]{3,2,1,0:T(8,128)(2,1)S(1)} collective-permute-done((bf16[2,4,144,1152]{3,2,1,0:T(8,128)(2,1)}, bf16[2,4,144,1152]{3,2,1,0:T(8,128)(2,1)S(1)}, u32[]{:S(2)}, u32[]{:S(2)}) %collective-permute-start.33) | collective-permute-done | bytes 2654240 | tf_op jit(solution)/shard_map/ppermute | solution.py:798
  360.8 2.0 collective-permute-start.39
  362.8 17.6 %table_gradient.1 = f32[128,128]{1,0:T(8,128)} custom-call(s32[256,256]{1,0:T(8,128)} %index_ref.3, f32[16,256,256]{2,1,0:T(8,128)} %get-tuple-element.139.pairs_ref), custom_call_target="tpu_custom_call" | custom-call | flops 17999998976 | bytes 1 | tf_op jit(solution)/shard_map/table_gradient/pallas_call | solution.py:167
  381.2 11.1 %collective-permute-done.38 = bf16[4,144,1152]{2,1,0:T(8,128)(2,1)} collective-permute-done((bf16[4,144,1152]{2,1,0:T(8,128)(2,1)}, bf16[4,144,1152]{2,1,0:T(8,128)(2,1)}, u32[]{:S(2)}, u32[]{:S(2)}) %collective-permute-start.38) | collective-permute-done | bytes 1327136 | tf_op jit(solution)/shard_map/ppermute | solution.py:798
  392.2 3.3 fusion.5
  395.6 9.3 %collective-permute-done.39 = bf16[2,4,144,1152]{3,2,1,0:T(8,128)(2,1)} collective-permute-done((bf16[2,4,144,1152]{3,2,1,0:T(8,128)(2,1)}, bf16[2,4,144,1152]{3,2,1,0:T(8,128)(2,1)}, u32[]{:S(2)}, u32[]{:S(2)}) %collective-permute-start.39) | collective-permute-done | bytes 2654240 | tf_op jit(solution)/shard_map/ppermute | solution.py:798
  404.9 3.2 fusion.1
  409.9 5.6 %collective-permute-done.35 = bf16[4,2304]{1,0:T(4,128)(2,1)S(1)} collective-permute-done((bf16[4,2304]{1,0:T(4,128)(2,1)S(1)}, bf16[4,2304]{1,0:T(4,128)(2,1)S(1)}, u32[]{:S(2)}, u32[]{:S(2)}) %collective-permute-start.35) | collective-permute-done | bytes 18464 | tf_op jit(solution)/shard_map/ppermute | solution.py:856
  416.9 8.7 %collective-permute-done.36 = f32[290,128]{1,0:T(8,128)S(1)} collective-permute-done((f32[290,128]{1,0:T(8,128)S(1)}, f32[290,128]{1,0:T(8,128)S(1)}, u32[]{:S(2)}, u32[]{:S(2)}) %collective-permute-start.36) | collective-permute-done | bytes 148512 | tf_op jit(solution)/shard_map/ppermute | solution.py:856
  426.8 3.3 fusion.3
  430.4 1.7 collective-permute-start.41
  432.1 3.6 collective-permute-done.37
  438.4 3.9 collective-permute-done.45
  442.4 1.5 collective-permute-start.46
  444.5 6.8 %collective-permute-done.46 = f32[218,128]{1,0:T(8,128)S(1)} collective-permute-done((f32[218,128]{1,0:T(8,128)S(1)}, f32[218,128]{1,0:T(8,128)S(1)}, u32[]{:S(2)}, u32[]{:S(2)}) %collective-permute-start.46) | collective-permute-done | bytes 111648 | tf_op jit(solution)/shard_map/ppermute | solution.py:856
  456.3 8.9 %collective-permute-done.42 = bf16[288,576]{0,1:T(8,128)(2,1)S(1)} collective-permute-done((bf16[288,576]{0,1:T(8,128)(2,1)S(1)}, bf16[288,576]{0,1:T(8,128)(2,1)S(1)}, u32[]{:S(2)}, u32[]{:S(2)}) %collective-permute-start.42) | collective-permute-done | bytes 331808 | tf_op jit(solution)/shard_map/ppermute | solution.py:856
  469.0 1.9 bitcast_convert_fusion
  (284 shorter events, 49.6 us)
Async XLA Ops:
  7.2 38.5 %all-gather.7.cloned.1.call-start = ((), (), s32[]{:S(2)}) async-start(), calls=%async_computation.6 | async-start | bytes 1658880 | tf_op jit(solution)/shard_map/all_gather | solution.py:1030
  9.3 83.5 %all-gather.11.cloned.1.call-start = ((), (), s32[]{:S(2)}) async-start(), calls=%async_computation.8 | async-start | bytes 1658880 | tf_op jit(solution)/shard_map/all_gather | solution.py:1031
  10.4 7.7 %collective-permute-start.2 = (bf16[144,576]{1,0:T(8,128)(2,1)S(1)}, bf16[144,576]{1,0:T(8,128)(2,1)S(1)}, u32[]{:S(2)}, u32[]{:S(2)}) collective-permute-start(bf16[144,576]{1,0:T(8,128)(2,1)S(1)} %pad_maximum_fusion.1), channel_id=1, source_target_pairs={{0,16},{4,20},{8,24},{12,28},{16,0},{20,4},{24,8},{28,12},{1,17},{... | collective-permute-start | bytes 497672 | tf_op jit(solution)/shard_map/ppermute | solution.py:856
  18.2 9.8 %collective-permute-start.3 = (bf16[2,144,576]{2,1,0:T(8,128)(2,1)S(1)}, bf16[2,144,576]{2,1,0:T(8,128)(2,1)S(1)}, u32[]{:S(2)}, u32[]{:S(2)}) collective-permute-start(bf16[2,144,576]{2,1,0:T(8,128)(2,1)S(1)} %maximum_select_fusion.3), channel_id=1, source_target_pairs={{0,8},{4,12},{8,0},{12,4},{16,24},{20,28},{24,16},{28,20},{1,9},{5... | collective-permute-start | bytes 995336 | tf_op jit(solution)/shard_map/ppermute | solution.py:856
  28.2 2.3 collective-permute-start.4
  31.0 22.0 %copy-start.1 = (bf16[2,256,1152]{2,1,0:T(8,128)(2,1)S(1)}, bf16[2,256,1152]{2,1,0:T(8,128)(2,1)}, u32[]{:S(2)}) copy-start(bf16[2,256,1152]{2,1,0:T(8,128)(2,1)} %param.23) | copy-start | bytes 3538948
  31.1 65.7 %copy-start.2 = (bf16[2,2,2,144,576]{4,3,2,1,0:T(8,128)(2,1)}, bf16[2,2,2,144,576]{4,3,2,1,0:T(8,128)(2,1)S(1)}, u32[]{:S(2)}) copy-start(bf16[2,2,2,144,576]{4,3,2,1,0:T(8,128)(2,1)S(1)} %copy.64) | copy-start | bytes 3981316
  45.7 24.5 %collective-permute-start.7 = (bf16[4,144,1152]{2,1,0:T(8,128)(2,1)}, bf16[4,144,1152]{2,1,0:T(8,128)(2,1)}, u32[]{:S(2)}, u32[]{:S(2)}) collective-permute-start(bf16[4,144,1152]{2,1,0:T(8,128)(2,1)} %bitcast.120), channel_id=1, source_target_pairs={{0,8},{4,20},{8,0},{12,28},{16,24},{20,4},{24,16},{28,12},{1,9},{5... | collective-permute-start | bytes 3981320 | tf_op jit(solution)/shard_map/ppermute | solution.py:798
  47.6 3.8 collective-permute-start
  51.4 5.0 %collective-permute-start.1 = (bf16[2,74,128]{2,1,0:T(8,128)(2,1)S(1)}, bf16[2,74,128]{2,1,0:T(8,128)(2,1)S(1)}, u32[]{:S(2)}, u32[]{:S(2)}) collective-permute-start(bf16[2,74,128]{2,1,0:T(8,128)(2,1)S(1)} %maximum_select_fusion.6), channel_id=1, source_target_pairs={{0,2},{1,3},{2,0},{3,1},{4,6},{5,7},{6,4},{7,5},{8,10},{9,11},{10,... | collective-permute-start | bytes 113672 | tf_op jit(solution)/shard_map/ppermute | solution.py:856
  56.5 70.4 %all-gather.9.cloned.1.call-start = ((), (), s32[]{:S(2)}) async-start(), calls=%async_computation.7 | async-start | bytes 1658880 | tf_op jit(solution)/shard_map/all_gather | solution.py:1032
  58.0 36.2 %copy-start.16 = (bf16[144,288]{0,1:T(8,128)(2,1)S(1)}, bf16[144,288]{0,1:T(8,128)(2,1)}, u32[]{:S(2)}) copy-start(bf16[144,288]{0,1:T(8,128)(2,1)} %get-tuple-element.219) | copy-start | bytes 248836
  58.0 34.9 %collective-permute-start.8 = (bf16[4,144,1152]{2,1,0:T(8,128)(2,1)}, bf16[4,144,1152]{2,1,0:T(8,128)(2,1)}, u32[]{:S(2)}, u32[]{:S(2)}) collective-permute-start(bf16[4,144,1152]{2,1,0:T(8,128)(2,1)} %bitcast.121), channel_id=1, source_target_pairs={{0,16},{4,12},{8,24},{12,4},{16,0},{20,28},{24,8},{28,20},{1,17},{... | collective-permute-start | bytes 3981320 | tf_op jit(solution)/shard_map/ppermute | solution.py:798
  70.2 31.7 %collective-permute-start.9 = (bf16[4,144,1152]{2,1,0:T(8,128)(2,1)}, bf16[4,144,1152]{2,1,0:T(8,128)(2,1)}, u32[]{:S(2)}, u32[]{:S(2)}) collective-permute-start(bf16[4,144,1152]{2,1,0:T(8,128)(2,1)} %collective-permute-done.7.refs_1_), channel_id=1, source_target_pairs={{0,16},{4,12},{8,24},{12,4},{16,0},{20,28},{24,8},{28,20},{1,17},{... | collective-permute-start | bytes 3981320 | tf_op jit(solution)/shard_map/ppermute | solution.py:798
  92.8 23.7 %collective-permute-start.16 = (bf16[4,144,1152]{2,1,0:T(8,128)(2,1)}, bf16[4,144,1152]{2,1,0:T(8,128)(2,1)}, u32[]{:S(2)}, u32[]{:S(2)}) collective-permute-start(bf16[4,144,1152]{2,1,0:T(8,128)(2,1)} %bitcast.20.refs_0_), channel_id=1, source_target_pairs={{0,8},{4,20},{8,0},{12,28},{16,24},{20,4},{24,16},{28,12},{1,9},{5... | collective-permute-start | bytes 3981320 | tf_op jit(solution)/shard_map/ppermute | solution.py:798
  96.1 357.2 %reduce-scatter.8.cloned.1.call-start = ((), (), s32[]{:S(2)}) async-start(), calls=%async_computation.5 | async-start | bytes 1658880 | tf_op jit(solution)/shard_map/reduce_scatter | solution.py:851
  96.8 53.8 %copy-start.19 = (bf16[8,1152]{1,0:T(8,128)(2,1)}, bf16[8,1152]{1,0:T(8,128)(2,1)S(1)}, u32[]{:S(2)}) copy-start(bf16[8,1152]{1,0:T(8,128)(2,1)S(1)} %reshape.434) | copy-start | bytes 55300
  97.1 3.8 collective-permute-start.5
  100.9 7.7 %collective-permute-start.6 = (f32[2,8,576]{2,1,0:T(8,128)S(1)}, f32[2,8,576]{2,1,0:T(8,128)S(1)}, u32[]{:S(2)}, u32[]{:S(2)}) collective-permute-start(f32[2,8,576]{2,1,0:T(8,128)S(1)} %maximum_select_fusion.7), channel_id=1, source_target_pairs={{0,2},{1,3},{2,0},{3,1},{4,6},{5,7},{6,4},{7,5},{8,10},{9,11},{10,... | collective-permute-start | bytes 110600 | tf_op jit(solution)/shard_map/ppermute | solution.py:856
  101.9 25.0 %collective-permute-start.10 = (bf16[4,144,1152]{2,1,0:T(8,128)(2,1)}, bf16[4,144,1152]{2,1,0:T(8,128)(2,1)}, u32[]{:S(2)}, u32[]{:S(2)}) collective-permute-start(bf16[4,144,1152]{2,1,0:T(8,128)(2,1)} %bitcast.122), channel_id=1, source_target_pairs={{0,4},{4,0},{8,12},{12,8},{16,20},{20,16},{24,28},{28,24},{1,5},{5... | collective-permute-start | bytes 3981320 | tf_op jit(solution)/shard_map/ppermute | solution.py:802
  101.9 19.3 %collective-permute-start.14 = (bf16[4,144,1152]{2,1,0:T(8,128)(2,1)}, bf16[4,144,1152]{2,1,0:T(8,128)(2,1)}, u32[]{:S(2)}, u32[]{:S(2)}) collective-permute-start(bf16[4,144,1152]{2,1,0:T(8,128)(2,1)} %bitcast.20.refs_0_), channel_id=1, source_target_pairs={{0,16},{4,12},{8,24},{12,4},{16,0},{20,28},{24,8},{28,20},{1,17},{... | collective-permute-start | bytes 3981320 | tf_op jit(solution)/shard_map/ppermute | solution.py:798
  102.7 26.4 %collective-permute-start.11 = (bf16[4,144,1152]{2,1,0:T(8,128)(2,1)}, bf16[4,144,1152]{2,1,0:T(8,128)(2,1)}, u32[]{:S(2)}, u32[]{:S(2)}) collective-permute-start(bf16[4,144,1152]{2,1,0:T(8,128)(2,1)} %collective-permute-done.7.refs_1_), channel_id=1, source_target_pairs={{0,4},{4,0},{8,12},{12,8},{16,20},{20,16},{24,28},{28,24},{1,5},{5... | collective-permute-start | bytes 3981320 | tf_op jit(solution)/shard_map/ppermute | solution.py:802
  108.6 20.5 %collective-permute-start.12 = (bf16[4,144,1152]{2,1,0:T(8,128)(2,1)}, bf16[4,144,1152]{2,1,0:T(8,128)(2,1)}, u32[]{:S(2)}, u32[]{:S(2)}) collective-permute-start(bf16[4,144,1152]{2,1,0:T(8,128)(2,1)} %collective-permute-done.8.refs_2_), channel_id=1, source_target_pairs={{0,4},{4,0},{8,12},{12,8},{16,20},{20,16},{24,28},{28,24},{1,5},{5... | collective-permute-start | bytes 3981320 | tf_op jit(solution)/shard_map/ppermute | solution.py:802
  116.5 13.0 %collective-permute-start.13 = (bf16[4,144,1152]{2,1,0:T(8,128)(2,1)}, bf16[4,144,1152]{2,1,0:T(8,128)(2,1)}, u32[]{:S(2)}, u32[]{:S(2)}) collective-permute-start(bf16[4,144,1152]{2,1,0:T(8,128)(2,1)} %collective-permute-done.9.refs_3_), channel_id=1, source_target_pairs={{0,4},{4,0},{8,12},{12,8},{16,20},{20,16},{24,28},{28,24},{1,5},{5... | collective-permute-start | bytes 3981320 | tf_op jit(solution)/shard_map/ppermute | solution.py:802
  118.0 32.6 %copy-start.22 = (f32[4,288]{1,0:T(4,128)}, f32[4,288]{1,0:T(4,128)S(1)}, u32[]{:S(2)}) copy-start(f32[4,288]{1,0:T(4,128)S(1)} %get-tuple-element.234) | copy-start | bytes 13828
  121.2 29.4 %collective-permute-start.17 = (bf16[4,144,1152]{2,1,0:T(8,128)(2,1)}, bf16[4,144,1152]{2,1,0:T(8,128)(2,1)}, u32[]{:S(2)}, u32[]{:S(2)}) collective-permute-start(bf16[4,144,1152]{2,1,0:T(8,128)(2,1)} %collective-permute-done.16.refs_1_), channel_id=1, source_target_pairs={{0,16},{4,12},{8,24},{12,4},{16,0},{20,28},{24,8},{28,20},{1,17},{... | collective-permute-start | bytes 3981320 | tf_op jit(solution)/shard_map/ppermute | solution.py:798
  126.9 29.6 %collective-permute-start.15 = (bf16[4,144,1152]{2,1,0:T(8,128)(2,1)}, bf16[4,144,1152]{2,1,0:T(8,128)(2,1)S(1)}, u32[]{:S(2)}, u32[]{:S(2)}) collective-permute-start(bf16[4,144,1152]{2,1,0:T(8,128)(2,1)} %bitcast.19.refs_0_), channel_id=1, source_target_pairs={{0,8},{4,20},{8,0},{12,28},{16,24},{20,4},{24,16},{28,12},{1,9},{5... | collective-permute-start | bytes 3981320 | tf_op jit(solution)/shard_map/ppermute | solution.py:798
  129.1 35.1 %collective-permute-start.18 = (bf16[4,144,1152]{2,1,0:T(8,128)(2,1)}, bf16[4,144,1152]{2,1,0:T(8,128)(2,1)}, u32[]{:S(2)}, u32[]{:S(2)}) collective-permute-start(bf16[4,144,1152]{2,1,0:T(8,128)(2,1)} %bitcast.20.refs_0_), channel_id=1, source_target_pairs={{0,4},{4,0},{8,12},{12,8},{16,20},{20,16},{24,28},{28,24},{1,5},{5... | collective-permute-start | bytes 3981320 | tf_op jit(solution)/shard_map/ppermute | solution.py:802
  129.1 39.8 %collective-permute-start.19 = (bf16[4,144,1152]{2,1,0:T(8,128)(2,1)}, bf16[4,144,1152]{2,1,0:T(8,128)(2,1)}, u32[]{:S(2)}, u32[]{:S(2)}) collective-permute-start(bf16[4,144,1152]{2,1,0:T(8,128)(2,1)} %collective-permute-done.16.refs_1_), channel_id=1, source_target_pairs={{0,4},{4,0},{8,12},{12,8},{16,20},{20,16},{24,28},{28,24},{1,5},{5... | collective-permute-start | bytes 3981320 | tf_op jit(solution)/shard_map/ppermute | solution.py:802
  150.6 18.3 %collective-permute-start.21 = (bf16[4,144,1152]{2,1,0:T(8,128)(2,1)}, bf16[4,144,1152]{2,1,0:T(8,128)(2,1)}, u32[]{:S(2)}, u32[]{:S(2)}) collective-permute-start(bf16[4,144,1152]{2,1,0:T(8,128)(2,1)} %collective-permute-done.17.refs_3_), channel_id=1, source_target_pairs={{0,4},{4,0},{8,12},{12,8},{16,20},{20,16},{24,28},{28,24},{1,5},{5... | collective-permute-start | bytes 3981320 | tf_op jit(solution)/shard_map/ppermute | solution.py:802
  154.0 14.9 %collective-permute-start.20 = (bf16[4,144,1152]{2,1,0:T(8,128)(2,1)}, bf16[4,144,1152]{2,1,0:T(8,128)(2,1)}, u32[]{:S(2)}, u32[]{:S(2)}) collective-permute-start(bf16[4,144,1152]{2,1,0:T(8,128)(2,1)} %collective-permute-done.14.refs_2_), channel_id=1, source_target_pairs={{0,4},{4,0},{8,12},{12,8},{16,20},{20,16},{24,28},{28,24},{1,5},{5... | collective-permute-start | bytes 3981320 | tf_op jit(solution)/shard_map/ppermute | solution.py:802
  156.5 27.0 %collective-permute-start.22 = (bf16[4,144,1152]{2,1,0:T(8,128)(2,1)}, bf16[4,144,1152]{2,1,0:T(8,128)(2,1)}, u32[]{:S(2)}, u32[]{:S(2)}) collective-permute-start(bf16[4,144,1152]{2,1,0:T(8,128)(2,1)} %bitcast.19.refs_0_), channel_id=1, source_target_pairs={{0,16},{4,12},{8,24},{12,4},{16,0},{20,28},{24,8},{28,20},{1,17},{... | collective-permute-start | bytes 3981320 | tf_op jit(solution)/shard_map/ppermute | solution.py:798
  163.7 48.9 %copy-start = (f32[512,1152]{1,0:T(8,128)}, f32[512,1152]{1,0:T(8,128)S(1)}, u32[]{:S(2)}) copy-start(f32[512,1152]{1,0:T(8,128)S(1)} %get-tuple-element.246.hidden_ref) | copy-start | bytes 7077892
  165.9 22.9 %collective-permute-start.23 = (bf16[4,144,1152]{2,1,0:T(8,128)(2,1)S(1)}, bf16[4,144,1152]{2,1,0:T(8,128)(2,1)S(1)}, u32[]{:S(2)}, u32[]{:S(2)}) collective-permute-start(bf16[4,144,1152]{2,1,0:T(8,128)(2,1)S(1)} %copy-done.41), channel_id=1, source_target_pairs={{0,16},{4,12},{8,24},{12,4},{16,0},{20,28},{24,8},{28,20},{1,17},{... | collective-permute-start | bytes 3981320 | tf_op jit(solution)/shard_map/ppermute | solution.py:798
  168.9 21.1 %collective-permute-start.24 = (bf16[4,144,1152]{2,1,0:T(8,128)(2,1)}, bf16[4,144,1152]{2,1,0:T(8,128)(2,1)}, u32[]{:S(2)}, u32[]{:S(2)}) collective-permute-start(bf16[4,144,1152]{2,1,0:T(8,128)(2,1)} %bitcast.19.refs_0_), channel_id=1, source_target_pairs={{0,4},{4,0},{8,12},{12,8},{16,20},{20,16},{24,28},{28,24},{1,5},{5... | collective-permute-start | bytes 3981320 | tf_op jit(solution)/shard_map/ppermute | solution.py:802
  183.5 6.5 %collective-permute-start.26 = (bf16[4,144,1152]{2,1,0:T(8,128)(2,1)}, bf16[4,144,1152]{2,1,0:T(8,128)(2,1)S(1)}, u32[]{:S(2)}, u32[]{:S(2)}) collective-permute-start(bf16[4,144,1152]{2,1,0:T(8,128)(2,1)} %collective-permute-done.22.refs_2_), channel_id=1, source_target_pairs={{0,4},{4,0},{8,12},{12,8},{16,20},{20,16},{24,28},{28,24},{1,5},{5... | collective-permute-start | bytes 3981320 | tf_op jit(solution)/shard_map/ppermute | solution.py:802
  184.0 5.9 %collective-permute-start.25 = (bf16[4,144,1152]{2,1,0:T(8,128)(2,1)S(1)}, bf16[4,144,1152]{2,1,0:T(8,128)(2,1)S(1)}, u32[]{:S(2)}, u32[]{:S(2)}) collective-permute-start(bf16[4,144,1152]{2,1,0:T(8,128)(2,1)S(1)} %copy-done.41), channel_id=1, source_target_pairs={{0,4},{4,0},{8,12},{12,8},{16,20},{20,16},{24,28},{28,24},{1,5},{5... | collective-permute-start | bytes 3981320 | tf_op jit(solution)/shard_map/ppermute | solution.py:802
  188.7 22.8 %copy-start.42 = (bf16[4,144,1152]{2,1,0:T(8,128)(2,1)}, bf16[4,144,1152]{2,1,0:T(8,128)(2,1)S(1)}, u32[]{:S(2)}) copy-start(bf16[4,144,1152]{2,1,0:T(8,128)(2,1)S(1)} %collective-permute-done.23.refs_3_) | copy-start | bytes 3981316
  188.7 3.1 collective-permute-start.27
  211.5 11.2 %collective-permute-start.28 = (bf16[4,4,144,1152]{3,2,1,0:T(8,128)(2,1)}, bf16[4,4,144,1152]{3,2,1,0:T(8,128)(2,1)}, u32[]{:S(2)}, u32[]{:S(2)}) collective-permute-start(bf16[4,4,144,1152]{3,2,1,0:T(8,128)(2,1)} %get-tuple-element.104), channel_id=1, source_target_pairs={{0,4},{4,0},{8,12},{12,8},{16,20},{20,16},{24,28},{28,24},{1,5},{5... | collective-permute-start | bytes 15925256 | tf_op jit(solution)/shard_map/ppermute | solution.py:802
  229.4 33.1 %collective-permute-start.29 = (bf16[2,4,144,1152]{3,2,1,0:T(8,128)(2,1)}, bf16[2,4,144,1152]{3,2,1,0:T(8,128)(2,1)S(1)}, u32[]{:S(2)}, u32[]{:S(2)}) collective-permute-start(bf16[2,4,144,1152]{3,2,1,0:T(8,128)(2,1)} %get-tuple-element.105), channel_id=1, source_target_pairs={{0,16},{4,12},{8,24},{12,4},{16,0},{20,28},{24,8},{28,20},{1,17},{... | collective-permute-start | bytes 7962632 | tf_op jit(solution)/shard_map/ppermute | solution.py:798
  229.4 33.1 %copy-start.12 = (bf16[4,144,1152]{2,1,0:T(8,128)(2,1)S(1)}, bf16[4,144,1152]{2,1,0:T(8,128)(2,1)}, u32[]{:S(2)}) copy-start(bf16[4,144,1152]{2,1,0:T(8,128)(2,1)} %get-tuple-element.111) | copy-start | bytes 3981316
  262.5 24.7 %copy-start.5 = (bf16[2,4,144,1152]{3,2,1,0:T(8,128)(2,1)}, bf16[2,4,144,1152]{3,2,1,0:T(8,128)(2,1)S(1)}, u32[]{:S(2)}) copy-start(bf16[2,4,144,1152]{3,2,1,0:T(8,128)(2,1)S(1)} %collective-permute-done.29) | copy-start | bytes 7962628
  264.1 23.1 %collective-permute-start.30 = (bf16[4,144,1152]{2,1,0:T(8,128)(2,1)}, bf16[4,144,1152]{2,1,0:T(8,128)(2,1)}, u32[]{:S(2)}, u32[]{:S(2)}) collective-permute-start(bf16[4,144,1152]{2,1,0:T(8,128)(2,1)} %fusion.9), channel_id=1, source_target_pairs={{0,8},{4,20},{8,0},{12,28},{16,24},{20,4},{24,16},{28,12},{1,9},{5... | collective-permute-start | bytes 3981320 | tf_op jit(solution)/shard_map/ppermute | solution.py:798
  265.3 21.9 %copy-start.4 = (bf16[512,1152]{1,0:T(8,128)(2,1)S(1)}, bf16[512,1152]{1,0:T(8,128)(2,1)}, u32[]{:S(2)}) copy-start(bf16[512,1152]{1,0:T(8,128)(2,1)} %fusion.13.normed_ref) | copy-start | bytes 3538948
  305.6 14.1 %collective-permute-start.31 = (bf16[4,4,144,1152]{3,2,1,0:T(8,128)(2,1)}, bf16[4,4,144,1152]{3,2,1,0:T(8,128)(2,1)}, u32[]{:S(2)}, u32[]{:S(2)}) collective-permute-start(bf16[4,4,144,1152]{3,2,1,0:T(8,128)(2,1)} %get-tuple-element.126), channel_id=1, source_target_pairs={{0,4},{4,0},{8,12},{12,8},{16,20},{20,16},{24,28},{28,24},{1,5},{5... | collective-permute-start | bytes 15925256 | tf_op jit(solution)/shard_map/ppermute | solution.py:802
  319.3 9.8 %collective-permute-start.32 = (bf16[4,4,144,1152]{3,2,1,0:T(8,128)(2,1)}, bf16[4,4,144,1152]{3,2,1,0:T(8,128)(2,1)}, u32[]{:S(2)}, u32[]{:S(2)}) collective-permute-start(bf16[4,4,144,1152]{3,2,1,0:T(8,128)(2,1)} %get-tuple-element.123), channel_id=1, source_target_pairs={{0,4},{4,0},{8,12},{12,8},{16,20},{20,16},{24,28},{28,24},{1,5},{5... | collective-permute-start | bytes 15925256 | tf_op jit(solution)/shard_map/ppermute | solution.py:802
  326.3 32.2 %collective-permute-start.33 = (bf16[2,4,144,1152]{3,2,1,0:T(8,128)(2,1)}, bf16[2,4,144,1152]{3,2,1,0:T(8,128)(2,1)S(1)}, u32[]{:S(2)}, u32[]{:S(2)}) collective-permute-start(bf16[2,4,144,1152]{3,2,1,0:T(8,128)(2,1)} %get-tuple-element.127), channel_id=1, source_target_pairs={{0,16},{4,12},{8,24},{12,4},{16,0},{20,28},{24,8},{28,20},{1,17},{... | collective-permute-start | bytes 7962632 | tf_op jit(solution)/shard_map/ppermute | solution.py:798
  329.1 127.2 %reduce-scatter.4.cloned.1.call-start = ((), (), s32[]{:S(2)}) async-start(), calls=%async_computation.3 | async-start | bytes 1658880 | tf_op jit(solution)/shard_map/reduce_scatter | solution.py:851
  336.1 22.4 %copy-start.10 = (bf16[4,144,1152]{2,1,0:T(8,128)(2,1)S(1)}, bf16[4,144,1152]{2,1,0:T(8,128)(2,1)}, u32[]{:S(2)}) copy-start(bf16[4,144,1152]{2,1,0:T(8,128)(2,1)} %get-tuple-element.138) | copy-start | bytes 3981316
  359.9 32.3 %collective-permute-start.38 = (bf16[4,144,1152]{2,1,0:T(8,128)(2,1)}, bf16[4,144,1152]{2,1,0:T(8,128)(2,1)}, u32[]{:S(2)}, u32[]{:S(2)}) collective-permute-start(bf16[4,144,1152]{2,1,0:T(8,128)(2,1)} %fusion.6), channel_id=1, source_target_pairs={{0,8},{4,20},{8,0},{12,28},{16,24},{20,4},{24,16},{28,12},{1,9},{5... | collective-permute-start | bytes 3981320 | tf_op jit(solution)/shard_map/ppermute | solution.py:798
  360.8 44.1 %collective-permute-start.39 = (bf16[2,4,144,1152]{3,2,1,0:T(8,128)(2,1)}, bf16[2,4,144,1152]{3,2,1,0:T(8,128)(2,1)}, u32[]{:S(2)}, u32[]{:S(2)}) collective-permute-start(bf16[2,4,144,1152]{3,2,1,0:T(8,128)(2,1)} %get-tuple-element.145), channel_id=1, source_target_pairs={{0,16},{4,12},{8,24},{12,4},{16,0},{20,28},{24,8},{28,20},{1,17},{... | collective-permute-start | bytes 7962632 | tf_op jit(solution)/shard_map/ppermute | solution.py:798
  380.7 28.2 %collective-permute-start.34 = (bf16[2,2304]{1,0:T(2,128)(2,1)S(1)}, bf16[2,2304]{1,0:T(2,128)(2,1)S(1)}, u32[]{:S(2)}, u32[]{:S(2)}) collective-permute-start(bf16[2,2304]{1,0:T(2,128)(2,1)S(1)} %reshape.445), channel_id=1, source_target_pairs={{0,1},{1,0},{2,3},{3,2},{4,5},{5,4},{6,7},{7,6},{8,9},{9,8},{10,11... | collective-permute-start | bytes 27656 | tf_op jit(solution)/shard_map/ppermute | solution.py:856
  395.5 73.5 %reduce-scatter.6.cloned.1.call-start = ((), (), s32[]{:S(2)}) async-start(), calls=%async_computation.4 | async-start | bytes 1658880 | tf_op jit(solution)/shard_map/reduce_scatter | solution.py:851
  408.1 18.7 %collective-permute-start.40 = (bf16[4,144,1152]{2,1,0:T(8,128)(2,1)}, bf16[4,144,1152]{2,1,0:T(8,128)(2,1)}, u32[]{:S(2)}, u32[]{:S(2)}) collective-permute-start(bf16[4,144,1152]{2,1,0:T(8,128)(2,1)} %fusion.1), channel_id=1, source_target_pairs={{0,8},{4,20},{8,0},{12,28},{16,24},{20,4},{24,16},{28,12},{1,9},{5... | collective-permute-start | bytes 3981320 | tf_op jit(solution)/shard_map/ppermute | solution.py:798
  409.0 6.5 %collective-permute-start.35 = (bf16[4,2304]{1,0:T(4,128)(2,1)S(1)}, bf16[4,2304]{1,0:T(4,128)(2,1)S(1)}, u32[]{:S(2)}, u32[]{:S(2)}) collective-permute-start(bf16[4,2304]{1,0:T(4,128)(2,1)S(1)} %maximum_select_fusion.8), channel_id=1, source_target_pairs={{0,2},{1,3},{2,0},{3,1},{4,6},{5,7},{6,4},{7,5},{8,10},{9,11},{10,... | collective-permute-start | bytes 55304 | tf_op jit(solution)/shard_map/ppermute | solution.py:856
  416.1 9.5 %collective-permute-start.36 = (f32[290,128]{1,0:T(8,128)S(1)}, f32[290,128]{1,0:T(8,128)S(1)}, u32[]{:S(2)}, u32[]{:S(2)}) collective-permute-start(f32[290,128]{1,0:T(8,128)S(1)} %pad_maximum_fusion.2), channel_id=1, source_target_pairs={{0,1},{1,0},{2,3},{3,2},{4,5},{5,4},{6,7},{7,6},{8,9},{9,8},{10,11... | collective-permute-start | bytes 445448 | tf_op jit(solution)/shard_map/ppermute | solution.py:856
  425.6 10.1 %collective-permute-start.37 = (f32[290,128]{1,0:T(8,128)S(1)}, f32[290,128]{1,0:T(8,128)S(1)}, u32[]{:S(2)}, u32[]{:S(2)}) collective-permute-start(f32[290,128]{1,0:T(8,128)S(1)} %fusion.29), channel_id=1, source_target_pairs={{0,2},{1,3},{2,0},{3,1},{4,6},{5,7},{6,4},{7,5},{8,10},{9,11},{10,... | collective-permute-start | bytes 445448 | tf_op jit(solution)/shard_map/ppermute | solution.py:856
  430.4 22.9 %collective-permute-start.41 = (bf16[576,576]{0,1:T(8,128)(2,1)S(1)}, bf16[576,576]{0,1:T(8,128)(2,1)S(1)}, u32[]{:S(2)}, u32[]{:S(2)}) collective-permute-start(bf16[576,576]{0,1:T(8,128)(2,1)S(1)} %broadcast_select_fusion), channel_id=1, source_target_pairs={{0,16},{4,20},{8,24},{12,28},{16,0},{20,4},{24,8},{28,12},{1,17},{... | collective-permute-start | bytes 1990664 | tf_op jit(solution)/shard_map/ppermute | solution.py:856
  435.7 1.4 collective-permute-start.44
  437.1 5.3 %collective-permute-start.45 = (f32[218,128]{1,0:T(8,128)S(1)}, f32[218,128]{1,0:T(8,128)S(1)}, u32[]{:S(2)}, u32[]{:S(2)}) collective-permute-start(f32[218,128]{1,0:T(8,128)S(1)} %add.159), channel_id=1, source_target_pairs={{0,8},{4,12},{8,0},{12,4},{16,24},{20,28},{24,16},{28,20},{1,9},{5... | collective-permute-start | bytes 334856 | tf_op jit(solution)/shard_map/ppermute | solution.py:856
  442.4 8.9 %collective-permute-start.46 = (f32[218,128]{1,0:T(8,128)S(1)}, f32[218,128]{1,0:T(8,128)S(1)}, u32[]{:S(2)}, u32[]{:S(2)}) collective-permute-start(f32[218,128]{1,0:T(8,128)S(1)} %add.160), channel_id=1, source_target_pairs={{0,16},{4,20},{8,24},{12,28},{16,0},{20,4},{24,8},{28,12},{1,17},{... | collective-permute-start | bytes 334856 | tf_op jit(solution)/shard_map/ppermute | solution.py:856
  453.8 11.3 %collective-permute-start.42 = (bf16[288,576]{0,1:T(8,128)(2,1)S(1)}, bf16[288,576]{0,1:T(8,128)(2,1)S(1)}, u32[]{:S(2)}, u32[]{:S(2)}) collective-permute-start(bf16[288,576]{0,1:T(8,128)(2,1)S(1)} %broadcast_select_fusion.1), channel_id=1, source_target_pairs={{0,8},{4,12},{8,0},{12,4},{16,24},{20,28},{24,16},{28,20},{1,9},{5... | collective-permute-start | bytes 995336 | tf_op jit(solution)/shard_map/ppermute | solution.py:856
  465.5 1.6 collective-permute-start.43
  (36 other events, 421.6 us)
Sparse Core Ops, SparseCore 0:
  10.2 35.5 all-gather.6
  56.6 30.9 all-gather.10
  96.2 30.5 all-gather.8
  329.2 28.8 reduce-scatter.7
  395.6 33.7 reduce-scatter.3
  435.9 30.6 reduce-scatter.5

commit v7 on v6

--- a/solution.py
+++ b/solution.py
@@ -595,7 +595,7 @@
         ],
         scratch_shapes=[pltpu.VMEM((rows, packed), jnp.float32)],
         compiler_params=params(),
-        cost_estimate=lasting(13),
+        cost_estimate=lasting(1),
         name="input_grad",
     )(right, weight, images, d_hidden, lines)
 
@@ -1089,12 +1089,10 @@
         )
         attn_move = Scatter(own, after(send, down_move.total()))
         down_sum = down_move.end()
-        second_t = after(second_low.T, send)
+        second_t = after(second_low.T, attn_move.near())
+        attn_move.send()
         own, send = slot_grad(one_grad_kernel, slot_of, [second_t], d_pre, parts, "up_grad")
-        up_move = Scatter(own, send)
-        attn_pair = attn_move.near(send)
-        attn_move.send()
-        attn_back = after(attn_full, up_move.near(attn_pair))
+        attn_back = after(attn_full, send)
     else:
         grad_down = jnp.concatenate([contract_rows(a, grad_low) for a in activ], axis=0)
         down_sum = scatter_sum(pack_down(grad_down.astype(low), groups, parts, shard_rows))
@@ -1119,12 +1117,14 @@
 
     if cube:
         attn_one = attn_move.back(images_grad)
-        up_move.send(attn_one)
-        pairs = after(pairs, attn_one)
+        up_move = Scatter(own, after(send, attn_one, down_sum))
+        up_pair = up_move.near(attn_one)
+        up_move.send()
+        attn_total = attn_move.total()
+        pairs = after(pairs, up_pair, attn_total)
     table_sum = table_gradient(offset_index, pairs)
     if cube:
         d_time = after(d_time, table_sum)
-        attn_total = attn_move.total(table_sum)
         up_one = up_move.back()
         up_total = up_move.total()
     d_time = jnp.concatenate(

time: 483 us -> 476 us (0.986)
    ppermute x15, waiting for transfers between devices: 1.84 us -> 18.4 us  [swap_core(): return lax.ppermute(value, 'dp', [(i, i ^ 1) for i in range(8)])]
    ppermute x15, waiting for transfers between devices: 53.4 us -> 42.5 us  [swap(): lax.ppermute(value, 'dp', [(i, i ^ NEAR[i & 1][hop]) for i in range(8)])]
    ppermute x17, waiting for transfers between devices: 64.5 us -> 58.2 us  [swap_bit(): return lax.ppermute(value, axis, [(i, i ^ 1 << bit) for i in range(size)])]
  transfers between devices with their start and end apart: 53 -> 53, of which waited for: 25 -> 27; matrix products, arithmetic and copies ran while one was open for 11% -> 10% of each run, Pallas kernels for 37% -> 36%
where the time goes in v7:
time: 476 us; the launch traced here: 471 us
  Pallas kernels  217 us (46%)
  waiting for transfers between devices  140 us (29%)
  starting transfers between devices  38.9 us (8%)
  other arithmetic  28.6 us (6%)
  local copies, waits for them, and re-layouts  25.9 us (5%)
  between operations  15.3 us (3%)
  matrix products  5.79 us (1%)
    ppermute x17, waiting for transfers between devices, swap_bit(): return lax.ppermute(value, axis, [(i, i ^ 1 << bit) for i in range(size)])  58.2 us
    ppermute x15, waiting for transfers between devices, swap(): lax.ppermute(value, 'dp', [(i, i ^ NEAR[i & 1][hop]) for i in range(8)])  42.5 us
    pallas_call x2, Pallas kernels, piece_call(): pl.pallas_call(kernel, grid_spec=pltpu.PrefetchScalarGridSpec(num_scalar_...  35.5 us
    pallas_call x1, Pallas kernels, down_back(): pl.pallas_call(down_back_kernel, grid=(groups,), in_specs=[whole, whole,...  33 us
    pallas_call x2, Pallas kernels, slot_grad(): pl.pallas_call(kernel, grid_spec=pltpu.PrefetchScalarGridSpec(num_scalar_...  26.3 us
    pallas_call x1, Pallas kernels, attend_back(): pl.pallas_call(attend_back_kernel, grid=(groups,), in_specs=[pl.BlockSpec...  22 us
    pallas_call x3, Pallas kernels, add_halves(): pl.pallas_call(add_kernel, grid=(groups,), in_specs=[pl.BlockSpec((1, 1,...  20.2 us
    pallas_call x1, Pallas kernels, position_bias(): pl.pallas_call(bias_kernel, grid=(4,), in_specs=[pl.BlockSpec((tokens, to...  20.1 us
  transfers between devices with their start and end apart: 53, of which 27 were waited for; matrix products, arithmetic and copies ran while one was open for 10% of the time, Pallas kernels for 36%

profile of v7, /device:TPU:0, one launch (start us, length us, event | category | flops | bytes accessed | tf_op | source)
XLA Modules:
  0.0 471.4 jit_solution(9176141315167169796)
XLA Ops:
  7.3 2.0 concatenate.137
  10.4 3.1 collective-permute-start.2
  14.5 3.6 collective-permute-done.2
  18.2 1.8 collective-permute-start.3
  20.2 7.8 %collective-permute-done.3 = bf16[2,144,576]{2,1,0:T(8,128)(2,1)S(1)} collective-permute-done((bf16[2,144,576]{2,1,0:T(8,128)(2,1)S(1)}, bf16[2,144,576]{2,1,0:T(8,128)(2,1)S(1)}, u32[]{:S(2)}, u32[]{:S(2)}) %collective-permute-start.3) | collective-permute-done | bytes 331808 | tf_op jit(solution)/shard_map/ppermute | solution.py:856
  28.7 1.8 collective-permute-done.4
  31.2 14.6 %all-gather.7.cloned.1.call-done = bf16[576,1152]{1,0:T(8,128)(2,1)} async-done(((bf16[144,1152]{1,0:T(8,128)(2,1)}), bf16[576,1152]{1,0:T(8,128)(2,1)}) %all-gather.7.cloned.1.call-update) | async-done | bytes 1327120 | tf_op jit(solution)/shard_map/all_gather | solution.py:1030
  45.7 1.5 collective-permute-start.7
  49.4 2.0 collective-permute-done
  51.4 1.6 collective-permute-start.1
  53.3 3.2 collective-permute-done.1
  57.5 1.5 collective-permute-start.8
  58.9 11.8 %collective-permute-done.7.refs_1_ = bf16[4,144,1152]{2,1,0:T(8,128)(2,1)} collective-permute-done((bf16[4,144,1152]{2,1,0:T(8,128)(2,1)}, bf16[4,144,1152]{2,1,0:T(8,128)(2,1)}, u32[]{:S(2)}, u32[]{:S(2)}) %collective-permute-start.7) | collective-permute-done | bytes 1327136 | tf_op jit(solution)/shard_map/ppermute | solution.py:798
  70.7 2.5 collective-permute-start.9
  73.3 20.1 %position_bias.1.bias_ref = f32[16,256,256]{2,1,0:T(8,128)} custom-call(s32[256,256]{1,0:T(8,128)} %index_ref.3, f32[16,1,1024]{2,1,0:T(1,128)} %reshape.453.table_ref), custom_call_target="tpu_custom_call" | custom-call | flops 20000000000 | bytes 1 | tf_op jit(solution)/shard_map/position_bias/pallas_call | solution.py:111
  93.4 1.3 collective-permute-start.16
  99.4 1.7 collective-permute-done.5
  102.9 5.9 %collective-permute-done.6 = f32[2,8,576]{2,1,0:T(8,128)S(1)} collective-permute-done((f32[2,8,576]{2,1,0:T(8,128)S(1)}, f32[2,8,576]{2,1,0:T(8,128)S(1)}, u32[]{:S(2)}, u32[]{:S(2)}) %collective-permute-start.6) | collective-permute-done | bytes 36896 | tf_op jit(solution)/shard_map/ppermute | solution.py:856
  108.9 8.6 %collective-permute-done.16.refs_1_ = bf16[4,144,1152]{2,1,0:T(8,128)(2,1)} collective-permute-done((bf16[4,144,1152]{2,1,0:T(8,128)(2,1)}, bf16[4,144,1152]{2,1,0:T(8,128)(2,1)}, u32[]{:S(2)}, u32[]{:S(2)}) %collective-permute-start.16) | collective-permute-done | bytes 1327136 | tf_op jit(solution)/shard_map/ppermute | solution.py:798
  119.1 1.5 fusion.13.normed_ref
  120.8 6.6 %all-gather.9.cloned.1.call-done = bf16[576,1152]{1,0:T(8,128)(2,1)} async-done(((bf16[144,1152]{1,0:T(8,128)(2,1)}), bf16[576,1152]{1,0:T(8,128)(2,1)}) %all-gather.9.cloned.1.call-update) | async-done | bytes 1327120 | tf_op jit(solution)/shard_map/all_gather | solution.py:1032
  127.4 1.4 collective-permute-start.15
  130.0 21.0 %attend.1 = (bf16[4,512,896]{2,1,0:T(8,128)(2,1)}, bf16[4,2,4,256,256]{4,3,2,1,0:T(8,128)(2,1)}, bf16[4,512,288]{2,1,0:T(8,128)(2,1)}, bf16[1152,1152]{1,0:T(8,128)(2,1)}, bf16[4,1152,1152]{2,1,0:T(8,128)(2,1)}) custom-call(s32[8]{0:T(128)} %fusion.27.part_ref, bf16[512,1152]{1,0:T(8,128)(2,1)} %fusion.13.normed_ref, ...), custom_call_target="tpu_custom_call" | custom-call | flops 12999999488 | bytes 1 | tf_op jit(solution)/shard_map/attend/pallas_call | solution.py:228
  151.0 3.6 collective-permute-start.21
  154.6 2.5 collective-permute-done.15.refs_1_
  158.2 1.7 copy.69
  159.8 4.3 fusion.37
  164.6 1.7 copy-done.40
  167.2 1.5 add_convert_fusion.second_ref
  168.8 14.5 %up_forward.1 = (bf16[4,512,1152]{2,1,0:T(8,128)(2,1)}, bf16[4,512,1152]{2,1,0:T(8,128)(2,1)}, bf16[4,1152,1152]{2,1,0:T(8,128)(2,1)}) custom-call(s32[8]{0:T(128)} %fusion.27.part_ref, bf16[512,1152]{1,0:T(8,128)(2,1)} %add_convert_fusion.second_ref, f32[4,1,1152]{2,1,0:T(1,128)} %reshape.458.bias_ref, bf16[4,144,1152]{2,1,0:T(8,128)(2,1)} %bitcast.127, ...), custom_call_target="tpu_custom_call" | custom-call | flops 12999999488 | bytes 1 | tf_op jit(solution)/shard_map/up_forward/pallas_call | solution.py:228
  183.9 5.3 %collective-permute-done.23.refs_3_ = bf16[4,144,1152]{2,1,0:T(8,128)(2,1)S(1)} collective-permute-done((bf16[4,144,1152]{2,1,0:T(8,128)(2,1)S(1)}, bf16[4,144,1152]{2,1,0:T(8,128)(2,1)S(1)}, u32[]{:S(2)}, u32[]{:S(2)}) %collective-permute-start.23) | collective-permute-done | bytes 1327136 | tf_op jit(solution)/shard_map/ppermute | solution.py:798
  190.5 1.8 collective-permute-done.27.refs_7_
  193.4 18.5 %down_grad.1 = (bf16[4,4,144,1152]{3,2,1,0:T(8,128)(2,1)}, bf16[4,4,144,1152]{3,2,1,0:T(8,128)(2,1)}) custom-call(s32[8]{0:T(128)} %fusion.26.slot_ref, bf16[4,512,1152]{2,1,0:T(8,128)(2,1)} %get-tuple-element.99.left_ref.activ_ref, bf16[512,1152]{1,0:T(8,128)(2,1)} %bitcast.128), custom_call_target="tpu_custom_call" | custom-call | flops 17999998976 | bytes 1 | tf_op jit(solution)/shard_map/down_grad/pallas_call | solution.py:690
  213.2 8.8 %unpack_pieces.1.down_ref = bf16[4608,1152]{1,0:T(8,128)(2,1)} custom-call(s32[8]{0:T(128)} %fusion.27.part_ref, bf16[4,144,1152]{2,1,0:T(8,128)(2,1)} %bitcast.19.refs_0_, bf16[4,144,1152]{2,1,0:T(8,128)(2,1)} %copy-done.39, bf16[4,144,1152]{2,1,0:T(8,128)(2,1)} %collective-permute-done.22.refs_2_, bf16[4,144,1152]{2,1,0:T(8,128)(2,1)} %copy-done.41, ...), custom_call_target="tpu_custom_call" | custom-call | flops 8999999488 | bytes 1 | tf_op jit(solution)/shard_map/unpack_pieces/pallas_call | solution.py:757
  222.0 6.6 %add_halves.3 = (bf16[4,144,1152]{2,1,0:T(8,128)(2,1)}, bf16[4,144,1152]{2,1,0:T(8,128)(2,1)}, bf16[2,4,144,1152]{3,2,1,0:T(8,128)(2,1)}) custom-call(bf16[4,4,144,1152]{3,2,1,0:T(8,128)(2,1)} %get-tuple-element.101.one_ref.two_ref.three_ref.four_ref, bf16[4,4,144,1152]{3,2,1,0:T(8,128)(2,1)} %get-tuple-element.101.one_ref.two_ref.three_ref.four_ref, ...), custom_call_target="tpu_custom_call" | custom-call | flops 7000000000 | bytes 1 | tf_op jit(solution)/shard_map/add_halves/pallas_call | solution.py:721
  228.7 33.0 %down_back.1 = (bf16[4,512,1152]{2,1,0:T(8,128)(2,1)}, bf16[512,1152]{1,0:T(8,128)(2,1)}, f32[512,1152]{1,0:T(8,128)}, bf16[512,1152]{1,0:T(8,128)(2,1)}, f32[8,1152]{1,0:T(8,128)}, /*index=5*/f32[4,1,1152]{2,1,0:T(1,128)}) custom-call(bf16[512,1152]{1,0:T(8,128)(2,1)} %bitcast.129, f32[512,1152]{1,0:T(8,128)} %copy-done, ...), custom_call_target="tpu_custom_call" | custom-call | flops 32999999488 | bytes 1 | tf_op jit(solution)/shard_map/down_back/pallas_call | solution.py:429
  261.7 1.6 fusion.9
  264.6 22.0 %attend_back.1 = (bf16[4,512,1152]{2,1,0:T(8,128)(2,1)}, f32[16,256,256]{2,1,0:T(8,128)}, f32[4,2,864]{2,1,0:T(2,128)}) custom-call(bf16[512,1152]{1,0:T(8,128)(2,1)} %get-tuple-element.110.hidden_ref, bf16[1152,1152]{1,0:T(8,128)(2,1)} %get-tuple-element.91.proj_ref, bf16[4,512,896]{2,1,0:T(8,128)(2,1)} %get-tuple-element.111.qkv_ref, ...), custom_call_target="tpu_custom_call" | custom-call | flops 19000000512 | bytes 1 | tf_op jit(solution)/shard_map/attend_back/pallas_call | solution.py:514
  286.7 1.4 copy.70.one_ref
  288.1 14.1 %pair_grad.1 = (bf16[4,4,144,1152]{3,2,1,0:T(8,128)(2,1)}, bf16[4,4,144,1152]{3,2,1,0:T(8,128)(2,1)}) custom-call(s32[8]{0:T(128)} %fusion.26.slot_ref, bf16[1152,512]{1,0:T(8,128)(2,1)} %copy.70.one_ref, bf16[1152,512]{1,0:T(8,128)(2,1)} %bitcast.104, bf16[4,512,1152]{2,1,0:T(8,128)(2,1)} %get-tuple-element.113.right_ref), custom_call_target="tpu_custom_call" | custom-call | flops 17999998976 | bytes 1 | tf_op jit(solution)/shard_map/pair_grad/pallas_call | solution.py:650
  302.2 1.6 fusion.8
  303.8 9.1 %collective-permute-done.31.came_ref = bf16[4,4,144,1152]{3,2,1,0:T(8,128)(2,1)} collective-permute-done((bf16[4,4,144,1152]{3,2,1,0:T(8,128)(2,1)}, bf16[4,4,144,1152]{3,2,1,0:T(8,128)(2,1)}, u32[]{:S(2)}, u32[]{:S(2)}) %collective-permute-start.31) | collective-permute-done | bytes 5308448 | tf_op jit(solution)/shard_map/ppermute | solution.py:802
  312.9 7.0 %add_halves.4 = (bf16[4,144,1152]{2,1,0:T(8,128)(2,1)}, bf16[4,144,1152]{2,1,0:T(8,128)(2,1)}, bf16[2,4,144,1152]{3,2,1,0:T(8,128)(2,1)}) custom-call(bf16[4,4,144,1152]{3,2,1,0:T(8,128)(2,1)} %get-tuple-element.116.one_ref.two_ref.three_ref.four_ref, bf16[4,4,144,1152]{3,2,1,0:T(8,128)(2,1)} %get-tuple-element.116.one_ref.two_ref.three_ref.four_ref, ...), custom_call_target="tpu_custom_call" | custom-call | flops 7000000000 | bytes 1 | tf_op jit(solution)/shard_map/add_halves/pallas_call | solution.py:721
  319.9 2.0 collective-permute-start.32
  323.9 1.6 copy.71.one_ref
  325.5 12.2 %up_grad.1 = (bf16[4,4,144,1152]{3,2,1,0:T(8,128)(2,1)}, bf16[4,4,144,1152]{3,2,1,0:T(8,128)(2,1)}) custom-call(s32[8]{0:T(128)} %fusion.26.slot_ref, bf16[1152,512]{1,0:T(8,128)(2,1)} %copy.71.one_ref, bf16[4,512,1152]{2,1,0:T(8,128)(2,1)} %get-tuple-element.122.right_ref), custom_call_target="tpu_custom_call" | custom-call | flops 17999998976 | bytes 1 | tf_op jit(solution)/shard_map/up_grad/pallas_call | solution.py:650
  337.6 14.3 %input_grad.1 = (bf16[512,1152]{1,0:T(8,128)(2,1)}, f32[8,1152]{1,0:T(8,128)}) custom-call(bf16[4,512,1152]{2,1,0:T(8,128)(2,1)} %get-tuple-element.113.right_ref, bf16[4,1152,1152]{2,1,0:T(8,128)(2,1)} %get-tuple-element.124.weight_ref, bf16[512,1152]{1,0:T(8,128)(2,1)} %bitcast.98, f32[512,1152]{1,0:T(8,128)} %get-tuple-element.125.d_hidden_ref, ...), custom_call_target="tpu_custom_call" | custom-call | flops 1000000000 | bytes 1 | tf_op jit(solution)/shard_map/input_grad/pallas_call | solution.py:581
  352.2 1.6 fusion.6
  355.6 7.5 %collective-permute-done.33.came_ref = bf16[4,4,144,1152]{3,2,1,0:T(8,128)(2,1)} collective-permute-done((bf16[4,4,144,1152]{3,2,1,0:T(8,128)(2,1)}, bf16[4,4,144,1152]{3,2,1,0:T(8,128)(2,1)}, u32[]{:S(2)}, u32[]{:S(2)}) %collective-permute-start.33) | collective-permute-done | bytes 5308448 | tf_op jit(solution)/shard_map/ppermute | solution.py:802
  363.0 6.6 %add_halves.5 = (bf16[4,144,1152]{2,1,0:T(8,128)(2,1)}, bf16[4,144,1152]{2,1,0:T(8,128)(2,1)}, bf16[2,4,144,1152]{3,2,1,0:T(8,128)(2,1)}) custom-call(bf16[4,4,144,1152]{3,2,1,0:T(8,128)(2,1)} %get-tuple-element.134.one_ref.two_ref.three_ref.four_ref, bf16[4,4,144,1152]{3,2,1,0:T(8,128)(2,1)} %get-tuple-element.134.one_ref.two_ref.three_ref.four_ref, ...), custom_call_target="tpu_custom_call" | custom-call | flops 7000000000 | bytes 1 | tf_op jit(solution)/shard_map/add_halves/pallas_call | solution.py:721
  369.7 2.0 collective-permute-start.39
  371.8 2.9 fusion.5
  374.8 17.7 %table_gradient.1 = f32[128,128]{1,0:T(8,128)} custom-call(s32[256,256]{1,0:T(8,128)} %index_ref.3, f32[16,256,256]{2,1,0:T(8,128)} %get-tuple-element.138.pairs_ref), custom_call_target="tpu_custom_call" | custom-call | flops 17999998976 | bytes 1 | tf_op jit(solution)/shard_map/table_gradient/pallas_call | solution.py:167
  393.7 8.3 %collective-permute-done.39 = bf16[2,4,144,1152]{3,2,1,0:T(8,128)(2,1)} collective-permute-done((bf16[2,4,144,1152]{3,2,1,0:T(8,128)(2,1)}, bf16[2,4,144,1152]{3,2,1,0:T(8,128)(2,1)}, u32[]{:S(2)}, u32[]{:S(2)}) %collective-permute-start.39) | collective-permute-done | bytes 2654240 | tf_op jit(solution)/shard_map/ppermute | solution.py:798
  402.0 2.7 fusion.1
  406.6 3.8 collective-permute-done.36
  412.2 4.1 collective-permute-done.37
  417.2 5.7 %collective-permute-done.40 = bf16[4,144,1152]{2,1,0:T(8,128)(2,1)} collective-permute-done((bf16[4,144,1152]{2,1,0:T(8,128)(2,1)}, bf16[4,144,1152]{2,1,0:T(8,128)(2,1)}, u32[]{:S(2)}, u32[]{:S(2)}) %collective-permute-start.40) | collective-permute-done | bytes 1327136 | tf_op jit(solution)/shard_map/ppermute | solution.py:798
  422.8 3.3 fusion.3
  426.4 2.1 collective-permute-start.41
  430.7 4.5 collective-permute-done.45
  435.9 10.1 %collective-permute-done.46 = f32[218,128]{1,0:T(8,128)S(1)} collective-permute-done((f32[218,128]{1,0:T(8,128)S(1)}, f32[218,128]{1,0:T(8,128)S(1)}, u32[]{:S(2)}, u32[]{:S(2)}) %collective-permute-start.46) | collective-permute-done | bytes 111648 | tf_op jit(solution)/shard_map/ppermute | solution.py:856
  450.7 7.9 %collective-permute-done.42 = bf16[288,576]{0,1:T(8,128)(2,1)S(1)} collective-permute-done((bf16[288,576]{0,1:T(8,128)(2,1)S(1)}, bf16[288,576]{0,1:T(8,128)(2,1)S(1)}, u32[]{:S(2)}, u32[]{:S(2)}) %collective-permute-start.42) | collective-permute-done | bytes 331808 | tf_op jit(solution)/shard_map/ppermute | solution.py:856
  462.5 1.9 bitcast_convert_fusion
  (284 shorter events, 46.0 us)
Async XLA Ops:
  7.2 38.5 %all-gather.7.cloned.1.call-start = ((), (), s32[]{:S(2)}) async-start(), calls=%async_computation.6 | async-start | bytes 1658880 | tf_op jit(solution)/shard_map/all_gather | solution.py:1030
  9.3 19.0 %copy-start.46 = (s32[2]{0:T(128)S(1)}, s32[2]{0:T(128)}, u32[]{:S(2)}) copy-start(s32[2]{0:T(128)} %param.25) | copy-start | bytes 28
  9.3 84.0 %all-gather.11.cloned.1.call-start = ((), (), s32[]{:S(2)}) async-start(), calls=%async_computation.8 | async-start | bytes 1658880 | tf_op jit(solution)/shard_map/all_gather | solution.py:1031
  10.4 7.7 %collective-permute-start.2 = (bf16[144,576]{1,0:T(8,128)(2,1)S(1)}, bf16[144,576]{1,0:T(8,128)(2,1)S(1)}, u32[]{:S(2)}, u32[]{:S(2)}) collective-permute-start(bf16[144,576]{1,0:T(8,128)(2,1)S(1)} %pad_maximum_fusion.1), channel_id=1, source_target_pairs={{0,16},{4,20},{8,24},{12,28},{16,0},{20,4},{24,8},{28,12},{1,17},{... | collective-permute-start | bytes 497672 | tf_op jit(solution)/shard_map/ppermute | solution.py:856
  18.2 9.8 %collective-permute-start.3 = (bf16[2,144,576]{2,1,0:T(8,128)(2,1)S(1)}, bf16[2,144,576]{2,1,0:T(8,128)(2,1)S(1)}, u32[]{:S(2)}, u32[]{:S(2)}) collective-permute-start(bf16[2,144,576]{2,1,0:T(8,128)(2,1)S(1)} %maximum_select_fusion.3), channel_id=1, source_target_pairs={{0,8},{4,12},{8,0},{12,4},{16,24},{20,28},{24,16},{28,20},{1,9},{5... | collective-permute-start | bytes 995336 | tf_op jit(solution)/shard_map/ppermute | solution.py:856
  28.2 2.3 collective-permute-start.4
  31.0 22.0 %copy-start.2 = (bf16[2,256,1152]{2,1,0:T(8,128)(2,1)S(1)}, bf16[2,256,1152]{2,1,0:T(8,128)(2,1)}, u32[]{:S(2)}) copy-start(bf16[2,256,1152]{2,1,0:T(8,128)(2,1)} %param.23) | copy-start | bytes 3538948
  31.1 65.8 %copy-start.3 = (bf16[2,2,2,144,576]{4,3,2,1,0:T(8,128)(2,1)}, bf16[2,2,2,144,576]{4,3,2,1,0:T(8,128)(2,1)S(1)}, u32[]{:S(2)}) copy-start(bf16[2,2,2,144,576]{4,3,2,1,0:T(8,128)(2,1)S(1)} %copy.64) | copy-start | bytes 3981316
  45.7 25.0 %collective-permute-start.7 = (bf16[4,144,1152]{2,1,0:T(8,128)(2,1)}, bf16[4,144,1152]{2,1,0:T(8,128)(2,1)}, u32[]{:S(2)}, u32[]{:S(2)}) collective-permute-start(bf16[4,144,1152]{2,1,0:T(8,128)(2,1)} %bitcast.120), channel_id=1, source_target_pairs={{0,8},{4,20},{8,0},{12,28},{16,24},{20,4},{24,16},{28,12},{1,9},{5... | collective-permute-start | bytes 3981320 | tf_op jit(solution)/shard_map/ppermute | solution.py:798
  47.6 3.8 collective-permute-start
  51.4 5.0 %collective-permute-start.1 = (bf16[2,74,128]{2,1,0:T(8,128)(2,1)S(1)}, bf16[2,74,128]{2,1,0:T(8,128)(2,1)S(1)}, u32[]{:S(2)}, u32[]{:S(2)}) collective-permute-start(bf16[2,74,128]{2,1,0:T(8,128)(2,1)S(1)} %maximum_select_fusion.6), channel_id=1, source_target_pairs={{0,2},{1,3},{2,0},{3,1},{4,6},{5,7},{6,4},{7,5},{8,10},{9,11},{10,... | collective-permute-start | bytes 113672 | tf_op jit(solution)/shard_map/ppermute | solution.py:856
  56.5 70.9 %all-gather.9.cloned.1.call-start = ((), (), s32[]{:S(2)}) async-start(), calls=%async_computation.7 | async-start | bytes 1658880 | tf_op jit(solution)/shard_map/all_gather | solution.py:1032
  57.4 37.2 %copy-start.20 = (bf16[144,288]{0,1:T(8,128)(2,1)S(1)}, bf16[144,288]{0,1:T(8,128)(2,1)}, u32[]{:S(2)}) copy-start(bf16[144,288]{0,1:T(8,128)(2,1)} %get-tuple-element.215) | copy-start | bytes 248836
  57.5 35.9 %collective-permute-start.8 = (bf16[4,144,1152]{2,1,0:T(8,128)(2,1)}, bf16[4,144,1152]{2,1,0:T(8,128)(2,1)}, u32[]{:S(2)}, u32[]{:S(2)}) collective-permute-start(bf16[4,144,1152]{2,1,0:T(8,128)(2,1)} %bitcast.121), channel_id=1, source_target_pairs={{0,16},{4,12},{8,24},{12,4},{16,0},{20,28},{24,8},{28,20},{1,17},{... | collective-permute-start | bytes 3981320 | tf_op jit(solution)/shard_map/ppermute | solution.py:798
  70.7 31.3 %collective-permute-start.9 = (bf16[4,144,1152]{2,1,0:T(8,128)(2,1)}, bf16[4,144,1152]{2,1,0:T(8,128)(2,1)}, u32[]{:S(2)}, u32[]{:S(2)}) collective-permute-start(bf16[4,144,1152]{2,1,0:T(8,128)(2,1)} %collective-permute-done.7.refs_1_), channel_id=1, source_target_pairs={{0,16},{4,12},{8,24},{12,4},{16,0},{20,28},{24,8},{28,20},{1,17},{... | collective-permute-start | bytes 3981320 | tf_op jit(solution)/shard_map/ppermute | solution.py:798
  93.4 24.1 %collective-permute-start.16 = (bf16[4,144,1152]{2,1,0:T(8,128)(2,1)}, bf16[4,144,1152]{2,1,0:T(8,128)(2,1)}, u32[]{:S(2)}, u32[]{:S(2)}) collective-permute-start(bf16[4,144,1152]{2,1,0:T(8,128)(2,1)} %bitcast.124), channel_id=1, source_target_pairs={{0,8},{4,20},{8,0},{12,28},{16,24},{20,4},{24,16},{28,12},{1,9},{5... | collective-permute-start | bytes 3981320 | tf_op jit(solution)/shard_map/ppermute | solution.py:798
  96.6 257.2 %reduce-scatter.4.cloned.1.call-start = ((), (), s32[]{:S(2)}) async-start(), calls=%async_computation.3 | async-start | bytes 1658880 | tf_op jit(solution)/shard_map/reduce_scatter | solution.py:851
  96.9 54.1 %copy-start.22 = (bf16[8,1152]{1,0:T(8,128)(2,1)}, bf16[8,1152]{1,0:T(8,128)(2,1)S(1)}, u32[]{:S(2)}) copy-start(bf16[8,1152]{1,0:T(8,128)(2,1)S(1)} %reshape.434) | copy-start | bytes 55300
  97.3 3.8 collective-permute-start.5
  101.1 7.8 %collective-permute-start.6 = (f32[2,8,576]{2,1,0:T(8,128)S(1)}, f32[2,8,576]{2,1,0:T(8,128)S(1)}, u32[]{:S(2)}, u32[]{:S(2)}) collective-permute-start(f32[2,8,576]{2,1,0:T(8,128)S(1)} %maximum_select_fusion.7), channel_id=1, source_target_pairs={{0,2},{1,3},{2,0},{3,1},{4,6},{5,7},{6,4},{7,5},{8,10},{9,11},{10,... | collective-permute-start | bytes 110600 | tf_op jit(solution)/shard_map/ppermute | solution.py:856
  102.1 25.3 %collective-permute-start.10 = (bf16[4,144,1152]{2,1,0:T(8,128)(2,1)}, bf16[4,144,1152]{2,1,0:T(8,128)(2,1)}, u32[]{:S(2)}, u32[]{:S(2)}) collective-permute-start(bf16[4,144,1152]{2,1,0:T(8,128)(2,1)} %bitcast.122), channel_id=1, source_target_pairs={{0,4},{4,0},{8,12},{12,8},{16,20},{20,16},{24,28},{28,24},{1,5},{5... | collective-permute-start | bytes 3981320 | tf_op jit(solution)/shard_map/ppermute | solution.py:802
  102.1 18.7 %collective-permute-start.14 = (bf16[4,144,1152]{2,1,0:T(8,128)(2,1)}, bf16[4,144,1152]{2,1,0:T(8,128)(2,1)}, u32[]{:S(2)}, u32[]{:S(2)}) collective-permute-start(bf16[4,144,1152]{2,1,0:T(8,128)(2,1)} %bitcast.125), channel_id=1, source_target_pairs={{0,16},{4,12},{8,24},{12,4},{16,0},{20,28},{24,8},{28,20},{1,17},{... | collective-permute-start | bytes 3981320 | tf_op jit(solution)/shard_map/ppermute | solution.py:798
  102.1 27.4 %collective-permute-start.11 = (bf16[4,144,1152]{2,1,0:T(8,128)(2,1)}, bf16[4,144,1152]{2,1,0:T(8,128)(2,1)}, u32[]{:S(2)}, u32[]{:S(2)}) collective-permute-start(bf16[4,144,1152]{2,1,0:T(8,128)(2,1)} %collective-permute-done.7.refs_1_), channel_id=1, source_target_pairs={{0,4},{4,0},{8,12},{12,8},{16,20},{20,16},{24,28},{28,24},{1,5},{5... | collective-permute-start | bytes 3981320 | tf_op jit(solution)/shard_map/ppermute | solution.py:802
  108.9 20.6 %collective-permute-start.12 = (bf16[4,144,1152]{2,1,0:T(8,128)(2,1)}, bf16[4,144,1152]{2,1,0:T(8,128)(2,1)}, u32[]{:S(2)}, u32[]{:S(2)}) collective-permute-start(bf16[4,144,1152]{2,1,0:T(8,128)(2,1)} %collective-permute-done.8.refs_2_), channel_id=1, source_target_pairs={{0,4},{4,0},{8,12},{12,8},{16,20},{20,16},{24,28},{28,24},{1,5},{5... | collective-permute-start | bytes 3981320 | tf_op jit(solution)/shard_map/ppermute | solution.py:802
  117.4 12.6 %collective-permute-start.13 = (bf16[4,144,1152]{2,1,0:T(8,128)(2,1)}, bf16[4,144,1152]{2,1,0:T(8,128)(2,1)}, u32[]{:S(2)}, u32[]{:S(2)}) collective-permute-start(bf16[4,144,1152]{2,1,0:T(8,128)(2,1)} %collective-permute-done.9.refs_3_), channel_id=1, source_target_pairs={{0,4},{4,0},{8,12},{12,8},{16,20},{20,16},{24,28},{28,24},{1,5},{5... | collective-permute-start | bytes 3981320 | tf_op jit(solution)/shard_map/ppermute | solution.py:802
  120.8 30.3 %collective-permute-start.17 = (bf16[4,144,1152]{2,1,0:T(8,128)(2,1)}, bf16[4,144,1152]{2,1,0:T(8,128)(2,1)}, u32[]{:S(2)}, u32[]{:S(2)}) collective-permute-start(bf16[4,144,1152]{2,1,0:T(8,128)(2,1)} %collective-permute-done.16.refs_1_), channel_id=1, source_target_pairs={{0,16},{4,12},{8,24},{12,4},{16,0},{20,28},{24,8},{28,20},{1,17},{... | collective-permute-start | bytes 3981320 | tf_op jit(solution)/shard_map/ppermute | solution.py:798
  127.4 29.6 %collective-permute-start.15 = (bf16[4,144,1152]{2,1,0:T(8,128)(2,1)}, bf16[4,144,1152]{2,1,0:T(8,128)(2,1)S(1)}, u32[]{:S(2)}, u32[]{:S(2)}) collective-permute-start(bf16[4,144,1152]{2,1,0:T(8,128)(2,1)} %bitcast.19.refs_0_), channel_id=1, source_target_pairs={{0,8},{4,20},{8,0},{12,28},{16,24},{20,4},{24,16},{28,12},{1,9},{5... | collective-permute-start | bytes 3981320 | tf_op jit(solution)/shard_map/ppermute | solution.py:798
  129.5 35.1 %collective-permute-start.18 = (bf16[4,144,1152]{2,1,0:T(8,128)(2,1)}, bf16[4,144,1152]{2,1,0:T(8,128)(2,1)}, u32[]{:S(2)}, u32[]{:S(2)}) collective-permute-start(bf16[4,144,1152]{2,1,0:T(8,128)(2,1)} %bitcast.126), channel_id=1, source_target_pairs={{0,4},{4,0},{8,12},{12,8},{16,20},{20,16},{24,28},{28,24},{1,5},{5... | collective-permute-start | bytes 3981320 | tf_op jit(solution)/shard_map/ppermute | solution.py:802
  129.5 39.2 %collective-permute-start.19 = (bf16[4,144,1152]{2,1,0:T(8,128)(2,1)}, bf16[4,144,1152]{2,1,0:T(8,128)(2,1)}, u32[]{:S(2)}, u32[]{:S(2)}) collective-permute-start(bf16[4,144,1152]{2,1,0:T(8,128)(2,1)} %collective-permute-done.16.refs_1_), channel_id=1, source_target_pairs={{0,4},{4,0},{8,12},{12,8},{16,20},{20,16},{24,28},{28,24},{1,5},{5... | collective-permute-start | bytes 3981320 | tf_op jit(solution)/shard_map/ppermute | solution.py:802
  151.0 17.8 %collective-permute-start.21 = (bf16[4,144,1152]{2,1,0:T(8,128)(2,1)}, bf16[4,144,1152]{2,1,0:T(8,128)(2,1)}, u32[]{:S(2)}, u32[]{:S(2)}) collective-permute-start(bf16[4,144,1152]{2,1,0:T(8,128)(2,1)} %collective-permute-done.17.refs_3_), channel_id=1, source_target_pairs={{0,4},{4,0},{8,12},{12,8},{16,20},{20,16},{24,28},{28,24},{1,5},{5... | collective-permute-start | bytes 3981320 | tf_op jit(solution)/shard_map/ppermute | solution.py:802
  154.6 14.2 %collective-permute-start.20 = (bf16[4,144,1152]{2,1,0:T(8,128)(2,1)}, bf16[4,144,1152]{2,1,0:T(8,128)(2,1)}, u32[]{:S(2)}, u32[]{:S(2)}) collective-permute-start(bf16[4,144,1152]{2,1,0:T(8,128)(2,1)} %collective-permute-done.14.refs_2_), channel_id=1, source_target_pairs={{0,4},{4,0},{8,12},{12,8},{16,20},{20,16},{24,28},{28,24},{1,5},{5... | collective-permute-start | bytes 3981320 | tf_op jit(solution)/shard_map/ppermute | solution.py:802
  157.0 26.3 %collective-permute-start.22 = (bf16[4,144,1152]{2,1,0:T(8,128)(2,1)}, bf16[4,144,1152]{2,1,0:T(8,128)(2,1)}, u32[]{:S(2)}, u32[]{:S(2)}) collective-permute-start(bf16[4,144,1152]{2,1,0:T(8,128)(2,1)} %bitcast.19.refs_0_), channel_id=1, source_target_pairs={{0,16},{4,12},{8,24},{12,4},{16,0},{20,28},{24,8},{28,20},{1,17},{... | collective-permute-start | bytes 3981320 | tf_op jit(solution)/shard_map/ppermute | solution.py:798
  166.3 22.9 %collective-permute-start.23 = (bf16[4,144,1152]{2,1,0:T(8,128)(2,1)S(1)}, bf16[4,144,1152]{2,1,0:T(8,128)(2,1)S(1)}, u32[]{:S(2)}, u32[]{:S(2)}) collective-permute-start(bf16[4,144,1152]{2,1,0:T(8,128)(2,1)S(1)} %copy-done.40), channel_id=1, source_target_pairs={{0,16},{4,12},{8,24},{12,4},{16,0},{20,28},{24,8},{28,20},{1,17},{... | collective-permute-start | bytes 3981320 | tf_op jit(solution)/shard_map/ppermute | solution.py:798
  168.7 21.8 %collective-permute-start.24 = (bf16[4,144,1152]{2,1,0:T(8,128)(2,1)}, bf16[4,144,1152]{2,1,0:T(8,128)(2,1)S(1)}, u32[]{:S(2)}, u32[]{:S(2)}) collective-permute-start(bf16[4,144,1152]{2,1,0:T(8,128)(2,1)} %bitcast.19.refs_0_), channel_id=1, source_target_pairs={{0,4},{4,0},{8,12},{12,8},{16,20},{20,16},{24,28},{28,24},{1,5},{5... | collective-permute-start | bytes 3981320 | tf_op jit(solution)/shard_map/ppermute | solution.py:802
  183.3 7.2 %collective-permute-start.26 = (bf16[4,144,1152]{2,1,0:T(8,128)(2,1)}, bf16[4,144,1152]{2,1,0:T(8,128)(2,1)S(1)}, u32[]{:S(2)}, u32[]{:S(2)}) collective-permute-start(bf16[4,144,1152]{2,1,0:T(8,128)(2,1)} %collective-permute-done.22.refs_2_), channel_id=1, source_target_pairs={{0,4},{4,0},{8,12},{12,8},{16,20},{20,16},{24,28},{28,24},{1,5},{5... | collective-permute-start | bytes 3981320 | tf_op jit(solution)/shard_map/ppermute | solution.py:802
  183.9 6.7 %collective-permute-start.25 = (bf16[4,144,1152]{2,1,0:T(8,128)(2,1)S(1)}, bf16[4,144,1152]{2,1,0:T(8,128)(2,1)S(1)}, u32[]{:S(2)}, u32[]{:S(2)}) collective-permute-start(bf16[4,144,1152]{2,1,0:T(8,128)(2,1)S(1)} %copy-done.40), channel_id=1, source_target_pairs={{0,4},{4,0},{8,12},{12,8},{16,20},{20,16},{24,28},{28,24},{1,5},{5... | collective-permute-start | bytes 3981320 | tf_op jit(solution)/shard_map/ppermute | solution.py:802
  189.3 22.7 %copy-start.41 = (bf16[4,144,1152]{2,1,0:T(8,128)(2,1)}, bf16[4,144,1152]{2,1,0:T(8,128)(2,1)S(1)}, u32[]{:S(2)}) copy-start(bf16[4,144,1152]{2,1,0:T(8,128)(2,1)S(1)} %collective-permute-done.23.refs_3_) | copy-start | bytes 3981316
  189.3 3.1 collective-permute-start.27
  190.5 21.4 %copy-start.42 = (bf16[4,144,1152]{2,1,0:T(8,128)(2,1)}, bf16[4,144,1152]{2,1,0:T(8,128)(2,1)S(1)}, u32[]{:S(2)}) copy-start(bf16[4,144,1152]{2,1,0:T(8,128)(2,1)S(1)} %collective-permute-done.24.refs_4_) | copy-start | bytes 3981316
  211.9 10.1 %collective-permute-start.28 = (bf16[4,4,144,1152]{3,2,1,0:T(8,128)(2,1)}, bf16[4,4,144,1152]{3,2,1,0:T(8,128)(2,1)}, u32[]{:S(2)}, u32[]{:S(2)}) collective-permute-start(bf16[4,4,144,1152]{3,2,1,0:T(8,128)(2,1)} %get-tuple-element.102), channel_id=1, source_target_pairs={{0,4},{4,0},{8,12},{12,8},{16,20},{20,16},{24,28},{28,24},{1,5},{5... | collective-permute-start | bytes 15925256 | tf_op jit(solution)/shard_map/ppermute | solution.py:802
  228.7 33.0 %collective-permute-start.29 = (bf16[2,4,144,1152]{3,2,1,0:T(8,128)(2,1)}, bf16[2,4,144,1152]{3,2,1,0:T(8,128)(2,1)S(1)}, u32[]{:S(2)}, u32[]{:S(2)}) collective-permute-start(bf16[2,4,144,1152]{3,2,1,0:T(8,128)(2,1)} %get-tuple-element.103), channel_id=1, source_target_pairs={{0,16},{4,12},{8,24},{12,4},{16,0},{20,28},{24,8},{28,20},{1,17},{... | collective-permute-start | bytes 7962632 | tf_op jit(solution)/shard_map/ppermute | solution.py:798
  228.7 33.0 %copy-start.16 = (bf16[4,144,1152]{2,1,0:T(8,128)(2,1)S(1)}, bf16[4,144,1152]{2,1,0:T(8,128)(2,1)}, u32[]{:S(2)}) copy-start(bf16[4,144,1152]{2,1,0:T(8,128)(2,1)} %get-tuple-element.109) | copy-start | bytes 3981316
  261.7 25.0 %copy-start.7 = (bf16[2,4,144,1152]{3,2,1,0:T(8,128)(2,1)}, bf16[2,4,144,1152]{3,2,1,0:T(8,128)(2,1)S(1)}, u32[]{:S(2)}) copy-start(bf16[2,4,144,1152]{3,2,1,0:T(8,128)(2,1)S(1)} %collective-permute-done.29) | copy-start | bytes 7962628
  263.3 23.3 %collective-permute-start.30 = (bf16[4,144,1152]{2,1,0:T(8,128)(2,1)}, bf16[4,144,1152]{2,1,0:T(8,128)(2,1)S(1)}, u32[]{:S(2)}, u32[]{:S(2)}) collective-permute-start(bf16[4,144,1152]{2,1,0:T(8,128)(2,1)} %fusion.9), channel_id=1, source_target_pairs={{0,8},{4,20},{8,0},{12,28},{16,24},{20,4},{24,16},{28,12},{1,9},{5... | collective-permute-start | bytes 3981320 | tf_op jit(solution)/shard_map/ppermute | solution.py:798
  264.6 22.0 %copy-start.5 = (bf16[512,1152]{1,0:T(8,128)(2,1)S(1)}, bf16[512,1152]{1,0:T(8,128)(2,1)}, u32[]{:S(2)}) copy-start(bf16[512,1152]{1,0:T(8,128)(2,1)} %fusion.13.normed_ref) | copy-start | bytes 3538948
  303.8 9.1 %collective-permute-start.31 = (bf16[4,4,144,1152]{3,2,1,0:T(8,128)(2,1)}, bf16[4,4,144,1152]{3,2,1,0:T(8,128)(2,1)}, u32[]{:S(2)}, u32[]{:S(2)}) collective-permute-start(bf16[4,4,144,1152]{3,2,1,0:T(8,128)(2,1)} %get-tuple-element.119), channel_id=1, source_target_pairs={{0,4},{4,0},{8,12},{12,8},{16,20},{20,16},{24,28},{28,24},{1,5},{5... | collective-permute-start | bytes 15925256 | tf_op jit(solution)/shard_map/ppermute | solution.py:802
  319.9 32.3 %collective-permute-start.32 = (bf16[2,4,144,1152]{3,2,1,0:T(8,128)(2,1)}, bf16[2,4,144,1152]{3,2,1,0:T(8,128)(2,1)}, u32[]{:S(2)}, u32[]{:S(2)}) collective-permute-start(bf16[2,4,144,1152]{3,2,1,0:T(8,128)(2,1)} %get-tuple-element.120), channel_id=1, source_target_pairs={{0,16},{4,12},{8,24},{12,4},{16,0},{20,28},{24,8},{28,20},{1,17},{... | collective-permute-start | bytes 7962632 | tf_op jit(solution)/shard_map/ppermute | solution.py:798
  322.6 128.1 %reduce-scatter.6.cloned.1.call-start = ((), (), s32[]{:S(2)}) async-start(), calls=%async_computation.4 | async-start | bytes 1658880 | tf_op jit(solution)/shard_map/reduce_scatter | solution.py:851
  353.9 9.2 %collective-permute-start.33 = (bf16[4,4,144,1152]{3,2,1,0:T(8,128)(2,1)}, bf16[4,4,144,1152]{3,2,1,0:T(8,128)(2,1)}, u32[]{:S(2)}, u32[]{:S(2)}) collective-permute-start(bf16[4,4,144,1152]{3,2,1,0:T(8,128)(2,1)} %get-tuple-element.135), channel_id=1, source_target_pairs={{0,4},{4,0},{8,12},{12,8},{16,20},{20,16},{24,28},{28,24},{1,5},{5... | collective-permute-start | bytes 15925256 | tf_op jit(solution)/shard_map/ppermute | solution.py:802
  354.0 17.8 %collective-permute-start.34 = (bf16[4,144,1152]{2,1,0:T(8,128)(2,1)S(1)}, bf16[4,144,1152]{2,1,0:T(8,128)(2,1)S(1)}, u32[]{:S(2)}, u32[]{:S(2)}) collective-permute-start(bf16[4,144,1152]{2,1,0:T(8,128)(2,1)S(1)} %fusion.6), channel_id=1, source_target_pairs={{0,8},{4,20},{8,0},{12,28},{16,24},{20,4},{24,16},{28,12},{1,9},{5... | collective-permute-start | bytes 3981320 | tf_op jit(solution)/shard_map/ppermute | solution.py:798
  369.7 32.3 %collective-permute-start.39 = (bf16[2,4,144,1152]{3,2,1,0:T(8,128)(2,1)}, bf16[2,4,144,1152]{3,2,1,0:T(8,128)(2,1)}, u32[]{:S(2)}, u32[]{:S(2)}) collective-permute-start(bf16[2,4,144,1152]{3,2,1,0:T(8,128)(2,1)} %get-tuple-element.136), channel_id=1, source_target_pairs={{0,16},{4,12},{8,24},{12,4},{16,0},{20,28},{24,8},{28,20},{1,17},{... | collective-permute-start | bytes 7962632 | tf_op jit(solution)/shard_map/ppermute | solution.py:798
  374.7 87.8 %reduce-scatter.8.cloned.1.call-start = ((), (), s32[]{:S(2)}) async-start(), calls=%async_computation.5 | async-start | bytes 1658880 | tf_op jit(solution)/shard_map/reduce_scatter | solution.py:851
  374.8 27.2 %copy-start.13 = (bf16[4,144,1152]{2,1,0:T(8,128)(2,1)S(1)}, bf16[4,144,1152]{2,1,0:T(8,128)(2,1)}, u32[]{:S(2)}) copy-start(bf16[4,144,1152]{2,1,0:T(8,128)(2,1)} %get-tuple-element.142) | copy-start | bytes 3981316
  392.8 12.7 %collective-permute-start.35 = (bf16[2,2304]{1,0:T(2,128)(2,1)S(1)}, bf16[2,2304]{1,0:T(2,128)(2,1)S(1)}, u32[]{:S(2)}, u32[]{:S(2)}) collective-permute-start(bf16[2,2304]{1,0:T(2,128)(2,1)S(1)} %reshape.445), channel_id=1, source_target_pairs={{0,1},{1,0},{2,3},{3,2},{4,5},{5,4},{6,7},{7,6},{8,9},{9,8},{10,11... | collective-permute-start | bytes 27656 | tf_op jit(solution)/shard_map/ppermute | solution.py:856
  404.7 18.1 %collective-permute-start.40 = (bf16[4,144,1152]{2,1,0:T(8,128)(2,1)}, bf16[4,144,1152]{2,1,0:T(8,128)(2,1)}, u32[]{:S(2)}, u32[]{:S(2)}) collective-permute-start(bf16[4,144,1152]{2,1,0:T(8,128)(2,1)} %fusion.1), channel_id=1, source_target_pairs={{0,8},{4,20},{8,0},{12,28},{16,24},{20,4},{24,16},{28,12},{1,9},{5... | collective-permute-start | bytes 3981320 | tf_op jit(solution)/shard_map/ppermute | solution.py:798
  405.5 4.9 %collective-permute-start.36 = (bf16[4,2304]{1,0:T(4,128)(2,1)S(1)}, bf16[4,2304]{1,0:T(4,128)(2,1)S(1)}, u32[]{:S(2)}, u32[]{:S(2)}) collective-permute-start(bf16[4,2304]{1,0:T(4,128)(2,1)S(1)} %maximum_select_fusion.8), channel_id=1, source_target_pairs={{0,2},{1,3},{2,0},{3,1},{4,6},{5,7},{6,4},{7,5},{8,10},{9,11},{10,... | collective-permute-start | bytes 55304 | tf_op jit(solution)/shard_map/ppermute | solution.py:856
  411.0 5.3 %collective-permute-start.37 = (f32[290,128]{1,0:T(8,128)S(1)}, f32[290,128]{1,0:T(8,128)S(1)}, u32[]{:S(2)}, u32[]{:S(2)}) collective-permute-start(f32[290,128]{1,0:T(8,128)S(1)} %pad_maximum_fusion.2), channel_id=1, source_target_pairs={{0,1},{1,0},{2,3},{3,2},{4,5},{5,4},{6,7},{7,6},{8,9},{9,8},{10,11... | collective-permute-start | bytes 445448 | tf_op jit(solution)/shard_map/ppermute | solution.py:856
  416.3 12.2 %collective-permute-start.38 = (f32[290,128]{1,0:T(8,128)S(1)}, f32[290,128]{1,0:T(8,128)S(1)}, u32[]{:S(2)}, u32[]{:S(2)}) collective-permute-start(f32[290,128]{1,0:T(8,128)S(1)} %fusion.29), channel_id=1, source_target_pairs={{0,2},{1,3},{2,0},{3,1},{4,6},{5,7},{6,4},{7,5},{8,10},{9,11},{10,... | collective-permute-start | bytes 445448 | tf_op jit(solution)/shard_map/ppermute | solution.py:856
  426.4 21.7 %collective-permute-start.41 = (bf16[576,576]{0,1:T(8,128)(2,1)S(1)}, bf16[576,576]{0,1:T(8,128)(2,1)S(1)}, u32[]{:S(2)}, u32[]{:S(2)}) collective-permute-start(bf16[576,576]{0,1:T(8,128)(2,1)S(1)} %broadcast_select_fusion), channel_id=1, source_target_pairs={{0,16},{4,20},{8,24},{12,28},{16,0},{20,4},{24,8},{28,12},{1,17},{... | collective-permute-start | bytes 1990664 | tf_op jit(solution)/shard_map/ppermute | solution.py:856
  428.5 1.4 collective-permute-start.44
  429.9 5.3 %collective-permute-start.45 = (f32[218,128]{1,0:T(8,128)S(1)}, f32[218,128]{1,0:T(8,128)S(1)}, u32[]{:S(2)}, u32[]{:S(2)}) collective-permute-start(f32[218,128]{1,0:T(8,128)S(1)} %add.159), channel_id=1, source_target_pairs={{0,8},{4,12},{8,0},{12,4},{16,24},{20,28},{24,16},{28,20},{1,9},{5... | collective-permute-start | bytes 334856 | tf_op jit(solution)/shard_map/ppermute | solution.py:856
  435.2 10.8 %collective-permute-start.46 = (f32[218,128]{1,0:T(8,128)S(1)}, f32[218,128]{1,0:T(8,128)S(1)}, u32[]{:S(2)}, u32[]{:S(2)}) collective-permute-start(f32[218,128]{1,0:T(8,128)S(1)} %add.160), channel_id=1, source_target_pairs={{0,16},{4,20},{8,24},{12,28},{16,0},{20,4},{24,8},{28,12},{1,17},{... | collective-permute-start | bytes 334856 | tf_op jit(solution)/shard_map/ppermute | solution.py:856
  448.6 10.1 %collective-permute-start.42 = (bf16[288,576]{0,1:T(8,128)(2,1)S(1)}, bf16[288,576]{0,1:T(8,128)(2,1)S(1)}, u32[]{:S(2)}, u32[]{:S(2)}) collective-permute-start(bf16[288,576]{0,1:T(8,128)(2,1)S(1)} %broadcast_select_fusion.1), channel_id=1, source_target_pairs={{0,8},{4,12},{8,0},{12,4},{16,24},{20,28},{24,16},{28,20},{1,9},{5... | collective-permute-start | bytes 995336 | tf_op jit(solution)/shard_map/ppermute | solution.py:856
  459.0 1.6 collective-permute-start.43
  (36 other events, 411.7 us)
Sparse Core Ops, SparseCore 0:
  10.2 35.5 all-gather.6
  56.6 30.9 all-gather.10
  96.8 30.5 all-gather.8
  322.8 28.8 reduce-scatter.3
  374.8 30.1 reduce-scatter.5
  428.8 28.6 reduce-scatter.7

commit v8 on v7

--- a/solution.py
+++ b/solution.py
@@ -899,6 +899,19 @@
     return value
 
 
+def scatter_core_first(value, axis):
+    if not is_cube():
+        return lax.psum_scatter(value, axis, scatter_dimension=0, tiled=True)
+    bits = lax.axis_size(axis).bit_length() - 1
+    value = value.reshape((2,) * bits + (-1, value.shape[1]))
+    for bit in range(bits):
+        place = bits - 1 - bit
+        low, high = (lax.index_in_dim(value, side, place, keepdims=False) for side in range(2))
+        on = bit_of(axis, bit)
+        value = jnp.where(on, high, low) + swap_bit(jnp.where(on, low, high), axis, bit)
+    return value
+
+
 def small_sum(value, axis):
     if not is_cube():
         return lax.psum(value, axis)
@@ -1138,7 +1151,7 @@
     time_grads = contract_rows(time_rows, d_time_cols).astype(low)
     if cube:
         time_grads = after(time_grads, up_total)
-    time_grads = small_scatter(time_grads, "dp")
+    time_grads = scatter_core_first(time_grads, "dp")
     back = times_transposed(d_time_cols, time_weight).reshape(-1, LANES)
 
     vectors = jnp.concatenate(

time: 476 us -> 473 us (level)
  waiting for transfers between devices: 140 us -> 132 us
    ppermute x17, waiting for transfers between devices: 58.2 us -> 51.4 us  [swap_bit(): return lax.ppermute(value, axis, [(i, i ^ 1 << bit) for i in range(size)])]
  transfers between devices with their start and end apart: 53 -> 53, of which waited for: 27 -> 28; matrix products, arithmetic and copies ran while one was open for 10% -> 11% of each run, Pallas kernels for 36% -> 36%
where the time goes in v8:
time: 473 us; the launch traced here: 468 us
  Pallas kernels  217 us (46%)
  waiting for transfers between devices  132 us (28%)
  starting transfers between devices  40.7 us (9%)
  other arithmetic  30.6 us (6%)
  local copies, waits for them, and re-layouts  26.7 us (6%)
  between operations  15.3 us (3%)
  matrix products  5.79 us (1%)
    ppermute x17, waiting for transfers between devices, swap_bit(): return lax.ppermute(value, axis, [(i, i ^ 1 << bit) for i in range(size)])  51.4 us
    ppermute x15, waiting for transfers between devices, swap(): lax.ppermute(value, 'dp', [(i, i ^ NEAR[i & 1][hop]) for i in range(8)])  41.6 us
    pallas_call x2, Pallas kernels, piece_call(): pl.pallas_call(kernel, grid_spec=pltpu.PrefetchScalarGridSpec(num_scalar_...  35.4 us
    pallas_call x1, Pallas kernels, down_back(): pl.pallas_call(down_back_kernel, grid=(groups,), in_specs=[whole, whole,...  32.9 us
    pallas_call x2, Pallas kernels, slot_grad(): pl.pallas_call(kernel, grid_spec=pltpu.PrefetchScalarGridSpec(num_scalar_...  26.3 us
    pallas_call x1, Pallas kernels, attend_back(): pl.pallas_call(attend_back_kernel, grid=(groups,), in_specs=[pl.BlockSpec...  22 us
    pallas_call x3, Pallas kernels, add_halves(): pl.pallas_call(add_kernel, grid=(groups,), in_specs=[pl.BlockSpec((1, 1,...  20.2 us
    pallas_call x1, Pallas kernels, position_bias(): pl.pallas_call(bias_kernel, grid=(4,), in_specs=[pl.BlockSpec((tokens, to...  20.1 us
  transfers between devices with their start and end apart: 53, of which 28 were waited for; matrix products, arithmetic and copies ran while one was open for 11% of the time, Pallas kernels for 36%

profile of v8, /device:TPU:0, one launch (start us, length us, event | category | flops | bytes accessed | tf_op | source)
XLA Modules:
  0.0 467.8 jit_solution(157529283764124509)
XLA Ops:
  7.3 2.0 concatenate.137
  10.4 3.1 collective-permute-start.2
  14.5 3.6 collective-permute-done.2
  18.2 1.8 collective-permute-start.3
  20.2 7.8 %collective-permute-done.3 = bf16[2,144,576]{2,1,0:T(8,128)(2,1)S(1)} collective-permute-done((bf16[2,144,576]{2,1,0:T(8,128)(2,1)S(1)}, bf16[2,144,576]{2,1,0:T(8,128)(2,1)S(1)}, u32[]{:S(2)}, u32[]{:S(2)}) %collective-permute-start.3) | collective-permute-done | bytes 331808 | tf_op jit(solution)/shard_map/ppermute | solution.py:856
  28.7 1.8 collective-permute-done.4
  31.1 14.6 %all-gather.7.cloned.1.call-done = bf16[576,1152]{1,0:T(8,128)(2,1)} async-done(((bf16[144,1152]{1,0:T(8,128)(2,1)}), bf16[576,1152]{1,0:T(8,128)(2,1)}) %all-gather.7.cloned.1.call-update) | async-done | bytes 1327120 | tf_op jit(solution)/shard_map/all_gather | solution.py:1043
  45.7 1.5 collective-permute-start.7
  49.4 2.0 collective-permute-done
  51.4 1.6 collective-permute-start.1
  53.3 3.2 collective-permute-done.1
  58.0 1.5 collective-permute-start.8
  59.5 10.8 %collective-permute-done.7.refs_1_ = bf16[4,144,1152]{2,1,0:T(8,128)(2,1)} collective-permute-done((bf16[4,144,1152]{2,1,0:T(8,128)(2,1)}, bf16[4,144,1152]{2,1,0:T(8,128)(2,1)}, u32[]{:S(2)}, u32[]{:S(2)}) %collective-permute-start.7) | collective-permute-done | bytes 1327136 | tf_op jit(solution)/shard_map/ppermute | solution.py:798
  70.2 2.5 collective-permute-start.9
  72.7 20.1 %position_bias.1.bias_ref = f32[16,256,256]{2,1,0:T(8,128)} custom-call(s32[256,256]{1,0:T(8,128)} %index_ref.3, f32[16,1,1024]{2,1,0:T(1,128)} %reshape.469.table_ref), custom_call_target="tpu_custom_call" | custom-call | flops 20000000000 | bytes 1 | tf_op jit(solution)/shard_map/position_bias/pallas_call | solution.py:111
  98.9 1.7 collective-permute-done.5
  103.1 5.2 %collective-permute-done.6 = f32[2,8,576]{2,1,0:T(8,128)S(1)} collective-permute-done((f32[2,8,576]{2,1,0:T(8,128)S(1)}, f32[2,8,576]{2,1,0:T(8,128)S(1)}, u32[]{:S(2)}, u32[]{:S(2)}) %collective-permute-start.6) | collective-permute-done | bytes 36896 | tf_op jit(solution)/shard_map/ppermute | solution.py:856
  108.3 8.6 %collective-permute-done.16.refs_1_ = bf16[4,144,1152]{2,1,0:T(8,128)(2,1)} collective-permute-done((bf16[4,144,1152]{2,1,0:T(8,128)(2,1)}, bf16[4,144,1152]{2,1,0:T(8,128)(2,1)}, u32[]{:S(2)}, u32[]{:S(2)}) %collective-permute-start.16) | collective-permute-done | bytes 1327136 | tf_op jit(solution)/shard_map/ppermute | solution.py:798
  116.9 1.4 fusion.41
  119.3 1.5 fusion.13.normed_ref
  121.0 5.8 %all-gather.9.cloned.1.call-done = bf16[576,1152]{1,0:T(8,128)(2,1)} async-done(((bf16[144,1152]{1,0:T(8,128)(2,1)}), bf16[576,1152]{1,0:T(8,128)(2,1)}) %all-gather.9.cloned.1.call-update) | async-done | bytes 1327120 | tf_op jit(solution)/shard_map/all_gather | solution.py:1045
  129.5 21.0 %attend.1 = (bf16[4,512,896]{2,1,0:T(8,128)(2,1)}, bf16[4,2,4,256,256]{4,3,2,1,0:T(8,128)(2,1)}, bf16[4,512,288]{2,1,0:T(8,128)(2,1)}, bf16[1152,1152]{1,0:T(8,128)(2,1)}, bf16[4,1152,1152]{2,1,0:T(8,128)(2,1)}) custom-call(s32[8]{0:T(128)} %fusion.34.part_ref, bf16[512,1152]{1,0:T(8,128)(2,1)} %fusion.13.normed_ref, ...), custom_call_target="tpu_custom_call" | custom-call | flops 12999999488 | bytes 1 | tf_op jit(solution)/shard_map/attend/pallas_call | solution.py:228
  150.5 3.5 collective-permute-start.21
  154.0 2.5 collective-permute-done.15.refs_1_
  157.6 1.7 copy.76
  159.3 4.3 fusion.44
  164.0 1.7 copy-done.40
  166.7 1.5 add_convert_fusion.second_ref
  168.3 14.5 %up_forward.1 = (bf16[4,512,1152]{2,1,0:T(8,128)(2,1)}, bf16[4,512,1152]{2,1,0:T(8,128)(2,1)}, bf16[4,1152,1152]{2,1,0:T(8,128)(2,1)}) custom-call(s32[8]{0:T(128)} %fusion.34.part_ref, bf16[512,1152]{1,0:T(8,128)(2,1)} %add_convert_fusion.second_ref, f32[4,1,1152]{2,1,0:T(1,128)} %reshape.474.bias_ref, bf16[4,144,1152]{2,1,0:T(8,128)(2,1)} %bitcast.176, ...), custom_call_target="tpu_custom_call" | custom-call | flops 12999999488 | bytes 1 | tf_op jit(solution)/shard_map/up_forward/pallas_call | solution.py:228
  183.4 5.3 %collective-permute-done.23.refs_3_ = bf16[4,144,1152]{2,1,0:T(8,128)(2,1)S(1)} collective-permute-done((bf16[4,144,1152]{2,1,0:T(8,128)(2,1)S(1)}, bf16[4,144,1152]{2,1,0:T(8,128)(2,1)S(1)}, u32[]{:S(2)}, u32[]{:S(2)}) %collective-permute-start.23) | collective-permute-done | bytes 1327136 | tf_op jit(solution)/shard_map/ppermute | solution.py:798
  190.0 1.8 collective-permute-done.27.refs_7_
  192.8 18.5 %down_grad.1 = (bf16[4,4,144,1152]{3,2,1,0:T(8,128)(2,1)}, bf16[4,4,144,1152]{3,2,1,0:T(8,128)(2,1)}) custom-call(s32[8]{0:T(128)} %fusion.33.slot_ref, bf16[4,512,1152]{2,1,0:T(8,128)(2,1)} %get-tuple-element.99.left_ref.activ_ref, bf16[512,1152]{1,0:T(8,128)(2,1)} %bitcast.177), custom_call_target="tpu_custom_call" | custom-call | flops 17999998976 | bytes 1 | tf_op jit(solution)/shard_map/down_grad/pallas_call | solution.py:690
  212.6 8.8 %unpack_pieces.1.down_ref = bf16[4608,1152]{1,0:T(8,128)(2,1)} custom-call(s32[8]{0:T(128)} %fusion.34.part_ref, bf16[4,144,1152]{2,1,0:T(8,128)(2,1)} %bitcast.19.refs_0_, bf16[4,144,1152]{2,1,0:T(8,128)(2,1)} %copy-done.39, bf16[4,144,1152]{2,1,0:T(8,128)(2,1)} %collective-permute-done.22.refs_2_, bf16[4,144,1152]{2,1,0:T(8,128)(2,1)} %copy-done.41, ...), custom_call_target="tpu_custom_call" | custom-call | flops 8999999488 | bytes 1 | tf_op jit(solution)/shard_map/unpack_pieces/pallas_call | solution.py:757
  221.5 6.6 %add_halves.3 = (bf16[4,144,1152]{2,1,0:T(8,128)(2,1)}, bf16[4,144,1152]{2,1,0:T(8,128)(2,1)}, bf16[2,4,144,1152]{3,2,1,0:T(8,128)(2,1)}) custom-call(bf16[4,4,144,1152]{3,2,1,0:T(8,128)(2,1)} %get-tuple-element.101.one_ref.two_ref.three_ref.four_ref, bf16[4,4,144,1152]{3,2,1,0:T(8,128)(2,1)} %get-tuple-element.101.one_ref.two_ref.three_ref.four_ref, ...), custom_call_target="tpu_custom_call" | custom-call | flops 7000000000 | bytes 1 | tf_op jit(solution)/shard_map/add_halves/pallas_call | solution.py:721
  228.1 32.9 %down_back.1 = (bf16[4,512,1152]{2,1,0:T(8,128)(2,1)}, bf16[512,1152]{1,0:T(8,128)(2,1)}, f32[512,1152]{1,0:T(8,128)}, bf16[512,1152]{1,0:T(8,128)(2,1)}, f32[8,1152]{1,0:T(8,128)}, /*index=5*/f32[4,1,1152]{2,1,0:T(1,128)}) custom-call(bf16[512,1152]{1,0:T(8,128)(2,1)} %bitcast.178, f32[512,1152]{1,0:T(8,128)} %copy-done, ...), custom_call_target="tpu_custom_call" | custom-call | flops 32999999488 | bytes 1 | tf_op jit(solution)/shard_map/down_back/pallas_call | solution.py:429
  261.1 1.6 fusion.9
  264.1 22.0 %attend_back.1 = (bf16[4,512,1152]{2,1,0:T(8,128)(2,1)}, f32[16,256,256]{2,1,0:T(8,128)}, f32[4,2,864]{2,1,0:T(2,128)}) custom-call(bf16[512,1152]{1,0:T(8,128)(2,1)} %get-tuple-element.110.hidden_ref, bf16[1152,1152]{1,0:T(8,128)(2,1)} %get-tuple-element.91.proj_ref, bf16[4,512,896]{2,1,0:T(8,128)(2,1)} %get-tuple-element.111.qkv_ref, ...), custom_call_target="tpu_custom_call" | custom-call | flops 19000000512 | bytes 1 | tf_op jit(solution)/shard_map/attend_back/pallas_call | solution.py:514
  287.6 14.1 %pair_grad.1 = (bf16[4,4,144,1152]{3,2,1,0:T(8,128)(2,1)}, bf16[4,4,144,1152]{3,2,1,0:T(8,128)(2,1)}) custom-call(s32[8]{0:T(128)} %fusion.33.slot_ref, bf16[1152,512]{1,0:T(8,128)(2,1)} %copy.77.one_ref, bf16[1152,512]{1,0:T(8,128)(2,1)} %bitcast.153, bf16[4,512,1152]{2,1,0:T(8,128)(2,1)} %get-tuple-element.113.right_ref), custom_call_target="tpu_custom_call" | custom-call | flops 17999998976 | bytes 1 | tf_op jit(solution)/shard_map/pair_grad/pallas_call | solution.py:650
  301.7 1.6 fusion.8
  303.3 9.1 %collective-permute-done.31.came_ref = bf16[4,4,144,1152]{3,2,1,0:T(8,128)(2,1)} collective-permute-done((bf16[4,4,144,1152]{3,2,1,0:T(8,128)(2,1)}, bf16[4,4,144,1152]{3,2,1,0:T(8,128)(2,1)}, u32[]{:S(2)}, u32[]{:S(2)}) %collective-permute-start.31) | collective-permute-done | bytes 5308448 | tf_op jit(solution)/shard_map/ppermute | solution.py:802
  312.4 7.0 %add_halves.4 = (bf16[4,144,1152]{2,1,0:T(8,128)(2,1)}, bf16[4,144,1152]{2,1,0:T(8,128)(2,1)}, bf16[2,4,144,1152]{3,2,1,0:T(8,128)(2,1)}) custom-call(bf16[4,4,144,1152]{3,2,1,0:T(8,128)(2,1)} %get-tuple-element.116.one_ref.two_ref.three_ref.four_ref, bf16[4,4,144,1152]{3,2,1,0:T(8,128)(2,1)} %get-tuple-element.116.one_ref.two_ref.three_ref.four_ref, ...), custom_call_target="tpu_custom_call" | custom-call | flops 7000000000 | bytes 1 | tf_op jit(solution)/shard_map/add_halves/pallas_call | solution.py:721
  319.4 2.0 collective-permute-start.32
  323.3 1.6 copy.78.one_ref
  324.9 12.2 %up_grad.1 = (bf16[4,4,144,1152]{3,2,1,0:T(8,128)(2,1)}, bf16[4,4,144,1152]{3,2,1,0:T(8,128)(2,1)}) custom-call(s32[8]{0:T(128)} %fusion.33.slot_ref, bf16[1152,512]{1,0:T(8,128)(2,1)} %copy.78.one_ref, bf16[4,512,1152]{2,1,0:T(8,128)(2,1)} %get-tuple-element.122.right_ref), custom_call_target="tpu_custom_call" | custom-call | flops 17999998976 | bytes 1 | tf_op jit(solution)/shard_map/up_grad/pallas_call | solution.py:650
  337.1 14.3 %input_grad.1 = (bf16[512,1152]{1,0:T(8,128)(2,1)}, f32[8,1152]{1,0:T(8,128)}) custom-call(bf16[4,512,1152]{2,1,0:T(8,128)(2,1)} %get-tuple-element.113.right_ref, bf16[4,1152,1152]{2,1,0:T(8,128)(2,1)} %get-tuple-element.124.weight_ref, bf16[512,1152]{1,0:T(8,128)(2,1)} %bitcast.145, f32[512,1152]{1,0:T(8,128)} %get-tuple-element.125.d_hidden_ref, ...), custom_call_target="tpu_custom_call" | custom-call | flops 1000000000 | bytes 1 | tf_op jit(solution)/shard_map/input_grad/pallas_call | solution.py:581
  351.7 1.6 fusion.6
  355.0 7.5 %collective-permute-done.33.came_ref = bf16[4,4,144,1152]{3,2,1,0:T(8,128)(2,1)} collective-permute-done((bf16[4,4,144,1152]{3,2,1,0:T(8,128)(2,1)}, bf16[4,4,144,1152]{3,2,1,0:T(8,128)(2,1)}, u32[]{:S(2)}, u32[]{:S(2)}) %collective-permute-start.33) | collective-permute-done | bytes 5308448 | tf_op jit(solution)/shard_map/ppermute | solution.py:802
  362.5 6.6 %add_halves.5 = (bf16[4,144,1152]{2,1,0:T(8,128)(2,1)}, bf16[4,144,1152]{2,1,0:T(8,128)(2,1)}, bf16[2,4,144,1152]{3,2,1,0:T(8,128)(2,1)}) custom-call(bf16[4,4,144,1152]{3,2,1,0:T(8,128)(2,1)} %get-tuple-element.134.one_ref.two_ref.three_ref.four_ref, bf16[4,4,144,1152]{3,2,1,0:T(8,128)(2,1)} %get-tuple-element.134.one_ref.two_ref.three_ref.four_ref, ...), custom_call_target="tpu_custom_call" | custom-call | flops 7000000000 | bytes 1 | tf_op jit(solution)/shard_map/add_halves/pallas_call | solution.py:721
  369.1 2.0 collective-permute-start.39
  371.3 2.9 fusion.5
  374.2 17.7 %table_gradient.1 = f32[128,128]{1,0:T(8,128)} custom-call(s32[256,256]{1,0:T(8,128)} %index_ref.3, f32[16,256,256]{2,1,0:T(8,128)} %get-tuple-element.138.pairs_ref), custom_call_target="tpu_custom_call" | custom-call | flops 17999998976 | bytes 1 | tf_op jit(solution)/shard_map/table_gradient/pallas_call | solution.py:167
  393.1 8.3 %collective-permute-done.39 = bf16[2,4,144,1152]{3,2,1,0:T(8,128)(2,1)} collective-permute-done((bf16[2,4,144,1152]{3,2,1,0:T(8,128)(2,1)}, bf16[2,4,144,1152]{3,2,1,0:T(8,128)(2,1)}, u32[]{:S(2)}, u32[]{:S(2)}) %collective-permute-start.39) | collective-permute-done | bytes 2654240 | tf_op jit(solution)/shard_map/ppermute | solution.py:798
  401.5 2.7 fusion.1
  405.9 4.0 collective-permute-done.36
  411.6 4.1 collective-permute-done.37
  416.5 5.8 %collective-permute-done.40 = bf16[4,144,1152]{2,1,0:T(8,128)(2,1)} collective-permute-done((bf16[4,144,1152]{2,1,0:T(8,128)(2,1)}, bf16[4,144,1152]{2,1,0:T(8,128)(2,1)}, u32[]{:S(2)}, u32[]{:S(2)}) %collective-permute-start.40) | collective-permute-done | bytes 1327136 | tf_op jit(solution)/shard_map/ppermute | solution.py:798
  422.3 3.7 fusion.3
  430.6 4.7 collective-permute-done.45
  435.3 2.1 collective-permute-start.46
  437.9 2.2 collective-permute-done.46
  444.5 7.4 %collective-permute-done.42 = bf16[2,144,576]{2,1,0:T(8,128)(2,1)S(1)} collective-permute-done((bf16[2,144,576]{2,1,0:T(8,128)(2,1)S(1)}, bf16[2,144,576]{2,1,0:T(8,128)(2,1)S(1)}, u32[]{:S(2)}, u32[]{:S(2)}) %collective-permute-start.42) | collective-permute-done | bytes 331808 | tf_op jit(solution)/shard_map/ppermute | solution.py:856
  452.1 1.8 collective-permute-start.43
  454.9 2.8 collective-permute-done.43
  458.9 1.9 bitcast_convert_fusion
  (283 shorter events, 50.6 us)
Async XLA Ops:
  7.2 38.5 %all-gather.7.cloned.1.call-start = ((), (), s32[]{:S(2)}) async-start(), calls=%async_computation.6 | async-start | bytes 1658880 | tf_op jit(solution)/shard_map/all_gather | solution.py:1043
  9.3 19.0 %copy-start.46 = (s32[2]{0:T(128)S(1)}, s32[2]{0:T(128)}, u32[]{:S(2)}) copy-start(s32[2]{0:T(128)} %param.25) | copy-start | bytes 28
  9.3 83.5 %all-gather.11.cloned.1.call-start = ((), (), s32[]{:S(2)}) async-start(), calls=%async_computation.8 | async-start | bytes 1658880 | tf_op jit(solution)/shard_map/all_gather | solution.py:1044
  10.4 7.7 %collective-permute-start.2 = (bf16[144,576]{1,0:T(8,128)(2,1)S(1)}, bf16[144,576]{1,0:T(8,128)(2,1)S(1)}, u32[]{:S(2)}, u32[]{:S(2)}) collective-permute-start(bf16[144,576]{1,0:T(8,128)(2,1)S(1)} %pad_maximum_fusion.1), channel_id=1, source_target_pairs={{0,16},{4,20},{8,24},{12,28},{16,0},{20,4},{24,8},{28,12},{1,17},{... | collective-permute-start | bytes 497672 | tf_op jit(solution)/shard_map/ppermute | solution.py:856
  18.2 9.8 %collective-permute-start.3 = (bf16[2,144,576]{2,1,0:T(8,128)(2,1)S(1)}, bf16[2,144,576]{2,1,0:T(8,128)(2,1)S(1)}, u32[]{:S(2)}, u32[]{:S(2)}) collective-permute-start(bf16[2,144,576]{2,1,0:T(8,128)(2,1)S(1)} %maximum_select_fusion.3), channel_id=1, source_target_pairs={{0,8},{4,12},{8,0},{12,4},{16,24},{20,28},{24,16},{28,20},{1,9},{5... | collective-permute-start | bytes 995336 | tf_op jit(solution)/shard_map/ppermute | solution.py:856
  28.2 2.3 collective-permute-start.4
  31.0 22.0 %copy-start.2 = (bf16[2,256,1152]{2,1,0:T(8,128)(2,1)S(1)}, bf16[2,256,1152]{2,1,0:T(8,128)(2,1)}, u32[]{:S(2)}) copy-start(bf16[2,256,1152]{2,1,0:T(8,128)(2,1)} %param.23) | copy-start | bytes 3538948
  31.1 65.3 %copy-start.3 = (bf16[2,2,2,144,576]{4,3,2,1,0:T(8,128)(2,1)}, bf16[2,2,2,144,576]{4,3,2,1,0:T(8,128)(2,1)S(1)}, u32[]{:S(2)}) copy-start(bf16[2,2,2,144,576]{4,3,2,1,0:T(8,128)(2,1)S(1)} %copy.71) | copy-start | bytes 3981316
  45.7 24.5 %collective-permute-start.7 = (bf16[4,144,1152]{2,1,0:T(8,128)(2,1)}, bf16[4,144,1152]{2,1,0:T(8,128)(2,1)}, u32[]{:S(2)}, u32[]{:S(2)}) collective-permute-start(bf16[4,144,1152]{2,1,0:T(8,128)(2,1)} %bitcast.169), channel_id=1, source_target_pairs={{0,8},{4,20},{8,0},{12,28},{16,24},{20,4},{24,16},{28,12},{1,9},{5... | collective-permute-start | bytes 3981320 | tf_op jit(solution)/shard_map/ppermute | solution.py:798
  47.6 3.8 collective-permute-start
  51.4 5.0 %collective-permute-start.1 = (bf16[2,74,128]{2,1,0:T(8,128)(2,1)S(1)}, bf16[2,74,128]{2,1,0:T(8,128)(2,1)S(1)}, u32[]{:S(2)}, u32[]{:S(2)}) collective-permute-start(bf16[2,74,128]{2,1,0:T(8,128)(2,1)S(1)} %maximum_select_fusion.6), channel_id=1, source_target_pairs={{0,2},{1,3},{2,0},{3,1},{4,6},{5,7},{6,4},{7,5},{8,10},{9,11},{10,... | collective-permute-start | bytes 113672 | tf_op jit(solution)/shard_map/ppermute | solution.py:856
  56.5 70.4 %all-gather.9.cloned.1.call-start = ((), (), s32[]{:S(2)}) async-start(), calls=%async_computation.7 | async-start | bytes 1658880 | tf_op jit(solution)/shard_map/all_gather | solution.py:1045
  58.0 36.2 %copy-start.19 = (bf16[144,288]{0,1:T(8,128)(2,1)S(1)}, bf16[144,288]{0,1:T(8,128)(2,1)}, u32[]{:S(2)}) copy-start(bf16[144,288]{0,1:T(8,128)(2,1)} %get-tuple-element.215) | copy-start | bytes 248836
  58.0 34.8 %collective-permute-start.8 = (bf16[4,144,1152]{2,1,0:T(8,128)(2,1)}, bf16[4,144,1152]{2,1,0:T(8,128)(2,1)}, u32[]{:S(2)}, u32[]{:S(2)}) collective-permute-start(bf16[4,144,1152]{2,1,0:T(8,128)(2,1)} %bitcast.170), channel_id=1, source_target_pairs={{0,16},{4,12},{8,24},{12,4},{16,0},{20,28},{24,8},{28,20},{1,17},{... | collective-permute-start | bytes 3981320 | tf_op jit(solution)/shard_map/ppermute | solution.py:798
  70.2 31.3 %collective-permute-start.9 = (bf16[4,144,1152]{2,1,0:T(8,128)(2,1)}, bf16[4,144,1152]{2,1,0:T(8,128)(2,1)}, u32[]{:S(2)}, u32[]{:S(2)}) collective-permute-start(bf16[4,144,1152]{2,1,0:T(8,128)(2,1)} %collective-permute-done.7.refs_1_), channel_id=1, source_target_pairs={{0,16},{4,12},{8,24},{12,4},{16,0},{20,28},{24,8},{28,20},{1,17},{... | collective-permute-start | bytes 3981320 | tf_op jit(solution)/shard_map/ppermute | solution.py:798
  92.8 24.1 %collective-permute-start.16 = (bf16[4,144,1152]{2,1,0:T(8,128)(2,1)}, bf16[4,144,1152]{2,1,0:T(8,128)(2,1)}, u32[]{:S(2)}, u32[]{:S(2)}) collective-permute-start(bf16[4,144,1152]{2,1,0:T(8,128)(2,1)} %bitcast.173), channel_id=1, source_target_pairs={{0,8},{4,20},{8,0},{12,28},{16,24},{20,4},{24,16},{28,12},{1,9},{5... | collective-permute-start | bytes 3981320 | tf_op jit(solution)/shard_map/ppermute | solution.py:798
  96.1 257.2 %reduce-scatter.4.cloned.1.call-start = ((), (), s32[]{:S(2)}) async-start(), calls=%async_computation.3 | async-start | bytes 1658880 | tf_op jit(solution)/shard_map/reduce_scatter | solution.py:851
  96.4 54.0 %copy-start.22 = (bf16[8,1152]{1,0:T(8,128)(2,1)}, bf16[8,1152]{1,0:T(8,128)(2,1)S(1)}, u32[]{:S(2)}) copy-start(bf16[8,1152]{1,0:T(8,128)(2,1)S(1)} %reshape.449) | copy-start | bytes 55300
  96.7 3.8 collective-permute-start.5
  100.6 7.8 %collective-permute-start.6 = (f32[2,8,576]{2,1,0:T(8,128)S(1)}, f32[2,8,576]{2,1,0:T(8,128)S(1)}, u32[]{:S(2)}, u32[]{:S(2)}) collective-permute-start(f32[2,8,576]{2,1,0:T(8,128)S(1)} %maximum_select_fusion.7), channel_id=1, source_target_pairs={{0,2},{1,3},{2,0},{3,1},{4,6},{5,7},{6,4},{7,5},{8,10},{9,11},{10,... | collective-permute-start | bytes 110600 | tf_op jit(solution)/shard_map/ppermute | solution.py:856
  101.5 25.3 %collective-permute-start.10 = (bf16[4,144,1152]{2,1,0:T(8,128)(2,1)}, bf16[4,144,1152]{2,1,0:T(8,128)(2,1)}, u32[]{:S(2)}, u32[]{:S(2)}) collective-permute-start(bf16[4,144,1152]{2,1,0:T(8,128)(2,1)} %bitcast.171), channel_id=1, source_target_pairs={{0,4},{4,0},{8,12},{12,8},{16,20},{20,16},{24,28},{28,24},{1,5},{5... | collective-permute-start | bytes 3981320 | tf_op jit(solution)/shard_map/ppermute | solution.py:802
  101.5 19.4 %collective-permute-start.14 = (bf16[4,144,1152]{2,1,0:T(8,128)(2,1)}, bf16[4,144,1152]{2,1,0:T(8,128)(2,1)}, u32[]{:S(2)}, u32[]{:S(2)}) collective-permute-start(bf16[4,144,1152]{2,1,0:T(8,128)(2,1)} %bitcast.174), channel_id=1, source_target_pairs={{0,16},{4,12},{8,24},{12,4},{16,0},{20,28},{24,8},{28,20},{1,17},{... | collective-permute-start | bytes 3981320 | tf_op jit(solution)/shard_map/ppermute | solution.py:798
  102.3 26.6 %collective-permute-start.11 = (bf16[4,144,1152]{2,1,0:T(8,128)(2,1)}, bf16[4,144,1152]{2,1,0:T(8,128)(2,1)}, u32[]{:S(2)}, u32[]{:S(2)}) collective-permute-start(bf16[4,144,1152]{2,1,0:T(8,128)(2,1)} %collective-permute-done.7.refs_1_), channel_id=1, source_target_pairs={{0,4},{4,0},{8,12},{12,8},{16,20},{20,16},{24,28},{28,24},{1,5},{5... | collective-permute-start | bytes 3981320 | tf_op jit(solution)/shard_map/ppermute | solution.py:802
  108.3 20.6 %collective-permute-start.12 = (bf16[4,144,1152]{2,1,0:T(8,128)(2,1)}, bf16[4,144,1152]{2,1,0:T(8,128)(2,1)}, u32[]{:S(2)}, u32[]{:S(2)}) collective-permute-start(bf16[4,144,1152]{2,1,0:T(8,128)(2,1)} %collective-permute-done.8.refs_2_), channel_id=1, source_target_pairs={{0,4},{4,0},{8,12},{12,8},{16,20},{20,16},{24,28},{28,24},{1,5},{5... | collective-permute-start | bytes 3981320 | tf_op jit(solution)/shard_map/ppermute | solution.py:802
  116.9 12.6 %collective-permute-start.13 = (bf16[4,144,1152]{2,1,0:T(8,128)(2,1)}, bf16[4,144,1152]{2,1,0:T(8,128)(2,1)}, u32[]{:S(2)}, u32[]{:S(2)}) collective-permute-start(bf16[4,144,1152]{2,1,0:T(8,128)(2,1)} %collective-permute-done.9.refs_3_), channel_id=1, source_target_pairs={{0,4},{4,0},{8,12},{12,8},{16,20},{20,16},{24,28},{28,24},{1,5},{5... | collective-permute-start | bytes 3981320 | tf_op jit(solution)/shard_map/ppermute | solution.py:802
  121.0 29.5 %collective-permute-start.17 = (bf16[4,144,1152]{2,1,0:T(8,128)(2,1)}, bf16[4,144,1152]{2,1,0:T(8,128)(2,1)}, u32[]{:S(2)}, u32[]{:S(2)}) collective-permute-start(bf16[4,144,1152]{2,1,0:T(8,128)(2,1)} %collective-permute-done.16.refs_1_), channel_id=1, source_target_pairs={{0,16},{4,12},{8,24},{12,4},{16,0},{20,28},{24,8},{28,20},{1,17},{... | collective-permute-start | bytes 3981320 | tf_op jit(solution)/shard_map/ppermute | solution.py:798
  126.9 29.6 %collective-permute-start.15 = (bf16[4,144,1152]{2,1,0:T(8,128)(2,1)}, bf16[4,144,1152]{2,1,0:T(8,128)(2,1)S(1)}, u32[]{:S(2)}, u32[]{:S(2)}) collective-permute-start(bf16[4,144,1152]{2,1,0:T(8,128)(2,1)} %bitcast.19.refs_0_), channel_id=1, source_target_pairs={{0,8},{4,20},{8,0},{12,28},{16,24},{20,4},{24,16},{28,12},{1,9},{5... | collective-permute-start | bytes 3981320 | tf_op jit(solution)/shard_map/ppermute | solution.py:798
  129.0 35.1 %collective-permute-start.18 = (bf16[4,144,1152]{2,1,0:T(8,128)(2,1)}, bf16[4,144,1152]{2,1,0:T(8,128)(2,1)}, u32[]{:S(2)}, u32[]{:S(2)}) collective-permute-start(bf16[4,144,1152]{2,1,0:T(8,128)(2,1)} %bitcast.175), channel_id=1, source_target_pairs={{0,4},{4,0},{8,12},{12,8},{16,20},{20,16},{24,28},{28,24},{1,5},{5... | collective-permute-start | bytes 3981320 | tf_op jit(solution)/shard_map/ppermute | solution.py:802
  129.0 39.2 %collective-permute-start.19 = (bf16[4,144,1152]{2,1,0:T(8,128)(2,1)}, bf16[4,144,1152]{2,1,0:T(8,128)(2,1)}, u32[]{:S(2)}, u32[]{:S(2)}) collective-permute-start(bf16[4,144,1152]{2,1,0:T(8,128)(2,1)} %collective-permute-done.16.refs_1_), channel_id=1, source_target_pairs={{0,4},{4,0},{8,12},{12,8},{16,20},{20,16},{24,28},{28,24},{1,5},{5... | collective-permute-start | bytes 3981320 | tf_op jit(solution)/shard_map/ppermute | solution.py:802
  150.5 17.8 %collective-permute-start.21 = (bf16[4,144,1152]{2,1,0:T(8,128)(2,1)}, bf16[4,144,1152]{2,1,0:T(8,128)(2,1)}, u32[]{:S(2)}, u32[]{:S(2)}) collective-permute-start(bf16[4,144,1152]{2,1,0:T(8,128)(2,1)} %collective-permute-done.17.refs_3_), channel_id=1, source_target_pairs={{0,4},{4,0},{8,12},{12,8},{16,20},{20,16},{24,28},{28,24},{1,5},{5... | collective-permute-start | bytes 3981320 | tf_op jit(solution)/shard_map/ppermute | solution.py:802
  154.0 14.2 %collective-permute-start.20 = (bf16[4,144,1152]{2,1,0:T(8,128)(2,1)}, bf16[4,144,1152]{2,1,0:T(8,128)(2,1)}, u32[]{:S(2)}, u32[]{:S(2)}) collective-permute-start(bf16[4,144,1152]{2,1,0:T(8,128)(2,1)} %collective-permute-done.14.refs_2_), channel_id=1, source_target_pairs={{0,4},{4,0},{8,12},{12,8},{16,20},{20,16},{24,28},{28,24},{1,5},{5... | collective-permute-start | bytes 3981320 | tf_op jit(solution)/shard_map/ppermute | solution.py:802
  156.5 26.3 %collective-permute-start.22 = (bf16[4,144,1152]{2,1,0:T(8,128)(2,1)}, bf16[4,144,1152]{2,1,0:T(8,128)(2,1)}, u32[]{:S(2)}, u32[]{:S(2)}) collective-permute-start(bf16[4,144,1152]{2,1,0:T(8,128)(2,1)} %bitcast.19.refs_0_), channel_id=1, source_target_pairs={{0,16},{4,12},{8,24},{12,4},{16,0},{20,28},{24,8},{28,20},{1,17},{... | collective-permute-start | bytes 3981320 | tf_op jit(solution)/shard_map/ppermute | solution.py:798
  165.8 22.9 %collective-permute-start.23 = (bf16[4,144,1152]{2,1,0:T(8,128)(2,1)S(1)}, bf16[4,144,1152]{2,1,0:T(8,128)(2,1)S(1)}, u32[]{:S(2)}, u32[]{:S(2)}) collective-permute-start(bf16[4,144,1152]{2,1,0:T(8,128)(2,1)S(1)} %copy-done.40), channel_id=1, source_target_pairs={{0,16},{4,12},{8,24},{12,4},{16,0},{20,28},{24,8},{28,20},{1,17},{... | collective-permute-start | bytes 3981320 | tf_op jit(solution)/shard_map/ppermute | solution.py:798
  168.2 21.8 %collective-permute-start.24 = (bf16[4,144,1152]{2,1,0:T(8,128)(2,1)}, bf16[4,144,1152]{2,1,0:T(8,128)(2,1)S(1)}, u32[]{:S(2)}, u32[]{:S(2)}) collective-permute-start(bf16[4,144,1152]{2,1,0:T(8,128)(2,1)} %bitcast.19.refs_0_), channel_id=1, source_target_pairs={{0,4},{4,0},{8,12},{12,8},{16,20},{20,16},{24,28},{28,24},{1,5},{5... | collective-permute-start | bytes 3981320 | tf_op jit(solution)/shard_map/ppermute | solution.py:802
  182.8 7.2 %collective-permute-start.26 = (bf16[4,144,1152]{2,1,0:T(8,128)(2,1)}, bf16[4,144,1152]{2,1,0:T(8,128)(2,1)S(1)}, u32[]{:S(2)}, u32[]{:S(2)}) collective-permute-start(bf16[4,144,1152]{2,1,0:T(8,128)(2,1)} %collective-permute-done.22.refs_2_), channel_id=1, source_target_pairs={{0,4},{4,0},{8,12},{12,8},{16,20},{20,16},{24,28},{28,24},{1,5},{5... | collective-permute-start | bytes 3981320 | tf_op jit(solution)/shard_map/ppermute | solution.py:802
  183.3 6.6 %collective-permute-start.25 = (bf16[4,144,1152]{2,1,0:T(8,128)(2,1)S(1)}, bf16[4,144,1152]{2,1,0:T(8,128)(2,1)S(1)}, u32[]{:S(2)}, u32[]{:S(2)}) collective-permute-start(bf16[4,144,1152]{2,1,0:T(8,128)(2,1)S(1)} %copy-done.40), channel_id=1, source_target_pairs={{0,4},{4,0},{8,12},{12,8},{16,20},{20,16},{24,28},{28,24},{1,5},{5... | collective-permute-start | bytes 3981320 | tf_op jit(solution)/shard_map/ppermute | solution.py:802
  188.7 22.7 %copy-start.41 = (bf16[4,144,1152]{2,1,0:T(8,128)(2,1)}, bf16[4,144,1152]{2,1,0:T(8,128)(2,1)S(1)}, u32[]{:S(2)}) copy-start(bf16[4,144,1152]{2,1,0:T(8,128)(2,1)S(1)} %collective-permute-done.23.refs_3_) | copy-start | bytes 3981316
  188.7 3.1 collective-permute-start.27
  189.9 21.4 %copy-start.42 = (bf16[4,144,1152]{2,1,0:T(8,128)(2,1)}, bf16[4,144,1152]{2,1,0:T(8,128)(2,1)S(1)}, u32[]{:S(2)}) copy-start(bf16[4,144,1152]{2,1,0:T(8,128)(2,1)S(1)} %collective-permute-done.24.refs_4_) | copy-start | bytes 3981316
  211.4 10.1 %collective-permute-start.28 = (bf16[4,4,144,1152]{3,2,1,0:T(8,128)(2,1)}, bf16[4,4,144,1152]{3,2,1,0:T(8,128)(2,1)}, u32[]{:S(2)}, u32[]{:S(2)}) collective-permute-start(bf16[4,4,144,1152]{3,2,1,0:T(8,128)(2,1)} %get-tuple-element.102), channel_id=1, source_target_pairs={{0,4},{4,0},{8,12},{12,8},{16,20},{20,16},{24,28},{28,24},{1,5},{5... | collective-permute-start | bytes 15925256 | tf_op jit(solution)/shard_map/ppermute | solution.py:802
  228.1 33.0 %collective-permute-start.29 = (bf16[2,4,144,1152]{3,2,1,0:T(8,128)(2,1)}, bf16[2,4,144,1152]{3,2,1,0:T(8,128)(2,1)S(1)}, u32[]{:S(2)}, u32[]{:S(2)}) collective-permute-start(bf16[2,4,144,1152]{3,2,1,0:T(8,128)(2,1)} %get-tuple-element.103), channel_id=1, source_target_pairs={{0,16},{4,12},{8,24},{12,4},{16,0},{20,28},{24,8},{28,20},{1,17},{... | collective-permute-start | bytes 7962632 | tf_op jit(solution)/shard_map/ppermute | solution.py:798
  228.1 33.0 %copy-start.15 = (bf16[4,144,1152]{2,1,0:T(8,128)(2,1)S(1)}, bf16[4,144,1152]{2,1,0:T(8,128)(2,1)}, u32[]{:S(2)}) copy-start(bf16[4,144,1152]{2,1,0:T(8,128)(2,1)} %get-tuple-element.109) | copy-start | bytes 3981316
  261.1 25.0 %copy-start.7 = (bf16[2,4,144,1152]{3,2,1,0:T(8,128)(2,1)}, bf16[2,4,144,1152]{3,2,1,0:T(8,128)(2,1)S(1)}, u32[]{:S(2)}) copy-start(bf16[2,4,144,1152]{3,2,1,0:T(8,128)(2,1)S(1)} %collective-permute-done.29) | copy-start | bytes 7962628
  262.8 23.4 %collective-permute-start.30 = (bf16[4,144,1152]{2,1,0:T(8,128)(2,1)}, bf16[4,144,1152]{2,1,0:T(8,128)(2,1)S(1)}, u32[]{:S(2)}, u32[]{:S(2)}) collective-permute-start(bf16[4,144,1152]{2,1,0:T(8,128)(2,1)} %fusion.9), channel_id=1, source_target_pairs={{0,8},{4,20},{8,0},{12,28},{16,24},{20,4},{24,16},{28,12},{1,9},{5... | collective-permute-start | bytes 3981320 | tf_op jit(solution)/shard_map/ppermute | solution.py:798
  264.1 22.0 %copy-start.5 = (bf16[512,1152]{1,0:T(8,128)(2,1)S(1)}, bf16[512,1152]{1,0:T(8,128)(2,1)}, u32[]{:S(2)}) copy-start(bf16[512,1152]{1,0:T(8,128)(2,1)} %fusion.13.normed_ref) | copy-start | bytes 3538948
  303.3 9.1 %collective-permute-start.31 = (bf16[4,4,144,1152]{3,2,1,0:T(8,128)(2,1)}, bf16[4,4,144,1152]{3,2,1,0:T(8,128)(2,1)}, u32[]{:S(2)}, u32[]{:S(2)}) collective-permute-start(bf16[4,4,144,1152]{3,2,1,0:T(8,128)(2,1)} %get-tuple-element.119), channel_id=1, source_target_pairs={{0,4},{4,0},{8,12},{12,8},{16,20},{20,16},{24,28},{28,24},{1,5},{5... | collective-permute-start | bytes 15925256 | tf_op jit(solution)/shard_map/ppermute | solution.py:802
  319.4 32.3 %collective-permute-start.32 = (bf16[2,4,144,1152]{3,2,1,0:T(8,128)(2,1)}, bf16[2,4,144,1152]{3,2,1,0:T(8,128)(2,1)}, u32[]{:S(2)}, u32[]{:S(2)}) collective-permute-start(bf16[2,4,144,1152]{3,2,1,0:T(8,128)(2,1)} %get-tuple-element.120), channel_id=1, source_target_pairs={{0,16},{4,12},{8,24},{12,4},{16,0},{20,28},{24,8},{28,20},{1,17},{... | collective-permute-start | bytes 7962632 | tf_op jit(solution)/shard_map/ppermute | solution.py:798
  322.1 122.4 %reduce-scatter.6.cloned.1.call-start = ((), (), s32[]{:S(2)}) async-start(), calls=%async_computation.4 | async-start | bytes 1658880 | tf_op jit(solution)/shard_map/reduce_scatter | solution.py:851
  353.3 9.2 %collective-permute-start.33 = (bf16[4,4,144,1152]{3,2,1,0:T(8,128)(2,1)}, bf16[4,4,144,1152]{3,2,1,0:T(8,128)(2,1)}, u32[]{:S(2)}, u32[]{:S(2)}) collective-permute-start(bf16[4,4,144,1152]{3,2,1,0:T(8,128)(2,1)} %get-tuple-element.135), channel_id=1, source_target_pairs={{0,4},{4,0},{8,12},{12,8},{16,20},{20,16},{24,28},{28,24},{1,5},{5... | collective-permute-start | bytes 15925256 | tf_op jit(solution)/shard_map/ppermute | solution.py:802
  353.4 17.8 %collective-permute-start.34 = (bf16[4,144,1152]{2,1,0:T(8,128)(2,1)S(1)}, bf16[4,144,1152]{2,1,0:T(8,128)(2,1)S(1)}, u32[]{:S(2)}, u32[]{:S(2)}) collective-permute-start(bf16[4,144,1152]{2,1,0:T(8,128)(2,1)S(1)} %fusion.6), channel_id=1, source_target_pairs={{0,8},{4,20},{8,0},{12,28},{16,24},{20,4},{24,16},{28,12},{1,9},{5... | collective-permute-start | bytes 3981320 | tf_op jit(solution)/shard_map/ppermute | solution.py:798
  369.1 32.3 %collective-permute-start.39 = (bf16[2,4,144,1152]{3,2,1,0:T(8,128)(2,1)}, bf16[2,4,144,1152]{3,2,1,0:T(8,128)(2,1)}, u32[]{:S(2)}, u32[]{:S(2)}) collective-permute-start(bf16[2,4,144,1152]{3,2,1,0:T(8,128)(2,1)} %get-tuple-element.136), channel_id=1, source_target_pairs={{0,16},{4,12},{8,24},{12,4},{16,0},{20,28},{24,8},{28,20},{1,17},{... | collective-permute-start | bytes 7962632 | tf_op jit(solution)/shard_map/ppermute | solution.py:798
  374.2 84.8 %reduce-scatter.8.cloned.1.call-start = ((), (), s32[]{:S(2)}) async-start(), calls=%async_computation.5 | async-start | bytes 1658880 | tf_op jit(solution)/shard_map/reduce_scatter | solution.py:851
  374.2 27.2 %copy-start.12 = (bf16[4,144,1152]{2,1,0:T(8,128)(2,1)S(1)}, bf16[4,144,1152]{2,1,0:T(8,128)(2,1)}, u32[]{:S(2)}) copy-start(bf16[4,144,1152]{2,1,0:T(8,128)(2,1)} %get-tuple-element.142) | copy-start | bytes 3981316
  392.3 12.7 %collective-permute-start.35 = (bf16[2,2304]{1,0:T(2,128)(2,1)S(1)}, bf16[2,2304]{1,0:T(2,128)(2,1)S(1)}, u32[]{:S(2)}, u32[]{:S(2)}) collective-permute-start(bf16[2,2304]{1,0:T(2,128)(2,1)S(1)} %reshape.460), channel_id=1, source_target_pairs={{0,1},{1,0},{2,3},{3,2},{4,5},{5,4},{6,7},{7,6},{8,9},{9,8},{10,11... | collective-permute-start | bytes 27656 | tf_op jit(solution)/shard_map/ppermute | solution.py:856
  404.2 18.1 %collective-permute-start.40 = (bf16[4,144,1152]{2,1,0:T(8,128)(2,1)}, bf16[4,144,1152]{2,1,0:T(8,128)(2,1)}, u32[]{:S(2)}, u32[]{:S(2)}) collective-permute-start(bf16[4,144,1152]{2,1,0:T(8,128)(2,1)} %fusion.1), channel_id=1, source_target_pairs={{0,8},{4,20},{8,0},{12,28},{16,24},{20,4},{24,16},{28,12},{1,9},{5... | collective-permute-start | bytes 3981320 | tf_op jit(solution)/shard_map/ppermute | solution.py:798
  405.0 4.9 %collective-permute-start.36 = (bf16[4,2304]{1,0:T(4,128)(2,1)S(1)}, bf16[4,2304]{1,0:T(4,128)(2,1)S(1)}, u32[]{:S(2)}, u32[]{:S(2)}) collective-permute-start(bf16[4,2304]{1,0:T(4,128)(2,1)S(1)} %maximum_select_fusion.8), channel_id=1, source_target_pairs={{0,2},{1,3},{2,0},{3,1},{4,6},{5,7},{6,4},{7,5},{8,10},{9,11},{10,... | collective-permute-start | bytes 55304 | tf_op jit(solution)/shard_map/ppermute | solution.py:856
  410.5 5.3 %collective-permute-start.37 = (f32[290,128]{1,0:T(8,128)S(1)}, f32[290,128]{1,0:T(8,128)S(1)}, u32[]{:S(2)}, u32[]{:S(2)}) collective-permute-start(f32[290,128]{1,0:T(8,128)S(1)} %pad_maximum_fusion.2), channel_id=1, source_target_pairs={{0,1},{1,0},{2,3},{3,2},{4,5},{5,4},{6,7},{7,6},{8,9},{9,8},{10,11... | collective-permute-start | bytes 445448 | tf_op jit(solution)/shard_map/ppermute | solution.py:856
  415.8 11.5 %collective-permute-start.38 = (f32[290,128]{1,0:T(8,128)S(1)}, f32[290,128]{1,0:T(8,128)}, u32[]{:S(2)}, u32[]{:S(2)}) collective-permute-start(f32[290,128]{1,0:T(8,128)S(1)} %fusion.36), channel_id=1, source_target_pairs={{0,2},{1,3},{2,0},{3,1},{4,6},{5,7},{6,4},{7,5},{8,10},{9,11},{10,... | collective-permute-start | bytes 445448 | tf_op jit(solution)/shard_map/ppermute | solution.py:856
  427.2 15.0 %collective-permute-start.41 = (bf16[2,2,144,576]{3,2,1,0:T(8,128)(2,1)S(1)}, bf16[2,2,144,576]{3,2,1,0:T(8,128)(2,1)S(1)}, u32[]{:S(2)}, u32[]{:S(2)}) collective-permute-start(bf16[2,2,144,576]{3,2,1,0:T(8,128)(2,1)S(1)} %fusion.16), channel_id=1, source_target_pairs={{0,4},{4,0},{8,12},{12,8},{16,20},{20,16},{24,28},{28,24},{1,5},{5... | collective-permute-start | bytes 1990664 | tf_op jit(solution)/shard_map/ppermute | solution.py:856
  428.2 1.5 collective-permute-start.44
  429.8 5.5 %collective-permute-start.45 = (f32[218,128]{1,0:T(8,128)S(1)}, f32[218,128]{1,0:T(8,128)S(1)}, u32[]{:S(2)}, u32[]{:S(2)}) collective-permute-start(f32[218,128]{1,0:T(8,128)S(1)} %add.159), channel_id=1, source_target_pairs={{0,8},{4,12},{8,0},{12,4},{16,24},{20,28},{24,16},{28,20},{1,9},{5... | collective-permute-start | bytes 334856 | tf_op jit(solution)/shard_map/ppermute | solution.py:856
  435.3 4.9 %collective-permute-start.46 = (f32[218,128]{1,0:T(8,128)S(1)}, f32[218,128]{1,0:T(8,128)S(1)}, u32[]{:S(2)}, u32[]{:S(2)}) collective-permute-start(f32[218,128]{1,0:T(8,128)S(1)} %add.160), channel_id=1, source_target_pairs={{0,16},{4,20},{8,24},{12,28},{16,0},{20,4},{24,8},{28,12},{1,17},{... | collective-permute-start | bytes 334856 | tf_op jit(solution)/shard_map/ppermute | solution.py:856
  442.4 9.6 %collective-permute-start.42 = (bf16[2,144,576]{2,1,0:T(8,128)(2,1)S(1)}, bf16[2,144,576]{2,1,0:T(8,128)(2,1)S(1)}, u32[]{:S(2)}, u32[]{:S(2)}) collective-permute-start(bf16[2,144,576]{2,1,0:T(8,128)(2,1)S(1)} %fusion.19), channel_id=1, source_target_pairs={{0,8},{4,12},{8,0},{12,4},{16,24},{20,28},{24,16},{28,20},{1,9},{5... | collective-permute-start | bytes 995336 | tf_op jit(solution)/shard_map/ppermute | solution.py:856
  452.1 5.6 %collective-permute-start.43 = (bf16[144,576]{1,0:T(8,128)(2,1)S(1)}, bf16[144,576]{1,0:T(8,128)(2,1)S(1)}, u32[]{:S(2)}, u32[]{:S(2)}) collective-permute-start(bf16[144,576]{1,0:T(8,128)(2,1)S(1)} %select_bitcast_fusion), channel_id=1, source_target_pairs={{0,16},{4,20},{8,24},{12,28},{16,0},{20,4},{24,8},{28,12},{1,17},{... | collective-permute-start | bytes 497672 | tf_op jit(solution)/shard_map/ppermute | solution.py:856
  (36 other events, 397.2 us)
Sparse Core Ops, SparseCore 0:
  10.2 35.5 all-gather.6
  56.6 30.9 all-gather.10
  96.2 30.5 all-gather.8
  322.2 28.9 reduce-scatter.3
  374.3 30.1 reduce-scatter.5
  428.9 29.9 reduce-scatter.7
